TPU v7x, 32 devices: a whole 2x2x4 slice. The times are simulated.
32 devices in a mesh: clip: 4 (over x, core), seq: 8 (over z, y).
Axes of the slice: x: 2, y: 2, z: 4, core: 2. Of those that a mesh axis runs over, the one named last changes fastest.
Arguments:
- tokens: bfloat16 [8, 4096, 1024], P('clip', 'seq'), may hold values from -6 to 6
- ctx_count: int32 [8], P('clip'), may hold values from 1 to 15
- noise_level: int32 [8, 16], P('clip'), may hold values from 1 to 999
- mod_weight: bfloat16 [1024, 6144], P(('clip', 'seq')), may hold values from -0.1875 to 0.1875
- mod_bias: bfloat16 [6144], P(('clip', 'seq')), may hold values from -3 to 3
- qkv_weight: bfloat16 [1024, 3072], P(('clip', 'seq')), may hold values from -0.1875 to 0.1875
- qkv_bias: bfloat16 [3072], P(('clip', 'seq')), may hold values from -2 to 2
- out_weight: bfloat16 [1024, 1024], P(('clip', 'seq')), may hold values from -6 to 6
- out_bias: bfloat16 [1024], P(('clip', 'seq')), may hold values from -3 to 3
- up_weight: bfloat16 [1024, 4096], P(('clip', 'seq')), may hold values from -0.1875 to 0.1875
- up_bias: bfloat16 [4096], P(('clip', 'seq')), may hold values from -3 to 3
- down_weight: bfloat16 [4096, 1024], P(('clip', 'seq')), may hold values from -0.09375 to 0.09375
- down_bias: bfloat16 [1024], P(('clip', 'seq')), may hold values from -3 to 3
- cotangent: bfloat16 [8, 4096, 1024], P('clip', 'seq'), may hold values from -6 to 6
Outputs:
- output: bfloat16 [8, 4096, 1024], P('clip', 'seq')
- grad_tokens: float32 [8, 4096, 1024], P('clip', 'seq')
- grad_mod_weight: float32 [1024, 6144], P(('clip', 'seq'))
- grad_mod_bias: float32 [6144], P(('clip', 'seq'))
- grad_qkv_weight: float32 [1024, 3072], P(('clip', 'seq'))
- grad_qkv_bias: float32 [3072], P(('clip', 'seq'))
- grad_out_weight: float32 [1024, 1024], P(('clip', 'seq'))
- grad_out_bias: float32 [1024], P(('clip', 'seq'))
- grad_up_weight: float32 [1024, 4096], P(('clip', 'seq'))
- grad_up_bias: float32 [4096], P(('clip', 'seq'))
- grad_down_weight: float32 [4096, 1024], P(('clip', 'seq'))
- grad_down_bias: float32 [1024], P(('clip', 'seq'))
All inputs are finite; a program needn't handle non-finite values.
Results may differ from a plain program's by a relative error of at most 0.014.
The roundings to bfloat16 on the way count: a program that leaves them out, or rounds other values in their place, can miss the bound.
Values may be sent and summed in bfloat16 or wider, within the bound.
No kernel may reach another device: no remote copies, remote signals or barrier semaphores. Data moves between devices by JAX's collectives and lax.ppermute only.
A program may use at most 320 MiB of HBM per device.

v0:
```python
import math

import jax
import jax.numpy as jnp
from jax import lax
from jax.sharding import PartitionSpec as P

HEADS = 16
HEAD_DIM = 64
FRAMES = 16
PATCHES = 256
MICRO = 2
HEAD_GROUP = 2


highest = lax.Precision.HIGHEST


def layer_norm(values):
    centre = values - jnp.mean(values, axis=-1, keepdims=True)
    spread = jnp.mean(centre * centre, axis=-1, keepdims=True)
    return centre * lax.rsqrt(spread + 1e-06)


def modulate(values, shifts, scales):
    return layer_norm(values) * (1.0 + scales) + shifts


def level_embed(levels, embed_width):
    half_width = embed_width // 2
    freqs = jnp.exp(-math.log(10000.0) * jnp.arange(half_width, dtype=jnp.float32) / half_width)
    angles = levels.astype(jnp.float32)[..., None] * freqs
    return jnp.concatenate([jnp.sin(angles), jnp.cos(angles)], axis=-1)


def rotary_tables(positions):
    half_dim = HEAD_DIM // 2
    freqs = jnp.exp(-math.log(10000.0) * 2.0 * jnp.arange(half_dim, dtype=jnp.float32) / HEAD_DIM)
    angles = positions.astype(jnp.float32)[:, None] * freqs[None, :]
    return (jnp.cos(angles), jnp.sin(angles))


def rotate(values, cosine, sine):
    heads_view = values.reshape(values.shape[:-1] + (HEADS, HEAD_DIM))
    half_dim = HEAD_DIM // 2
    first_half = heads_view[..., :half_dim]
    second_half = heads_view[..., half_dim:]
    cos_part = cosine[:, None, :]
    sin_part = sine[:, None, :]
    turned = jnp.concatenate(
        [
            first_half * cos_part - second_half * sin_part,
            second_half * cos_part + first_half * sin_part,
        ],
        axis=-1,
    )
    return turned.reshape(values.shape)


def group_slice(array, first_col):
    group_span = HEAD_GROUP * HEAD_DIM
    picked = lax.dynamic_slice_in_dim(array, first_col, group_span, 2)
    return picked.reshape(array.shape[0], array.shape[1], HEAD_GROUP, HEAD_DIM)


def merge_groups(stacked):
    group_total, clip_count, row_count, group_span = stacked.shape
    return stacked.transpose(1, 2, 0, 3).reshape(clip_count, row_count, group_total * group_span)


def attend_forward(queries, keys_all, values_all, allowed):
    model_width = queries.shape[2]
    group_span = HEAD_GROUP * HEAD_DIM
    score_scale = 1.0 / math.sqrt(HEAD_DIM)

    def one_group(group_index):
        first_col = group_index * group_span
        query_group = group_slice(queries, first_col)
        key_group = group_slice(keys_all, first_col)
        value_group = group_slice(values_all, first_col)
        scores = (
            jnp.einsum(
                "cqhd,ckhd->chqk", query_group, key_group, preferred_element_type=jnp.float32
            )
            * score_scale
        )
        scores = jnp.where(allowed[None, None], scores, -1e30)
        peak = jnp.max(scores, axis=-1, keepdims=True)
        raised = jnp.exp(scores - peak)
        totals = jnp.sum(raised, axis=-1, keepdims=True)
        probs = (raised / totals).astype(jnp.bfloat16)
        mixed = jnp.einsum(
            "chqk,ckhd->cqhd", probs, value_group, preferred_element_type=jnp.float32
        )
        mixed = mixed.reshape(queries.shape[0], queries.shape[1], group_span)
        return (mixed, (peak + jnp.log(totals))[..., 0])

    mixed_all, log_totals = lax.map(one_group, jnp.arange(model_width // group_span))
    return (merge_groups(mixed_all), log_totals)


def attend_backward(queries, keys_all, values_all, d_mixed, log_totals, allowed):
    clip_count, row_count, model_width = queries.shape
    seq_total = keys_all.shape[1]
    group_span = HEAD_GROUP * HEAD_DIM
    score_scale = 1.0 / math.sqrt(HEAD_DIM)

    def one_group(pieces):
        group_index, log_group = pieces
        first_col = group_index * group_span
        query_group = group_slice(queries, first_col)
        key_group = group_slice(keys_all, first_col)
        value_group = group_slice(values_all, first_col)
        d_group = group_slice(d_mixed, first_col)
        scores = (
            jnp.einsum(
                "cqhd,ckhd->chqk", query_group, key_group, preferred_element_type=jnp.float32
            )
            * score_scale
        )
        scores = jnp.where(allowed[None, None], scores, -1e30)
        probs = jnp.exp(scores - log_group[..., None])
        d_probs = jnp.einsum(
            "cqhd,ckhd->chqk", d_group, value_group, preferred_element_type=jnp.float32
        )
        centre = jnp.sum(probs * d_probs, axis=-1, keepdims=True)
        d_scores = (probs * (d_probs - centre)).astype(jnp.bfloat16)
        d_query = (
            jnp.einsum("chqk,ckhd->cqhd", d_scores, key_group, preferred_element_type=jnp.float32)
            * score_scale
        )
        d_key_term = (
            jnp.einsum("chqk,cqhd->ckhd", d_scores, query_group, preferred_element_type=jnp.float32)
            * score_scale
        )
        d_value_term = jnp.einsum(
            "chqk,cqhd->ckhd",
            probs.astype(jnp.bfloat16),
            d_group,
            preferred_element_type=jnp.float32,
        )
        d_key, d_value = (
            lax.psum_scatter(
                d_key_term.reshape(clip_count, seq_total, group_span).astype(jnp.bfloat16),
                "seq",
                scatter_dimension=1,
                tiled=True,
            ).astype(jnp.float32),
            lax.psum_scatter(
                d_value_term.reshape(clip_count, seq_total, group_span).astype(jnp.bfloat16),
                "seq",
                scatter_dimension=1,
                tiled=True,
            ).astype(jnp.float32),
        )
        return (d_query.reshape(clip_count, row_count, group_span), d_key, d_value)

    d_query_all, d_key_all, d_value_all = lax.map(
        one_group, (jnp.arange(model_width // group_span), log_totals)
    )
    return (merge_groups(d_query_all), merge_groups(d_key_all), merge_groups(d_value_all))


def body(
    tokens,
    ctx_count,
    noise_level,
    mod_weight,
    mod_bias,
    qkv_weight,
    qkv_bias,
    out_weight,
    out_bias,
    up_weight,
    up_bias,
    down_weight,
    down_bias,
    cotangent,
):
    shards = (
        mod_weight,
        mod_bias,
        qkv_weight,
        qkv_bias,
        out_weight,
        out_bias,
        up_weight,
        up_bias,
        down_weight,
        down_bias,
    )
    clip_total, row_count, model_width = tokens.shape
    clips_micro = clip_total // MICRO
    seq_devices = lax.axis_size("seq")
    seq_total = row_count * seq_devices
    device_count = lax.axis_size("clip") * seq_devices
    positions = lax.axis_index("seq") * row_count + jnp.arange(row_count, dtype=jnp.int32)
    token_frame = positions // PATCHES
    frame_table = (token_frame[:, None] == jnp.arange(FRAMES, dtype=jnp.int32)[None, :]).astype(
        jnp.float32
    )
    key_frame = jnp.arange(seq_total, dtype=jnp.int32) // PATCHES
    allowed = key_frame[None, :] <= token_frame[:, None]
    cosine, sine = rotary_tables(positions)

    def turn(values):
        return rotate(values, cosine, sine)

    grads = [
        jnp.zeros((piece.shape[0] * device_count,) + piece.shape[1:], jnp.float32)
        for piece in shards
    ]
    outputs_all = []
    inputs_grad = []
    for batch_index in range(MICRO):
        first_clip = batch_index * clips_micro
        last_clip = first_clip + clips_micro
        gathered = (
            lax.all_gather(mod_weight, ("clip", "seq"), axis=0, tiled=True),
            lax.all_gather(mod_bias, ("clip", "seq"), axis=0, tiled=True),
            lax.all_gather(qkv_weight, ("clip", "seq"), axis=0, tiled=True),
            lax.all_gather(qkv_bias, ("clip", "seq"), axis=0, tiled=True),
            lax.all_gather(out_weight, ("clip", "seq"), axis=0, tiled=True),
            lax.all_gather(out_bias, ("clip", "seq"), axis=0, tiled=True),
            lax.all_gather(up_weight, ("clip", "seq"), axis=0, tiled=True),
            lax.all_gather(up_bias, ("clip", "seq"), axis=0, tiled=True),
            lax.all_gather(down_weight, ("clip", "seq"), axis=0, tiled=True),
            lax.all_gather(down_bias, ("clip", "seq"), axis=0, tiled=True),
        )
        (
            full_mod_weight,
            full_mod_bias,
            full_qkv_weight,
            full_qkv_bias,
            full_out_weight,
            full_out_bias,
            full_up_weight,
            full_up_bias,
            full_down_weight,
            full_down_bias,
        ) = gathered
        tokens_now = tokens[first_clip:last_clip].astype(jnp.float32)
        contexts = ctx_count[first_clip:last_clip]
        noises = noise_level[first_clip:last_clip]
        levels = jnp.where(
            jnp.arange(FRAMES, dtype=jnp.int32)[None, :] < contexts[:, None], 0, noises
        )
        cond_low = jax.nn.silu(level_embed(levels, model_width)).astype(jnp.bfloat16)
        modulation = jnp.einsum(
            "cfd,de->cfe", cond_low, full_mod_weight, preferred_element_type=jnp.float32
        ) + full_mod_bias.astype(jnp.float32)
        per_token = jnp.einsum("rf,cfe->cre", frame_table, modulation, precision=highest)
        shift_one, scale_one, gate_one, shift_two, scale_two, gate_two = jnp.split(
            per_token, 6, axis=-1
        )
        normed_full, norm_back_one = jax.vjp(modulate, tokens_now, shift_one, scale_one)
        normed = normed_full.astype(jnp.bfloat16)
        projected = jnp.einsum(
            "crd,de->cre", normed, full_qkv_weight, preferred_element_type=jnp.float32
        ) + full_qkv_bias.astype(jnp.float32)
        query_raw, key_raw, value_raw = jnp.split(projected, 3, axis=-1)
        queries = turn(query_raw).astype(jnp.bfloat16)
        keys_local = turn(key_raw).astype(jnp.bfloat16)
        values_local = value_raw.astype(jnp.bfloat16)
        keys_all, values_all = (
            lax.all_gather(keys_local, "seq", axis=1, tiled=True),
            lax.all_gather(values_local, "seq", axis=1, tiled=True),
        )
        mixed_full, log_totals = attend_forward(queries, keys_all, values_all, allowed)
        mixed = mixed_full.astype(jnp.bfloat16)
        attn_out = jnp.einsum(
            "crd,de->cre", mixed, full_out_weight, preferred_element_type=jnp.float32
        ) + full_out_bias.astype(jnp.float32)
        resid = tokens_now + gate_one * attn_out
        normed_two_full, norm_back_two = jax.vjp(modulate, resid, shift_two, scale_two)
        normed_two = normed_two_full.astype(jnp.bfloat16)
        hidden = jnp.einsum(
            "crd,df->crf", normed_two, full_up_weight, preferred_element_type=jnp.float32
        ) + full_up_bias.astype(jnp.float32)
        active_full, gelu_back = jax.vjp(jax.nn.gelu, hidden)
        active = active_full.astype(jnp.bfloat16)
        mlp_out = jnp.einsum(
            "crf,fd->crd", active, full_down_weight, preferred_element_type=jnp.float32
        ) + full_down_bias.astype(jnp.float32)
        outputs_all.append((resid + gate_two * mlp_out).astype(jnp.bfloat16))
        gathered = (
            lax.all_gather(mod_weight, ("clip", "seq"), axis=0, tiled=True),
            lax.all_gather(mod_bias, ("clip", "seq"), axis=0, tiled=True),
            lax.all_gather(qkv_weight, ("clip", "seq"), axis=0, tiled=True),
            lax.all_gather(qkv_bias, ("clip", "seq"), axis=0, tiled=True),
            lax.all_gather(out_weight, ("clip", "seq"), axis=0, tiled=True),
            lax.all_gather(out_bias, ("clip", "seq"), axis=0, tiled=True),
            lax.all_gather(up_weight, ("clip", "seq"), axis=0, tiled=True),
            lax.all_gather(up_bias, ("clip", "seq"), axis=0, tiled=True),
            lax.all_gather(down_weight, ("clip", "seq"), axis=0, tiled=True),
            lax.all_gather(down_bias, ("clip", "seq"), axis=0, tiled=True),
        )
        (
            full_mod_weight,
            full_mod_bias,
            full_qkv_weight,
            full_qkv_bias,
            full_out_weight,
            full_out_bias,
            full_up_weight,
            full_up_bias,
            full_down_weight,
            full_down_bias,
        ) = gathered
        grad_out = cotangent[first_clip:last_clip].astype(jnp.float32)
        d_mlp = (gate_two * grad_out).astype(jnp.bfloat16)
        grads[8] = grads[8] + jnp.einsum(
            "crf,crd->fd", active, d_mlp, preferred_element_type=jnp.float32
        )
        grads[9] = grads[9] + jnp.sum(d_mlp.astype(jnp.float32), axis=(0, 1))
        d_active = jnp.einsum(
            "crd,fd->crf", d_mlp, full_down_weight, preferred_element_type=jnp.float32
        )
        d_hidden = gelu_back(d_active)[0].astype(jnp.bfloat16)
        grads[6] = grads[6] + jnp.einsum(
            "crd,crf->df", normed_two, d_hidden, preferred_element_type=jnp.float32
        )
        grads[7] = grads[7] + jnp.sum(d_hidden.astype(jnp.float32), axis=(0, 1))
        d_normed_two = jnp.einsum(
            "crf,df->crd", d_hidden, full_up_weight, preferred_element_type=jnp.float32
        )
        d_resid_norm, d_shift_two, d_scale_two = norm_back_two(d_normed_two)
        d_resid = grad_out + d_resid_norm
        d_attn = (gate_one * d_resid).astype(jnp.bfloat16)
        grads[4] = grads[4] + jnp.einsum(
            "crd,cre->de", mixed, d_attn, preferred_element_type=jnp.float32
        )
        grads[5] = grads[5] + jnp.sum(d_attn.astype(jnp.float32), axis=(0, 1))
        d_mixed = jnp.einsum(
            "cre,de->crd", d_attn, full_out_weight, preferred_element_type=jnp.float32
        ).astype(jnp.bfloat16)
        keys_all, values_all = (
            lax.all_gather(keys_local, "seq", axis=1, tiled=True),
            lax.all_gather(values_local, "seq", axis=1, tiled=True),
        )
        d_query, d_key, d_value = attend_backward(
            queries, keys_all, values_all, d_mixed, log_totals, allowed
        )
        unused_rot, turn_back = jax.vjp(turn, query_raw)
        d_projected = jnp.concatenate(
            [turn_back(d_query)[0], turn_back(d_key)[0], d_value], axis=-1
        ).astype(jnp.bfloat16)
        grads[2] = grads[2] + jnp.einsum(
            "crd,cre->de", normed, d_projected, preferred_element_type=jnp.float32
        )
        grads[3] = grads[3] + jnp.sum(d_projected.astype(jnp.float32), axis=(0, 1))
        d_normed = jnp.einsum(
            "cre,de->crd", d_projected, full_qkv_weight, preferred_element_type=jnp.float32
        )
        d_tokens_norm, d_shift_one, d_scale_one = norm_back_one(d_normed)
        inputs_grad.append(d_resid + d_tokens_norm)
        d_per_token = jnp.concatenate(
            [
                d_shift_one,
                d_scale_one,
                d_resid * attn_out,
                d_shift_two,
                d_scale_two,
                grad_out * mlp_out,
            ],
            axis=-1,
        )
        d_modulation = jnp.einsum("rf,cre->cfe", frame_table, d_per_token, precision=highest)
        grads[0] = grads[0] + jnp.einsum(
            "cfd,cfe->de", cond_low.astype(jnp.float32), d_modulation, precision=highest
        )
        grads[1] = grads[1] + jnp.sum(d_modulation, axis=(0, 1))
    summed = (
        lax.psum_scatter(grads[0], ("clip", "seq"), scatter_dimension=0, tiled=True),
        lax.psum_scatter(grads[1], ("clip", "seq"), scatter_dimension=0, tiled=True),
        lax.psum_scatter(grads[2], ("clip", "seq"), scatter_dimension=0, tiled=True),
        lax.psum_scatter(grads[3], ("clip", "seq"), scatter_dimension=0, tiled=True),
        lax.psum_scatter(grads[4], ("clip", "seq"), scatter_dimension=0, tiled=True),
        lax.psum_scatter(grads[5], ("clip", "seq"), scatter_dimension=0, tiled=True),
        lax.psum_scatter(grads[6], ("clip", "seq"), scatter_dimension=0, tiled=True),
        lax.psum_scatter(grads[7], ("clip", "seq"), scatter_dimension=0, tiled=True),
        lax.psum_scatter(grads[8], ("clip", "seq"), scatter_dimension=0, tiled=True),
        lax.psum_scatter(grads[9], ("clip", "seq"), scatter_dimension=0, tiled=True),
    )
    output = jnp.concatenate(outputs_all, axis=0)
    grad_tokens = jnp.concatenate(inputs_grad, axis=0)
    return (output, grad_tokens) + tuple(summed)


def solution(mesh):
    placed = (
        P("clip", "seq", None),
        P("clip"),
        P("clip", None),
        P(("clip", "seq"), None),
        P(("clip", "seq")),
        P(("clip", "seq"), None),
        P(("clip", "seq")),
        P(("clip", "seq"), None),
        P(("clip", "seq")),
        P(("clip", "seq"), None),
        P(("clip", "seq")),
        P(("clip", "seq"), None),
        P(("clip", "seq")),
        P("clip", "seq", None),
    )
    return jax.shard_map(
        body,
        mesh=mesh,
        in_specs=placed,
        out_specs=(
            P("clip", "seq", None),
            P("clip", "seq", None),
            P(("clip", "seq"), None),
            P(("clip", "seq")),
            P(("clip", "seq"), None),
            P(("clip", "seq")),
            P(("clip", "seq"), None),
            P(("clip", "seq")),
            P(("clip", "seq"), None),
            P(("clip", "seq")),
            P(("clip", "seq"), None),
            P(("clip", "seq")),
        ),
        check_vma=False,
    )
```

profile of v0, /device:TPU:0, one launch (start us, length us, event | category | flops | bytes accessed | tf_op | source)
XLA Modules:
  0.0 5283.1 jit_solution(6095283720630056380)
XLA Ops:
  224.4 66.4 %all-gather = bf16[32,1,128]{2,1,0:T(2,128)(2,1)S(1)} all-gather(bf16[1,1,128]{2,1,0:T(2,128)(2,1)S(1)} %bitcast.527), channel_id=1, replica_groups=mesh['clip'=4,'seq'=8] {'clip','seq'}, dimensions={0}, use_global_device_ids=true | all-gather | bytes 8448 | tf_op jit(solution)/shard_map/all_gather | solution.py:226
  326.9 113.8 %all-gather.17.cloned.1.call-done = bf16[1,4096,1024]{1,2,0:T(8,128)(2,1)} async-done(((bf16[1,512,1024]{1,2,0:T(8,128)(2,1)}), bf16[1,4096,1024]{1,2,0:T(8,128)(2,1)}) %all-gather.17.cloned.1.call-update) | async-done | bytes 8388624 | tf_op jit(solution)/shard_map/all_gather | solution.py:266
  440.7 147.5 %while.56 = (s32[]{:T(128)}, bf16[8,1,512,128]{2,3,1,0:T(8,128)(2,1)S(1)}, f32[8,1,2,512]{3,2,1,0:T(2,128)S(1)}, s32[8]{0:T(128)S(1)}, bf16[1,4096,1024]{1,2,0:T...) while((s32[]{:T(128)}, ...), condition=%wide.region_5.6_spmd.clone, body=%wide.region_2.5_spmd.clone.sunk | while | flops 1126169600 | bytes 65849544 | solution.py:98
  703.3 1388.7 %while.58 = (s32[]{:T(128)}, f32[8,1,512,128]{2,3,1,0:T(8,128)}, f32[8,1,512,128]{2,3,1,0:T(8,128)}, bf16[8,1,512,128]{2,3,1,0:T(8,128)(2,1)}, s32[8]{0:T(128)S(...) while((s32[]{:T(128)}, f32[8,1,512,128]{2,3,1,0:T(8,128)}, ...), condition=%wide.region_22.23_spmd.clone, body=%wide.region_18.22_spmd.clone.sunk | while | flops 2751134720 | bytes 195606928 | solution.py:158
  810.3 65.0 %reduce-scatter.22.cloned.1.call-done = bf16[1,512,128]{1,2,0:T(8,128)(2,1)} async-done(((bf16[1,4096,128]{1,2,0:T(8,128)(2,1)}), bf16[1,512,128]{1,2,0:T(8,128)(2,1)}) %reduce-scatter.22.cloned.1.call-update) | async-done | bytes 131088 | tf_op jit(solution)/shard_map/while/body/eval_jaxpr/reduce_scatter | solution.py:149
  983.9 65.1 %reduce-scatter.22.cloned.1.call-done = bf16[1,512,128]{1,2,0:T(8,128)(2,1)} async-done(((bf16[1,4096,128]{1,2,0:T(8,128)(2,1)}), bf16[1,512,128]{1,2,0:T(8,128)(2,1)}) %reduce-scatter.22.cloned.1.call-update) | async-done | bytes 131088 | tf_op jit(solution)/shard_map/while/body/eval_jaxpr/reduce_scatter | solution.py:149
  1157.6 65.1 %reduce-scatter.22.cloned.1.call-done = bf16[1,512,128]{1,2,0:T(8,128)(2,1)} async-done(((bf16[1,4096,128]{1,2,0:T(8,128)(2,1)}), bf16[1,512,128]{1,2,0:T(8,128)(2,1)}) %reduce-scatter.22.cloned.1.call-update) | async-done | bytes 131088 | tf_op jit(solution)/shard_map/while/body/eval_jaxpr/reduce_scatter | solution.py:149
  1678.1 65.0 %reduce-scatter.22.cloned.1.call-done = bf16[1,512,128]{1,2,0:T(8,128)(2,1)} async-done(((bf16[1,4096,128]{1,2,0:T(8,128)(2,1)}), bf16[1,512,128]{1,2,0:T(8,128)(2,1)}) %reduce-scatter.22.cloned.1.call-update) | async-done | bytes 131088 | tf_op jit(solution)/shard_map/while/body/eval_jaxpr/reduce_scatter | solution.py:149
  1851.5 65.1 %reduce-scatter.22.cloned.1.call-done = bf16[1,512,128]{1,2,0:T(8,128)(2,1)} async-done(((bf16[1,4096,128]{1,2,0:T(8,128)(2,1)}), bf16[1,512,128]{1,2,0:T(8,128)(2,1)}) %reduce-scatter.22.cloned.1.call-update) | async-done | bytes 131088 | tf_op jit(solution)/shard_map/while/body/eval_jaxpr/reduce_scatter | solution.py:149
  2025.2 65.1 %reduce-scatter.22.cloned.1.call-done = bf16[1,512,128]{1,2,0:T(8,128)(2,1)} async-done(((bf16[1,4096,128]{1,2,0:T(8,128)(2,1)}), bf16[1,512,128]{1,2,0:T(8,128)(2,1)}) %reduce-scatter.22.cloned.1.call-update) | async-done | bytes 131088 | tf_op jit(solution)/shard_map/while/body/eval_jaxpr/reduce_scatter | solution.py:149
  2111.8 106.8 %all-gather.25.cloned.1.call-done = bf16[1,4096,1024]{2,1,0:T(8,128)(2,1)} async-done(((bf16[1,512,1024]{2,1,0:T(8,128)(2,1)}), bf16[1,4096,1024]{2,1,0:T(8,128)(2,1)}) %all-gather.25.cloned.1.call-update) | async-done | bytes 8388624 | tf_op jit(solution)/shard_map/all_gather | solution.py:267
  2253.7 91.2 %all-gather.27.cloned.1.call-done = bf16[1,4096,1024]{1,2,0:T(8,128)(2,1)} async-done(((bf16[1,512,1024]{1,2,0:T(8,128)(2,1)}), bf16[1,4096,1024]{1,2,0:T(8,128)(2,1)}) %all-gather.27.cloned.1.call-update) | async-done | bytes 8388624 | tf_op jit(solution)/shard_map/all_gather | solution.py:266
  2345.0 171.3 %while.57 = (s32[]{:T(128)}, bf16[8,1,512,128]{2,3,1,0:T(8,128)(2,1)S(1)}, f32[8,1,2,512]{3,2,1,0:T(2,128)S(1)}, s32[8]{0:T(128)S(1)}, bf16[1,4096,1024]{1,2,0:T...) while((s32[]{:T(128)}, ...), condition=%wide.region_13.14_spmd.clone, body=%wide.region_10.13_spmd.clone.sunk | while | flops 1126169600 | bytes 65849544 | solution.py:98
  2598.6 1399.1 %while.59 = (s32[]{:T(128)}, f32[8,1,512,128]{2,3,1,0:T(8,128)}, f32[8,1,512,128]{2,3,1,0:T(8,128)}, bf16[8,1,512,128]{2,3,1,0:T(8,128)(2,1)}, s32[8]{0:T(128)S(...) while((s32[]{:T(128)}, f32[8,1,512,128]{2,3,1,0:T(8,128)}, ...), condition=%wide.region_31.32_spmd.clone, body=%wide.region_27.31_spmd.clone.sunk | while | flops 2751134720 | bytes 195606928 | solution.py:158
  2706.3 65.0 %reduce-scatter.26.cloned.1.call-done = bf16[1,512,128]{1,2,0:T(8,128)(2,1)} async-done(((bf16[1,4096,128]{1,2,0:T(8,128)(2,1)}), bf16[1,512,128]{1,2,0:T(8,128)(2,1)}) %reduce-scatter.26.cloned.1.call-update) | async-done | bytes 131088 | tf_op jit(solution)/shard_map/while/body/eval_jaxpr/reduce_scatter | solution.py:149
  2881.2 65.1 %reduce-scatter.26.cloned.1.call-done = bf16[1,512,128]{1,2,0:T(8,128)(2,1)} async-done(((bf16[1,4096,128]{1,2,0:T(8,128)(2,1)}), bf16[1,512,128]{1,2,0:T(8,128)(2,1)}) %reduce-scatter.26.cloned.1.call-update) | async-done | bytes 131088 | tf_op jit(solution)/shard_map/while/body/eval_jaxpr/reduce_scatter | solution.py:149
  3056.3 65.1 %reduce-scatter.26.cloned.1.call-done = bf16[1,512,128]{1,2,0:T(8,128)(2,1)} async-done(((bf16[1,4096,128]{1,2,0:T(8,128)(2,1)}), bf16[1,512,128]{1,2,0:T(8,128)(2,1)}) %reduce-scatter.26.cloned.1.call-update) | async-done | bytes 131088 | tf_op jit(solution)/shard_map/while/body/eval_jaxpr/reduce_scatter | solution.py:149
  3406.1 65.1 %reduce-scatter.26.cloned.1.call-done = bf16[1,512,128]{1,2,0:T(8,128)(2,1)} async-done(((bf16[1,4096,128]{1,2,0:T(8,128)(2,1)}), bf16[1,512,128]{1,2,0:T(8,128)(2,1)}) %reduce-scatter.26.cloned.1.call-update) | async-done | bytes 131088 | tf_op jit(solution)/shard_map/while/body/eval_jaxpr/reduce_scatter | solution.py:149
  3581.0 65.0 %reduce-scatter.26.cloned.1.call-done = bf16[1,512,128]{1,2,0:T(8,128)(2,1)} async-done(((bf16[1,4096,128]{1,2,0:T(8,128)(2,1)}), bf16[1,512,128]{1,2,0:T(8,128)(2,1)}) %reduce-scatter.26.cloned.1.call-update) | async-done | bytes 131088 | tf_op jit(solution)/shard_map/while/body/eval_jaxpr/reduce_scatter | solution.py:149
  3930.7 65.0 %reduce-scatter.26.cloned.1.call-done = bf16[1,512,128]{1,2,0:T(8,128)(2,1)} async-done(((bf16[1,4096,128]{1,2,0:T(8,128)(2,1)}), bf16[1,512,128]{1,2,0:T(8,128)(2,1)}) %reduce-scatter.26.cloned.1.call-update) | async-done | bytes 131088 | tf_op jit(solution)/shard_map/while/body/eval_jaxpr/reduce_scatter | solution.py:149
  4208.6 94.8 %reduce-scatter.12.cloned.1.call-done = f32[32,3072]{1,0:T(8,128)} async-done(((f32[1024,3072]{1,0:T(8,128)}), f32[32,3072]{1,0:T(8,128)}) %reduce-scatter.12.cloned.1.call-update) | async-done | bytes 393232 | tf_op jit(solution)/shard_map/reduce_scatter | solution.py:376
  4303.3 360.2 %reduce-scatter.18.cloned.1.call-done = f32[128,1024]{1,0:T(8,128)} async-done(((f32[4096,1024]{1,0:T(8,128)}), f32[128,1024]{1,0:T(8,128)}) %reduce-scatter.18.cloned.1.call-update) | async-done | bytes 524304 | tf_op jit(solution)/shard_map/reduce_scatter | solution.py:382
  4663.5 360.2 %reduce-scatter.16.cloned.1.call-done = f32[32,4096]{1,0:T(8,128)} async-done(((f32[1024,4096]{1,0:T(8,128)}), f32[32,4096]{1,0:T(8,128)}) %reduce-scatter.16.cloned.1.call-update) | async-done | bytes 524304 | tf_op jit(solution)/shard_map/reduce_scatter | solution.py:380
  5023.6 252.7 %reduce-scatter.10.cloned.1.call-done = f32[32,6144]{1,0:T(8,128)} async-done(((f32[1024,6144]{1,0:T(8,128)}), f32[32,6144]{1,0:T(8,128)}) %reduce-scatter.10.cloned.1.call-update) | async-done | bytes 786448 | tf_op jit(solution)/shard_map/reduce_scatter | solution.py:374
  (1016 shorter events, 3015.8 us)
Async XLA Ops:
  7.9 173.4 %all-gather.13.cloned.1.call-start = ((), (), s32[]{:S(2)}) async-start(), calls=%async_computation.10 | async-start | bytes 6488064 | tf_op jit(solution)/shard_map/all_gather | solution.py:221
  8.7 305.9 %all-gather.15.cloned.1.call-start = ((), (), s32[]{:S(2)}) async-start(), calls=%async_computation.11 | async-start | bytes 9437184 | tf_op jit(solution)/shard_map/all_gather | solution.py:267
  190.7 249.9 %all-gather.17.cloned.1.call-start = ((), (), s32[]{:S(2)}) async-start(), calls=%async_computation.12 | async-start | bytes 9437184 | tf_op jit(solution)/shard_map/all_gather | solution.py:266
  215.8 372.5 %all-gather.19.cloned.1.call-start = ((), (), s32[]{:S(2)}) async-start(), calls=%async_computation.13 | async-start | bytes 2162688 | tf_op jit(solution)/shard_map/all_gather | solution.py:223
  216.3 382.8 %all-gather.21.cloned.1.call-start = ((), (), s32[]{:S(2)}) async-start(), calls=%async_computation.14 | async-start | bytes 8650752 | tf_op jit(solution)/shard_map/all_gather | solution.py:225
  216.9 439.6 %all-gather.23.cloned.1.call-start = ((), (), s32[]{:S(2)}) async-start(), calls=%async_computation.15 | async-start | bytes 8650752 | tf_op jit(solution)/shard_map/all_gather | solution.py:227
  919.3 129.7 %reduce-scatter.22.cloned.1.call-start = ((), (), s32[]{:S(2)}) async-start(), calls=%async_computation.24 | async-start | bytes 1179648 | tf_op jit(solution)/shard_map/while/body/eval_jaxpr/reduce_scatter | solution.py:149
  1092.9 129.8 %reduce-scatter.22.cloned.1.call-start = ((), (), s32[]{:S(2)}) async-start(), calls=%async_computation.24 | async-start | bytes 1179648 | tf_op jit(solution)/shard_map/while/body/eval_jaxpr/reduce_scatter | solution.py:149
  1613.5 129.6 %reduce-scatter.22.cloned.1.call-start = ((), (), s32[]{:S(2)}) async-start(), calls=%async_computation.24 | async-start | bytes 1179648 | tf_op jit(solution)/shard_map/while/body/eval_jaxpr/reduce_scatter | solution.py:149
  1787.0 129.7 %reduce-scatter.22.cloned.1.call-start = ((), (), s32[]{:S(2)}) async-start(), calls=%async_computation.24 | async-start | bytes 1179648 | tf_op jit(solution)/shard_map/while/body/eval_jaxpr/reduce_scatter | solution.py:149
  1960.5 129.8 %reduce-scatter.22.cloned.1.call-start = ((), (), s32[]{:S(2)}) async-start(), calls=%async_computation.24 | async-start | bytes 1179648 | tf_op jit(solution)/shard_map/while/body/eval_jaxpr/reduce_scatter | solution.py:149
  2092.6 252.3 %all-gather.27.cloned.1.call-start = ((), (), s32[]{:S(2)}) async-start(), calls=%async_computation.17 | async-start | bytes 9437184 | tf_op jit(solution)/shard_map/all_gather | solution.py:266
  2816.5 129.7 %reduce-scatter.26.cloned.1.call-start = ((), (), s32[]{:S(2)}) async-start(), calls=%async_computation.26 | async-start | bytes 1179648 | tf_op jit(solution)/shard_map/while/body/eval_jaxpr/reduce_scatter | solution.py:149
  2991.5 129.9 %reduce-scatter.26.cloned.1.call-start = ((), (), s32[]{:S(2)}) async-start(), calls=%async_computation.26 | async-start | bytes 1179648 | tf_op jit(solution)/shard_map/while/body/eval_jaxpr/reduce_scatter | solution.py:149
  3166.6 129.5 %reduce-scatter.26.cloned.1.call-start = ((), (), s32[]{:S(2)}) async-start(), calls=%async_computation.26 | async-start | bytes 1179648 | tf_op jit(solution)/shard_map/while/body/eval_jaxpr/reduce_scatter | solution.py:149
  3341.4 129.7 %reduce-scatter.26.cloned.1.call-start = ((), (), s32[]{:S(2)}) async-start(), calls=%async_computation.26 | async-start | bytes 1179648 | tf_op jit(solution)/shard_map/while/body/eval_jaxpr/reduce_scatter | solution.py:149
  3516.4 129.6 %reduce-scatter.26.cloned.1.call-start = ((), (), s32[]{:S(2)}) async-start(), calls=%async_computation.26 | async-start | bytes 1179648 | tf_op jit(solution)/shard_map/while/body/eval_jaxpr/reduce_scatter | solution.py:149
  3691.2 129.5 %reduce-scatter.26.cloned.1.call-start = ((), (), s32[]{:S(2)}) async-start(), calls=%async_computation.26 | async-start | bytes 1179648 | tf_op jit(solution)/shard_map/while/body/eval_jaxpr/reduce_scatter | solution.py:149
  3866.0 129.7 %reduce-scatter.26.cloned.1.call-start = ((), (), s32[]{:S(2)}) async-start(), calls=%async_computation.26 | async-start | bytes 1179648 | tf_op jit(solution)/shard_map/while/body/eval_jaxpr/reduce_scatter | solution.py:149
  3997.8 210.8 %reduce-scatter.14.cloned.1.call-start = ((), (), s32[]{:S(2)}) async-start(), calls=%async_computation.20 | async-start | bytes 4325376 | tf_op jit(solution)/shard_map/reduce_scatter | solution.py:378
  3998.5 304.8 %reduce-scatter.12.cloned.1.call-start = ((), (), s32[]{:S(2)}) async-start(), calls=%async_computation.19 | async-start | bytes 12976128 | tf_op jit(solution)/shard_map/reduce_scatter | solution.py:376
  4018.2 645.3 %reduce-scatter.18.cloned.1.call-start = ((), (), s32[]{:S(2)}) async-start(), calls=%async_computation.22 | async-start | bytes 17301504 | tf_op jit(solution)/shard_map/reduce_scatter | solution.py:382
  4050.3 973.4 %reduce-scatter.16.cloned.1.call-start = ((), (), s32[]{:S(2)}) async-start(), calls=%async_computation.21 | async-start | bytes 17301504 | tf_op jit(solution)/shard_map/reduce_scatter | solution.py:380
  4075.4 1200.9 %reduce-scatter.10.cloned.1.call-start = ((), (), s32[]{:S(2)}) async-start(), calls=%async_computation.18 | async-start | bytes 25952256 | tf_op jit(solution)/shard_map/reduce_scatter | solution.py:374
  (195 other events, 7916.1 us)
Sparse Core Ops, SparseCore 0:
  10.9 99.6 all-gather.10
  113.5 67.7 all-gather.12
  190.9 123.6 all-gather.14
  317.1 123.5 all-gather.16
  501.1 76.4 all-gather.20
  580.6 75.8 all-gather.22
  1093.0 62.9 reduce-scatter.19
  1159.7 62.9 reduce-scatter.21
  1853.7 62.8 reduce-scatter.21
  1960.7 62.9 reduce-scatter.19
  2094.7 123.9 all-gather.24
  2221.3 123.5 all-gather.26
  2708.3 62.9 reduce-scatter.25
  2816.6 62.8 reduce-scatter.23
  2991.6 62.9 reduce-scatter.23
  3058.4 62.9 reduce-scatter.25
  3408.2 62.8 reduce-scatter.25
  3583.0 62.8 reduce-scatter.25
  3866.1 62.8 reduce-scatter.23
  4001.5 143.1 reduce-scatter.13
  4151.1 152.1 reduce-scatter.11
  4306.3 357.1 reduce-scatter.17
  4666.3 357.2 reduce-scatter.15
  5031.6 244.6 reduce-scatter.9
  (22 shorter events, 1371.9 us)
where the time goes:
time: 5300 us; the launch traced here: 5280 us
  waiting for transfers between devices  3320 us (63%)
  matrix products  1090 us (21%)
  other arithmetic  420 us (8%)
  local copies, waits for them, and re-layouts  253 us (5%)
  blocking collectives  151 us (3%)
    reduce_scatter x16, waiting for transfers between devices, one_group(): lax.psum_scatter(d_value_term.reshape(clip_count, seq_total, group_span)....  1040 us
    reduce_scatter x16, waiting for transfers between devices, one_group(): lax.psum_scatter(d_key_term.reshape(clip_count, seq_total, group_span).as...  743 us
    reduce_scatter x1, waiting for transfers between devices, body(): lax.psum_scatter(grads[8], ('clip', 'seq'), scatter_dimension=0, tiled=True)  360 us
    reduce_scatter x1, waiting for transfers between devices, body(): lax.psum_scatter(grads[6], ('clip', 'seq'), scatter_dimension=0, tiled=True)  360 us
    reduce_scatter x1, waiting for transfers between devices, body(): lax.psum_scatter(grads[0], ('clip', 'seq'), scatter_dimension=0, tiled=True)  253 us
    dot_general x16, matrix products, one_group(): jnp.einsum('cqhd,ckhd->chqk', d_group, value_group, preferred_element_typ...  206 us
    all_gather x2, waiting for transfers between devices, body(): lax.all_gather(keys_local, 'seq', axis=1, tiled=True)  205 us
    convert_element_type x16, other arithmetic, one_group(): d_scores = (probs * (d_probs - centre)).astype(jnp.bfloat16)  196 us
  transfers between devices with their start and end apart: 46, of which 42 were waited for; matrix products, arithmetic and copies ran while one was open for 14% of the time, Pallas kernels for 0%

commit v1 on v0

v1 whole, which is shorter than its diff:
```python
import functools
import math

import jax
import jax.numpy as jnp
from jax import lax
from jax.experimental import pallas as pl
from jax.experimental.pallas import tpu as pltpu
from jax.sharding import PartitionSpec as P

HEADS = 16
HEAD_DIM = 64
FRAMES = 16
PATCHES = 256
BOTH = ("clip", "seq")
NT = (((1,), (1,)), ((), ()))
NN = (((1,), (0,)), ((), ()))
TN = (((0,), (0,)), ((), ()))
bf16 = jnp.bfloat16
f32 = jnp.float32
highest = lax.Precision.HIGHEST


def dot(left, right, dims=NN):
    return lax.dot_general(left, right, dims, preferred_element_type=f32)


def swap_bit(value, axis, bit):
    count = lax.axis_size(axis)
    return lax.ppermute(value, axis, [(i, i ^ bit) for i in range(count)])


def own_bit(axis, bit):
    return (lax.axis_index(axis) // bit) % 2


def axis_bits(axis):
    bits = []
    bit = 1
    while bit < lax.axis_size(axis):
        bits.append((axis, bit))
        bit *= 2
    return bits[::-1]


def exchange_order(bits):
    return sorted(range(len(bits)), key=lambda place: bits[place])


def mesh_bits():
    return axis_bits("clip") + axis_bits("seq")


def halve_sum(parts, bits, wire=f32):
    parts = parts.reshape((2,) * len(bits) + parts.shape[1:])
    for place in exchange_order(bits):
        axis, bit = bits[place]
        mine = own_bit(axis, bit)
        keep = lax.dynamic_index_in_dim(parts, mine, place)
        send = lax.dynamic_index_in_dim(parts, 1 - mine, place)
        parts = keep + swap_bit(send.astype(wire), axis, bit).astype(f32)
    return parts.reshape(parts.shape[len(bits) :])


def double_rows(row, bits):
    rows = row[None]
    for axis, bit in reversed(bits):
        other = swap_bit(rows, axis, bit)
        low = own_bit(axis, bit) == 0
        rows = jnp.concatenate([jnp.where(low, rows, other), jnp.where(low, other, rows)], axis=0)
    return rows


def weight_grad(left, right):
    tokens, rows = left.shape
    quarter = rows // lax.axis_size("clip")
    mine = lax.axis_index("clip")

    def part(flip):
        piece = lax.dynamic_slice_in_dim(left, (mine ^ flip) * quarter, quarter, 1)
        return dot(piece, right, TN)

    far = swap_bit(part(3).astype(bf16), "clip", 1)
    near = swap_bit(part(1).astype(bf16), "clip", 1)
    across = swap_bit((part(2) + far.astype(f32)).astype(bf16), "clip", 2)
    total = part(0) + near.astype(f32) + across.astype(f32)
    return halve_sum(total.reshape((lax.axis_size("seq"), -1, right.shape[1])), axis_bits("seq"), bf16)


def norm_parts(values):
    centre = values - jnp.mean(values, axis=-1, keepdims=True)
    spread = jnp.mean(centre * centre, axis=-1, keepdims=True)
    inverse = lax.rsqrt(spread + 1e-06)
    return centre * inverse, inverse


def norm_back(unit, inverse, grad, scales):
    scaled = grad * (1.0 + scales)
    mean = jnp.mean(scaled, axis=-1, keepdims=True)
    along = jnp.mean(scaled * unit, axis=-1, keepdims=True)
    return inverse * (scaled - mean - unit * along)


def rotary_lanes(positions, width):
    half = HEAD_DIM // 2
    lane = jnp.arange(width, dtype=jnp.int32) % HEAD_DIM
    freqs = jnp.exp(-math.log(10000.0) * 2.0 * (lane % half).astype(f32) / HEAD_DIM)
    angles = positions.astype(f32)[:, None] * freqs[None, :]
    sign = jnp.where(lane < half, -1.0, 1.0).astype(f32)
    return jnp.cos(angles), jnp.sin(angles) * sign[None, :]


def partner(values):
    width = values.shape[1]
    half = HEAD_DIM // 2
    lane = lax.broadcasted_iota(jnp.int32, (1, width), 1) % HEAD_DIM
    return jnp.where(lane < half, pltpu.roll(values, width - half, 1), pltpu.roll(values, half, 1))


def project_kernel(x_ref, wq_ref, wk_ref, wv_ref, bq_ref, bk_ref, bv_ref, cos_ref, sin_ref, out_ref, *, span):
    x = x_ref[...]
    cosine, sine = cos_ref[...], sin_ref[...]
    groups = wq_ref.shape[1] // span
    for place, (w_ref, b_ref) in enumerate(((wq_ref, bq_ref), (wk_ref, bk_ref), (wv_ref, bv_ref))):
        value = dot(x, w_ref[...]) + b_ref[...]
        if place < 2:
            value = value * cosine + partner(value) * sine
        value = value.astype(bf16)
        for g in range(groups):
            out_ref[g, :, place * span : (place + 1) * span] = value[:, g * span : (g + 1) * span]


def project(x, weight, bias, cosine, sine, groups):
    rows, width = x.shape
    span = width // groups
    block = max(span, 256)
    per_step = block // span
    steps = groups // per_step
    weight_specs = [
        pl.BlockSpec((width, block), functools.partial(lambda p, j: (0, p * steps + j), p)) for p in range(3)
    ]
    bias_specs = [pl.BlockSpec((1, block), functools.partial(lambda p, j: (0, p * steps + j), p)) for p in range(3)]
    whole = pl.BlockSpec((rows, block), lambda j: (0, 0))
    return pl.pallas_call(
        functools.partial(project_kernel, span=span),
        grid=(steps,),
        in_specs=[pl.BlockSpec((rows, width), lambda j: (0, 0))] + weight_specs + bias_specs + [whole, whole],
        out_specs=pl.BlockSpec((per_step, rows, 3 * span), lambda j: (j, 0, 0)),
        out_shape=jax.ShapeDtypeStruct((groups, rows, 3 * span), bf16),
        compiler_params=pltpu.CompilerParams(vmem_limit_bytes=32 << 20),
        cost_estimate=pl.CostEstimate(
            flops=2 * rows * width * 3 * width, bytes_accessed=2 * width * 3 * width + 8 * rows * width, transcendentals=0
        ),
        name="project",
    )(x, weight, weight, weight, bias, bias, bias, cosine, sine)


def attend_kernel(qkv_ref, mix_ref, full_ref, log_ref, vt_ref, *, total, span, block):
    heads = span // HEAD_DIM
    head = lax.broadcasted_iota(jnp.int32, (1, span), 1) // HEAD_DIM
    key_frame = lax.broadcasted_iota(jnp.int32, (block, block), 0) // PATCHES
    query_frame = lax.broadcasted_iota(jnp.int32, (block, block), 1) // PATCHES
    kept = key_frame <= query_frame

    def flip(j, carry):
        rows = pl.ds(pl.multiple_of(j * block, block), block)
        vt_ref[:, rows] = jnp.transpose(qkv_ref[rows, 2 * span : 3 * span])
        return carry

    lax.fori_loop(0, total // block, flip, 0)

    def query_block(i, carry):
        rows = pl.ds(pl.multiple_of(i * block, block), block)
        query = qkv_ref[rows, 0:span] * jnp.asarray(HEAD_DIM**-0.5, bf16)
        queries = [jnp.where(head == h, query, jnp.zeros_like(query)) for h in range(heads)]

        def step(j, state, masked):
            peaks, sums, mixes = state
            columns = pl.ds(pl.multiple_of(j * block, block), block)
            key = qkv_ref[columns, span : 2 * span]
            new = ([], [], [])
            for h in range(heads):
                scores = dot(key, queries[h], NT)
                if masked:
                    scores = jnp.where(kept, scores, -1e30)
                peak = jnp.maximum(peaks[h], jnp.max(scores, axis=0, keepdims=True))
                raised = jnp.exp(scores - peak)
                fade = jnp.exp(peaks[h] - peak)
                new[0].append(peak)
                new[1].append(fade * sums[h] + jnp.sum(raised, axis=0, keepdims=True))
                term = dot(vt_ref[h * HEAD_DIM : (h + 1) * HEAD_DIM, columns], raised.astype(bf16))
                new[2].append(mixes[h] * fade + term)
            return tuple(map(tuple, new))

        state = (
            tuple(jnp.full((1, block), -1e30, f32) for _ in range(heads)),
            tuple(jnp.zeros((1, block), f32) for _ in range(heads)),
            tuple(jnp.zeros((HEAD_DIM, block), f32) for _ in range(heads)),
        )
        state = lax.fori_loop(0, i, lambda j, s: step(j, s, False), state)
        peaks, sums, mixes = step(i, state, True)
        mixed = jnp.transpose(jnp.concatenate([mixes[h] / sums[h] for h in range(heads)], axis=0))
        full_ref[rows, :] = mixed
        mix_ref[rows, :] = mixed.astype(bf16)
        for h in range(heads):
            log_ref[h : h + 1, rows] = peaks[h] + jnp.log(sums[h])
        return carry

    lax.fori_loop(0, total // block, query_block, 0)


def attend(qkv, span):
    total = qkv.shape[0]
    heads = span // HEAD_DIM
    block = min(1024, total)
    return pl.pallas_call(
        functools.partial(attend_kernel, total=total, span=span, block=block),
        out_shape=(
            jax.ShapeDtypeStruct((total, span), bf16),
            jax.ShapeDtypeStruct((total, span), f32),
            jax.ShapeDtypeStruct((heads, total), f32),
        ),
        scratch_shapes=[pltpu.VMEM((span, total), bf16)],
        compiler_params=pltpu.CompilerParams(vmem_limit_bytes=52 << 20),
        cost_estimate=pl.CostEstimate(
            flops=8 * total * total * span, bytes_accessed=12 * total * span, transcendentals=total * total * heads // 2
        ),
        name="attend",
    )(qkv)


def attend_back_kernel(
    qkv_ref, grad_ref, full_ref, log_ref, cos_ref, sin_ref, out_ref, dq_ref, dk_ref, dv_ref, along_ref, *, total, span, block
):
    heads = span // HEAD_DIM
    scale = HEAD_DIM**-0.5
    head = lax.broadcasted_iota(jnp.int32, (1, span), 1) // HEAD_DIM
    key_frame = lax.broadcasted_iota(jnp.int32, (block, block), 0) // PATCHES
    query_frame = lax.broadcasted_iota(jnp.int32, (block, block), 1) // PATCHES
    kept = key_frame <= query_frame
    blocks = total // block
    dq_ref[...] = jnp.zeros_like(dq_ref)

    def only(value, h):
        return jnp.where(head == h, value, jnp.zeros_like(value))

    def lead(i, carry):
        rows = pl.ds(pl.multiple_of(i * block, block), block)
        product = jnp.transpose(grad_ref[rows, :].astype(f32) * full_ref[rows, :])
        for h in range(heads):
            along_ref[h : h + 1, rows] = jnp.sum(product[h * HEAD_DIM : (h + 1) * HEAD_DIM], axis=0, keepdims=True)
        return carry

    lax.fori_loop(0, blocks, lead, 0)

    def key_block(j, carry):
        columns = pl.ds(pl.multiple_of(j * block, block), block)
        key = qkv_ref[columns, span : 2 * span]
        value = qkv_ref[columns, 2 * span : 3 * span]
        key_flat = jnp.transpose(key)
        dk_ref[...] = jnp.zeros_like(dk_ref)
        dv_ref[...] = jnp.zeros_like(dv_ref)

        def step(i, masked):
            rows = pl.ds(pl.multiple_of(i * block, block), block)
            query = qkv_ref[rows, 0:span] * jnp.asarray(scale, bf16)
            grad = grad_ref[rows, :]
            dk = dv = None
            for h in range(heads):
                query_h, grad_h = only(query, h), only(grad, h)
                scores = dot(key, query_h, NT)
                if masked:
                    scores = jnp.where(kept, scores, -1e30)
                probs = jnp.exp(scores - log_ref[h : h + 1, rows])
                d_probs = dot(value, grad_h, NT)
                d_scores = (probs * (d_probs - along_ref[h : h + 1, rows])).astype(bf16)
                dv_term = dot(probs.astype(bf16), grad_h)
                dk_term = dot(d_scores, query_h)
                band = slice(h * HEAD_DIM, (h + 1) * HEAD_DIM)
                dq_ref[band, rows] += dot(key_flat[band], d_scores)
                dv = dv_term if dv is None else dv + dv_term
                dk = dk_term if dk is None else dk + dk_term
            dv_ref[...] += dv
            dk_ref[...] += dk

        step(j, True)

        def later(i, c):
            step(i, False)
            return c

        lax.fori_loop(j + 1, blocks, later, 0)
        dk = dk_ref[...]
        out_ref[columns, span : 2 * span] = (dk * cos_ref[columns, :] - partner(dk) * sin_ref[columns, :]).astype(bf16)
        out_ref[columns, 2 * span : 3 * span] = dv_ref[...].astype(bf16)
        return carry

    lax.fori_loop(0, blocks, key_block, 0)

    def last(i, carry):
        rows = pl.ds(pl.multiple_of(i * block, block), block)
        dq = jnp.transpose(dq_ref[:, rows]) * scale
        out_ref[rows, 0:span] = (dq * cos_ref[rows, :] - partner(dq) * sin_ref[rows, :]).astype(bf16)
        return carry

    lax.fori_loop(0, blocks, last, 0)


def attend_back(qkv, grad, full, logs, cosine, sine, span):
    total = qkv.shape[0]
    heads = span // HEAD_DIM
    block = min(1024, total)
    return pl.pallas_call(
        functools.partial(attend_back_kernel, total=total, span=span, block=block),
        out_shape=jax.ShapeDtypeStruct((total, 3 * span), bf16),
        scratch_shapes=[
            pltpu.VMEM((span, total), f32),
            pltpu.VMEM((block, span), f32),
            pltpu.VMEM((block, span), f32),
            pltpu.VMEM((heads, total), f32),
        ],
        compiler_params=pltpu.CompilerParams(vmem_limit_bytes=56 << 20),
        cost_estimate=pl.CostEstimate(
            flops=20 * total * total * span, bytes_accessed=26 * total * span, transcendentals=total * total * heads // 2
        ),
        name="attend_back",
    )(qkv, grad, full, logs, cosine, sine)


def gathered_forward(queries, keys, values, allowed):
    def one(pieces):
        q, k, v = pieces
        scores = jnp.where(allowed, dot(q, k, NT) * HEAD_DIM**-0.5, -1e30)
        peak = jnp.max(scores, axis=-1, keepdims=True)
        raised = jnp.exp(scores - peak)
        totals = jnp.sum(raised, axis=-1, keepdims=True)
        return dot((raised / totals).astype(bf16), v), peak + jnp.log(totals)

    return lax.map(one, (queries, keys, values))


def gathered_back(queries, keys, values, grads, logs, allowed):
    scale = HEAD_DIM**-0.5

    def one(pieces):
        q, k, v, grad, log = pieces
        scores = jnp.where(allowed, dot(q, k, NT) * scale, -1e30)
        probs = jnp.exp(scores - log)
        d_probs = dot(grad, v, NT)
        centre = jnp.sum(probs * d_probs, axis=-1, keepdims=True)
        d_scores = (probs * (d_probs - centre)).astype(bf16)
        dv = dot(probs.astype(bf16), grad, TN)
        return dot(d_scores, k) * scale, dot(d_scores, q, TN) * scale, dv

    return lax.map(one, (queries, keys, values, grads, logs))


def body(
    tokens,
    ctx_count,
    noise_level,
    mod_weight,
    mod_bias,
    qkv_weight,
    qkv_bias,
    out_weight,
    out_bias,
    up_weight,
    up_bias,
    down_weight,
    down_bias,
    cotangent,
):
    clips, rows, width = tokens.shape
    seq_devices = lax.axis_size("seq")
    devices = lax.axis_size("clip") * seq_devices
    bits = mesh_bits()
    here = lax.axis_index("clip") * seq_devices + lax.axis_index("seq")
    total = rows * seq_devices
    frames = max(1, rows // PATCHES)
    patch_rows = rows // frames
    by_heads = HEADS % seq_devices == 0
    span = width // seq_devices

    full_qkv = lax.all_gather(qkv_weight, BOTH, axis=0, tiled=True)
    full_out = lax.all_gather(out_weight, BOTH, axis=0, tiled=True)
    full_up = lax.all_gather(up_weight, BOTH, axis=0, tiled=True)
    full_down = lax.all_gather(down_weight, BOTH, axis=0, tiled=True)
    biases = (qkv_bias, out_bias, up_bias, down_bias)
    bias_rows = double_rows(jnp.concatenate(biases).astype(f32), bits)
    full_biases = []
    first = 0
    for piece in biases:
        full_biases.append(bias_rows[:, first : first + piece.shape[0]].reshape(1, -1))
        first += piece.shape[0]
    bias_qkv, bias_out, bias_up, bias_down = full_biases

    plan = jnp.concatenate([ctx_count[:, None], noise_level], axis=1)
    plan = double_rows(plan, axis_bits("clip"))
    levels = jnp.where(jnp.arange(FRAMES, dtype=jnp.int32) < plan[..., :1], 0, plan[..., 1:])
    if rows < PATCHES:
        levels = jnp.repeat(levels, PATCHES // rows, axis=-1)
    levels = levels.reshape(-1, clips, seq_devices, frames).transpose(0, 2, 1, 3)
    depth = mod_weight.shape[0]
    half_width = width // 2
    feature = here * depth + jnp.arange(depth, dtype=jnp.int32)
    freqs = jnp.exp(-math.log(10000.0) * (feature % half_width).astype(f32) / half_width)
    angles = levels.reshape(devices * clips * frames, 1).astype(f32) * freqs
    cond = jax.nn.silu(jnp.where(feature < half_width, jnp.sin(angles), jnp.cos(angles))).astype(bf16)
    mod_width = mod_weight.shape[1]
    bias_place = lax.dynamic_update_slice_in_dim(
        jnp.zeros((mod_width,), f32), mod_bias.astype(f32), here * mod_bias.shape[0], 0
    )
    partial = dot(cond, mod_weight) + bias_place
    modulation = halve_sum(partial.reshape(devices, clips * frames, mod_width), bits)
    modulation = modulation.reshape(clips, frames, 1, mod_width)

    positions = lax.axis_index("seq") * rows + jnp.arange(rows, dtype=jnp.int32)
    cos_local, sin_local = rotary_lanes(positions, max(span, 256))
    if by_heads:
        cos_all, sin_all = rotary_lanes(jnp.arange(total, dtype=jnp.int32), span)
    else:
        key_frame = jnp.arange(total, dtype=jnp.int32) // PATCHES
        allowed = key_frame[None, :] <= (positions // PATCHES)[:, None]

    def flat(value):
        return value.reshape(rows, value.shape[-1])

    def split(value):
        return value.reshape(frames, patch_rows, value.shape[-1])

    def to_heads(value):
        return value.reshape(rows, HEADS, HEAD_DIM).transpose(1, 0, 2)

    saved = []
    for c in range(clips):
        mods = jnp.split(modulation[c], 6, axis=-1)
        tokens_now = split(tokens[c].astype(f32))
        unit, inverse = norm_parts(tokens_now)
        normed = flat((unit * (1.0 + mods[1]) + mods[0]).astype(bf16))
        if by_heads:
            sent = project(normed, full_qkv, bias_qkv, cos_local, sin_local, seq_devices)
            qkv = lax.all_to_all(sent, "seq", 0, 0, tiled=True).reshape(total, 3 * span)
            mix, full, logs = attend(qkv, span)
            back = lax.all_to_all(mix.reshape(seq_devices, rows, span), "seq", 0, 0, tiled=True)
            mixed = back.transpose(1, 0, 2).reshape(rows, width)
            kept = (qkv, full, logs)
        else:
            projected = dot(normed, full_qkv) + bias_qkv
            views = []
            for place in range(3):
                view = to_heads(projected[:, place * width : (place + 1) * width])
                if place < 2:
                    cosine, sine = cos_local[:, :HEAD_DIM], sin_local[:, :HEAD_DIM]
                    view = view * cosine + jnp.roll(view, HEAD_DIM // 2, -1) * sine
                views.append(view.astype(bf16))
            queries, keys, values = views
            keys = lax.all_gather(keys, "seq", axis=1, tiled=True)
            values = lax.all_gather(values, "seq", axis=1, tiled=True)
            mix, logs = gathered_forward(queries, keys, values, allowed)
            mixed = mix.transpose(1, 0, 2).reshape(rows, width).astype(bf16)
            kept = (queries, keys, values, logs)
        saved.append((mods, tokens_now, unit, inverse, normed, kept, mixed))

    outputs = []
    middle = []
    for c in range(clips):
        mods, tokens_now, unit, inverse, normed, kept, mixed = saved[c]
        _, _, gate_one, shift_two, scale_two, gate_two = mods
        attn_out = split(dot(mixed, full_out) + bias_out)
        resid = tokens_now + gate_one * attn_out
        unit_two, inverse_two = norm_parts(resid)
        normed_two = flat((unit_two * (1.0 + scale_two) + shift_two).astype(bf16))
        hidden = dot(normed_two, full_up) + bias_up
        active_full, gelu_back = jax.vjp(jax.nn.gelu, hidden)
        active = active_full.astype(bf16)
        mlp_out = split(dot(active, full_down) + bias_down)
        outputs.append(flat((resid + gate_two * mlp_out).astype(bf16)))
        grad_out = split(cotangent[c].astype(f32))
        d_mlp = flat((gate_two * grad_out).astype(bf16))
        d_hidden = gelu_back(dot(d_mlp, full_down, NT))[0].astype(bf16)
        d_normed_two = split(dot(d_hidden, full_up, NT))
        d_resid = grad_out + norm_back(unit_two, inverse_two, d_normed_two, scale_two)
        d_attn = flat((gate_one * d_resid).astype(bf16))
        d_mixed = dot(d_attn, full_out, NT).astype(bf16)
        d_early = jnp.concatenate(
            [
                jnp.sum(d_resid * attn_out, axis=1),
                jnp.sum(d_normed_two, axis=1),
                jnp.sum(d_normed_two * unit_two, axis=1),
                jnp.sum(grad_out * mlp_out, axis=1),
            ],
            axis=-1,
        )
        middle.append((mixed, d_attn, normed_two, d_hidden, active, d_mlp, d_resid, d_mixed, d_early))

    def both(place):
        return jnp.concatenate([m[place] for m in middle], axis=0)

    d_attn_all, d_hidden_all, d_mlp_all = both(1), both(3), both(5)
    grad_down = weight_grad(both(4), d_mlp_all)
    grad_up = weight_grad(both(2), d_hidden_all)
    grad_out_weight = weight_grad(both(0), d_attn_all)
    early_rows = lax.all_gather(both(8), BOTH, axis=0, tiled=True)

    inputs_grad = []
    late = []
    projected_grads = []
    for c in range(clips):
        mods, tokens_now, unit, inverse, normed, kept, mixed = saved[c]
        d_resid, d_mixed = middle[c][6], middle[c][7]
        if by_heads:
            sent = d_mixed.reshape(rows, seq_devices, span).transpose(1, 0, 2)
            grad = lax.all_to_all(sent, "seq", 0, 0, tiled=True).reshape(total, span)
            qkv, full, logs = kept
            d_qkv = attend_back(qkv, grad, full, logs, cos_all, sin_all, span)
            back = lax.all_to_all(d_qkv.reshape(seq_devices, rows, 3 * span), "seq", 0, 0, tiled=True)
            d_projected = back.reshape(seq_devices, rows, 3, span).transpose(1, 2, 0, 3).reshape(rows, 3 * width)
        else:
            queries, keys, values, logs = kept
            dq, dk, dv = gathered_back(queries, keys, values, to_heads(d_mixed), logs, allowed)
            dk = lax.psum_scatter(dk.astype(bf16), "seq", scatter_dimension=1, tiled=True).astype(f32)
            dv = lax.psum_scatter(dv.astype(bf16), "seq", scatter_dimension=1, tiled=True).astype(f32)
            cosine, sine = cos_local[:, :HEAD_DIM], sin_local[:, :HEAD_DIM]
            views = [g * cosine - jnp.roll(g, HEAD_DIM // 2, -1) * sine for g in (dq, dk)] + [dv]
            d_projected = jnp.concatenate([g.transpose(1, 0, 2).reshape(rows, width) for g in views], axis=1).astype(bf16)
        projected_grads.append(d_projected)
        d_normed = split(dot(d_projected, full_qkv, NT))
        inputs_grad.append(flat(d_resid + norm_back(unit, inverse, d_normed, mods[1])))
        late.append(jnp.concatenate([jnp.sum(d_normed, axis=1), jnp.sum(d_normed * unit, axis=1)], axis=-1))

    d_projected_all = jnp.concatenate(projected_grads, axis=0)
    grad_qkv = weight_grad(jnp.concatenate([s[4] for s in saved], axis=0), d_projected_all)
    bias_grads = [
        jnp.sum(g.astype(f32), axis=0).reshape(devices, -1) for g in (d_projected_all, d_attn_all, d_hidden_all, d_mlp_all)
    ]
    bias_sum = halve_sum(jnp.concatenate(bias_grads, axis=1), bits)
    grad_biases = []
    first = 0
    for piece in bias_grads:
        grad_biases.append(bias_sum[first : first + piece.shape[1]])
        first += piece.shape[1]

    late_rows = double_rows(jnp.concatenate(late, axis=0), bits).reshape(-1, 2 * width)
    grad_mod = jnp.concatenate(
        [
            lax.dot_general(cond.astype(f32), r, TN, precision=highest, preferred_element_type=f32)
            for r in (late_rows, early_rows)
        ],
        axis=1,
    )
    mod_sum = jnp.concatenate([jnp.sum(late_rows, axis=0), jnp.sum(early_rows, axis=0)])
    grad_mod_bias = lax.dynamic_slice_in_dim(mod_sum, here * mod_bias.shape[0], mod_bias.shape[0], 0)
    return (
        jnp.stack(outputs),
        jnp.stack(inputs_grad),
        grad_mod,
        grad_mod_bias,
        grad_qkv,
        grad_biases[0],
        grad_out_weight,
        grad_biases[1],
        grad_up,
        grad_biases[2],
        grad_down,
        grad_biases[3],
    )


def solution(mesh):
    token_place = P("clip", "seq", None)
    matrix, vector = P(BOTH, None), P(BOTH)
    weights = (matrix, vector) * 5
    return jax.shard_map(
        body,
        mesh=mesh,
        in_specs=(token_place, P("clip"), P("clip", None)) + weights + (token_place,),
        out_specs=(token_place, token_place) + weights,
        check_vma=False,
    )
```

time: 5300 us -> 1120 us (0.21)
  waiting for transfers between devices: 3320 us -> 341 us
  matrix products: 1090 us -> 195 us
  other arithmetic: 420 us -> 90.3 us
  Pallas kernels: 0 us -> 211 us
  local copies, waits for them, and re-layouts: 253 us -> 84.2 us
  starting transfers between devices: 12.5 us -> 89.3 us
  blocking collectives: 151 us -> 84.6 us
    reduce_scatter x37 -> x0, waiting for transfers between devices: 2850 us -> none  [the longest x16 1040 us: one_group(): lax.psum_scatter(d_value_term.reshape(clip_count, seq_total, group_span)....]
    dot_general x144 -> x33, matrix products: 1090 us -> 195 us  [the longest x31 193 us: dot(): return lax.dot_general(left, right, dims, preferred_element_type=f32)]
    all_gather x9 -> x5, waiting for transfers between devices: 463 us -> 44.5 us  [the longest x1 44.4 us: body(): full_down = lax.all_gather(down_weight, BOTH, axis=0, tiled=True)]
    pallas_call x0 -> x6, Pallas kernels: none -> 211 us  [the longest x2 128 us: attend_back(): pl.pallas_call(functools.partial(attend_back_kernel, total=total, span=sp...]
    ppermute x0 -> x46, waiting for transfers between devices: none -> 197 us  [swap_bit(): return lax.ppermute(value, axis, [(i, i ^ bit) for i in range(count)])]
    convert_element_type x22 -> x11, other arithmetic: 198 us -> 20.6 us  [the longest x2 8.87 us: body(): d_attn = flat((gate_one * d_resid).astype(bf16))]
    dynamic_slice x128 -> x10, local copies, waits for them, and re-layouts: 121 us -> 3.05 us  [halve_sum(): send = lax.dynamic_index_in_dim(parts, 1 - mine, place)]
    all_to_all x0 -> x7, waiting for transfers between devices: none -> 97.2 us  [the longest x1 68.9 us: body(): qkv = lax.all_to_all(sent, 'seq', 0, 0, tiled=True).reshape(total, 3 * span)]
  transfers between devices with their start and end apart: 46 -> 58, of which waited for: 42 -> 25; matrix products, arithmetic and copies ran while one was open for 14% -> 18% of each run, Pallas kernels for 0% -> 15%
where the time goes in v1:
time: 1120 us; the launch traced here: 1110 us
  waiting for transfers between devices  341 us (30%)
  Pallas kernels  211 us (19%)
  matrix products  195 us (17%)
  other arithmetic  90.3 us (8%)
  starting transfers between devices  89.3 us (8%)
  blocking collectives  84.6 us (8%)
  local copies, waits for them, and re-layouts  84.2 us (8%)
  between operations  15.9 us (1%)
    ppermute x46, waiting for transfers between devices, swap_bit(): return lax.ppermute(value, axis, [(i, i ^ bit) for i in range(count)])  197 us
    dot_general x31, matrix products, dot(): return lax.dot_general(left, right, dims, preferred_element_type=f32)  193 us
    pallas_call x2, Pallas kernels, attend_back(): pl.pallas_call(functools.partial(attend_back_kernel, total=total, span=sp...  128 us
    all_to_all x1, blocking collectives, body(): qkv = lax.all_to_all(sent, 'seq', 0, 0, tiled=True).reshape(total, 3 * span)  84.6 us
    pallas_call x2, Pallas kernels, attend(): pl.pallas_call(functools.partial(attend_kernel, total=total, span=span, b...  69.9 us
    all_to_all x1, waiting for transfers between devices, body(): qkv = lax.all_to_all(sent, 'seq', 0, 0, tiled=True).reshape(total, 3 * span)  68.9 us
    ppermute x46, starting transfers between devices, swap_bit(): return lax.ppermute(value, axis, [(i, i ^ bit) for i in range(count)])  53.5 us
    all_gather x1, waiting for transfers between devices, body(): full_down = lax.all_gather(down_weight, BOTH, axis=0, tiled=True)  44.4 us
  transfers between devices with their start and end apart: 58, of which 25 were waited for; matrix products, arithmetic and copies ran while one was open for 18% of the time, Pallas kernels for 15%

profile of v1, /device:TPU:0, one launch (start us, length us, event | category | flops | bytes accessed | tf_op | source)
XLA Modules:
  0.0 1110.7 jit_solution(422672757355383579)
XLA Ops:
  42.1 17.9 %collective-permute-done.3 = f32[1,1,2,2,2,4,6144]{6,5,4,3,2,1,0:T(4,128)S(1)} collective-permute-done((f32[1,1,2,2,2,4,6144]{6,5,4,3,2,1,0:T(4,128)S(1)}, f32[1,1,2,2,2,4,6144]{6,5,4,3,2,1,0:T(4,128)S(1)}, u32[]{:S(2)}, u32[]{:S(2)}) %collective-permute-start.3) | collective-permute-done | bytes 786464 | tf_op jit(solution)/shard_map/ppermute | solution.py:30
  64.9 14.0 %collective-permute-done.4 = f32[1,1,2,2,1,4,6144]{6,5,4,3,2,1,0:T(4,128)S(1)} collective-permute-done((f32[1,1,2,2,1,4,6144]{6,5,4,3,2,1,0:T(4,128)S(1)}, f32[1,1,2,2,1,4,6144]{6,5,4,3,2,1,0:T(4,128)S(1)}, u32[]{:S(2)}, u32[]{:S(2)}) %collective-permute-start.4) | collective-permute-done | bytes 393248 | tf_op jit(solution)/shard_map/ppermute | solution.py:30
  80.1 12.5 %collective-permute-done.5 = f32[1,1,2,1,1,4,6144]{6,5,4,3,2,1,0:T(4,128)S(1)} collective-permute-done((f32[1,1,2,1,1,4,6144]{6,5,4,3,2,1,0:T(4,128)S(1)}, f32[1,1,2,1,1,4,6144]{6,5,4,3,2,1,0:T(4,128)S(1)}, u32[]{:S(2)}, u32[]{:S(2)}) %collective-permute-start.5) | collective-permute-done | bytes 196640 | tf_op jit(solution)/shard_map/ppermute | solution.py:30
  109.2 84.6 %all_to_all.40 = bf16[8,512,384]{2,1,0:T(8,128)(2,1)} all-to-all(bf16[8,512,384]{2,1,0:T(8,128)(2,1)S(1)} %project.2), channel_id=1, replica_groups=mesh['clip'=4,'seq'=8] {'seq'}, dimensions={0} | all-to-all | bytes 6291456 | tf_op jit(solution)/shard_map/all_to_all | solution.py:443
  193.8 35.0 %attend.2 = (bf16[4096,128]{1,0:T(8,128)(2,1)S(1)}, f32[4096,128]{1,0:T(8,128)}, f32[2,4096]{1,0:T(2,128)S(1)}) custom-call(bf16[4096,384]{1,0:T(8,128)(2,1)} %bitcast.363), custom_call_target="tpu_custom_call" | custom-call | flops 17179869184 | bytes 6291456 | tf_op jit(solution)/shard_map/attend/pallas_call | solution.py:216
  236.5 28.3 %all-to-all-done.1 = bf16[8,512,128]{1,2,0:T(8,128)(2,1)} async-done(((bf16[8,512,128]{1,2,0:T(8,128)(2,1)}), bf16[8,512,128]{1,2,0:T(8,128)(2,1)}, u32[]{:S(2)}, u32[]{:S(2)}) %all-to-all-start.1) | async-done | bytes 1048608 | tf_op jit(solution)/shard_map/all_to_all | solution.py:445
  277.6 11.5 %fusion.181 = f32[512,4096]{1,0:T(8,128)} fusion(bf16[512,1024]{1,0:T(8,128)(2,1)} %fusion.22, bf16[1024,4096]{1,0:T(8,128)(2,1)} %all-gather.11.cloned.1.call-done), kind=kOutput, calls=%fused_computation.434 | convolution fusion | flops 4294967296 | bytes 17825792 | tf_op jit(solution)/shard_map/dot_general | solution.py:25
  289.2 44.4 %all-gather.13.cloned.1.call-done = bf16[4096,1024]{1,0:T(8,128)(2,1)} async-done(((bf16[128,1024]{1,0:T(8,128)(2,1)}), bf16[4096,1024]{1,0:T(8,128)(2,1)}) %all-gather.13.cloned.1.call-update) | async-done | bytes 8388624 | tf_op jit(solution)/shard_map/all_gather | solution.py:388
  333.6 16.6 %fusion.6 = (bf16[512,4096]{1,0:T(8,128)(2,1)}, bf16[512,4096]{1,0:T(8,128)(2,1)}) fusion(f32[512,4096]{1,0:T(8,128)} %fusion.181, f32[4096]{0:T(1024)S(1)} %fusion.133, bf16[512,1024]{1,0:T(8,128)(2,1)S(1)} %fusion.20, bf16[4096,1024]{1,0:T(8,128)(2,1)} %all-gather.13.cloned.1.call-done), kind=kOutput, calls=%fused_computation.20 | convolution fusion | flops 4343201792 | bytes 26230784 | tf_op jit(solution)/shard_map/dot_general | solution.py:25
  376.5 68.9 %all-to-all-done.2 = bf16[8,512,384]{2,1,0:T(8,128)(2,1)} async-done(((bf16[8,512,384]{2,1,0:T(8,128)(2,1)}), bf16[8,512,384]{2,1,0:T(8,128)(2,1)}, u32[]{:S(2)}, u32[]{:S(2)}) %all-to-all-start.2) | async-done | bytes 3145760 | tf_op jit(solution)/shard_map/all_to_all | solution.py:443
  445.4 34.9 %attend.3 = (bf16[4096,128]{1,0:T(8,128)(2,1)S(1)}, f32[4096,128]{1,0:T(8,128)}, f32[2,4096]{1,0:T(2,128)S(1)}) custom-call(bf16[4096,384]{1,0:T(8,128)(2,1)} %bitcast.40.qkv_ref), custom_call_target="tpu_custom_call" | custom-call | flops 17179869184 | bytes 6291456 | tf_op jit(solution)/shard_map/attend/pallas_call | solution.py:216
  491.4 9.4 fusion.18
  503.2 11.6 %fusion.48 = (bf16[1,512,1024]{2,1,0:T(8,128)(2,1)}, f32[512,1024]{1,0:T(8,128)}) fusion(f32[1,512,1024]{2,1,0:T(8,128)} %get-tuple-element.114, f32[2,1024]{1,0:T(2,128)S(1)} %get-tuple-element.80, f32[1024]{0:T(1024)S(1)} %add.659, bf16[512,4096]{1,0:T(8,128)(2,1)} %get-tuple-element.57, bf16[4096,1024]{1,0:T(8,128)(2,1)} %all-gather.13.cloned.1.call-done), kind=kOutput, calls=%fused_computation.132 | convolution fusion | flops 4297064448 | bytes 17838080 | tf_op jit(solution)/shard_map/dot_general | solution.py:25
  530.8 10.5 fusion.182
  541.4 16.7 %fusion.13 = (bf16[512,4096]{1,0:T(8,128)(2,1)}, bf16[512,4096]{1,0:T(8,128)(2,1)}) fusion(f32[512,4096]{1,0:T(8,128)} %fusion.182, f32[4096]{0:T(1024)S(1)} %fusion.133, bf16[512,1024]{1,0:T(8,128)(2,1)S(1)} %get-tuple-element.66, bf16[4096,1024]{1,0:T(8,128)(2,1)} %all-gather.13.cloned.1.call-done), kind=kOutput, calls=%fused_computation.27 | convolution fusion | flops 4343201792 | bytes 26230784 | tf_op jit(solution)/shard_map/dot_general | solution.py:25
  668.5 64.0 %attend_back.3 = bf16[4096,384]{1,0:T(8,128)(2,1)} custom-call(bf16[4096,384]{1,0:T(8,128)(2,1)} %bitcast.40.qkv_ref, bf16[4096,128]{1,0:T(8,128)(2,1)} %bitcast.70.grad_ref, f32[4096,128]{1,0:T(8,128)} %get-tuple-element.22.full_ref, f32[2,4096]{1,0:T(2,128)} %copy-done.7, f32[4096,128]{1,0:T(8,128)} %get-tuple-element.99.cos_ref, ...), custom_call_target="tpu_custom_call" | custom-call | flops 42949672960 | bytes 13631488 | tf_op jit(solution)/shard_map/attend_back/pallas_call | solution.py:313
  759.0 64.4 %attend_back.2 = bf16[4096,384]{1,0:T(8,128)(2,1)} custom-call(bf16[4096,384]{1,0:T(8,128)(2,1)} %bitcast.364, bf16[4096,128]{1,0:T(8,128)(2,1)} %bitcast.367, f32[4096,128]{1,0:T(8,128)} %get-tuple-element.20.full_ref, f32[2,4096]{1,0:T(2,128)} %copy-done.6, f32[4096,128]{1,0:T(8,128)} %get-tuple-element.99.cos_ref, f32[4096,128]{1,0:T(8,128)} %get-tuple-element.98.sin_ref), custom_call_target="tpu_custom_call" | custom-call | flops 42949672960 | bytes 13631488 | tf_op jit(solution)/shard_map/attend_back/pallas_call | solution.py:313
  841.1 46.6 %collective-permute-done.32 = bf16[2,1,1,32,1024]{4,3,2,1,0:T(8,128)(2,1)S(1)} collective-permute-done((bf16[2,1,1,32,1024]{4,3,2,1,0:T(8,128)(2,1)S(1)}, bf16[2,1,1,32,1024]{4,3,2,1,0:T(8,128)(2,1)S(1)}, u32[]{:S(2)}, u32[]{:S(2)}) %collective-permute-start.32) | collective-permute-done | bytes 131104 | tf_op jit(solution)/shard_map/ppermute | solution.py:30
  892.6 12.9 %collective-permute-done.44 = bf16[2,1,1,128,1024]{4,3,2,1,0:T(8,128)(2,1)S(1)} collective-permute-done((bf16[2,1,1,128,1024]{4,3,2,1,0:T(8,128)(2,1)S(1)}, bf16[2,1,1,128,1024]{4,3,2,1,0:T(8,128)(2,1)S(1)}, u32[]{:S(2)}, u32[]{:S(2)}) %collective-permute-start.44) | collective-permute-done | bytes 524320 | tf_op jit(solution)/shard_map/ppermute | solution.py:30
  905.8 9.2 collective-permute-done.38
  919.7 9.8 collective-permute-done.39
  960.2 11.8 %multiply_reduce_fusion.4 = (f32[2,1024]{1,0:T(2,128)S(1)}, f32[2,256]{1,0:T(2,128)S(1)}, f32[2,256]{1,0:T(2,128)S(1)}, f32[2,1024]{1,0:T(2,128)S(1)}, f32[2,102...) fusion(f32[2,256,1024]{2,1,0:T(8,128)} %bitcast.352, ...), kind=kOutput, calls=%fused_computation.154 | convolution fusion | flops 3234843648 | bytes 22110208 | tf_op jit(solution)/shard_map/dot_general | solution.py:25
  977.9 11.7 %multiply_reduce_fusion.5 = (f32[2,1024]{1,0:T(2,128)S(1)}, f32[2,256]{1,0:T(2,128)S(1)}, f32[2,256]{1,0:T(2,128)S(1)}, f32[2,1024]{1,0:T(2,128)S(1)}, f32[2,102...) fusion(f32[2,256,1024]{2,1,0:T(8,128)} %bitcast.350, ...), kind=kOutput, calls=%fused_computation.155 | convolution fusion | flops 3234843648 | bytes 22110208 | tf_op jit(solution)/shard_map/dot_general | solution.py:25
  1025.9 34.5 %collective-permute-done.19 = bf16[256,3072]{1,0:T(8,128)(2,1)S(1)} collective-permute-done((bf16[256,3072]{1,0:T(8,128)(2,1)S(1)}, bf16[256,3072]{1,0:T(8,128)(2,1)S(1)}, u32[]{:S(2)}, u32[]{:S(2)}) %collective-permute-start.19) | collective-permute-done | bytes 1572896 | tf_op jit(solution)/shard_map/ppermute | solution.py:30
  (512 shorter events, 413.0 us)
Async XLA Ops:
  7.2 93.6 %all-gather.7.cloned.1.call-start = ((), (), s32[]{:S(2)}) async-start(), calls=%async_computation.8 | async-start | bytes 6488064 | tf_op jit(solution)/shard_map/all_gather | solution.py:385
  7.9 228.6 %all-gather.9.cloned.1.call-start = ((), (), s32[]{:S(2)}) async-start(), calls=%async_computation.9 | async-start | bytes 2162688 | tf_op jit(solution)/shard_map/all_gather | solution.py:386
  8.7 268.9 %all-gather.11.cloned.1.call-start = ((), (), s32[]{:S(2)}) async-start(), calls=%async_computation.10 | async-start | bytes 8650752 | tf_op jit(solution)/shard_map/all_gather | solution.py:387
  9.4 324.2 %all-gather.13.cloned.1.call-start = ((), (), s32[]{:S(2)}) async-start(), calls=%async_computation.11 | async-start | bytes 8650752 | tf_op jit(solution)/shard_map/all_gather | solution.py:388
  369.4 76.0 %all-to-all-start.2 = ((bf16[8,512,384]{2,1,0:T(8,128)(2,1)}), bf16[8,512,384]{2,1,0:T(8,128)(2,1)}, u32[]{:S(2)}, u32[]{:S(2)}) async-start(bf16[8,512,384]{2,1,0:T(8,128)(2,1)} %project.3), calls=%async_computation.2 | async-start | bytes 6291456 | tf_op jit(solution)/shard_map/all_to_all | solution.py:443
  586.7 77.1 %all-to-all-start.6 = ((bf16[8,512,128]{2,1,0:T(8,128)(2,1)}), bf16[8,512,128]{2,1,0:T(8,128)(2,1)}, u32[]{:S(2)}, u32[]{:S(2)}) async-start(bf16[8,512,128]{2,1,0:T(8,128)(2,1)} %bitcast.360), calls=%async_computation.6 | async-start | bytes 2097152 | tf_op jit(solution)/shard_map/all_to_all | solution.py:514
  597.9 43.9 %collective-permute-start.28 = (bf16[256,1024]{1,0:T(8,128)(2,1)}, bf16[256,1024]{1,0:T(8,128)(2,1)}, u32[]{:S(2)}, u32[]{:S(2)}) collective-permute-start(bf16[256,1024]{1,0:T(8,128)(2,1)} %convolution_convert_fusion.7), channel_id=1, source_target_pairs={{0,8},{8,0},{16,24},{24,16},{1,9},{9,1},{17,25},{25,17},{2,10},{10... | collective-permute-start | bytes 1572872 | tf_op jit(solution)/shard_map/ppermute | solution.py:30
  598.4 53.1 %collective-permute-start.35 = (bf16[256,4096]{1,0:T(8,128)(2,1)}, bf16[256,4096]{1,0:T(8,128)(2,1)}, u32[]{:S(2)}, u32[]{:S(2)}) collective-permute-start(bf16[256,4096]{1,0:T(8,128)(2,1)} %convolution_convert_fusion), channel_id=1, source_target_pairs={{0,8},{8,0},{16,24},{24,16},{1,9},{9,1},{17,25},{25,17},{2,10},{10... | collective-permute-start | bytes 6291464 | tf_op jit(solution)/shard_map/ppermute | solution.py:30
  606.7 137.6 %collective-permute-start.34 = (bf16[256,4096]{1,0:T(8,128)(2,1)}, bf16[256,4096]{1,0:T(8,128)(2,1)}, u32[]{:S(2)}, u32[]{:S(2)}) collective-permute-start(bf16[256,4096]{1,0:T(8,128)(2,1)} %convolution_convert_fusion.1), channel_id=1, source_target_pairs={{0,8},{8,0},{16,24},{24,16},{1,9},{9,1},{17,25},{25,17},{2,10},{10... | collective-permute-start | bytes 6291464 | tf_op jit(solution)/shard_map/ppermute | solution.py:30
  611.4 46.5 %collective-permute-start.41 = (bf16[1024,1024]{1,0:T(8,128)(2,1)}, bf16[1024,1024]{1,0:T(8,128)(2,1)}, u32[]{:S(2)}, u32[]{:S(2)}) collective-permute-start(bf16[1024,1024]{1,0:T(8,128)(2,1)} %fusion.58), channel_id=1, source_target_pairs={{0,8},{8,0},{16,24},{24,16},{1,9},{9,1},{17,25},{25,17},{2,10},{10... | collective-permute-start | bytes 6291464 | tf_op jit(solution)/shard_map/ppermute | solution.py:30
  641.8 109.2 %collective-permute-start.40 = (bf16[1024,1024]{1,0:T(8,128)(2,1)}, bf16[1024,1024]{1,0:T(8,128)(2,1)}, u32[]{:S(2)}, u32[]{:S(2)}) collective-permute-start(bf16[1024,1024]{1,0:T(8,128)(2,1)} %fusion.55), channel_id=1, source_target_pairs={{0,8},{8,0},{16,24},{24,16},{1,9},{9,1},{17,25},{25,17},{2,10},{10... | collective-permute-start | bytes 6291464 | tf_op jit(solution)/shard_map/ppermute | solution.py:30
  649.8 183.1 %collective-permute-start.31 = (bf16[2,2,1,32,1024]{4,3,2,1,0:T(8,128)(2,1)}, bf16[2,2,1,32,1024]{4,3,2,1,0:T(8,128)(2,1)S(1)}, u32[]{:S(2)}, u32[]{:S(2)}) collective-permute-start(bf16[2,2,1,32,1024]{4,3,2,1,0:T(8,128)(2,1)} %dynamic-slice_convert_fusion.8), channel_id=1, source_target_pairs={{0,1},{1,0},{2,3},{3,2},{4,5},{5,4},{6,7},{7,6},{8,9},{9,8},{10,11... | collective-permute-start | bytes 786440 | tf_op jit(solution)/shard_map/ppermute | solution.py:30
  656.4 87.9 %collective-permute-start.36 = (bf16[256,4096]{1,0:T(8,128)(2,1)}, bf16[256,4096]{1,0:T(8,128)(2,1)}, u32[]{:S(2)}, u32[]{:S(2)}) collective-permute-start(bf16[256,4096]{1,0:T(8,128)(2,1)} %add_convert_fusion.1), channel_id=1, source_target_pairs={{0,16},{8,24},{16,0},{24,8},{1,17},{9,25},{17,1},{25,9},{2,18},{10... | collective-permute-start | bytes 6291464 | tf_op jit(solution)/shard_map/ppermute | solution.py:30
  663.2 87.9 %collective-permute-start.42 = (bf16[1024,1024]{1,0:T(8,128)(2,1)}, bf16[1024,1024]{1,0:T(8,128)(2,1)}, u32[]{:S(2)}, u32[]{:S(2)}) collective-permute-start(bf16[1024,1024]{1,0:T(8,128)(2,1)} %add_convert_fusion), channel_id=1, source_target_pairs={{0,16},{8,24},{16,0},{24,8},{1,17},{9,25},{17,1},{25,9},{2,18},{10... | collective-permute-start | bytes 6291464 | tf_op jit(solution)/shard_map/ppermute | solution.py:30
  663.8 73.5 %all-to-all-start.4 = ((bf16[8,512,128]{2,1,0:T(8,128)(2,1)}), bf16[8,512,128]{2,1,0:T(8,128)(2,1)S(1)}, u32[]{:S(2)}, u32[]{:S(2)}) async-start(bf16[8,512,128]{2,1,0:T(8,128)(2,1)} %bitcast.325), calls=%async_computation.4 | async-start | bytes 2097152 | tf_op jit(solution)/shard_map/all_to_all | solution.py:514
  738.3 89.8 %all-to-all-start.7 = ((bf16[8,512,384]{1,2,0:T(8,128)(2,1)}), bf16[8,512,384]{1,2,0:T(8,128)(2,1)}, u32[]{:S(2)}, u32[]{:S(2)}) async-start(bf16[8,512,384]{1,2,0:T(8,128)(2,1)} %copy.140), calls=%async_computation.7 | async-start | bytes 6291456 | tf_op jit(solution)/shard_map/all_to_all | solution.py:517
  749.0 88.7 %collective-permute-start.37 = (bf16[2,2,1,32,4096]{4,3,2,1,0:T(8,128)(2,1)S(1)}, bf16[2,2,1,32,4096]{4,3,2,1,0:T(8,128)(2,1)}, u32[]{:S(2)}, u32[]{:S(2)}) collective-permute-start(bf16[2,2,1,32,4096]{4,3,2,1,0:T(8,128)(2,1)S(1)} %dynamic-slice_convert_fusion.1), channel_id=1, source_target_pairs={{0,1},{1,0},{2,3},{3,2},{4,5},{5,4},{6,7},{7,6},{8,9},{9,8},{10,11... | collective-permute-start | bytes 3145736 | tf_op jit(solution)/shard_map/ppermute | solution.py:30
  757.7 77.4 %collective-permute-start.43 = (bf16[2,2,1,128,1024]{4,3,2,1,0:T(8,128)(2,1)}, bf16[2,2,1,128,1024]{4,3,2,1,0:T(8,128)(2,1)}, u32[]{:S(2)}, u32[]{:S(2)}) collective-permute-start(bf16[2,2,1,128,1024]{4,3,2,1,0:T(8,128)(2,1)} %dynamic-slice_convert_fusion), channel_id=1, source_target_pairs={{0,1},{1,0},{2,3},{3,2},{4,5},{5,4},{6,7},{7,6},{8,9},{9,8},{10,11... | collective-permute-start | bytes 3145736 | tf_op jit(solution)/shard_map/ppermute | solution.py:30
  828.1 111.0 %all-to-all-start.5 = ((bf16[8,512,384]{1,2,0:T(8,128)(2,1)}), bf16[8,512,384]{1,2,0:T(8,128)(2,1)}, u32[]{:S(2)}, u32[]{:S(2)}) async-start(bf16[8,512,384]{1,2,0:T(8,128)(2,1)} %copy.137), calls=%async_computation.5 | async-start | bytes 6291456 | tf_op jit(solution)/shard_map/all_to_all | solution.py:517
  832.9 250.1 %all-gather.15.cloned.1.call-start = ((), (), s32[]{:S(2)}) async-start(), calls=%async_computation.12 | async-start | bytes 2162688 | tf_op jit(solution)/shard_map/all_gather | solution.py:504
  833.0 54.7 %collective-permute-start.32 = (bf16[2,1,1,32,1024]{4,3,2,1,0:T(8,128)(2,1)S(1)}, bf16[2,1,1,32,1024]{4,3,2,1,0:T(8,128)(2,1)S(1)}, u32[]{:S(2)}, u32[]{:S(2)}) collective-permute-start(bf16[2,1,1,32,1024]{4,3,2,1,0:T(8,128)(2,1)S(1)} %dynamic-slice_convert_fusion.10), channel_id=1, source_target_pairs={{0,2},{1,3},{2,0},{3,1},{4,6},{5,7},{6,4},{7,5},{8,10},{9,11},{10,... | collective-permute-start | bytes 393224 | tf_op jit(solution)/shard_map/ppermute | solution.py:30
  837.4 68.1 %collective-permute-start.44 = (bf16[2,1,1,128,1024]{4,3,2,1,0:T(8,128)(2,1)S(1)}, bf16[2,1,1,128,1024]{4,3,2,1,0:T(8,128)(2,1)S(1)}, u32[]{:S(2)}, u32[]{:S(2)}) collective-permute-start(bf16[2,1,1,128,1024]{4,3,2,1,0:T(8,128)(2,1)S(1)} %dynamic-slice_convert_fusion.3), channel_id=1, source_target_pairs={{0,2},{1,3},{2,0},{3,1},{4,6},{5,7},{6,4},{7,5},{8,10},{9,11},{10,... | collective-permute-start | bytes 1572872 | tf_op jit(solution)/shard_map/ppermute | solution.py:30
  839.2 75.8 %collective-permute-start.38 = (bf16[2,1,1,32,4096]{4,3,2,1,0:T(8,128)(2,1)S(1)}, bf16[2,1,1,32,4096]{4,3,2,1,0:T(8,128)(2,1)S(1)}, u32[]{:S(2)}, u32[]{:S(2)}) collective-permute-start(bf16[2,1,1,32,4096]{4,3,2,1,0:T(8,128)(2,1)S(1)} %dynamic-slice_convert_fusion.4), channel_id=1, source_target_pairs={{0,2},{1,3},{2,0},{3,1},{4,6},{5,7},{6,4},{7,5},{8,10},{9,11},{10,... | collective-permute-start | bytes 1572872 | tf_op jit(solution)/shard_map/ppermute | solution.py:30
  1024.5 44.1 %collective-permute-start.16 = (f32[16,4,2048]{2,1,0:T(4,128)S(1)}, f32[16,4,2048]{2,1,0:T(4,128)S(1)}, u32[]{:S(2)}, u32[]{:S(2)}) collective-permute-start(f32[16,4,2048]{2,1,0:T(4,128)S(1)} %pad_maximum_fusion.8), channel_id=1, source_target_pairs={{0,16},{8,24},{16,0},{24,8},{1,17},{9,25},{17,1},{25,9},{2,18},{10... | collective-permute-start | bytes 1572872 | tf_op jit(solution)/shard_map/ppermute | solution.py:30
  (134 other events, 2882.7 us)
Sparse Core Ops, SparseCore 0:
  10.9 83.4 all-gather.6
  97.4 66.1 all-gather.8
  166.5 81.6 all-gather.10
  251.1 82.4 all-gather.12
  990.4 58.5 all-gather.14

commit v2 on v1

--- a/solution.py
+++ b/solution.py
@@ -31,7 +31,7 @@
 
 
 def own_bit(axis, bit):
-    return (lax.axis_index(axis) // bit) % 2
+    return lax.shift_right_logical(lax.axis_index(axis), bit.bit_length() - 1) & 1
 
 
 def axis_bits(axis):
@@ -62,6 +62,32 @@
     return parts.reshape(parts.shape[len(bits) :])
 
 
+def near_order():
+    return axis_bits("clip")[::-1] + axis_bits("seq")[::-1]
+
+
+def halve_rows(parts, bits):
+    for axis, bit in bits:
+        half = parts.shape[0] // 2
+        mine = own_bit(axis, bit)
+        keep = lax.dynamic_slice_in_dim(parts, mine * half, half, 0)
+        send = lax.dynamic_slice_in_dim(parts, (1 - mine) * half, half, 0)
+        parts = keep + swap_bit(send, axis, bit)
+    return parts
+
+
+def spread_rows(rows, bits):
+    for axis, bit in reversed(bits):
+        other = swap_bit(rows, axis, bit)
+        low = own_bit(axis, bit) == 0
+        rows = jnp.concatenate([jnp.where(low, rows, other), jnp.where(low, other, rows)], axis=0)
+    return rows
+
+
+def after(value, *others):
+    return lax.optimization_barrier((value,) + others)[0]
+
+
 def double_rows(row, bits):
     rows = row[None]
     for axis, bit in reversed(bits):
@@ -117,8 +143,20 @@
     return jnp.where(lane < half, pltpu.roll(values, width - half, 1), pltpu.roll(values, half, 1))
 
 
-def project_kernel(x_ref, wq_ref, wk_ref, wv_ref, bq_ref, bk_ref, bv_ref, cos_ref, sin_ref, out_ref, *, span):
-    x = x_ref[...]
+def project_kernel(
+    token_ref, mod_ref, wq_ref, wk_ref, wv_ref, bq_ref, bk_ref, bv_ref, cos_ref, sin_ref, out_ref, normed_ref, *, span
+):
+    frames = mod_ref.shape[1]
+    patch = token_ref.shape[0] // frames
+
+    @pl.when(pl.program_id(0) == 0)
+    def _():
+        for f in range(frames):
+            rows = slice(f * patch, (f + 1) * patch)
+            unit, _ = norm_parts(token_ref[rows, :].astype(f32))
+            normed_ref[rows, :] = (unit * (1.0 + mod_ref[1, f : f + 1, :]) + mod_ref[0, f : f + 1, :]).astype(bf16)
+
+    x = normed_ref[...]
     cosine, sine = cos_ref[...], sin_ref[...]
     groups = wq_ref.shape[1] // span
     for place, (w_ref, b_ref) in enumerate(((wq_ref, bq_ref), (wk_ref, bk_ref), (wv_ref, bv_ref))):
@@ -130,29 +168,331 @@
             out_ref[g, :, place * span : (place + 1) * span] = value[:, g * span : (g + 1) * span]
 
 
-def project(x, weight, bias, cosine, sine, groups):
-    rows, width = x.shape
+def whole_block(shape):
+    return pl.BlockSpec(shape, lambda j: (0,) * len(shape))
+
+
+def column_specs(height, block, steps):
+    return [pl.BlockSpec((height, block), functools.partial(lambda p, j: (0, p * steps + j), p)) for p in range(3)]
+
+
+def project(tokens, mods, weight, bias, cosine, sine, groups):
+    rows, width = tokens.shape
     span = width // groups
     block = max(span, 256)
     per_step = block // span
     steps = groups // per_step
-    weight_specs = [
-        pl.BlockSpec((width, block), functools.partial(lambda p, j: (0, p * steps + j), p)) for p in range(3)
-    ]
-    bias_specs = [pl.BlockSpec((1, block), functools.partial(lambda p, j: (0, p * steps + j), p)) for p in range(3)]
-    whole = pl.BlockSpec((rows, block), lambda j: (0, 0))
     return pl.pallas_call(
         functools.partial(project_kernel, span=span),
         grid=(steps,),
-        in_specs=[pl.BlockSpec((rows, width), lambda j: (0, 0))] + weight_specs + bias_specs + [whole, whole],
-        out_specs=pl.BlockSpec((per_step, rows, 3 * span), lambda j: (j, 0, 0)),
-        out_shape=jax.ShapeDtypeStruct((groups, rows, 3 * span), bf16),
+        in_specs=[whole_block((rows, width)), whole_block(mods.shape)]
+        + column_specs(width, block, steps)
+        + column_specs(1, block, steps)
+        + [whole_block((rows, block))] * 2,
+        out_specs=(pl.BlockSpec((per_step, rows, 3 * span), lambda j: (j, 0, 0)), whole_block((rows, width))),
+        out_shape=(
+            jax.ShapeDtypeStruct((groups, rows, 3 * span), bf16),
+            jax.ShapeDtypeStruct((rows, width), bf16),
+        ),
         compiler_params=pltpu.CompilerParams(vmem_limit_bytes=32 << 20),
         cost_estimate=pl.CostEstimate(
-            flops=2 * rows * width * 3 * width, bytes_accessed=2 * width * 3 * width + 8 * rows * width, transcendentals=0
+            flops=6 * rows * width * width, bytes_accessed=6 * width * width + 10 * rows * width, transcendentals=0
         ),
         name="project",
-    )(x, weight, weight, weight, bias, bias, bias, cosine, sine)
+    )(tokens, mods, weight, weight, weight, bias, bias, bias, cosine, sine)
+
+
+def project_back_kernel(
+    back_ref, wq_ref, wk_ref, wv_ref, token_ref, scale_ref, resid_ref, grad_ref, proj_ref, sums_ref, bias_ref, acc_ref, *, span
+):
+    frames = scale_ref.shape[0]
+    rows_all, width = token_ref.shape
+    patch = rows_all // frames
+    step = pl.program_id(0)
+    block = wq_ref.shape[1]
+
+    @pl.when(step == 0)
+    def _():
+        acc_ref[...] = jnp.zeros_like(acc_ref)
+
+    for place, w_ref in enumerate((wq_ref, wk_ref, wv_ref)):
+        band = slice(place * span, (place + 1) * span)
+        piece = jnp.concatenate([back_ref[g, :, band] for g in range(block // span)], axis=1)
+        columns = pl.ds(pl.multiple_of(place * width + step * block, block), block)
+        proj_ref[:, columns] = piece
+        bias_ref[:, columns] = jnp.sum(piece.astype(f32), axis=0, keepdims=True)
+        acc_ref[...] += dot(piece, w_ref[...], NT)
+
+    @pl.when(step == pl.num_programs(0) - 1)
+    def _():
+        for f in range(frames):
+            rows = slice(f * patch, (f + 1) * patch)
+            unit, inverse = norm_parts(token_ref[rows, :].astype(f32))
+            grad = acc_ref[rows, :]
+            grad_ref[rows, :] = resid_ref[rows, :] + norm_back(unit, inverse, grad, scale_ref[f : f + 1, :])
+            sums_ref[0, f : f + 1, :] = jnp.sum(grad, axis=0, keepdims=True)
+            sums_ref[1, f : f + 1, :] = jnp.sum(grad * unit, axis=0, keepdims=True)
+
+
+def project_back(back, weight, tokens, scales, d_resid):
+    groups, rows, _ = back.shape
+    width = tokens.shape[1]
+    span = width // groups
+    block = max(span, 256)
+    per_step = block // span
+    steps = groups // per_step
+    return pl.pallas_call(
+        functools.partial(project_back_kernel, span=span),
+        grid=(steps,),
+        in_specs=[pl.BlockSpec((per_step, rows, 3 * span), lambda j: (j, 0, 0))]
+        + column_specs(width, block, steps)
+        + [whole_block((rows, width)), whole_block(scales.shape), whole_block((rows, width))],
+        out_specs=(
+            whole_block((rows, width)),
+            whole_block((rows, 3 * width)),
+            whole_block((2,) + scales.shape),
+            whole_block((1, 3 * width)),
+        ),
+        out_shape=(
+            jax.ShapeDtypeStruct((rows, width), f32),
+            jax.ShapeDtypeStruct((rows, 3 * width), bf16),
+            jax.ShapeDtypeStruct((2,) + scales.shape, f32),
+            jax.ShapeDtypeStruct((1, 3 * width), f32),
+        ),
+        scratch_shapes=[pltpu.VMEM((rows, width), f32)],
+        compiler_params=pltpu.CompilerParams(vmem_limit_bytes=40 << 20),
+        cost_estimate=pl.CostEstimate(
+            flops=6 * rows * width * width, bytes_accessed=6 * width * width + 22 * rows * width, transcendentals=0
+        ),
+        name="project_back",
+    )(back, weight, weight, weight, tokens, scales, d_resid)
+
+
+GELU_RATE = math.sqrt(2.0 / math.pi)
+GELU_CUBE = 0.044715
+
+
+def middle_kernel(
+    back_ref,
+    token_ref,
+    cot_ref,
+    mod_ref,
+    wo_ref,
+    bo_ref,
+    up_ref,
+    bup_ref,
+    down_ref,
+    bdown_ref,
+    out_ref,
+    dres_ref,
+    mixed_ref,
+    normed_ref,
+    act_ref,
+    dhid_ref,
+    dmlp_ref,
+    dattn_ref,
+    dmix_ref,
+    sums_ref,
+    bup_sum_ref,
+    bsum_ref,
+    attn_ref,
+    res_ref,
+    mlp_ref,
+    dn_ref,
+):
+    groups, rows_all, span = back_ref.shape
+    width = token_ref.shape[1]
+    frames = mod_ref.shape[1]
+    patch = rows_all // frames
+    step = pl.program_id(0)
+
+    @pl.when(step == 0)
+    def _():
+        for g in range(groups):
+            mixed_ref[:, g * span : (g + 1) * span] = back_ref[g]
+        attn_ref[...] = dot(mixed_ref[...], wo_ref[...].reshape(width, width)) + bo_ref[...]
+        for f in range(frames):
+            rows = slice(f * patch, (f + 1) * patch)
+            resid = token_ref[rows, :].astype(f32) + mod_ref[0, f : f + 1, :] * attn_ref[rows, :]
+            res_ref[rows, :] = resid
+            unit, _ = norm_parts(resid)
+            normed_ref[rows, :] = (unit * (1.0 + mod_ref[2, f : f + 1, :]) + mod_ref[1, f : f + 1, :]).astype(bf16)
+            dmlp_ref[rows, :] = (mod_ref[3, f : f + 1, :] * cot_ref[rows, :].astype(f32)).astype(bf16)
+        mlp_ref[...] = jnp.zeros_like(mlp_ref)
+        dn_ref[...] = jnp.zeros_like(dn_ref)
+
+    up = up_ref[...].reshape(width, -1)
+    down = down_ref[...].reshape(-1, width)
+    hidden = dot(normed_ref[...], up) + bup_ref[...]
+    square = hidden * hidden
+    bend = jnp.tanh(GELU_RATE * (hidden + GELU_CUBE * (square * hidden)))
+    share = 0.5 * (1.0 + bend)
+    active = (hidden * share).astype(bf16)
+    act_ref[...] = active
+    mlp_ref[...] += dot(active, down)
+    slope = share + 0.5 * hidden * (1.0 - bend * bend) * (GELU_RATE + (3.0 * GELU_RATE * GELU_CUBE) * square)
+    d_hidden = (dot(dmlp_ref[...], down, NT) * slope).astype(bf16)
+    dhid_ref[...] = d_hidden
+    bup_sum_ref[...] = jnp.sum(d_hidden.astype(f32), axis=0, keepdims=True)
+    dn_ref[...] += dot(d_hidden, up, NT)
+
+    @pl.when(step == pl.num_programs(0) - 1)
+    def _():
+        bsum = None
+        for f in range(frames):
+            rows = slice(f * patch, (f + 1) * patch)
+            resid = res_ref[rows, :]
+            mlp = mlp_ref[rows, :] + bdown_ref[...]
+            out_ref[rows, :] = (resid + mod_ref[3, f : f + 1, :] * mlp).astype(bf16)
+            cot = cot_ref[rows, :].astype(f32)
+            sums_ref[3, f : f + 1, :] = jnp.sum(cot * mlp, axis=0, keepdims=True)
+            unit, inverse = norm_parts(resid)
+            grad = dn_ref[rows, :]
+            sums_ref[1, f : f + 1, :] = jnp.sum(grad, axis=0, keepdims=True)
+            sums_ref[2, f : f + 1, :] = jnp.sum(grad * unit, axis=0, keepdims=True)
+            d_resid = cot + norm_back(unit, inverse, grad, mod_ref[2, f : f + 1, :])
+            dres_ref[rows, :] = d_resid
+            sums_ref[0, f : f + 1, :] = jnp.sum(d_resid * attn_ref[rows, :], axis=0, keepdims=True)
+            d_attn = (mod_ref[0, f : f + 1, :] * d_resid).astype(bf16)
+            dattn_ref[rows, :] = d_attn
+            term = jnp.concatenate(
+                [
+                    jnp.sum(d_attn.astype(f32), axis=0, keepdims=True),
+                    jnp.sum(dmlp_ref[rows, :].astype(f32), axis=0, keepdims=True),
+                ],
+                axis=0,
+            )
+            bsum = term if bsum is None else bsum + term
+        bsum_ref[...] = bsum
+        d_mixed = dot(dattn_ref[...], wo_ref[...].reshape(width, width), NT).astype(bf16)
+        for g in range(groups):
+            dmix_ref[g] = d_mixed[:, g * span : (g + 1) * span]
+
+
+def middle(back, tokens, cot, mods, packed, biases):
+    groups, rows, span = back.shape
+    width = tokens.shape[1]
+    devices, _, piece, _ = packed.shape
+    hidden = 4 * width
+    steps = 8
+    block = hidden // steps
+    halves = width // block
+    owners = block // (4 * piece)
+    bias_out, bias_up, bias_down = biases
+    token_block = whole_block((rows, width))
+    hidden_block = pl.BlockSpec((rows, block), lambda j: (0, j))
+    return pl.pallas_call(
+        middle_kernel,
+        grid=(steps,),
+        in_specs=[
+            whole_block(back.shape),
+            token_block,
+            token_block,
+            whole_block(mods.shape),
+            pl.BlockSpec((devices, 1, piece, width), lambda j: (0, 8, 0, 0), pipeline_mode=pl.Buffered(1)),
+            whole_block((1, width)),
+            pl.BlockSpec((devices, 1, piece, block), lambda j: (0, 4 + j // halves, 0, j % halves)),
+            pl.BlockSpec((1, block), lambda j: (0, j)),
+            pl.BlockSpec((owners, 4, piece, width), lambda j: (j, 0, 0, 0)),
+            whole_block((1, width)),
+        ],
+        out_specs=(
+            token_block,
+            token_block,
+            token_block,
+            token_block,
+            hidden_block,
+            hidden_block,
+            token_block,
+            token_block,
+            whole_block(back.shape),
+            whole_block(mods.shape),
+            pl.BlockSpec((1, block), lambda j: (0, j)),
+            whole_block((2, width)),
+        ),
+        out_shape=(
+            jax.ShapeDtypeStruct((rows, width), bf16),
+            jax.ShapeDtypeStruct((rows, width), f32),
+            jax.ShapeDtypeStruct((rows, width), bf16),
+            jax.ShapeDtypeStruct((rows, width), bf16),
+            jax.ShapeDtypeStruct((rows, hidden), bf16),
+            jax.ShapeDtypeStruct((rows, hidden), bf16),
+            jax.ShapeDtypeStruct((rows, width), bf16),
+            jax.ShapeDtypeStruct((rows, width), bf16),
+            jax.ShapeDtypeStruct(back.shape, bf16),
+            jax.ShapeDtypeStruct(mods.shape, f32),
+            jax.ShapeDtypeStruct((1, hidden), f32),
+            jax.ShapeDtypeStruct((2, width), f32),
+        ),
+        scratch_shapes=[pltpu.VMEM((rows, width), f32)] * 4,
+        compiler_params=pltpu.CompilerParams(vmem_limit_bytes=54 << 20),
+        cost_estimate=pl.CostEstimate(
+            flops=36 * rows * width * width, bytes_accessed=18 * width * width + 50 * rows * width, transcendentals=4 * rows * width
+        ),
+        name="middle",
+    )(back, tokens, cot, mods, packed, bias_out, packed, bias_up, packed, bias_down)
+
+
+def weight_part_kernel(index_ref, *refs, clips, addends):
+    left, right = refs[:clips], refs[clips : 2 * clips]
+    extra = refs[2 * clips : 2 * clips + addends]
+    out_ref, flat_ref = refs[2 * clips + addends :]
+    rows = left[0].shape[0]
+
+    @pl.when(pl.program_id(1) == 0)
+    def _():
+        for c in range(clips):
+            flat_ref[:, c * rows : (c + 1) * rows] = jnp.transpose(left[c][...])
+
+    total = dot(flat_ref[:, 0:rows], right[0][...])
+    for c in range(1, clips):
+        total += dot(flat_ref[:, c * rows : (c + 1) * rows], right[c][...])
+    for ref in extra:
+        total += ref[0].astype(f32)
+    out_ref[0] = total.astype(out_ref.dtype)
+
+
+def weight_part(left, right, quarters, addends, kind):
+    rows, height = left[0].shape
+    columns = right[0].shape[1]
+    quarter = height // lax.axis_size("clip")
+    block = 512
+    count = quarters.shape[0]
+    in_specs = [pl.BlockSpec((rows, quarter), lambda i, j, q: (0, q[i]))] * len(left)
+    in_specs += [pl.BlockSpec((rows, block), lambda i, j, q: (0, j))] * len(right)
+    in_specs += [
+        pl.BlockSpec((1, quarter, block), functools.partial(lambda place, i, j, q: (place, 0, j), place)) for _, place in addends
+    ]
+    return pl.pallas_call(
+        functools.partial(weight_part_kernel, clips=len(left), addends=len(addends)),
+        grid_spec=pltpu.PrefetchScalarGridSpec(
+            num_scalar_prefetch=1,
+            grid=(count, columns // block),
+            in_specs=in_specs,
+            out_specs=pl.BlockSpec((1, quarter, block), lambda i, j, q: (i, 0, j)),
+            scratch_shapes=[pltpu.VMEM((quarter, len(left) * rows), bf16)],
+        ),
+        out_shape=jax.ShapeDtypeStruct((count, quarter, columns), kind),
+        compiler_params=pltpu.CompilerParams(vmem_limit_bytes=32 << 20),
+        cost_estimate=pl.CostEstimate(
+            flops=2 * count * len(left) * rows * quarter * columns,
+            bytes_accessed=len(left) * rows * (quarter + columns) * 2 + 4 * count * quarter * columns,
+            transcendentals=0,
+        ),
+        name="weight_part",
+    )(quarters, *left, *right, *[array for array, _ in addends])
+
+
+def weight_grad_kernels(left, right):
+    mine = lax.axis_index("clip").astype(jnp.int32)
+
+    def quarters(*flips):
+        return jnp.stack([mine ^ flip for flip in flips])
+
+    core = swap_bit(weight_part(left, right, quarters(3, 1), (), bf16), "clip", 1)
+    across = swap_bit(weight_part(left, right, quarters(2), ((core, 0),), bf16), "clip", 2)
+    total = weight_part(left, right, quarters(0), ((core, 1), (across, 0)), f32)
+    return halve_sum(total.reshape((lax.axis_size("seq"), -1, right[0].shape[1])), axis_bits("seq"), bf16)
 
 
 def attend_kernel(qkv_ref, mix_ref, full_ref, log_ref, vt_ref, *, total, span, block):
@@ -355,7 +695,197 @@
     return lax.map(one, (queries, keys, values, grads, logs))
 
 
-def body(
+def level_rows(ctx_count, noise_level, rows):
+    clips = ctx_count.shape[0]
+    seq_devices = lax.axis_size("seq")
+    plan = jnp.concatenate([ctx_count[:, None], noise_level], axis=1)
+    plan = double_rows(plan, axis_bits("clip"))
+    levels = jnp.where(jnp.arange(FRAMES, dtype=jnp.int32) < plan[..., :1], 0, plan[..., 1:])
+    if rows < PATCHES:
+        levels = jnp.repeat(levels, PATCHES // rows, axis=-1)
+    frames = max(1, rows // PATCHES)
+    levels = levels.reshape(-1, clips, seq_devices, frames).transpose(0, 2, 1, 3)
+    return levels.reshape(-1, seq_devices, clips * frames)
+
+
+def condition(levels, here, depth, width):
+    half_width = width // 2
+    feature = here * depth + jnp.arange(depth, dtype=jnp.int32)
+    low_half = feature < half_width
+    freqs = jnp.exp(-math.log(10000.0) * jnp.where(low_half, feature, feature - half_width).astype(f32) / half_width)
+    angles = levels.reshape(-1, 1).astype(f32) * freqs
+    return jax.nn.silu(jnp.where(low_half, jnp.sin(angles), jnp.cos(angles))).astype(bf16)
+
+
+def own_place(shard, here):
+    count = lax.axis_size("clip") * lax.axis_size("seq")
+    whole = jnp.zeros((count * shard.shape[0],), f32)
+    return lax.dynamic_update_slice_in_dim(whole, shard.astype(f32), here * shard.shape[0], 0)
+
+
+def body_by_heads(
+    tokens,
+    ctx_count,
+    noise_level,
+    mod_weight,
+    mod_bias,
+    qkv_weight,
+    qkv_bias,
+    out_weight,
+    out_bias,
+    up_weight,
+    up_bias,
+    down_weight,
+    down_bias,
+    cotangent,
+):
+    clips, rows, width = tokens.shape
+    seq_devices = lax.axis_size("seq")
+    devices = lax.axis_size("clip") * seq_devices
+    order = near_order()
+    here = lax.axis_index("clip") * seq_devices + lax.axis_index("seq")
+    total = rows * seq_devices
+    frames = max(1, rows // PATCHES)
+    span = width // seq_devices
+    lines = clips * frames
+    piece = out_weight.shape[0]
+
+    full_qkv = lax.all_gather(qkv_weight, BOTH, axis=0, tiled=True)
+    shards = jnp.concatenate(
+        [
+            down_weight.reshape(4, piece, width),
+            up_weight.reshape(piece, 4, width).transpose(1, 0, 2),
+            out_weight[None],
+        ],
+        axis=0,
+    )
+    packed = lax.all_gather(shards, BOTH, axis=0)
+
+    levels = level_rows(ctx_count, noise_level, rows)
+    flat_bits = (2,) * len(order)
+    bits_clip, bits_seq = len(axis_bits("clip")), len(axis_bits("seq"))
+    turn = tuple(range(bits_clip))[::-1] + tuple(range(bits_clip, bits_clip + bits_seq))[::-1] + (len(order),)
+    near_levels = levels.reshape(flat_bits + (lines,)).transpose(turn)
+    cond_near = condition(near_levels, here, mod_weight.shape[0], width)
+    cond = condition(levels, here, mod_weight.shape[0], width)
+    mod_place = own_place(mod_bias, here)
+
+    def modulate(columns, biases):
+        weight = mod_weight[:, columns]
+        bias = jnp.concatenate([own_place(b, here) for b in biases]).reshape(lines, -1)
+        rest = jnp.concatenate([jnp.broadcast_to(mod_place[columns], (lines, weight.shape[1])), bias], axis=1)
+        part = jnp.pad(dot(cond_near, weight), ((0, 0), (0, bias.shape[1])))
+        line_rows = halve_rows(part + jnp.tile(rest, (devices, 1)), order)
+        return line_rows[:, : weight.shape[1]], line_rows[:, weight.shape[1] :].reshape(1, -1)
+
+    mod_first, bias_qkv = modulate(slice(0, 2 * width), (qkv_bias,))
+    mod_rest, bias_rest = modulate(slice(2 * width, 6 * width), (out_bias, up_bias, down_bias))
+    bias_out = bias_rest[:, :width]
+    bias_up = bias_rest[:, width : 5 * width]
+    bias_down = bias_rest[:, 5 * width :]
+
+    def blocks(line_rows):
+        return line_rows.reshape(clips, frames, -1, width).transpose(0, 2, 1, 3)
+
+    mods_one, mods_two = blocks(mod_first), blocks(mod_rest)
+
+    positions = lax.axis_index("seq") * rows + jnp.arange(rows, dtype=jnp.int32)
+    cos_local, sin_local = rotary_lanes(positions, max(span, 256))
+    cos_all, sin_all = rotary_lanes(jnp.arange(total, dtype=jnp.int32), span)
+
+    def exchange(value):
+        return lax.all_to_all(value, "seq", 0, 0, tiled=True)
+
+    normed, qkv, mixes, fulls, logs = [], [], [], [], []
+    for c in range(clips):
+        sent, normed_c = project(tokens[c], mods_one[c], full_qkv, bias_qkv, cos_local, sin_local, seq_devices)
+        normed.append(normed_c)
+        if qkv:
+            sent = after(sent, qkv[-1])
+        qkv.append(exchange(sent))
+    backs = []
+    for c in range(clips):
+        mix, full, log = attend(qkv[c].reshape(total, 3 * span), span)
+        mixes.append(mix)
+        fulls.append(full)
+        logs.append(log)
+        backs.append(exchange(after(mix.reshape(seq_devices, rows, span), qkv[-1] if c == 0 else backs[-1])))
+
+    results = []
+    d_mixed = []
+    for c in range(clips):
+        back = after(backs[c], mixes[-1])
+        results.append(middle(back, tokens[c], cotangent[c], mods_two[c], packed, (bias_out, bias_up, bias_down)))
+        d_mixed.append(exchange(after(results[c][8], backs[-1] if c == 0 else d_mixed[-1])))
+
+    d_qkv, exchanged = [], []
+    for c in range(clips):
+        grad = after(d_mixed[c], results[-1][8] if c == 0 else d_qkv[-1])
+        grad = grad.reshape(total, span)
+        d_qkv.append(attend_back(qkv[c].reshape(total, 3 * span), grad, fulls[c], logs[c], cos_all, sin_all, span))
+        sent = d_qkv[c].reshape(seq_devices, rows, 3 * span)
+        exchanged.append(exchange(after(sent, d_mixed[-1] if c == 0 else exchanged[-1])))
+
+    def late(place):
+        return list(lax.optimization_barrier(tuple(r[place] for r in results) + (d_qkv[-1],))[:-1])
+
+    mixed_all, normed_two, active, d_hidden, d_mlp, d_attn = [late(place) for place in (2, 3, 4, 5, 6, 7)]
+    grad_down = weight_grad_kernels(active, d_mlp)
+    grad_up = weight_grad_kernels(normed_two, d_hidden)
+    grad_out = weight_grad_kernels(mixed_all, d_attn)
+
+    def line_sums(sums):
+        return sums.transpose(1, 0, 2).reshape(frames, -1)
+
+    def with_bias(lines_now, vectors):
+        return jnp.concatenate([jnp.concatenate(lines_now, axis=0), jnp.concatenate(vectors).reshape(lines, -1)], axis=1)
+
+    bias_up_sum = sum(r[10][0] for r in results)
+    bias_pair = sum(r[11] for r in results)
+    early = with_bias([line_sums(r[9]) for r in results], [bias_pair[0], bias_up_sum, bias_pair[1]])
+    early_rows = lax.all_gather(early, BOTH, axis=0, tiled=True)
+
+    last = [
+        project_back(exchanged[c], full_qkv, tokens[c], mods_one[c][1], results[c][1]) for c in range(clips)
+    ]
+    grad_qkv = weight_grad_kernels(normed, [r[1] for r in last])
+    late_rows = with_bias([line_sums(r[2]) for r in last], [sum(r[3][0] for r in last)])
+    late_rows = spread_rows(late_rows, order)
+
+    def own_columns(sums, shard):
+        return lax.dynamic_slice_in_dim(sums, here * shard.shape[0], shard.shape[0], 0)
+
+    def spans(all_rows, columns):
+        vectors = jnp.sum(all_rows[:, columns:].reshape(devices, -1), axis=0)
+        return all_rows[:, :columns], vectors
+
+    late_mod, late_vectors = spans(late_rows, 2 * width)
+    early_mod, early_vectors = spans(early_rows, 4 * width)
+    grad_mod = jnp.concatenate(
+        [
+            lax.dot_general(rows_cond.astype(f32), r, TN, precision=highest, preferred_element_type=f32)
+            for rows_cond, r in ((cond_near, late_mod), (cond, early_mod))
+        ],
+        axis=1,
+    )
+    mod_sum = jnp.concatenate([jnp.sum(late_mod, axis=0), jnp.sum(early_mod, axis=0)])
+    return (
+        jnp.stack([r[0] for r in results]),
+        jnp.stack([r[0] for r in last]),
+        grad_mod,
+        own_columns(mod_sum, mod_bias),
+        grad_qkv,
+        own_columns(late_vectors, qkv_bias),
+        grad_out,
+        own_columns(early_vectors[:width], out_bias),
+        grad_up,
+        own_columns(early_vectors[width : 5 * width], up_bias),
+        grad_down,
+        own_columns(early_vectors[5 * width :], down_bias),
+    )
+
+
+def body_gathered(
     tokens,
     ctx_count,
     noise_level,
@@ -379,8 +909,6 @@
     total = rows * seq_devices
     frames = max(1, rows // PATCHES)
     patch_rows = rows // frames
-    by_heads = HEADS % seq_devices == 0
-    span = width // seq_devices
 
     full_qkv = lax.all_gather(qkv_weight, BOTH, axis=0, tiled=True)
     full_out = lax.all_gather(out_weight, BOTH, axis=0, tiled=True)
@@ -395,33 +923,17 @@
         first += piece.shape[0]
     bias_qkv, bias_out, bias_up, bias_down = full_biases
 
-    plan = jnp.concatenate([ctx_count[:, None], noise_level], axis=1)
-    plan = double_rows(plan, axis_bits("clip"))
-    levels = jnp.where(jnp.arange(FRAMES, dtype=jnp.int32) < plan[..., :1], 0, plan[..., 1:])
-    if rows < PATCHES:
-        levels = jnp.repeat(levels, PATCHES // rows, axis=-1)
-    levels = levels.reshape(-1, clips, seq_devices, frames).transpose(0, 2, 1, 3)
-    depth = mod_weight.shape[0]
-    half_width = width // 2
-    feature = here * depth + jnp.arange(depth, dtype=jnp.int32)
-    freqs = jnp.exp(-math.log(10000.0) * (feature % half_width).astype(f32) / half_width)
-    angles = levels.reshape(devices * clips * frames, 1).astype(f32) * freqs
-    cond = jax.nn.silu(jnp.where(feature < half_width, jnp.sin(angles), jnp.cos(angles))).astype(bf16)
+    levels = level_rows(ctx_count, noise_level, rows)
+    cond = condition(levels, here, mod_weight.shape[0], width)
     mod_width = mod_weight.shape[1]
-    bias_place = lax.dynamic_update_slice_in_dim(
-        jnp.zeros((mod_width,), f32), mod_bias.astype(f32), here * mod_bias.shape[0], 0
-    )
-    partial = dot(cond, mod_weight) + bias_place
+    partial = dot(cond, mod_weight) + own_place(mod_bias, here)
     modulation = halve_sum(partial.reshape(devices, clips * frames, mod_width), bits)
     modulation = modulation.reshape(clips, frames, 1, mod_width)
 
     positions = lax.axis_index("seq") * rows + jnp.arange(rows, dtype=jnp.int32)
-    cos_local, sin_local = rotary_lanes(positions, max(span, 256))
-    if by_heads:
-        cos_all, sin_all = rotary_lanes(jnp.arange(total, dtype=jnp.int32), span)
-    else:
-        key_frame = jnp.arange(total, dtype=jnp.int32) // PATCHES
-        allowed = key_frame[None, :] <= (positions // PATCHES)[:, None]
+    cosine, sine = rotary_lanes(positions, HEAD_DIM)
+    key_frame = jnp.arange(total, dtype=jnp.int32) // PATCHES
+    allowed = key_frame[None, :] <= (positions // PATCHES)[:, None]
 
     def flat(value):
         return value.reshape(rows, value.shape[-1])
@@ -438,28 +950,19 @@
         tokens_now = split(tokens[c].astype(f32))
         unit, inverse = norm_parts(tokens_now)
         normed = flat((unit * (1.0 + mods[1]) + mods[0]).astype(bf16))
-        if by_heads:
-            sent = project(normed, full_qkv, bias_qkv, cos_local, sin_local, seq_devices)
-            qkv = lax.all_to_all(sent, "seq", 0, 0, tiled=True).reshape(total, 3 * span)
-            mix, full, logs = attend(qkv, span)
-            back = lax.all_to_all(mix.reshape(seq_devices, rows, span), "seq", 0, 0, tiled=True)
-            mixed = back.transpose(1, 0, 2).reshape(rows, width)
-            kept = (qkv, full, logs)
-        else:
-            projected = dot(normed, full_qkv) + bias_qkv
-            views = []
-            for place in range(3):
-                view = to_heads(projected[:, place * width : (place + 1) * width])
-                if place < 2:
-                    cosine, sine = cos_local[:, :HEAD_DIM], sin_local[:, :HEAD_DIM]
+        projected = dot(normed, full_qkv) + bias_qkv
+        views = []
+        for place in range(3):
+            view = to_heads(projected[:, place * width : (place + 1) * width])
+            if place < 2:
                     view = view * cosine + jnp.roll(view, HEAD_DIM // 2, -1) * sine
-                views.append(view.astype(bf16))
-            queries, keys, values = views
-            keys = lax.all_gather(keys, "seq", axis=1, tiled=True)
-            values = lax.all_gather(values, "seq", axis=1, tiled=True)
-            mix, logs = gathered_forward(queries, keys, values, allowed)
-            mixed = mix.transpose(1, 0, 2).reshape(rows, width).astype(bf16)
-            kept = (queries, keys, values, logs)
+            views.append(view.astype(bf16))
+        queries, keys, values = views
+        keys = lax.all_gather(keys, "seq", axis=1, tiled=True)
+        values = lax.all_gather(values, "seq", axis=1, tiled=True)
+        mix, logs = gathered_forward(queries, keys, values, allowed)
+        mixed = mix.transpose(1, 0, 2).reshape(rows, width).astype(bf16)
+        kept = (queries, keys, values, logs)
         saved.append((mods, tokens_now, unit, inverse, normed, kept, mixed))
 
     outputs = []
@@ -509,21 +1012,12 @@
     for c in range(clips):
         mods, tokens_now, unit, inverse, normed, kept, mixed = saved[c]
         d_resid, d_mixed = middle[c][6], middle[c][7]
-        if by_heads:
-            sent = d_mixed.reshape(rows, seq_devices, span).transpose(1, 0, 2)
-            grad = lax.all_to_all(sent, "seq", 0, 0, tiled=True).reshape(total, span)
-            qkv, full, logs = kept
-            d_qkv = attend_back(qkv, grad, full, logs, cos_all, sin_all, span)
-            back = lax.all_to_all(d_qkv.reshape(seq_devices, rows, 3 * span), "seq", 0, 0, tiled=True)
-            d_projected = back.reshape(seq_devices, rows, 3, span).transpose(1, 2, 0, 3).reshape(rows, 3 * width)
-        else:
-            queries, keys, values, logs = kept
-            dq, dk, dv = gathered_back(queries, keys, values, to_heads(d_mixed), logs, allowed)
-            dk = lax.psum_scatter(dk.astype(bf16), "seq", scatter_dimension=1, tiled=True).astype(f32)
-            dv = lax.psum_scatter(dv.astype(bf16), "seq", scatter_dimension=1, tiled=True).astype(f32)
-            cosine, sine = cos_local[:, :HEAD_DIM], sin_local[:, :HEAD_DIM]
-            views = [g * cosine - jnp.roll(g, HEAD_DIM // 2, -1) * sine for g in (dq, dk)] + [dv]
-            d_projected = jnp.concatenate([g.transpose(1, 0, 2).reshape(rows, width) for g in views], axis=1).astype(bf16)
+        queries, keys, values, logs = kept
+        dq, dk, dv = gathered_back(queries, keys, values, to_heads(d_mixed), logs, allowed)
+        dk = lax.psum_scatter(dk.astype(bf16), "seq", scatter_dimension=1, tiled=True).astype(f32)
+        dv = lax.psum_scatter(dv.astype(bf16), "seq", scatter_dimension=1, tiled=True).astype(f32)
+        views = [g * cosine - jnp.roll(g, HEAD_DIM // 2, -1) * sine for g in (dq, dk)] + [dv]
+        d_projected = jnp.concatenate([g.transpose(1, 0, 2).reshape(rows, width) for g in views], axis=1).astype(bf16)
         projected_grads.append(d_projected)
         d_normed = split(dot(d_projected, full_qkv, NT))
         inputs_grad.append(flat(d_resid + norm_back(unit, inverse, d_normed, mods[1])))
@@ -568,6 +1062,8 @@
 
 
 def solution(mesh):
+    by_heads = HEADS % mesh.shape["seq"] == 0
+    body = body_by_heads if by_heads else body_gathered
     token_place = P("clip", "seq", None)
     matrix, vector = P(BOTH, None), P(BOTH)
     weights = (matrix, vector) * 5

time: 1120 us -> 983 us (0.88)
  matrix products: 195 us -> 5.82 us
  Pallas kernels: 211 us -> 370 us
  blocking collectives: 84.6 us -> 0 us
  other arithmetic: 90.3 us -> 42.3 us
  waiting for transfers between devices: 341 us -> 371 us
    dot_general x31 -> x2, matrix products: 193 us -> 1.31 us  [dot(): return lax.dot_general(left, right, dims, preferred_element_type=f32)]
    pallas_call x0 -> x16, Pallas kernels: none -> 158 us  [the longest x12 71.7 us: weight_part(): pl.pallas_call(functools.partial(weight_part_kernel, clips=len(left), add...]
    all_to_all x1 -> x0, blocking collectives: 84.6 us -> none  [body(): qkv = lax.all_to_all(sent, 'seq', 0, 0, tiled=True).reshape(total, 3 * span)]
    ppermute x46 -> x37, waiting for transfers between devices: 197 us -> 248 us  [swap_bit(): return lax.ppermute(value, axis, [(i, i ^ bit) for i in range(count)])]
    unnamed x201 -> x229, local copies, waits for them, and re-layouts: 18.9 us -> 57.6 us
    convert_element_type x9 -> x1, other arithmetic: 20.6 us -> 0.09 us  [condition(): angles = levels.reshape(-1, 1).astype(f32) * freqs]
    all_gather x5 -> x3, waiting for transfers between devices: 44.5 us -> 27.6 us  [the longest x1 27.6 us: body_by_heads(): full_qkv = lax.all_gather(qkv_weight, BOTH, axis=0, tiled=True)]
    transpose x4 -> x0, local copies, waits for them, and re-layouts: 16 us -> none  [body(): back.reshape(seq_devices, rows, 3, span).transpose(1, 2, 0, 3)]
  transfers between devices with their start and end apart: 58 -> 48, of which waited for: 25 -> 24; matrix products, arithmetic and copies ran while one was open for 18% -> 8% of each run, Pallas kernels for 15% -> 34%
where the time goes in v2:
time: 983 us; the launch traced here: 973 us
  waiting for transfers between devices  371 us (38%)
  Pallas kernels  370 us (38%)
  starting transfers between devices  84.9 us (9%)
  local copies, waits for them, and re-layouts  83.1 us (8%)
  other arithmetic  42.3 us (4%)
  between operations  15.6 us (2%)
    ppermute x37, waiting for transfers between devices, swap_bit(): return lax.ppermute(value, axis, [(i, i ^ bit) for i in range(count)])  248 us
    pallas_call x2, Pallas kernels, attend_back(): pl.pallas_call(functools.partial(attend_back_kernel, total=total, span=sp...  128 us
    all_to_all x8, waiting for transfers between devices, exchange(): return lax.all_to_all(value, 'seq', 0, 0, tiled=True)  94.8 us
    pallas_call x12, Pallas kernels, weight_part(): pl.pallas_call(functools.partial(weight_part_kernel, clips=len(left), add...  71.7 us
    pallas_call x2, Pallas kernels, attend(): pl.pallas_call(functools.partial(attend_kernel, total=total, span=span, b...  70.9 us
    pallas_call x2, Pallas kernels, middle(): pl.pallas_call(middle_kernel, grid=(steps,), in_specs=[whole_block(back.s...  68.9 us
    unnamed x229, local copies, waits for them, and re-layouts  57.6 us
    ppermute x37, starting transfers between devices, swap_bit(): return lax.ppermute(value, axis, [(i, i ^ bit) for i in range(count)])  44.3 us
  transfers between devices with their start and end apart: 48, of which 24 were waited for; matrix products, arithmetic and copies ran while one was open for 8% of the time, Pallas kernels for 34%

profile of v2, /device:TPU:0, one launch (start us, length us, event | category | flops | bytes accessed | tf_op | source)
XLA Modules:
  0.0 972.9 jit_solution(3025501488859244824)
XLA Ops:
  57.1 27.6 %all-gather.6.cloned.1.call-done.wq_ref.wk_ref.wv_ref = bf16[1024,3072]{1,0:T(8,128)(2,1)} async-done(((bf16[32,3072]{1,0:T(8,128)(2,1)}), bf16[1024,3072]{1,0:T(8,128)(2,1)}) %all-gather.6.cloned.1.call-update) | async-done | bytes 6291472 | tf_op jit(solution)/shard_map/all_gather | solution.py:753
  105.6 16.4 %collective-permute-done.8 = f32[32,5632]{1,0:T(8,128)S(1)} collective-permute-done((f32[32,5632]{1,0:T(8,128)S(1)}, f32[32,5632]{1,0:T(8,128)S(1)}, u32[]{:S(2)}, u32[]{:S(2)}) %collective-permute-start.8) | collective-permute-done | bytes 720928 | tf_op jit(solution)/shard_map/ppermute | solution.py:30
  133.1 71.7 %all-to-all-done = bf16[8,512,384]{2,1,0:T(8,128)(2,1)} async-done(((bf16[8,512,384]{2,1,0:T(8,128)(2,1)}), bf16[8,512,384]{2,1,0:T(8,128)(2,1)}, u32[]{:S(2)}, u32[]{:S(2)}) %all-to-all-start) | async-done | bytes 3145760 | tf_op jit(solution)/shard_map/all_to_all | solution.py:797
  208.6 9.4 fusion
  223.3 85.9 %collective-permute-done.10 = f32[8,5632]{1,0:T(8,128)} collective-permute-done((f32[8,5632]{1,0:T(8,128)S(1)}, f32[8,5632]{1,0:T(8,128)}, u32[]{:S(2)}, u32[]{:S(2)}) %collective-permute-start.10) | collective-permute-done | bytes 180256 | tf_op jit(solution)/shard_map/ppermute | solution.py:30
  310.3 35.7 %attend.2 = (bf16[4096,128]{1,0:T(8,128)(2,1)}, f32[4096,128]{1,0:T(8,128)}, f32[2,4096]{1,0:T(2,128)S(1)}) custom-call(bf16[4096,384]{1,0:T(8,128)(2,1)} %bitcast.11.qkv_ref), custom_call_target="tpu_custom_call" | custom-call | flops 17179869184 | bytes 6291456 | tf_op jit(solution)/shard_map/attend/pallas_call | solution.py:556
  346.5 6.9 all-to-all-start.2
  357.0 35.3 %attend.3 = (bf16[4096,128]{1,0:T(8,128)(2,1)}, f32[4096,128]{1,0:T(8,128)}, f32[2,4096]{1,0:T(2,128)S(1)}) custom-call(bf16[4096,384]{1,0:T(8,128)(2,1)} %bitcast.124), custom_call_target="tpu_custom_call" | custom-call | flops 17179869184 | bytes 6291456 | tf_op jit(solution)/shard_map/attend/pallas_call | solution.py:556
  398.8 23.1 %all-to-all-done.3.back_ref = bf16[8,512,128]{2,1,0:T(8,128)(2,1)S(1)} async-done(((bf16[8,512,128]{2,1,0:T(8,128)(2,1)}), bf16[8,512,128]{2,1,0:T(8,128)(2,1)S(1)}, u32[]{:S(2)}, u32[]{:S(2)}) %all-to-all-start.3) | async-done | bytes 1048608 | tf_op jit(solution)/shard_map/all_to_all | solution.py:797
  422.0 34.6 %middle.2 = (bf16[512,1024]{1,0:T(8,128)(2,1)}, f32[512,1024]{1,0:T(8,128)}, bf16[512,1024]{1,0:T(8,128)(2,1)}, bf16[512,1024]{1,0:T(8,128)(2,1)}, bf16[512,4096...) custom-call(bf16[8,512,128]{2,1,0:T(8,128)(2,1)} %all-to-all-done.2., ...), custom_call_target="tpu_custom_call" | custom-call | flops 19327352832 | bytes 45088768 | tf_op jit(solution)/shard_map/middle/pallas_call | solution.py:384
  460.7 34.3 %middle.3 = (bf16[512,1024]{1,0:T(8,128)(2,1)}, f32[512,1024]{1,0:T(8,128)}, bf16[512,1024]{1,0:T(8,128)(2,1)}, bf16[512,1024]{1,0:T(8,128)(2,1)}, bf16[512,4096...) custom-call(bf16[8,512,128]{2,1,0:T(8,128)(2,1)} %copy-done.85, ...), custom_call_target="tpu_custom_call" | custom-call | flops 19327352832 | bytes 45088768 | tf_op jit(solution)/shard_map/middle/pallas_call | solution.py:384
  504.1 64.1 %attend_back.2 = bf16[4096,384]{1,0:T(8,128)(2,1)} custom-call(bf16[4096,384]{1,0:T(8,128)(2,1)} %bitcast.11.qkv_ref, bf16[4096,128]{1,0:T(8,128)(2,1)} %bitcast.127, f32[4096,128]{1,0:T(8,128)} %get-tuple-element.92.full_ref, f32[2,4096]{1,0:T(2,128)} %copy-done.67, f32[4096,128]{1,0:T(8,128)} %get-tuple-element.167.cos_ref, ...), custom_call_target="tpu_custom_call" | custom-call | flops 42949672960 | bytes 13631488 | tf_op jit(solution)/shard_map/attend_back/pallas_call | solution.py:653
  575.5 64.2 %attend_back.3 = bf16[4096,384]{1,0:T(8,128)(2,1)} custom-call(bf16[4096,384]{1,0:T(8,128)(2,1)} %bitcast.125, bf16[4096,128]{1,0:T(8,128)(2,1)} %bitcast.128, f32[4096,128]{1,0:T(8,128)} %get-tuple-element.99.full_ref, f32[2,4096]{1,0:T(2,128)} %copy-done.68, f32[4096,128]{1,0:T(8,128)} %get-tuple-element.167.cos_ref, f32[4096,128]{1,0:T(8,128)} %get-tuple-element.166.sin_ref), custom_call_target="tpu_custom_call" | custom-call | flops 42949672960 | bytes 13631488 | tf_op jit(solution)/shard_map/attend_back/pallas_call | solution.py:653
  644.4 9.0 weight_part.21
  653.5 11.8 %weight_part.18 = bf16[2,256,4096]{2,1,0:T(8,128)(2,1)} custom-call(s32[2]{0:T(128)S(1)} %pad_add_fusion.5.index_ref, bf16[512,1024]{1,0:T(8,128)(2,1)S(1)} %copy-done.45, bf16[512,1024]{1,0:T(8,128)(2,1)S(1)} %copy-done.51, bf16[512,4096]{1,0:T(8,128)(2,1)S(1)} %copy-done.1, bf16[512,4096]{1,0:T(8,128)(2,1)S(1)} %copy-done.7), custom_call_target="tpu_custom_call" | custom-call | flops 4294967296 | bytes 17301504 | tf_op jit(solution)/shard_map/weight_part/pallas_call | solution.py:466
  700.6 7.9 weight_part.19
  737.7 37.8 %collective-permute-done.25 = bf16[2,1,1,32,1024]{4,3,2,1,0:T(8,128)(2,1)S(1)} collective-permute-done((bf16[2,1,1,32,1024]{4,3,2,1,0:T(8,128)(2,1)S(1)}, bf16[2,1,1,32,1024]{4,3,2,1,0:T(8,128)(2,1)S(1)}, u32[]{:S(2)}, u32[]{:S(2)}) %collective-permute-start.25) | collective-permute-done | bytes 131104 | tf_op jit(solution)/shard_map/ppermute | solution.py:30
  793.9 7.5 weight_part.20
  808.1 8.2 project_back.2
  820.7 17.5 %collective-permute-done.29 = bf16[2,2,1,32,4096]{4,3,2,1,0:T(8,128)(2,1)S(1)} collective-permute-done((bf16[2,2,1,32,4096]{4,3,2,1,0:T(8,128)(2,1)S(1)}, bf16[2,2,1,32,4096]{4,3,2,1,0:T(8,128)(2,1)S(1)}, u32[]{:S(2)}, u32[]{:S(2)}) %collective-permute-start.29) | collective-permute-done | bytes 1048608 | tf_op jit(solution)/shard_map/ppermute | solution.py:30
  846.0 8.7 project_back.3
  863.3 7.8 weight_part.12
  898.3 28.1 %collective-permute-done.18.refs_5_ = bf16[1,256,3072]{2,1,0:T(8,128)(2,1)S(1)} collective-permute-done((bf16[1,256,3072]{2,1,0:T(8,128)(2,1)S(1)}, bf16[1,256,3072]{2,1,0:T(8,128)(2,1)S(1)}, u32[]{:S(2)}, u32[]{:S(2)}) %collective-permute-start.18) | collective-permute-done | bytes 1572896 | tf_op jit(solution)/shard_map/ppermute | solution.py:30
  932.9 15.1 %collective-permute-done.19 = bf16[2,2,1,32,3072]{4,3,2,1,0:T(8,128)(2,1)S(1)} collective-permute-done((bf16[2,2,1,32,3072]{4,3,2,1,0:T(8,128)(2,1)S(1)}, bf16[2,2,1,32,3072]{4,3,2,1,0:T(8,128)(2,1)S(1)}, u32[]{:S(2)}, u32[]{:S(2)}) %collective-permute-start.19) | collective-permute-done | bytes 786464 | tf_op jit(solution)/shard_map/ppermute | solution.py:30
  (474 shorter events, 289.0 us)
Async XLA Ops:
  7.3 77.4 %all-gather.6.cloned.1.call-start = ((), (), s32[]{:S(2)}) async-start(), calls=%async_computation.8 | async-start | bytes 6488064 | tf_op jit(solution)/shard_map/all_gather | solution.py:753
  8.0 414.0 %all-gather.8.cloned.1.call-start = ((), (), s32[]{:S(2)}) async-start(), calls=%async_computation.9 | async-start | bytes 19464192 | tf_op jit(solution)/shard_map/all_gather | solution.py:762
  52.4 49.0 %collective-permute-start.7 = (f32[64,5632]{1,0:T(8,128)}, f32[64,5632]{1,0:T(8,128)}, u32[]{:S(2)}, u32[]{:S(2)}) collective-permute-start(f32[64,5632]{1,0:T(8,128)} %constant_dynamic-slice_fusion.4), channel_id=1, source_target_pairs={{0,8},{8,0},{16,24},{24,16},{1,9},{9,1},{17,25},{25,17},{2,10},{10... | collective-permute-start | bytes 4325384 | tf_op jit(solution)/shard_map/ppermute | solution.py:30
  96.6 108.2 %all-to-all-start = ((bf16[8,512,384]{2,1,0:T(8,128)(2,1)}), bf16[8,512,384]{2,1,0:T(8,128)(2,1)}, u32[]{:S(2)}, u32[]{:S(2)}) async-start(bf16[8,512,384]{2,1,0:T(8,128)(2,1)} %copy-done.60), calls=%async_computation | async-start | bytes 6291456 | tf_op jit(solution)/shard_map/all_to_all | solution.py:797
  122.1 95.9 %collective-permute-start.9 = (f32[16,5632]{1,0:T(8,128)S(1)}, f32[16,5632]{1,0:T(8,128)}, u32[]{:S(2)}, u32[]{:S(2)}) collective-permute-start(f32[16,5632]{1,0:T(8,128)S(1)} %constant_dynamic-slice_fusion.2), channel_id=1, source_target_pairs={{0,1},{1,0},{2,3},{3,2},{4,5},{5,4},{6,7},{7,6},{8,9},{9,8},{10,11... | collective-permute-start | bytes 1081352 | tf_op jit(solution)/shard_map/ppermute | solution.py:30
  204.8 141.7 %all-to-all-start.1 = ((bf16[8,512,384]{2,1,0:T(8,128)(2,1)}), bf16[8,512,384]{2,1,0:T(8,128)(2,1)S(1)}, u32[]{:S(2)}, u32[]{:S(2)}) async-start(bf16[8,512,384]{2,1,0:T(8,128)(2,1)} %copy-done.59), calls=%async_computation.1 | async-start | bytes 6291456 | tf_op jit(solution)/shard_map/all_to_all | solution.py:797
  219.8 89.5 %collective-permute-start.10 = (f32[8,5632]{1,0:T(8,128)S(1)}, f32[8,5632]{1,0:T(8,128)}, u32[]{:S(2)}, u32[]{:S(2)}) collective-permute-start(f32[8,5632]{1,0:T(8,128)S(1)} %constant_dynamic-slice_fusion.1), channel_id=1, source_target_pairs={{0,2},{1,3},{2,0},{3,1},{4,6},{5,7},{6,4},{7,5},{8,10},{9,11},{10,... | collective-permute-start | bytes 540680 | tf_op jit(solution)/shard_map/ppermute | solution.py:30
  346.5 46.3 %all-to-all-start.2 = ((bf16[8,512,128]{2,1,0:T(8,128)(2,1)}), bf16[8,512,128]{2,1,0:T(8,128)(2,1)}, u32[]{:S(2)}, u32[]{:S(2)}) async-start(bf16[8,512,128]{2,1,0:T(8,128)(2,1)} %bitcast.12), calls=%async_computation.2 | async-start | bytes 2097152 | tf_op jit(solution)/shard_map/all_to_all | solution.py:797
  354.0 42.7 %collective-permute-start.11 = (f32[4,5632]{1,0:T(4,128)}, f32[4,5632]{1,0:T(4,128)S(1)}, u32[]{:S(2)}, u32[]{:S(2)}) collective-permute-start(f32[4,5632]{1,0:T(4,128)} %constant_dynamic-slice_fusion), channel_id=1, source_target_pairs={{0,4},{1,5},{2,6},{3,7},{4,0},{5,1},{6,2},{7,3},{8,12},{9,13},{10,... | collective-permute-start | bytes 270344 | tf_op jit(solution)/shard_map/ppermute | solution.py:30
  456.6 41.4 %all-to-all-start.4 = ((bf16[8,512,128]{2,1,0:T(8,128)(2,1)}), bf16[8,512,128]{2,1,0:T(8,128)(2,1)S(1)}, u32[]{:S(2)}, u32[]{:S(2)}) async-start(bf16[8,512,128]{2,1,0:T(8,128)(2,1)} %get-tuple-element.89), calls=%async_computation.4 | async-start | bytes 2097152 | tf_op jit(solution)/shard_map/all_to_all | solution.py:797
  460.1 267.7 %all-gather.10.cloned.1.call-start = ((), (), s32[]{:S(2)}) async-start(), calls=%async_computation.10 | async-start | bytes 2973696 | tf_op jit(solution)/shard_map/all_gather | solution.py:846
  498.0 70.2 %all-to-all-start.5 = ((bf16[8,512,128]{2,1,0:T(8,128)(2,1)}), bf16[8,512,128]{2,1,0:T(8,128)(2,1)S(1)}, u32[]{:S(2)}, u32[]{:S(2)}) async-start(bf16[8,512,128]{2,1,0:T(8,128)(2,1)} %get-tuple-element.94), calls=%async_computation.5 | async-start | bytes 2097152 | tf_op jit(solution)/shard_map/all_to_all | solution.py:797
  569.3 146.0 %all-to-all-start.6 = ((bf16[8,512,384]{2,1,0:T(8,128)(2,1)}), bf16[8,512,384]{2,1,0:T(8,128)(2,1)S(1)}, u32[]{:S(2)}, u32[]{:S(2)}) async-start(bf16[8,512,384]{2,1,0:T(8,128)(2,1)} %bitcast.126), calls=%async_computation.6 | async-start | bytes 6291456 | tf_op jit(solution)/shard_map/all_to_all | solution.py:797
  653.5 30.4 %collective-permute-start.32 = (bf16[2,1024,1024]{2,1,0:T(8,128)(2,1)}, bf16[2,1024,1024]{2,1,0:T(8,128)(2,1)}, u32[]{:S(2)}, u32[]{:S(2)}) collective-permute-start(bf16[2,1024,1024]{2,1,0:T(8,128)(2,1)} %weight_part.21), channel_id=1, source_target_pairs={{0,8},{8,0},{16,24},{24,16},{1,9},{9,1},{17,25},{25,17},{2,10},{10... | collective-permute-start | bytes 12582920 | tf_op jit(solution)/shard_map/ppermute | solution.py:30
  692.8 86.7 %collective-permute-start.33 = (bf16[1,1024,1024]{2,1,0:T(8,128)(2,1)}, bf16[1,1024,1024]{2,1,0:T(8,128)(2,1)}, u32[]{:S(2)}, u32[]{:S(2)}) collective-permute-start(bf16[1,1024,1024]{2,1,0:T(8,128)(2,1)} %weight_part.22), channel_id=1, source_target_pairs={{0,16},{8,24},{16,0},{24,8},{1,17},{9,25},{17,1},{25,9},{2,18},{10... | collective-permute-start | bytes 6291464 | tf_op jit(solution)/shard_map/ppermute | solution.py:30
  708.4 85.5 %collective-permute-start.28 = (bf16[1,256,4096]{2,1,0:T(8,128)(2,1)}, bf16[1,256,4096]{2,1,0:T(8,128)(2,1)}, u32[]{:S(2)}, u32[]{:S(2)}) collective-permute-start(bf16[1,256,4096]{2,1,0:T(8,128)(2,1)} %weight_part.19), channel_id=1, source_target_pairs={{0,16},{8,24},{16,0},{24,8},{1,17},{9,25},{17,1},{25,9},{2,18},{10... | collective-permute-start | bytes 6291464 | tf_op jit(solution)/shard_map/ppermute | solution.py:30
  717.0 126.2 %all-to-all-start.7 = ((bf16[8,512,384]{2,1,0:T(8,128)(2,1)}), bf16[8,512,384]{2,1,0:T(8,128)(2,1)}, u32[]{:S(2)}, u32[]{:S(2)}) async-start(bf16[8,512,384]{2,1,0:T(8,128)(2,1)} %bitcast.123), calls=%async_computation.7 | async-start | bytes 6291456 | tf_op jit(solution)/shard_map/all_to_all | solution.py:797
  725.8 49.7 %collective-permute-start.25 = (bf16[2,1,1,32,1024]{4,3,2,1,0:T(8,128)(2,1)S(1)}, bf16[2,1,1,32,1024]{4,3,2,1,0:T(8,128)(2,1)S(1)}, u32[]{:S(2)}, u32[]{:S(2)}) collective-permute-start(bf16[2,1,1,32,1024]{4,3,2,1,0:T(8,128)(2,1)S(1)} %dynamic-slice_convert_fusion.10), channel_id=1, source_target_pairs={{0,2},{1,3},{2,0},{3,1},{4,6},{5,7},{6,4},{7,5},{8,10},{9,11},{10,... | collective-permute-start | bytes 393224 | tf_op jit(solution)/shard_map/ppermute | solution.py:30
  775.5 31.9 %collective-permute-start.26 = (bf16[1,1,1,32,1024]{4,3,2,1,0:T(8,128)(2,1)S(1)}, bf16[1,1,1,32,1024]{4,3,2,1,0:T(8,128)(2,1)S(1)}, u32[]{:S(2)}, u32[]{:S(2)}) collective-permute-start(bf16[1,1,1,32,1024]{4,3,2,1,0:T(8,128)(2,1)S(1)} %dynamic-slice_convert_fusion.11), channel_id=1, source_target_pairs={{0,4},{1,5},{2,6},{3,7},{4,0},{5,1},{6,2},{7,3},{8,12},{9,13},{10,... | collective-permute-start | bytes 196616 | tf_op jit(solution)/shard_map/ppermute | solution.py:30
  801.6 36.6 %collective-permute-start.29 = (bf16[2,2,1,32,4096]{4,3,2,1,0:T(8,128)(2,1)S(1)}, bf16[2,2,1,32,4096]{4,3,2,1,0:T(8,128)(2,1)S(1)}, u32[]{:S(2)}, u32[]{:S(2)}) collective-permute-start(bf16[2,2,1,32,4096]{4,3,2,1,0:T(8,128)(2,1)S(1)} %dynamic-slice_convert_fusion.1), channel_id=1, source_target_pairs={{0,1},{1,0},{2,3},{3,2},{4,5},{5,4},{6,7},{7,6},{8,9},{9,8},{10,11... | collective-permute-start | bytes 3145736 | tf_op jit(solution)/shard_map/ppermute | solution.py:30
  839.4 34.0 %collective-permute-start.30 = (bf16[2,1,1,32,4096]{4,3,2,1,0:T(8,128)(2,1)}, bf16[2,1,1,32,4096]{4,3,2,1,0:T(8,128)(2,1)}, u32[]{:S(2)}, u32[]{:S(2)}) collective-permute-start(bf16[2,1,1,32,4096]{4,3,2,1,0:T(8,128)(2,1)} %dynamic-slice_convert_fusion.4), channel_id=1, source_target_pairs={{0,2},{1,3},{2,0},{3,1},{4,6},{5,7},{6,4},{7,5},{8,10},{9,11},{10,... | collective-permute-start | bytes 1572872 | tf_op jit(solution)/shard_map/ppermute | solution.py:30
  841.4 52.2 %collective-permute-start.36 = (bf16[1,1,1,128,1024]{4,3,2,1,0:T(8,128)(2,1)}, bf16[1,1,1,128,1024]{4,3,2,1,0:T(8,128)(2,1)S(1)}, u32[]{:S(2)}, u32[]{:S(2)}) collective-permute-start(bf16[1,1,1,128,1024]{4,3,2,1,0:T(8,128)(2,1)} %dynamic-slice_convert_fusion.6), channel_id=1, source_target_pairs={{0,4},{1,5},{2,6},{3,7},{4,0},{5,1},{6,2},{7,3},{8,12},{9,13},{10,... | collective-permute-start | bytes 786440 | tf_op jit(solution)/shard_map/ppermute | solution.py:30
  887.6 38.8 %collective-permute-start.18 = (bf16[1,256,3072]{2,1,0:T(8,128)(2,1)S(1)}, bf16[1,256,3072]{2,1,0:T(8,128)(2,1)S(1)}, u32[]{:S(2)}, u32[]{:S(2)}) collective-permute-start(bf16[1,256,3072]{2,1,0:T(8,128)(2,1)S(1)} %weight_part.13), channel_id=1, source_target_pairs={{0,16},{8,24},{16,0},{24,8},{1,17},{9,25},{17,1},{25,9},{2,18},{10... | collective-permute-start | bytes 4718600 | tf_op jit(solution)/shard_map/ppermute | solution.py:30
  894.7 37.2 %collective-permute-start.16 = (f32[64,2816]{1,0:T(8,128)S(1)}, f32[64,2816]{1,0:T(8,128)S(1)}, u32[]{:S(2)}, u32[]{:S(2)}) collective-permute-start(f32[64,2816]{1,0:T(8,128)S(1)} %pad_maximum_fusion.3), channel_id=1, source_target_pairs={{0,8},{8,0},{16,24},{24,16},{1,9},{9,1},{17,25},{25,17},{2,10},{10... | collective-permute-start | bytes 2162696 | tf_op jit(solution)/shard_map/ppermute | solution.py:30
  (136 other events, 1520.5 us)
Sparse Core Ops, SparseCore 0:
  11.0 73.6 all-gather.5
  87.6 229.4 all-gather.7
  498.1 66.5 all-gather.9

commit v3 on v2

--- a/solution.py
+++ b/solution.py
@@ -66,13 +66,16 @@
     return axis_bits("clip")[::-1] + axis_bits("seq")[::-1]
 
 
-def halve_rows(parts, bits):
-    for axis, bit in bits:
+def halve_rows(parts, bits, gates=()):
+    for place, (axis, bit) in enumerate(bits):
         half = parts.shape[0] // 2
         mine = own_bit(axis, bit)
         keep = lax.dynamic_slice_in_dim(parts, mine * half, half, 0)
         send = lax.dynamic_slice_in_dim(parts, (1 - mine) * half, half, 0)
-        parts = keep + swap_bit(send, axis, bit)
+        other = swap_bit(send, axis, bit)
+        if place < len(gates) and gates[place] is not None:
+            other = after(other, gates[place])
+        parts = keep + other
     return parts
 
 
@@ -176,8 +179,12 @@
     return [pl.BlockSpec((height, block), functools.partial(lambda p, j: (0, p * steps + j), p)) for p in range(3)]
 
 
-def project(tokens, mods, weight, bias, cosine, sine, groups):
-    rows, width = tokens.shape
+def clip_block(shape, c):
+    return pl.BlockSpec((None,) + shape[1:], lambda j: (c,) + (0,) * (len(shape) - 1))
+
+
+def project(tokens, c, mods, weight, bias, cosine, sine, groups):
+    _, rows, width = tokens.shape
     span = width // groups
     block = max(span, 256)
     per_step = block // span
@@ -185,7 +192,7 @@
     return pl.pallas_call(
         functools.partial(project_kernel, span=span),
         grid=(steps,),
-        in_specs=[whole_block((rows, width)), whole_block(mods.shape)]
+        in_specs=[clip_block(tokens.shape, c), whole_block(mods.shape)]
         + column_specs(width, block, steps)
         + column_specs(1, block, steps)
         + [whole_block((rows, block))] * 2,
@@ -203,8 +210,9 @@
 
 
 def project_back_kernel(
-    back_ref, wq_ref, wk_ref, wv_ref, token_ref, scale_ref, resid_ref, grad_ref, proj_ref, sums_ref, bias_ref, acc_ref, *, span
+    back_ref, wq_ref, wk_ref, wv_ref, token_ref, scale_ref, resid_ref, *rest, span
 ):
+    grad_ref, proj_ref, sums_ref, bias_ref, acc_ref = rest[-5:]
     frames = scale_ref.shape[0]
     rows_all, width = token_ref.shape
     patch = rows_all // frames
@@ -234,83 +242,88 @@
             sums_ref[1, f : f + 1, :] = jnp.sum(grad * unit, axis=0, keepdims=True)
 
 
-def project_back(back, weight, tokens, scales, d_resid):
+def project_back(back, weight, tokens, c, scales, d_resid, grads):
     groups, rows, _ = back.shape
-    width = tokens.shape[1]
+    width = tokens.shape[2]
     span = width // groups
     block = max(span, 256)
     per_step = block // span
     steps = groups // per_step
+    earlier = [] if grads is None else [grads]
     return pl.pallas_call(
         functools.partial(project_back_kernel, span=span),
         grid=(steps,),
         in_specs=[pl.BlockSpec((per_step, rows, 3 * span), lambda j: (j, 0, 0))]
         + column_specs(width, block, steps)
-        + [whole_block((rows, width)), whole_block(scales.shape), whole_block((rows, width))],
+        + [clip_block(tokens.shape, c), whole_block(scales.shape), whole_block((rows, width))]
+        + [pl.BlockSpec(memory_space=pl.ANY)] * len(earlier),
         out_specs=(
-            whole_block((rows, width)),
+            clip_block(tokens.shape, c),
             whole_block((rows, 3 * width)),
             whole_block((2,) + scales.shape),
             whole_block((1, 3 * width)),
         ),
         out_shape=(
-            jax.ShapeDtypeStruct((rows, width), f32),
+            jax.ShapeDtypeStruct(tokens.shape, f32),
             jax.ShapeDtypeStruct((rows, 3 * width), bf16),
             jax.ShapeDtypeStruct((2,) + scales.shape, f32),
             jax.ShapeDtypeStruct((1, 3 * width), f32),
         ),
+        input_output_aliases={7: 0} if earlier else {},
         scratch_shapes=[pltpu.VMEM((rows, width), f32)],
         compiler_params=pltpu.CompilerParams(vmem_limit_bytes=40 << 20),
         cost_estimate=pl.CostEstimate(
             flops=6 * rows * width * width, bytes_accessed=6 * width * width + 22 * rows * width, transcendentals=0
         ),
         name="project_back",
-    )(back, weight, weight, weight, tokens, scales, d_resid)
+    )(back, weight, weight, weight, tokens, scales, d_resid, *earlier)
 
 
 GELU_RATE = math.sqrt(2.0 / math.pi)
 GELU_CUBE = 0.044715
 
 
-def middle_kernel(
-    back_ref,
-    token_ref,
-    cot_ref,
-    mod_ref,
-    wo_ref,
-    bo_ref,
-    up_ref,
-    bup_ref,
-    down_ref,
-    bdown_ref,
-    out_ref,
-    dres_ref,
-    mixed_ref,
-    normed_ref,
-    act_ref,
-    dhid_ref,
-    dmlp_ref,
-    dattn_ref,
-    dmix_ref,
-    sums_ref,
-    bup_sum_ref,
-    bsum_ref,
-    attn_ref,
-    res_ref,
-    mlp_ref,
-    dn_ref,
-):
+def middle_kernel(clip_ref, back_ref, token_ref, cot_ref, mod_ref, bo_ref, bup_ref, bdown_ref, *refs):
+    wo_refs, up_refs, down_refs = refs[0:4], refs[4:8], refs[8:12]
+    (
+        out_ref,
+        dres_ref,
+        mixed_ref,
+        normed_ref,
+        act_ref,
+        dhid_ref,
+        dmlp_ref,
+        dattn_ref,
+        dmix_ref,
+        sums_ref,
+        bup_sum_ref,
+        bsum_ref,
+        attn_ref,
+        res_ref,
+        mlp_ref,
+        dn_ref,
+        wo_ref,
+        up_ref,
+        down_ref,
+    ) = refs[-19:]
     groups, rows_all, span = back_ref.shape
     width = token_ref.shape[1]
+    quarter = width // 4
     frames = mod_ref.shape[1]
     patch = rows_all // frames
     step = pl.program_id(0)
+    mine = clip_ref[0]
+
+    def owner_rows(place):
+        return pl.ds(pl.multiple_of((mine ^ FLIPS[place]) * quarter, quarter), quarter)
 
     @pl.when(step == 0)
     def _():
+        for place in range(4):
+            wo_ref[owner_rows(place), :] = wo_refs[place][...].reshape(quarter, width)
         for g in range(groups):
             mixed_ref[:, g * span : (g + 1) * span] = back_ref[g]
-        attn_ref[...] = dot(mixed_ref[...], wo_ref[...].reshape(width, width)) + bo_ref[...]
+        attn_ref[...] = dot(mixed_ref[...], wo_ref[...]) + bo_ref[...]
         for f in range(frames):
             rows = slice(f * patch, (f + 1) * patch)
             resid = token_ref[rows, :].astype(f32) + mod_ref[0, f : f + 1, :] * attn_ref[rows, :]
@@ -321,8 +334,15 @@
         mlp_ref[...] = jnp.zeros_like(mlp_ref)
         dn_ref[...] = jnp.zeros_like(dn_ref)
 
-    up = up_ref[...].reshape(width, -1)
-    down = down_ref[...].reshape(-1, width)
+    for place in range(4):
+        up_ref[owner_rows(place), :] = up_refs[place][...].reshape(quarter, -1)
+
+        @pl.when(step // 2 == place)
+        def _(place=place):
+            down_ref[...] = down_refs[place][...].reshape(-1, width)
+
+    up = up_ref[...]
+    down = down_ref[...]
     hidden = dot(normed_ref[...], up) + bup_ref[...]
     square = hidden * hidden
     bend = jnp.tanh(GELU_RATE * (hidden + GELU_CUBE * (square * hidden)))
@@ -364,54 +384,92 @@
             )
             bsum = term if bsum is None else bsum + term
         bsum_ref[...] = bsum
-        d_mixed = dot(dattn_ref[...], wo_ref[...].reshape(width, width), NT).astype(bf16)
+        d_mixed = dot(dattn_ref[...], wo_ref[...], NT).astype(bf16)
         for g in range(groups):
             dmix_ref[g] = d_mixed[:, g * span : (g + 1) * span]
 
 
-def middle(back, tokens, cot, mods, packed, biases):
+FLIPS = (0, 2, 1, 3)
+
+
+def middle(back, tokens, cot, c, mods, up_shares, down_shares, biases, outputs):
     groups, rows, span = back.shape
-    width = tokens.shape[1]
-    devices, _, piece, _ = packed.shape
+    _, _, width = tokens.shape
+    high, low, _, piece, _ = up_shares[0].shape
     hidden = 4 * width
     steps = 8
     block = hidden // steps
-    halves = width // block
-    owners = block // (4 * piece)
     bias_out, bias_up, bias_down = biases
-    token_block = whole_block((rows, width))
-    hidden_block = pl.BlockSpec((rows, block), lambda j: (0, j))
+    mine = lax.axis_index("clip").astype(jnp.int32)[None]
+    earlier = [] if outputs is None else [outputs]
+
+    def fixed(shape, **options):
+        return pl.BlockSpec(shape, lambda j, q: (0,) * len(shape), **options)
+
+    def clip_part(shape):
+        return pl.BlockSpec((None,) + shape[1:], lambda j, q: (c,) + (0,) * (len(shape) - 1))
+
+    def unit_block(j, q):
+        owner = q[0] ^ jnp.where(j // 2 == 1, 2, jnp.where(j // 2 == 2, 1, j // 2))
+        return owner, j % 2
+
+    def up_index(j, q):
+        owner, half = unit_block(j, q)
+        return (0, 0, owner, 0, half)
+
+    def hidden_index(j, q):
+        owner, half = unit_block(j, q)
+        return (0, owner * 2 + half)
+
+    def down_index(place, j, q):
+        return (0, jnp.clip(j - 2 * place, 0, 1), 0, 0, 0)
+
+    token_block = fixed((rows, width))
+    hidden_block = pl.BlockSpec((rows, block), hidden_index)
+    out_spec = [
+        pl.BlockSpec((high, low, 1, piece, width), lambda j, q: (0, 0, 4, 0, 0), pipeline_mode=pl.Buffered(1)) for _ in range(4)
+    ]
+    up_spec = [pl.BlockSpec((high, low, 1, piece, block), up_index) for _ in range(4)]
+    down_spec = [
+        pl.BlockSpec((high, 1, 4, piece, width), functools.partial(down_index, place)) for place in range(4)
+    ]
     return pl.pallas_call(
         middle_kernel,
-        grid=(steps,),
-        in_specs=[
-            whole_block(back.shape),
-            token_block,
-            token_block,
-            whole_block(mods.shape),
-            pl.BlockSpec((devices, 1, piece, width), lambda j: (0, 8, 0, 0), pipeline_mode=pl.Buffered(1)),
-            whole_block((1, width)),
-            pl.BlockSpec((devices, 1, piece, block), lambda j: (0, 4 + j // halves, 0, j % halves)),
-            pl.BlockSpec((1, block), lambda j: (0, j)),
-            pl.BlockSpec((owners, 4, piece, width), lambda j: (j, 0, 0, 0)),
-            whole_block((1, width)),
-        ],
-        out_specs=(
-            token_block,
-            token_block,
-            token_block,
-            token_block,
-            hidden_block,
-            hidden_block,
-            token_block,
-            token_block,
-            whole_block(back.shape),
-            whole_block(mods.shape),
-            pl.BlockSpec((1, block), lambda j: (0, j)),
-            whole_block((2, width)),
+        grid_spec=pltpu.PrefetchScalarGridSpec(
+            num_scalar_prefetch=1,
+            grid=(steps,),
+            in_specs=[
+                fixed(back.shape),
+                clip_part(tokens.shape),
+                clip_part(tokens.shape),
+                fixed(mods.shape),
+                fixed((1, width)),
+                pl.BlockSpec((1, block), hidden_index),
+                fixed((1, width)),
+            ]
+            + out_spec
+            + up_spec
+            + down_spec
+            + [pl.BlockSpec(memory_space=pl.ANY)] * len(earlier),
+            out_specs=(
+                clip_part(tokens.shape),
+                token_block,
+                token_block,
+                token_block,
+                hidden_block,
+                hidden_block,
+                token_block,
+                token_block,
+                fixed(back.shape),
+                fixed(mods.shape),
+                pl.BlockSpec((1, block), hidden_index),
+                fixed((2, width)),
+            ),
+            scratch_shapes=[pltpu.VMEM((rows, width), f32)] * 4
+            + [pltpu.VMEM((width, width), bf16), pltpu.VMEM((width, block), bf16), pltpu.VMEM((block, width), bf16)],
         ),
         out_shape=(
-            jax.ShapeDtypeStruct((rows, width), bf16),
+            jax.ShapeDtypeStruct(tokens.shape, bf16),
             jax.ShapeDtypeStruct((rows, width), f32),
             jax.ShapeDtypeStruct((rows, width), bf16),
             jax.ShapeDtypeStruct((rows, width), bf16),
@@ -424,13 +482,13 @@
             jax.ShapeDtypeStruct((1, hidden), f32),
             jax.ShapeDtypeStruct((2, width), f32),
         ),
-        scratch_shapes=[pltpu.VMEM((rows, width), f32)] * 4,
-        compiler_params=pltpu.CompilerParams(vmem_limit_bytes=54 << 20),
+        input_output_aliases={20: 0} if earlier else {},
+        compiler_params=pltpu.CompilerParams(vmem_limit_bytes=58 << 20),
         cost_estimate=pl.CostEstimate(
-            flops=36 * rows * width * width, bytes_accessed=18 * width * width + 50 * rows * width, transcendentals=4 * rows * width
+            flops=4 * rows * width * width, bytes_accessed=2 * width * width + 5 * rows * width, transcendentals=rows * width
         ),
         name="middle",
-    )(back, tokens, cot, mods, packed, bias_out, packed, bias_up, packed, bias_down)
+    )(mine, back, tokens, cot, mods, bias_out, bias_up, bias_down, *up_shares, *up_shares, *down_shares, *earlier)
 
 
 def weight_part_kernel(index_ref, *refs, clips, addends):
@@ -452,16 +510,16 @@
     out_ref[0] = total.astype(out_ref.dtype)
 
 
-def weight_part(left, right, quarters, addends, kind):
-    rows, height = left[0].shape
+def weight_part(left, right, indices, addends, kind, height):
+    rows = left[0].shape[0]
     columns = right[0].shape[1]
-    quarter = height // lax.axis_size("clip")
     block = 512
-    count = quarters.shape[0]
-    in_specs = [pl.BlockSpec((rows, quarter), lambda i, j, q: (0, q[i]))] * len(left)
+    count = indices.shape[0]
+    in_specs = [pl.BlockSpec((rows, height), lambda i, j, q: (0, q[i]))] * len(left)
     in_specs += [pl.BlockSpec((rows, block), lambda i, j, q: (0, j))] * len(right)
     in_specs += [
-        pl.BlockSpec((1, quarter, block), functools.partial(lambda place, i, j, q: (place, 0, j), place)) for _, place in addends
+        pl.BlockSpec((1, height, block), functools.partial(lambda first, i, j, q: (first + i, 0, j), first))
+        for _, first in addends
     ]
     return pl.pallas_call(
         functools.partial(weight_part_kernel, clips=len(left), addends=len(addends)),
@@ -469,30 +527,65 @@
             num_scalar_prefetch=1,
             grid=(count, columns // block),
             in_specs=in_specs,
-            out_specs=pl.BlockSpec((1, quarter, block), lambda i, j, q: (i, 0, j)),
-            scratch_shapes=[pltpu.VMEM((quarter, len(left) * rows), bf16)],
+            out_specs=pl.BlockSpec((1, height, block), lambda i, j, q: (i, 0, j)),
+            scratch_shapes=[pltpu.VMEM((height, len(left) * rows), bf16)],
         ),
-        out_shape=jax.ShapeDtypeStruct((count, quarter, columns), kind),
+        out_shape=jax.ShapeDtypeStruct((count, height, columns), kind),
         compiler_params=pltpu.CompilerParams(vmem_limit_bytes=32 << 20),
         cost_estimate=pl.CostEstimate(
-            flops=2 * count * len(left) * rows * quarter * columns,
-            bytes_accessed=len(left) * rows * (quarter + columns) * 2 + 4 * count * quarter * columns,
+            flops=2 * count * len(left) * rows * height * columns,
+            bytes_accessed=len(left) * rows * (count * height + columns) * 2 + 4 * count * height * columns,
             transcendentals=0,
         ),
         name="weight_part",
-    )(quarters, *left, *right, *[array for array, _ in addends])
-
-
-def weight_grad_kernels(left, right):
-    mine = lax.axis_index("clip").astype(jnp.int32)
-
-    def quarters(*flips):
-        return jnp.stack([mine ^ flip for flip in flips])
-
-    core = swap_bit(weight_part(left, right, quarters(3, 1), (), bf16), "clip", 1)
-    across = swap_bit(weight_part(left, right, quarters(2), ((core, 0),), bf16), "clip", 2)
-    total = weight_part(left, right, quarters(0), ((core, 1), (across, 0)), f32)
+    )(indices, *left, *right, *[array for array, _ in addends])
+
+
+def mine_on(axis):
+    return lax.axis_index(axis).astype(jnp.int32)
+
+
+def gate(arrays, *others):
+    return list(lax.optimization_barrier((tuple(arrays), others))[0])
+
+
+def across_first(left, right):
+    mine = mine_on("clip")
+    return weight_part(left, right, jnp.stack([mine ^ 3, mine ^ 1]), (), bf16, left[0].shape[1] // 4)
+
+
+def across_second(left, right, core):
+    return weight_part(left, right, (mine_on("clip") ^ 2)[None], ((core, 0),), bf16, left[0].shape[1] // 4)
+
+
+def across_total(left, right, core, across):
+    height = left[0].shape[1] // 4
+    total = weight_part(left, right, mine_on("clip")[None], ((core, 1), (across, 0)), f32, height)
     return halve_sum(total.reshape((lax.axis_size("seq"), -1, right[0].shape[1])), axis_bits("seq"), bf16)
+
+
+def along_block(clip_flip, low_flip):
+    return (mine_on("clip") ^ clip_flip) * 2 + ((mine_on("seq") & 1) ^ low_flip)
+
+
+def along_first(left, right):
+    blocks = jnp.stack([along_block(1, 1), along_block(3, 1), along_block(1, 0), along_block(3, 0)])
+    return weight_part(left, right, blocks, (), bf16, left[0].shape[1] // 8)
+
+
+def along_second(left, right, core):
+    blocks = jnp.stack([along_block(0, 1), along_block(2, 1)])
+    return weight_part(left, right, blocks, ((core, 0),), bf16, left[0].shape[1] // 8)
+
+
+def along_total(left, right, core, along):
+    height = left[0].shape[1] // 8
+    far, near = along_block(2, 0), along_block(0, 0)
+    across = weight_part(left, right, far[None], ((core, 3), (along, 1)), bf16, height)
+    across = swap_bit(across, "clip", 2)
+    total = weight_part(left, right, near[None], ((core, 2), (along, 0), (across, 0)), f32, height)
+    bits = axis_bits("seq")[:-1]
+    return halve_sum(total.reshape((2 ** len(bits), -1, right[0].shape[1])), bits, bf16)
 
 
 def attend_kernel(qkv_ref, mix_ref, full_ref, log_ref, vt_ref, *, total, span, block):
@@ -751,15 +844,12 @@
     piece = out_weight.shape[0]
 
     full_qkv = lax.all_gather(qkv_weight, BOTH, axis=0, tiled=True)
-    shards = jnp.concatenate(
-        [
-            down_weight.reshape(4, piece, width),
-            up_weight.reshape(piece, 4, width).transpose(1, 0, 2),
-            out_weight[None],
-        ],
-        axis=0,
-    )
-    packed = lax.all_gather(shards, BOTH, axis=0)
+    unit = down_weight.shape[0]
+    owners = (4, seq_devices // 2, 2, unit)
+    near_owners = (4, 2, seq_devices // 2, unit)
+    down_shard = down_weight.reshape(4, piece, width)
+    up_shard = up_weight.reshape((piece,) + owners).transpose(1, 0, 3, 2, 4).reshape(4, piece, width)
+    up_shard = jnp.concatenate([up_shard, out_weight[None]], axis=0)
 
     levels = level_rows(ctx_count, noise_level, rows)
     flat_bits = (2,) * len(order)
@@ -770,35 +860,48 @@
     cond = condition(levels, here, mod_weight.shape[0], width)
     mod_place = own_place(mod_bias, here)
 
-    def modulate(columns, biases):
+    def modulate(columns, biases, gates=()):
         weight = mod_weight[:, columns]
         bias = jnp.concatenate([own_place(b, here) for b in biases]).reshape(lines, -1)
         rest = jnp.concatenate([jnp.broadcast_to(mod_place[columns], (lines, weight.shape[1])), bias], axis=1)
         part = jnp.pad(dot(cond_near, weight), ((0, 0), (0, bias.shape[1])))
-        line_rows = halve_rows(part + jnp.tile(rest, (devices, 1)), order)
+        line_rows = halve_rows((part.reshape(devices, lines, -1) + rest).reshape(devices * lines, -1), order, gates)
         return line_rows[:, : weight.shape[1]], line_rows[:, weight.shape[1] :].reshape(1, -1)
-
-    mod_first, bias_qkv = modulate(slice(0, 2 * width), (qkv_bias,))
-    mod_rest, bias_rest = modulate(slice(2 * width, 6 * width), (out_bias, up_bias, down_bias))
-    bias_out = bias_rest[:, :width]
-    bias_up = bias_rest[:, width : 5 * width]
-    bias_down = bias_rest[:, 5 * width :]
 
     def blocks(line_rows):
         return line_rows.reshape(clips, frames, -1, width).transpose(0, 2, 1, 3)
 
-    mods_one, mods_two = blocks(mod_first), blocks(mod_rest)
+    mod_first, bias_qkv = modulate(slice(0, 2 * width), (qkv_bias,))
+    mods_one = blocks(mod_first)
 
     positions = lax.axis_index("seq") * rows + jnp.arange(rows, dtype=jnp.int32)
     cos_local, sin_local = rotary_lanes(positions, max(span, 256))
-    cos_all, sin_all = rotary_lanes(jnp.arange(total, dtype=jnp.int32), span)
+    cos_row, sin_row = rotary_lanes(jnp.arange(rows, dtype=jnp.int32), span)
+    cos_far, sin_far = rotary_lanes(jnp.arange(seq_devices, dtype=jnp.int32) * rows, span)
+    cos_all = (cos_far[:, None] * cos_row[None] - sin_far[:, None] * sin_row[None]).reshape(total, span)
+    sin_all = (sin_far[:, None] * cos_row[None] + cos_far[:, None] * sin_row[None]).reshape(total, span)
 
     def exchange(value):
         return lax.all_to_all(value, "seq", 0, 0, tiled=True)
 
-    normed, qkv, mixes, fulls, logs = [], [], [], [], []
+    def doubled(share, axis, bit):
+        other = swap_bit(share, axis, bit)
+        mine = own_bit(axis, bit) == 0
+        pair = jnp.stack([jnp.where(mine, share, other), jnp.where(mine, other, share)], axis=1)
+        return pair.reshape((-1,) + share.shape[1:])
+
+    high_bits, low_bit = axis_bits("seq")[:-1], axis_bits("seq")[-1]
+    down_share, up_share = down_shard[None], up_shard[None]
+    for axis, bit in high_bits:
+        down_share, up_share = doubled(down_share, axis, bit), doubled(up_share, axis, bit)
+    full_qkv = after(full_qkv, down_share, up_share)
+    up_pair = (up_share, swap_bit(up_share, "clip", 2))
+    down_share = doubled(down_share, *low_bit)
+
+    normed, qkv, mixes, fulls, logs, sents = [], [], [], [], [], []
     for c in range(clips):
-        sent, normed_c = project(tokens[c], mods_one[c], full_qkv, bias_qkv, cos_local, sin_local, seq_devices)
+        weight = full_qkv if c == 0 else after(full_qkv, down_share, up_pair[1])
+        sent, normed_c = project(tokens, c, mods_one[c], weight, bias_qkv, cos_local, sin_local, seq_devices)
         normed.append(normed_c)
         if qkv:
             sent = after(sent, qkv[-1])
@@ -811,11 +914,27 @@
         logs.append(log)
         backs.append(exchange(after(mix.reshape(seq_devices, rows, span), qkv[-1] if c == 0 else backs[-1])))
 
+    mod_rest, bias_rest = modulate(
+        slice(2 * width, 6 * width), (out_bias, up_bias, down_bias), (None, None, normed[-1], mixes[0], mixes[-1])
+    )
+    mods_two = blocks(mod_rest)
+    bias_out = bias_rest[:, :width]
+    bias_up = bias_rest[:, width : 5 * width].reshape(owners).transpose(0, 2, 1, 3).reshape(1, -1)
+    bias_down = bias_rest[:, 5 * width :]
+    def from_clips(pair):
+        near, across = [p.reshape((seq_devices // 2, 2) + p.shape[1:]) for p in pair]
+        far = swap_bit(after(across, qkv[-1]), "clip", 1)
+        return (near, across, swap_bit(near, "clip", 1), far)
+
+    down_shares = from_clips((down_share, swap_bit(down_share, "clip", 2)))
+    up_shares = from_clips([doubled(p, *low_bit) for p in up_pair])
+
     results = []
     d_mixed = []
     for c in range(clips):
         back = after(backs[c], mixes[-1])
-        results.append(middle(back, tokens[c], cotangent[c], mods_two[c], packed, (bias_out, bias_up, bias_down)))
+        outputs = results[-1][0] if results else None
+        results.append(middle(back, tokens, cotangent, c, mods_two[c], up_shares, down_shares, (bias_out, bias_up, bias_down), outputs))
         d_mixed.append(exchange(after(results[c][8], backs[-1] if c == 0 else d_mixed[-1])))
 
     d_qkv, exchanged = [], []
@@ -824,15 +943,27 @@
         grad = grad.reshape(total, span)
         d_qkv.append(attend_back(qkv[c].reshape(total, 3 * span), grad, fulls[c], logs[c], cos_all, sin_all, span))
         sent = d_qkv[c].reshape(seq_devices, rows, 3 * span)
-        exchanged.append(exchange(after(sent, d_mixed[-1] if c == 0 else exchanged[-1])))
+        exchanged.append(exchange(after(sent, d_mixed[-1]) if c == 0 else sent))
 
     def late(place):
-        return list(lax.optimization_barrier(tuple(r[place] for r in results) + (d_qkv[-1],))[:-1])
+        return [r[place] for r in results]
 
     mixed_all, normed_two, active, d_hidden, d_mlp, d_attn = [late(place) for place in (2, 3, 4, 5, 6, 7)]
-    grad_down = weight_grad_kernels(active, d_mlp)
-    grad_up = weight_grad_kernels(normed_two, d_hidden)
-    grad_out = weight_grad_kernels(mixed_all, d_attn)
+    active = gate(active, d_qkv[-1])
+    down_first = along_first(active, d_mlp)
+    normed_two = gate(normed_two, down_first)
+    up_first = across_first(normed_two, d_hidden)
+    down_core, up_core = swap_bit(down_first, "clip", 1), swap_bit(up_first, "clip", 1)
+    d_mlp = gate(d_mlp, up_first)
+    down_second = along_second(active, d_mlp, down_core)
+    d_hidden = gate(d_hidden, down_second)
+    up_second = across_second(normed_two, d_hidden, up_core)
+    mixed_all = gate(mixed_all, up_second)
+    out_first = across_first(mixed_all, d_attn)
+    out_core = swap_bit(out_first, "clip", 1)
+    down_along, up_across = swap_bit(down_second, "seq", 1), swap_bit(up_second, "clip", 2)
+    exchanged[0] = after(exchanged[0], out_first)
+    exchanged[-1] = after(exchanged[-1], down_along)
 
     def line_sums(sums):
         return sums.transpose(1, 0, 2).reshape(frames, -1)
@@ -840,17 +971,28 @@
     def with_bias(lines_now, vectors):
         return jnp.concatenate([jnp.concatenate(lines_now, axis=0), jnp.concatenate(vectors).reshape(lines, -1)], axis=1)
 
-    bias_up_sum = sum(r[10][0] for r in results)
+    bias_up_sum = sum(r[10][0] for r in results).reshape(near_owners).transpose(0, 2, 1, 3).reshape(-1)
     bias_pair = sum(r[11] for r in results)
     early = with_bias([line_sums(r[9]) for r in results], [bias_pair[0], bias_up_sum, bias_pair[1]])
     early_rows = lax.all_gather(early, BOTH, axis=0, tiled=True)
 
-    last = [
-        project_back(exchanged[c], full_qkv, tokens[c], mods_one[c][1], results[c][1]) for c in range(clips)
-    ]
-    grad_qkv = weight_grad_kernels(normed, [r[1] for r in last])
+    last = []
+    for c in range(clips):
+        grads = last[-1][0] if last else None
+        last.append(project_back(exchanged[c], full_qkv, tokens, c, mods_one[c][1], results[c][1], grads))
+    d_projected = [r[1] for r in last]
+    d_attn = gate(d_attn, last[0][1])
+    out_across = swap_bit(across_second(mixed_all, d_attn, out_core), "clip", 2)
+    qkv_first = across_first(normed, d_projected)
+    qkv_core = swap_bit(qkv_first, "clip", 1)
+    grad_down = along_total(active, gate(d_mlp, qkv_first), down_core, down_along)
+    qkv_across = swap_bit(across_second(gate(normed, up_across), d_projected, qkv_core), "clip", 2)
+    grad_up = across_total(normed_two, gate(d_hidden, qkv_first), up_core, up_across)
+    grad_up = grad_up.reshape((-1,) + near_owners).transpose(0, 1, 3, 2, 4).reshape(-1, 4 * width)
+    grad_out = across_total(mixed_all, gate(d_attn, qkv_first), out_core, out_across)
+    grad_qkv = across_total(normed, d_projected, qkv_core, qkv_across)
     late_rows = with_bias([line_sums(r[2]) for r in last], [sum(r[3][0] for r in last)])
-    late_rows = spread_rows(late_rows, order)
+    late_rows = spread_rows(after(late_rows, qkv_first), order)
 
     def own_columns(sums, shard):
         return lax.dynamic_slice_in_dim(sums, here * shard.shape[0], shard.shape[0], 0)
@@ -870,8 +1012,8 @@
     )
     mod_sum = jnp.concatenate([jnp.sum(late_mod, axis=0), jnp.sum(early_mod, axis=0)])
     return (
-        jnp.stack([r[0] for r in results]),
-        jnp.stack([r[0] for r in last]),
+        results[-1][0],
+        last[-1][0],
         grad_mod,
         own_columns(mod_sum, mod_bias),
         grad_qkv,

time: 983 us -> 861 us (0.88)
  waiting for transfers between devices: 371 us -> 202 us
  starting transfers between devices: 84.9 us -> 112 us
  Pallas kernels: 370 us -> 389 us
    ppermute x37 -> x50, waiting for transfers between devices: 248 us -> 147 us  [swap_bit(): return lax.ppermute(value, axis, [(i, i ^ bit) for i in range(count)])]
    all_to_all x8, waiting for transfers between devices: 94.8 us -> 49.6 us  [exchange(): return lax.all_to_all(value, 'seq', 0, 0, tiled=True)]
    ppermute x37 -> x50, starting transfers between devices: 44.3 us -> 68.2 us  [swap_bit(): return lax.ppermute(value, axis, [(i, i ^ bit) for i in range(count)])]
    all_gather x1, waiting for transfers between devices: 27.6 us -> 4.6 us  [body_by_heads(): full_qkv = lax.all_gather(qkv_weight, BOTH, axis=0, tiled=True)]
    pallas_call x12 -> x13, Pallas kernels: 71.7 us -> 80.8 us  [weight_part(): pl.pallas_call(functools.partial(weight_part_kernel, clips=len(left), add...]
    unnamed x229 -> x213, local copies, waits for them, and re-layouts: 57.6 us -> 52.1 us
  transfers between devices with their start and end apart: 48 -> 60, of which waited for: 24 -> 23; matrix products, arithmetic and copies ran while one was open for 8% -> 9% of each run, Pallas kernels for 34% -> 46%
where the time goes in v3:
time: 861 us; the launch traced here: 850 us
  Pallas kernels  389 us (45%)
  waiting for transfers between devices  202 us (23%)
  starting transfers between devices  112 us (13%)
  local copies, waits for them, and re-layouts  84.1 us (10%)
  other arithmetic  41.4 us (5%)
  between operations  16.2 us (2%)
    ppermute x50, waiting for transfers between devices, swap_bit(): return lax.ppermute(value, axis, [(i, i ^ bit) for i in range(count)])  147 us
    pallas_call x2, Pallas kernels, attend_back(): pl.pallas_call(functools.partial(attend_back_kernel, total=total, span=sp...  128 us
    pallas_call x13, Pallas kernels, weight_part(): pl.pallas_call(functools.partial(weight_part_kernel, clips=len(left), add...  80.8 us
    pallas_call x2, Pallas kernels, middle(): pl.pallas_call(middle_kernel, grid_spec=pltpu.PrefetchScalarGridSpec(num_...  76.5 us
    pallas_call x2, Pallas kernels, attend(): pl.pallas_call(functools.partial(attend_kernel, total=total, span=span, b...  70.6 us
    ppermute x50, starting transfers between devices, swap_bit(): return lax.ppermute(value, axis, [(i, i ^ bit) for i in range(count)])  68.2 us
    unnamed x213, local copies, waits for them, and re-layouts  52.1 us
    all_to_all x8, waiting for transfers between devices, exchange(): return lax.all_to_all(value, 'seq', 0, 0, tiled=True)  49.6 us
  transfers between devices with their start and end apart: 60, of which 23 were waited for; matrix products, arithmetic and copies ran while one was open for 9% of the time, Pallas kernels for 46%

profile of v3, /device:TPU:0, one launch (start us, length us, event | category | flops | bytes accessed | tf_op | source)
XLA Modules:
  0.0 850.2 jit_solution(5714309396971370572)
XLA Ops:
  30.5 14.3 %collective-permute-done.7 = bf16[1,4,32,1024]{3,2,1,0:T(8,128)(2,1)} collective-permute-done((bf16[1,4,32,1024]{3,2,1,0:T(8,128)(2,1)}, bf16[1,4,32,1024]{3,2,1,0:T(8,128)(2,1)}, u32[]{:S(2)}, u32[]{:S(2)}) %collective-permute-start.7) | collective-permute-done | bytes 262176 | tf_op jit(solution)/shard_map/ppermute | solution.py:30
  51.0 9.4 %collective-permute-done.3 = f32[32,2816]{1,0:T(8,128)S(1)} collective-permute-done((f32[32,2816]{1,0:T(8,128)S(1)}, f32[32,2816]{1,0:T(8,128)S(1)}, u32[]{:S(2)}, u32[]{:S(2)}) %collective-permute-start.3) | collective-permute-done | bytes 360480 | tf_op jit(solution)/shard_map/ppermute | solution.py:30
  70.3 20.5 %collective-permute-done.10 = bf16[2,5,32,1024]{3,2,1,0:T(8,128)(2,1)S(1)} collective-permute-done((bf16[2,5,32,1024]{3,2,1,0:T(8,128)(2,1)S(1)}, bf16[2,5,32,1024]{3,2,1,0:T(8,128)(2,1)S(1)}, u32[]{:S(2)}, u32[]{:S(2)}) %collective-permute-start.10) | collective-permute-done | bytes 655392 | tf_op jit(solution)/shard_map/ppermute | solution.py:30
  130.4 18.2 %collective-permute-done.18 = bf16[4,5,32,1024]{3,2,1,0:T(8,128)(2,1)} collective-permute-done((bf16[4,5,32,1024]{3,2,1,0:T(8,128)(2,1)}, bf16[4,5,32,1024]{3,2,1,0:T(8,128)(2,1)}, u32[]{:S(2)}, u32[]{:S(2)}) %collective-permute-start.18) | collective-permute-done | bytes 1310752 | tf_op jit(solution)/shard_map/ppermute | solution.py:30
  168.0 26.6 %all-to-all-done = bf16[8,512,384]{2,1,0:T(8,128)(2,1)} async-done(((bf16[8,512,384]{2,1,0:T(8,128)(2,1)}), bf16[8,512,384]{2,1,0:T(8,128)(2,1)}, u32[]{:S(2)}, u32[]{:S(2)}) %all-to-all-start) | async-done | bytes 3145760 | tf_op jit(solution)/shard_map/all_to_all | solution.py:885
  209.7 10.6 %collective-permute-start.16 = (f32[8,5632]{1,0:T(8,128)S(1)}, f32[8,5632]{1,0:T(8,128)S(1)}, u32[]{:S(2)}, u32[]{:S(2)}) collective-permute-start(f32[8,5632]{1,0:T(8,128)S(1)} %constant_dynamic-slice_fusion.1), channel_id=1, source_target_pairs={{0,2},{1,3},{2,0},{3,1},{4,6},{5,7},{6,4},{7,5},{8,10},{9,11},{10,... | collective-permute-start | bytes 540680 | tf_op jit(solution)/shard_map/ppermute | solution.py:30
  220.3 35.3 %attend.3 = (bf16[4096,128]{1,0:T(8,128)(2,1)}, f32[4096,128]{1,0:T(8,128)}, f32[2,4096]{1,0:T(2,128)S(1)}) custom-call(bf16[4096,384]{1,0:T(8,128)(2,1)} %bitcast.36.qkv_ref), custom_call_target="tpu_custom_call" | custom-call | flops 17179869184 | bytes 6291456 | tf_op jit(solution)/shard_map/attend/pallas_call | solution.py:649
  256.2 13.4 %all-to-all-done.1 = bf16[8,512,384]{2,1,0:T(8,128)(2,1)} async-done(((bf16[8,512,384]{2,1,0:T(8,128)(2,1)}), bf16[8,512,384]{2,1,0:T(8,128)(2,1)}, u32[]{:S(2)}, u32[]{:S(2)}) %all-to-all-start.1) | async-done | bytes 3145760 | tf_op jit(solution)/shard_map/all_to_all | solution.py:885
  277.2 35.3 %attend.2 = (bf16[4096,128]{1,0:T(8,128)(2,1)}, f32[4096,128]{1,0:T(8,128)}, f32[2,4096]{1,0:T(2,128)S(1)}) custom-call(bf16[4096,384]{1,0:T(8,128)(2,1)} %bitcast.34.qkv_ref), custom_call_target="tpu_custom_call" | custom-call | flops 17179869184 | bytes 6291456 | tf_op jit(solution)/shard_map/attend/pallas_call | solution.py:649
  320.1 38.3 %middle.2 = (bf16[2,512,1024]{2,1,0:T(8,128)(2,1)}, f32[512,1024]{1,0:T(8,128)}, bf16[512,1024]{1,0:T(8,128)(2,1)}, bf16[512,1024]{1,0:T(8,128)(2,1)}, bf16[512,...) custom-call(s32[1]{0:T(128)} %bitcast.clip_ref.index_ref, ...), custom_call_target="tpu_custom_call" | custom-call | flops 2147483648 | bytes 4718592 | tf_op jit(solution)/shard_map/middle/pallas_call | solution.py:436
  368.4 38.2 %middle.3 = (bf16[2,512,1024]{2,1,0:T(8,128)(2,1)}, f32[512,1024]{1,0:T(8,128)}, bf16[512,1024]{1,0:T(8,128)(2,1)}, bf16[512,1024]{1,0:T(8,128)(2,1)}, bf16[512,...) custom-call(s32[1]{0:T(128)} %bitcast.clip_ref.index_ref, ...), custom_call_target="tpu_custom_call", output_to_operand_aliasing={{0}: (20, {})} | custom-call | flops 2147483648 | bytes 4718592 | tf_op jit(solution)/shard_map/middle/pallas_call | solution.py:436
  414.6 64.1 %attend_back.2 = bf16[4096,384]{1,0:T(8,128)(2,1)} custom-call(bf16[4096,384]{1,0:T(8,128)(2,1)} %bitcast.36.qkv_ref, bf16[4096,128]{1,0:T(8,128)(2,1)} %bitcast.189, f32[4096,128]{1,0:T(8,128)} %get-tuple-element.118.full_ref, f32[2,4096]{1,0:T(2,128)} %copy-done.63, f32[4096,128]{1,0:T(8,128)} %bitcast.186, f32[4096,128]{1,0:T(8,128)} %bitcast.184), custom_call_target="tpu_custom_call" | custom-call | flops 42949672960 | bytes 13631488 | tf_op jit(solution)/shard_map/attend_back/pallas_call | solution.py:746
  486.7 64.3 %attend_back.3 = bf16[4096,384]{1,0:T(8,128)(2,1)} custom-call(bf16[4096,384]{1,0:T(8,128)(2,1)} %bitcast.34.qkv_ref, bf16[4096,128]{1,0:T(8,128)(2,1)} %bitcast.190, f32[4096,128]{1,0:T(8,128)} %get-tuple-element.121.full_ref, f32[2,4096]{1,0:T(2,128)} %copy-done.64, f32[4096,128]{1,0:T(8,128)} %bitcast.187, f32[4096,128]{1,0:T(8,128)} %bitcast.185), custom_call_target="tpu_custom_call" | custom-call | flops 42949672960 | bytes 13631488 | tf_op jit(solution)/shard_map/attend_back/pallas_call | solution.py:746
  555.6 9.7 %weight_part.13 = bf16[4,512,1024]{2,1,0:T(8,128)(2,1)} custom-call(s32[4]{0:T(128)S(1)} %pad_add_fusion.7.index_ref, bf16[512,4096]{1,0:T(8,128)(2,1)S(1)} %copy-done.3, bf16[512,4096]{1,0:T(8,128)(2,1)S(1)} %copy-done.7, bf16[512,1024]{1,0:T(8,128)(2,1)S(1)} %copy-done.26, bf16[512,1024]{1,0:T(8,128)(2,1)S(1)} %copy-done.29), custom_call_target="tpu_custom_call" | custom-call | flops 4294967296 | bytes 14680064 | tf_op jit(solution)/shard_map/weight_part/pallas_call | solution.py:524
  565.4 11.4 %weight_part.14 = bf16[2,256,4096]{2,1,0:T(8,128)(2,1)} custom-call(s32[2]{0:T(128)S(1)} %pad_add_fusion.6.index_ref, bf16[512,1024]{1,0:T(8,128)(2,1)S(1)} %copy-done.52, bf16[512,1024]{1,0:T(8,128)(2,1)S(1)} %copy-done.55, bf16[512,4096]{1,0:T(8,128)(2,1)S(1)} %copy-done.11, bf16[512,4096]{1,0:T(8,128)(2,1)S(1)} %copy-done.14), custom_call_target="tpu_custom_call" | custom-call | flops 4294967296 | bytes 17825792 | tf_op jit(solution)/shard_map/weight_part/pallas_call | solution.py:524
  633.5 9.4 %project_back.2 = (f32[2,512,1024]{2,1,0:T(8,128)}, bf16[512,3072]{1,0:T(8,128)(2,1)S(1)}, f32[2,2,1024]{2,1,0:T(2,128)S(1)}, f32[1,3072]{1,0:T(1,128)S(1)}) custom-call(bf16[8,512,384]{2,1,0:T(8,128)(2,1)S(1)} %copy-done.18, bf16[1024,3072]{1,0:T(8,128)(2,1)} %all-gather.4.cloned.1.call-done.wq_ref.wk_ref.wv_ref, ...), custom_call_target="tpu_custom_call" | custom-call | flops 3221225472 | bytes 17825792 | tf_op jit(solution)/shard_map/project_back/pallas_call | solution.py:253
  646.5 9.6 %all-to-all-done.6.back_ref = bf16[8,512,384]{2,1,0:T(8,128)(2,1)} async-done(((bf16[8,512,384]{2,1,0:T(8,128)(2,1)}), bf16[8,512,384]{2,1,0:T(8,128)(2,1)}, u32[]{:S(2)}, u32[]{:S(2)}) %all-to-all-start.6) | async-done | bytes 3145760 | tf_op jit(solution)/shard_map/all_to_all | solution.py:885
  656.2 11.2 %collective-permute-done.26.refs_5_ = bf16[2,512,1024]{2,1,0:T(8,128)(2,1)} collective-permute-done((bf16[2,512,1024]{2,1,0:T(8,128)(2,1)}, bf16[2,512,1024]{2,1,0:T(8,128)(2,1)}, u32[]{:S(2)}, u32[]{:S(2)}) %collective-permute-start.26) | collective-permute-done | bytes 2097184 | tf_op jit(solution)/shard_map/ppermute | solution.py:30
  668.9 9.9 %project_back.3 = (f32[2,512,1024]{2,1,0:T(8,128)}, bf16[512,3072]{1,0:T(8,128)(2,1)S(1)}, f32[2,2,1024]{2,1,0:T(2,128)S(1)}, f32[1,3072]{1,0:T(1,128)S(1)}) custom-call(bf16[8,512,384]{2,1,0:T(8,128)(2,1)} %all-to-all-done.6.back_ref, bf16[1024,3072]{1,0:T(8,128)(2,1)} %all-gather.4.cloned.1.call-done.wq_ref.wk_ref.wv_ref, ...), custom_call_target="tpu_custom_call", output_to_operand_aliasing={{0}: (7, {})} | custom-call | flops 3221225472 | bytes 17825792 | tf_op jit(solution)/shard_map/project_back/pallas_call | solution.py:253
  684.9 9.3 %weight_part.18 = bf16[2,256,3072]{2,1,0:T(8,128)(2,1)} custom-call(s32[2]{0:T(128)S(1)} %pad_add_fusion.6.index_ref, bf16[512,1024]{1,0:T(8,128)(2,1)S(1)} %copy-done.45, bf16[512,1024]{1,0:T(8,128)(2,1)S(1)} %copy-done.49, bf16[512,3072]{1,0:T(8,128)(2,1)S(1)} %copy-done.20, bf16[512,3072]{1,0:T(8,128)(2,1)S(1)} %copy-done.23), custom_call_target="tpu_custom_call" | custom-call | flops 3221225472 | bytes 13631488 | tf_op jit(solution)/shard_map/weight_part/pallas_call | solution.py:524
  716.6 7.3 weight_part.23
  745.1 9.9 %collective-permute-done.44 = bf16[2,2,1,32,4096]{4,3,2,1,0:T(8,128)(2,1)S(1)} collective-permute-done((bf16[2,2,1,32,4096]{4,3,2,1,0:T(8,128)(2,1)S(1)}, bf16[2,2,1,32,4096]{4,3,2,1,0:T(8,128)(2,1)S(1)}, u32[]{:S(2)}, u32[]{:S(2)}) %collective-permute-start.44) | collective-permute-done | bytes 1048608 | tf_op jit(solution)/shard_map/ppermute | solution.py:30
  781.5 18.7 %collective-permute-done.35.refs_5_ = bf16[1,256,3072]{2,1,0:T(8,128)(2,1)} collective-permute-done((bf16[1,256,3072]{2,1,0:T(8,128)(2,1)}, bf16[1,256,3072]{2,1,0:T(8,128)(2,1)}, u32[]{:S(2)}, u32[]{:S(2)}) %collective-permute-start.35) | collective-permute-done | bytes 1572896 | tf_op jit(solution)/shard_map/ppermute | solution.py:30
  810.7 11.6 %collective-permute-done.36 = bf16[2,2,1,32,3072]{4,3,2,1,0:T(8,128)(2,1)S(1)} collective-permute-done((bf16[2,2,1,32,3072]{4,3,2,1,0:T(8,128)(2,1)S(1)}, bf16[2,2,1,32,3072]{4,3,2,1,0:T(8,128)(2,1)S(1)}, u32[]{:S(2)}, u32[]{:S(2)}) %collective-permute-start.36) | collective-permute-done | bytes 786464 | tf_op jit(solution)/shard_map/ppermute | solution.py:30
  (505 shorter events, 327.7 us)
Async XLA Ops:
  7.3 99.2 %all-gather.4.cloned.1.call-start = ((), (), s32[]{:S(2)}) async-start(), calls=%async_computation.8 | async-start | bytes 6488064 | tf_op jit(solution)/shard_map/all_gather | solution.py:846
  30.5 92.6 %collective-permute-start.13 = (f32[64,5632]{1,0:T(8,128)}, f32[64,5632]{1,0:T(8,128)}, u32[]{:S(2)}, u32[]{:S(2)}) collective-permute-start(f32[64,5632]{1,0:T(8,128)} %constant_dynamic-slice_fusion.4), channel_id=1, source_target_pairs={{0,8},{8,0},{16,24},{24,16},{1,9},{9,1},{17,25},{25,17},{2,10},{10... | collective-permute-start | bytes 4325384 | tf_op jit(solution)/shard_map/ppermute | solution.py:30
  68.1 58.7 %collective-permute-start.11 = (bf16[4,4,32,1024]{3,2,1,0:T(8,128)(2,1)}, bf16[4,4,32,1024]{3,2,1,0:T(8,128)(2,1)}, u32[]{:S(2)}, u32[]{:S(2)}) collective-permute-start(bf16[4,4,32,1024]{3,2,1,0:T(8,128)(2,1)} %bitcast.18), channel_id=1, source_target_pairs={{0,1},{1,0},{2,3},{3,2},{4,5},{5,4},{6,7},{7,6},{8,9},{9,8},{10,11... | collective-permute-start | bytes 3145736 | tf_op jit(solution)/shard_map/ppermute | solution.py:30
  97.3 55.0 %collective-permute-start.12 = (bf16[4,5,32,1024]{3,2,1,0:T(8,128)(2,1)}, bf16[4,5,32,1024]{3,2,1,0:T(8,128)(2,1)}, u32[]{:S(2)}, u32[]{:S(2)}) collective-permute-start(bf16[4,5,32,1024]{3,2,1,0:T(8,128)(2,1)} %bitcast.28), channel_id=1, source_target_pairs={{0,16},{8,24},{16,0},{24,8},{1,17},{9,25},{17,1},{25,9},{2,18},{10... | collective-permute-start | bytes 3932168 | tf_op jit(solution)/shard_map/ppermute | solution.py:30
  98.8 49.9 %collective-permute-start.18 = (bf16[4,5,32,1024]{3,2,1,0:T(8,128)(2,1)}, bf16[4,5,32,1024]{3,2,1,0:T(8,128)(2,1)}, u32[]{:S(2)}, u32[]{:S(2)}) collective-permute-start(bf16[4,5,32,1024]{3,2,1,0:T(8,128)(2,1)} %bitcast.28), channel_id=1, source_target_pairs={{0,1},{1,0},{2,3},{3,2},{4,5},{5,4},{6,7},{7,6},{8,9},{9,8},{10,11... | collective-permute-start | bytes 3932168 | tf_op jit(solution)/shard_map/ppermute | solution.py:30
  118.5 76.1 %all-to-all-start = ((bf16[8,512,384]{2,1,0:T(8,128)(2,1)}), bf16[8,512,384]{2,1,0:T(8,128)(2,1)}, u32[]{:S(2)}, u32[]{:S(2)}) async-start(bf16[8,512,384]{2,1,0:T(8,128)(2,1)} %copy-done.58), calls=%async_computation | async-start | bytes 6291456 | tf_op jit(solution)/shard_map/all_to_all | solution.py:885
  130.0 190.1 %collective-permute-start.23 = (bf16[4,2,4,32,1024]{4,3,2,1,0:T(8,128)(2,1)}, bf16[4,2,4,32,1024]{4,3,2,1,0:T(8,128)(2,1)}, u32[]{:S(2)}, u32[]{:S(2)}) collective-permute-start(bf16[4,2,4,32,1024]{4,3,2,1,0:T(8,128)(2,1)} %pad_maximum_fusion.2.refs_8_), channel_id=1, source_target_pairs={{0,8},{8,0},{16,24},{24,16},{1,9},{9,1},{17,25},{25,17},{2,10},{10... | collective-permute-start | bytes 6291464 | tf_op jit(solution)/shard_map/ppermute | solution.py:30
  130.0 183.1 %collective-permute-start.22 = (bf16[8,4,32,1024]{3,2,1,0:T(8,128)(2,1)}, bf16[8,4,32,1024]{3,2,1,0:T(8,128)(2,1)}, u32[]{:S(2)}, u32[]{:S(2)}) collective-permute-start(bf16[8,4,32,1024]{3,2,1,0:T(8,128)(2,1)} %bitcast.32), channel_id=1, source_target_pairs={{0,16},{8,24},{16,0},{24,8},{1,17},{9,25},{17,1},{25,9},{2,18},{10... | collective-permute-start | bytes 6291464 | tf_op jit(solution)/shard_map/ppermute | solution.py:30
  152.3 48.9 %collective-permute-start.20 = (bf16[4,2,5,32,1024]{4,3,2,0,1:T(8,128)(2,1)}, bf16[4,2,5,32,1024]{4,3,2,0,1:T(8,128)(2,1)}, u32[]{:S(2)}, u32[]{:S(2)}) collective-permute-start(bf16[4,2,5,32,1024]{4,3,2,0,1:T(8,128)(2,1)} %pad_maximum_fusion), channel_id=1, source_target_pairs={{0,8},{8,0},{16,24},{24,16},{1,9},{9,1},{17,25},{25,17},{2,10},{10... | collective-permute-start | bytes 7864328 | tf_op jit(solution)/shard_map/ppermute | solution.py:30
  152.3 46.8 %collective-permute-start.19 = (bf16[4,5,32,1024]{3,2,1,0:T(8,128)(2,1)}, bf16[4,5,32,1024]{3,2,1,0:T(8,128)(2,1)}, u32[]{:S(2)}, u32[]{:S(2)}) collective-permute-start(bf16[4,5,32,1024]{3,2,1,0:T(8,128)(2,1)} %collective-permute-done.12), channel_id=1, source_target_pairs={{0,1},{1,0},{2,3},{3,2},{4,5},{5,4},{6,7},{7,6},{8,9},{9,8},{10,11... | collective-permute-start | bytes 3932168 | tf_op jit(solution)/shard_map/ppermute | solution.py:30
  155.0 53.7 %collective-permute-start.15 = (f32[16,5632]{1,0:T(8,128)S(1)}, f32[16,5632]{1,0:T(8,128)}, u32[]{:S(2)}, u32[]{:S(2)}) collective-permute-start(f32[16,5632]{1,0:T(8,128)S(1)} %constant_dynamic-slice_fusion.2), channel_id=1, source_target_pairs={{0,1},{1,0},{2,3},{3,2},{4,5},{5,4},{6,7},{7,6},{8,9},{9,8},{10,11... | collective-permute-start | bytes 1081352 | tf_op jit(solution)/shard_map/ppermute | solution.py:30
  194.6 75.0 %all-to-all-start.1 = ((bf16[8,512,384]{2,1,0:T(8,128)(2,1)}), bf16[8,512,384]{2,1,0:T(8,128)(2,1)}, u32[]{:S(2)}, u32[]{:S(2)}) async-start(bf16[8,512,384]{2,1,0:T(8,128)(2,1)} %copy-done.59), calls=%async_computation.1 | async-start | bytes 6291456 | tf_op jit(solution)/shard_map/all_to_all | solution.py:885
  209.7 46.5 %collective-permute-start.16 = (f32[8,5632]{1,0:T(8,128)S(1)}, f32[8,5632]{1,0:T(8,128)S(1)}, u32[]{:S(2)}, u32[]{:S(2)}) collective-permute-start(f32[8,5632]{1,0:T(8,128)S(1)} %constant_dynamic-slice_fusion.1), channel_id=1, source_target_pairs={{0,2},{1,3},{2,0},{3,1},{4,6},{5,7},{6,4},{7,5},{8,10},{9,11},{10,... | collective-permute-start | bytes 540680 | tf_op jit(solution)/shard_map/ppermute | solution.py:30
  358.4 49.8 %all-to-all-start.4 = ((bf16[8,512,128]{2,1,0:T(8,128)(2,1)}), bf16[8,512,128]{2,1,0:T(8,128)(2,1)S(1)}, u32[]{:S(2)}, u32[]{:S(2)}) async-start(bf16[8,512,128]{2,1,0:T(8,128)(2,1)} %get-tuple-element.115), calls=%async_computation.4 | async-start | bytes 2097152 | tf_op jit(solution)/shard_map/all_to_all | solution.py:885
  408.2 70.5 %all-to-all-start.5 = ((bf16[8,512,128]{2,1,0:T(8,128)(2,1)}), bf16[8,512,128]{2,1,0:T(8,128)(2,1)S(1)}, u32[]{:S(2)}, u32[]{:S(2)}) async-start(bf16[8,512,128]{2,1,0:T(8,128)(2,1)} %get-tuple-element.116), calls=%async_computation.5 | async-start | bytes 2097152 | tf_op jit(solution)/shard_map/all_to_all | solution.py:885
  479.7 97.6 %all-to-all-start.7 = ((bf16[8,512,384]{2,1,0:T(8,128)(2,1)}), bf16[8,512,384]{2,1,0:T(8,128)(2,1)S(1)}, u32[]{:S(2)}, u32[]{:S(2)}) async-start(bf16[8,512,384]{2,1,0:T(8,128)(2,1)} %bitcast.183), calls=%async_computation.7 | async-start | bytes 6291456 | tf_op jit(solution)/shard_map/all_to_all | solution.py:885
  485.7 131.2 %all-gather.6.cloned.1.call-start = ((), (), s32[]{:S(2)}) async-start(), calls=%async_computation.9 | async-start | bytes 2973696 | tf_op jit(solution)/shard_map/all_gather | solution.py:977
  579.0 77.2 %all-to-all-start.6 = ((bf16[8,512,384]{2,1,0:T(8,128)(2,1)}), bf16[8,512,384]{2,1,0:T(8,128)(2,1)}, u32[]{:S(2)}, u32[]{:S(2)}) async-start(bf16[8,512,384]{2,1,0:T(8,128)(2,1)} %bitcast.182), calls=%async_computation.6 | async-start | bytes 6291456 | tf_op jit(solution)/shard_map/all_to_all | solution.py:885
  598.8 68.5 %collective-permute-start.26 = (bf16[2,512,1024]{2,1,0:T(8,128)(2,1)}, bf16[2,512,1024]{2,1,0:T(8,128)(2,1)}, u32[]{:S(2)}, u32[]{:S(2)}) collective-permute-start(bf16[2,512,1024]{2,1,0:T(8,128)(2,1)} %weight_part.15), channel_id=1, source_target_pairs={{0,1},{1,0},{2,3},{3,2},{4,5},{5,4},{6,7},{7,6},{8,9},{9,8},{10,11... | collective-permute-start | bytes 6291464 | tf_op jit(solution)/shard_map/ppermute | solution.py:30
  630.1 84.3 %collective-permute-start.34 = (bf16[1,256,4096]{2,1,0:T(8,128)(2,1)}, bf16[1,256,4096]{2,1,0:T(8,128)(2,1)}, u32[]{:S(2)}, u32[]{:S(2)}) collective-permute-start(bf16[1,256,4096]{2,1,0:T(8,128)(2,1)} %copy-done.62), channel_id=1, source_target_pairs={{0,16},{8,24},{16,0},{24,8},{1,17},{9,25},{17,1},{25,9},{2,18},{10... | collective-permute-start | bytes 6291464 | tf_op jit(solution)/shard_map/ppermute | solution.py:30
  646.0 55.6 %collective-permute-start.40 = (bf16[1,256,1024]{2,1,0:T(8,128)(2,1)}, bf16[1,256,1024]{2,1,0:T(8,128)(2,1)}, u32[]{:S(2)}, u32[]{:S(2)}) collective-permute-start(bf16[1,256,1024]{2,1,0:T(8,128)(2,1)} %weight_part.21), channel_id=1, source_target_pairs={{0,16},{8,24},{16,0},{24,8},{1,17},{9,25},{17,1},{25,9},{2,18},{10... | collective-permute-start | bytes 1572872 | tf_op jit(solution)/shard_map/ppermute | solution.py:30
  694.2 63.1 %collective-permute-start.33 = (bf16[2,256,3072]{2,1,0:T(8,128)(2,1)}, bf16[2,256,3072]{2,1,0:T(8,128)(2,1)}, u32[]{:S(2)}, u32[]{:S(2)}) collective-permute-start(bf16[2,256,3072]{2,1,0:T(8,128)(2,1)} %weight_part.18), channel_id=1, source_target_pairs={{0,8},{8,0},{16,24},{24,16},{1,9},{9,1},{17,25},{25,17},{2,10},{10... | collective-permute-start | bytes 9437192 | tf_op jit(solution)/shard_map/ppermute | solution.py:30
  756.1 51.3 %collective-permute-start.45 = (bf16[2,1,1,32,4096]{4,3,2,1,0:T(8,128)(2,1)}, bf16[2,1,1,32,4096]{4,3,2,1,0:T(8,128)(2,1)}, u32[]{:S(2)}, u32[]{:S(2)}) collective-permute-start(bf16[2,1,1,32,4096]{4,3,2,1,0:T(8,128)(2,1)} %dynamic-slice_convert_fusion.3), channel_id=1, source_target_pairs={{0,2},{1,3},{2,0},{3,1},{4,6},{5,7},{6,4},{7,5},{8,10},{9,11},{10,... | collective-permute-start | bytes 1572872 | tf_op jit(solution)/shard_map/ppermute | solution.py:30
  779.2 54.8 %collective-permute-start.49 = (bf16[1,1,128,1024]{3,2,1,0:T(8,128)(2,1)}, bf16[1,1,128,1024]{3,2,1,0:T(8,128)(2,1)}, u32[]{:S(2)}, u32[]{:S(2)}) collective-permute-start(bf16[1,1,128,1024]{3,2,1,0:T(8,128)(2,1)} %dynamic-slice_convert_fusion.5), channel_id=1, source_target_pairs={{0,4},{1,5},{2,6},{3,7},{4,0},{5,1},{6,2},{7,3},{8,12},{9,13},{10,... | collective-permute-start | bytes 786440 | tf_op jit(solution)/shard_map/ppermute | solution.py:30
  (141 other events, 1602.3 us)
Sparse Core Ops, SparseCore 0:
  14.7 91.6 all-gather.3
  490.0 93.0 all-gather.5

commit v4 on v3

--- a/solution.py
+++ b/solution.py
@@ -201,7 +201,7 @@
             jax.ShapeDtypeStruct((groups, rows, 3 * span), bf16),
             jax.ShapeDtypeStruct((rows, width), bf16),
         ),
-        compiler_params=pltpu.CompilerParams(vmem_limit_bytes=32 << 20),
+        compiler_params=pltpu.CompilerParams(vmem_limit_bytes=60 << 20),
         cost_estimate=pl.CostEstimate(
             flops=6 * rows * width * width, bytes_accessed=6 * width * width + 10 * rows * width, transcendentals=0
         ),
@@ -271,7 +271,7 @@
         ),
         input_output_aliases={7: 0} if earlier else {},
         scratch_shapes=[pltpu.VMEM((rows, width), f32)],
-        compiler_params=pltpu.CompilerParams(vmem_limit_bytes=40 << 20),
+        compiler_params=pltpu.CompilerParams(vmem_limit_bytes=60 << 20),
         cost_estimate=pl.CostEstimate(
             flops=6 * rows * width * width, bytes_accessed=6 * width * width + 22 * rows * width, transcendentals=0
         ),
@@ -483,7 +483,7 @@
             jax.ShapeDtypeStruct((2, width), f32),
         ),
         input_output_aliases={20: 0} if earlier else {},
-        compiler_params=pltpu.CompilerParams(vmem_limit_bytes=58 << 20),
+        compiler_params=pltpu.CompilerParams(vmem_limit_bytes=60 << 20),
         cost_estimate=pl.CostEstimate(
             flops=4 * rows * width * width, bytes_accessed=2 * width * width + 5 * rows * width, transcendentals=rows * width
         ),
@@ -510,17 +510,18 @@
     out_ref[0] = total.astype(out_ref.dtype)
 
 
-def weight_part(left, right, indices, addends, kind, height):
+def weight_part(left, right, indices, addends, kind, height, first_column=0, columns=None):
     rows = left[0].shape[0]
-    columns = right[0].shape[1]
+    columns = right[0].shape[1] if columns is None else columns
     block = 512
+    start = first_column // block
     count = indices.shape[0]
     in_specs = [pl.BlockSpec((rows, height), lambda i, j, q: (0, q[i]))] * len(left)
-    in_specs += [pl.BlockSpec((rows, block), lambda i, j, q: (0, j))] * len(right)
-    in_specs += [
-        pl.BlockSpec((1, height, block), functools.partial(lambda first, i, j, q: (first + i, 0, j), first))
-        for _, first in addends
-    ]
+    in_specs += [pl.BlockSpec((rows, block), lambda i, j, q: (0, start + j))] * len(right)
+    for array, first in addends:
+        shift = start if array.shape[2] > columns else 0
+        where = functools.partial(lambda first, shift, i, j, q: (first + i, 0, shift + j), first, shift)
+        in_specs.append(pl.BlockSpec((1, height, block), where))
     return pl.pallas_call(
         functools.partial(weight_part_kernel, clips=len(left), addends=len(addends)),
         grid_spec=pltpu.PrefetchScalarGridSpec(
@@ -531,7 +532,7 @@
             scratch_shapes=[pltpu.VMEM((height, len(left) * rows), bf16)],
         ),
         out_shape=jax.ShapeDtypeStruct((count, height, columns), kind),
-        compiler_params=pltpu.CompilerParams(vmem_limit_bytes=32 << 20),
+        compiler_params=pltpu.CompilerParams(vmem_limit_bytes=60 << 20),
         cost_estimate=pl.CostEstimate(
             flops=2 * count * len(left) * rows * height * columns,
             bytes_accessed=len(left) * rows * (count * height + columns) * 2 + 4 * count * height * columns,
@@ -578,12 +579,13 @@
     return weight_part(left, right, blocks, ((core, 0),), bf16, left[0].shape[1] // 8)
 
 
-def along_total(left, right, core, along):
-    height = left[0].shape[1] // 8
-    far, near = along_block(2, 0), along_block(0, 0)
-    across = weight_part(left, right, far[None], ((core, 3), (along, 1)), bf16, height)
-    across = swap_bit(across, "clip", 2)
-    total = weight_part(left, right, near[None], ((core, 2), (along, 0), (across, 0)), f32, height)
+def along_third(left, right, core, along):
+    return weight_part(left, right, along_block(2, 0)[None], ((core, 3), (along, 1)), bf16, left[0].shape[1] // 8)
+
+
+def along_total(left, right, core, along, across):
+    addends = ((core, 2), (along, 0), (across, 0))
+    total = weight_part(left, right, along_block(0, 0)[None], addends, f32, left[0].shape[1] // 8)
     bits = axis_bits("seq")[:-1]
     return halve_sum(total.reshape((2 ** len(bits), -1, right[0].shape[1])), bits, bf16)
 
@@ -654,7 +656,7 @@
             jax.ShapeDtypeStruct((heads, total), f32),
         ),
         scratch_shapes=[pltpu.VMEM((span, total), bf16)],
-        compiler_params=pltpu.CompilerParams(vmem_limit_bytes=52 << 20),
+        compiler_params=pltpu.CompilerParams(vmem_limit_bytes=60 << 20),
         cost_estimate=pl.CostEstimate(
             flops=8 * total * total * span, bytes_accessed=12 * total * span, transcendentals=total * total * heads // 2
         ),
@@ -668,9 +670,6 @@
     heads = span // HEAD_DIM
     scale = HEAD_DIM**-0.5
     head = lax.broadcasted_iota(jnp.int32, (1, span), 1) // HEAD_DIM
-    key_frame = lax.broadcasted_iota(jnp.int32, (block, block), 0) // PATCHES
-    query_frame = lax.broadcasted_iota(jnp.int32, (block, block), 1) // PATCHES
-    kept = key_frame <= query_frame
     blocks = total // block
     dq_ref[...] = jnp.zeros_like(dq_ref)
 
@@ -687,39 +686,40 @@
     lax.fori_loop(0, blocks, lead, 0)
 
     def key_block(j, carry):
-        columns = pl.ds(pl.multiple_of(j * block, block), block)
+        first = pl.multiple_of(j * block, block)
+        columns = pl.ds(first, block)
         key = qkv_ref[columns, span : 2 * span]
         value = qkv_ref[columns, 2 * span : 3 * span]
         key_flat = jnp.transpose(key)
         dk_ref[...] = jnp.zeros_like(dk_ref)
         dv_ref[...] = jnp.zeros_like(dv_ref)
 
-        def step(i, masked):
-            rows = pl.ds(pl.multiple_of(i * block, block), block)
+        def tile(rows, keys, h, query_h, grad_h):
+            band = slice(h * HEAD_DIM, (h + 1) * HEAD_DIM)
+            probs = jnp.exp(dot(key[:keys], query_h, NT) - log_ref[h : h + 1, rows])
+            d_probs = dot(value[:keys], grad_h, NT)
+            d_scores = (probs * (d_probs - along_ref[h : h + 1, rows])).astype(bf16)
+            dq_ref[band, rows] += dot(key_flat[band, :keys], d_scores)
+            return dot(probs.astype(bf16), grad_h), dot(d_scores, query_h)
+
+        def heads_of(rows):
             query = qkv_ref[rows, 0:span] * jnp.asarray(scale, bf16)
             grad = grad_ref[rows, :]
-            dk = dv = None
-            for h in range(heads):
-                query_h, grad_h = only(query, h), only(grad, h)
-                scores = dot(key, query_h, NT)
-                if masked:
-                    scores = jnp.where(kept, scores, -1e30)
-                probs = jnp.exp(scores - log_ref[h : h + 1, rows])
-                d_probs = dot(value, grad_h, NT)
-                d_scores = (probs * (d_probs - along_ref[h : h + 1, rows])).astype(bf16)
-                dv_term = dot(probs.astype(bf16), grad_h)
-                dk_term = dot(d_scores, query_h)
-                band = slice(h * HEAD_DIM, (h + 1) * HEAD_DIM)
-                dq_ref[band, rows] += dot(key_flat[band], d_scores)
-                dv = dv_term if dv is None else dv + dv_term
-                dk = dk_term if dk is None else dk + dk_term
-            dv_ref[...] += dv
-            dk_ref[...] += dk
-
-        step(j, True)
+            return [(h, only(query, h), only(grad, h)) for h in range(heads)]
+
+        for f in range(block // PATCHES):
+            rows = pl.ds(pl.multiple_of(first + f * PATCHES, PATCHES), PATCHES)
+            keys = (f + 1) * PATCHES
+            for h, query_h, grad_h in heads_of(rows):
+                dv, dk = tile(rows, keys, h, query_h, grad_h)
+                dv_ref[:keys] += dv
+                dk_ref[:keys] += dk
 
         def later(i, c):
-            step(i, False)
+            rows = pl.ds(pl.multiple_of(i * block, block), block)
+            terms = [tile(rows, block, h, query_h, grad_h) for h, query_h, grad_h in heads_of(rows)]
+            dv_ref[...] += sum(t[0] for t in terms)
+            dk_ref[...] += sum(t[1] for t in terms)
             return c
 
         lax.fori_loop(j + 1, blocks, later, 0)
@@ -752,7 +752,7 @@
             pltpu.VMEM((block, span), f32),
             pltpu.VMEM((heads, total), f32),
         ],
-        compiler_params=pltpu.CompilerParams(vmem_limit_bytes=56 << 20),
+        compiler_params=pltpu.CompilerParams(vmem_limit_bytes=60 << 20),
         cost_estimate=pl.CostEstimate(
             flops=20 * total * total * span, bytes_accessed=26 * total * span, transcendentals=total * total * heads // 2
         ),
@@ -949,7 +949,7 @@
         return [r[place] for r in results]
 
     mixed_all, normed_two, active, d_hidden, d_mlp, d_attn = [late(place) for place in (2, 3, 4, 5, 6, 7)]
-    active = gate(active, d_qkv[-1])
+    active = gate(active, d_qkv[-1], exchanged[0])
     down_first = along_first(active, d_mlp)
     normed_two = gate(normed_two, down_first)
     up_first = across_first(normed_two, d_hidden)
@@ -963,7 +963,7 @@
     out_core = swap_bit(out_first, "clip", 1)
     down_along, up_across = swap_bit(down_second, "seq", 1), swap_bit(up_second, "clip", 2)
     exchanged[0] = after(exchanged[0], out_first)
-    exchanged[-1] = after(exchanged[-1], down_along)
+    exchanged[-1] = after(exchanged[-1], down_along, up_across)
 
     def line_sums(sums):
         return sums.transpose(1, 0, 2).reshape(frames, -1)
@@ -981,18 +981,36 @@
         grads = last[-1][0] if last else None
         last.append(project_back(exchanged[c], full_qkv, tokens, c, mods_one[c][1], results[c][1], grads))
     d_projected = [r[1] for r in last]
-    d_attn = gate(d_attn, last[0][1])
-    out_across = swap_bit(across_second(mixed_all, d_attn, out_core), "clip", 2)
+    mine = mine_on("clip")
+    height, half = width // 4, 3 * width // 2
     qkv_first = across_first(normed, d_projected)
     qkv_core = swap_bit(qkv_first, "clip", 1)
-    grad_down = along_total(active, gate(d_mlp, qkv_first), down_core, down_along)
-    qkv_across = swap_bit(across_second(gate(normed, up_across), d_projected, qkv_core), "clip", 2)
-    grad_up = across_total(normed_two, gate(d_hidden, qkv_first), up_core, up_across)
+    down_across = swap_bit(along_third(active, gate(d_mlp, qkv_first), down_core, down_along), "clip", 2)
+    qkv_second = weight_part(normed, d_projected, (mine ^ 2)[None], ((qkv_core, 0),), bf16, height, 0, half)
+    qkv_across = swap_bit(qkv_second, "clip", 2)
+    far_part = weight_part(
+        gate(normed, qkv_second), d_projected, (mine ^ 2)[None], ((qkv_core, 0),), f32, height, half, half
+    )
+    near_part = weight_part(
+        gate(normed, qkv_second), d_projected, mine[None], ((qkv_core, 1),), f32, height, half, half
+    )
+    pair = jnp.stack([near_part[0], far_part[0]]).reshape(2, seq_devices // 2, 2, -1, half)
+    low = own_bit("seq", 1)
+    along = swap_bit(lax.dynamic_index_in_dim(pair, 1 - low, 2, keepdims=False).astype(bf16), "seq", 1)
+    d_attn = gate(d_attn, qkv_second)
+    out_across = swap_bit(across_second(mixed_all, d_attn, out_core), "clip", 2)
+    pair = lax.dynamic_index_in_dim(pair, low, 2, keepdims=False) + along.astype(f32)
+    grad_second = pair[0] + swap_bit(pair[1].astype(bf16), "clip", 2).astype(f32)
+    grad_second = halve_sum(grad_second, axis_bits("seq")[:-1], bf16)
+    total_first = weight_part(normed, d_projected, mine[None], ((qkv_core, 1), (qkv_across, 0)), f32, height, 0, half)
+    grad_first = halve_sum(total_first.reshape(seq_devices, -1, half), axis_bits("seq"), bf16)
+    grad_qkv = jnp.concatenate([grad_first, grad_second], axis=1)
+    grad_up = across_total(normed_two, gate(d_hidden, qkv_second), up_core, up_across)
+    grad_down = along_total(active, gate(d_mlp, qkv_second), down_core, down_along, down_across)
     grad_up = grad_up.reshape((-1,) + near_owners).transpose(0, 1, 3, 2, 4).reshape(-1, 4 * width)
-    grad_out = across_total(mixed_all, gate(d_attn, qkv_first), out_core, out_across)
-    grad_qkv = across_total(normed, d_projected, qkv_core, qkv_across)
+    grad_out = across_total(mixed_all, d_attn, out_core, out_across)
     late_rows = with_bias([line_sums(r[2]) for r in last], [sum(r[3][0] for r in last)])
-    late_rows = spread_rows(after(late_rows, qkv_first), order)
+    late_rows = spread_rows(after(late_rows, qkv_second), order)
 
     def own_columns(sums, shard):
         return lax.dynamic_slice_in_dim(sums, here * shard.shape[0], shard.shape[0], 0)

time: 861 us -> 908 us (1.055)
  Pallas kernels: 389 us -> 425 us
  local copies, waits for them, and re-layouts: 84.1 us -> 51 us
  waiting for transfers between devices: 202 us -> 234 us
  other arithmetic: 41.4 us -> 50.8 us
    unnamed x213 -> x113, local copies, waits for them, and re-layouts: 52.1 us -> 11.2 us
    pallas_call x13 -> x15, Pallas kernels: 80.8 us -> 117 us  [weight_part(): pl.pallas_call(functools.partial(weight_part_kernel, clips=len(left), add...]
    all_to_all x8, waiting for transfers between devices: 49.6 us -> 78.5 us  [exchange(): return lax.all_to_all(value, 'seq', 0, 0, tiled=True)]
    pallas_call x2, Pallas kernels: 128 us -> 118 us  [attend_back(): pl.pallas_call(functools.partial(attend_back_kernel, total=total, span=sp...]
    ppermute x50 -> x54, waiting for transfers between devices: 147 us -> 152 us  [swap_bit(): return lax.ppermute(value, axis, [(i, i ^ bit) for i in range(count)])]
    ppermute x50 -> x54, starting transfers between devices: 68.2 us -> 72.6 us  [swap_bit(): return lax.ppermute(value, axis, [(i, i ^ bit) for i in range(count)])]
  transfers between devices with their start and end apart: 60 -> 64, of which waited for: 23 -> 22; matrix products, arithmetic and copies ran while one was open for 9% -> 11% of each run, Pallas kernels for 46% -> 46%
where the time goes in v4:
time: 908 us; the launch traced here: 897 us
  Pallas kernels  425 us (47%)
  waiting for transfers between devices  234 us (26%)
  starting transfers between devices  114 us (13%)
  local copies, waits for them, and re-layouts  51 us (6%)
  other arithmetic  50.8 us (6%)
  between operations  16 us (2%)
    ppermute x54, waiting for transfers between devices, swap_bit(): return lax.ppermute(value, axis, [(i, i ^ bit) for i in range(count)])  152 us
    pallas_call x2, Pallas kernels, attend_back(): pl.pallas_call(functools.partial(attend_back_kernel, total=total, span=sp...  118 us
    pallas_call x15, Pallas kernels, weight_part(): pl.pallas_call(functools.partial(weight_part_kernel, clips=len(left), add...  117 us
    all_to_all x8, waiting for transfers between devices, exchange(): return lax.all_to_all(value, 'seq', 0, 0, tiled=True)  78.5 us
    pallas_call x2, Pallas kernels, middle(): pl.pallas_call(middle_kernel, grid_spec=pltpu.PrefetchScalarGridSpec(num_...  76.5 us
    ppermute x54, starting transfers between devices, swap_bit(): return lax.ppermute(value, axis, [(i, i ^ bit) for i in range(count)])  72.6 us
    pallas_call x2, Pallas kernels, attend(): pl.pallas_call(functools.partial(attend_kernel, total=total, span=span, b...  70.6 us
    all_to_all x8, starting transfers between devices, exchange(): return lax.all_to_all(value, 'seq', 0, 0, tiled=True)  40.8 us
  transfers between devices with their start and end apart: 64, of which 22 were waited for; matrix products, arithmetic and copies ran while one was open for 11% of the time, Pallas kernels for 46%

profile of v4, /device:TPU:0, one launch (start us, length us, event | category | flops | bytes accessed | tf_op | source)
XLA Modules:
  0.0 897.0 jit_solution(1654492181826249576)
XLA Ops:
  31.6 13.2 %collective-permute-done.7 = bf16[1,4,32,1024]{3,2,1,0:T(8,128)(2,1)} collective-permute-done((bf16[1,4,32,1024]{3,2,1,0:T(8,128)(2,1)}, bf16[1,4,32,1024]{3,2,1,0:T(8,128)(2,1)}, u32[]{:S(2)}, u32[]{:S(2)}) %collective-permute-start.7) | collective-permute-done | bytes 262176 | tf_op jit(solution)/shard_map/ppermute | solution.py:30
  51.0 9.5 %collective-permute-done.3 = f32[32,2816]{1,0:T(8,128)S(1)} collective-permute-done((f32[32,2816]{1,0:T(8,128)S(1)}, f32[32,2816]{1,0:T(8,128)S(1)}, u32[]{:S(2)}, u32[]{:S(2)}) %collective-permute-start.3) | collective-permute-done | bytes 360480 | tf_op jit(solution)/shard_map/ppermute | solution.py:30
  70.5 20.6 %collective-permute-done.10 = bf16[2,5,32,1024]{3,2,1,0:T(8,128)(2,1)S(1)} collective-permute-done((bf16[2,5,32,1024]{3,2,1,0:T(8,128)(2,1)S(1)}, bf16[2,5,32,1024]{3,2,1,0:T(8,128)(2,1)S(1)}, u32[]{:S(2)}, u32[]{:S(2)}) %collective-permute-start.10) | collective-permute-done | bytes 655392 | tf_op jit(solution)/shard_map/ppermute | solution.py:30
  127.5 21.6 %collective-permute-done.18 = bf16[4,5,32,1024]{3,2,1,0:T(8,128)(2,1)} collective-permute-done((bf16[4,5,32,1024]{3,2,1,0:T(8,128)(2,1)}, bf16[4,5,32,1024]{3,2,1,0:T(8,128)(2,1)}, u32[]{:S(2)}, u32[]{:S(2)}) %collective-permute-start.18) | collective-permute-done | bytes 1310752 | tf_op jit(solution)/shard_map/ppermute | solution.py:30
  169.3 22.7 %all-to-all-done = bf16[8,512,384]{2,1,0:T(8,128)(2,1)} async-done(((bf16[8,512,384]{2,1,0:T(8,128)(2,1)}), bf16[8,512,384]{2,1,0:T(8,128)(2,1)}, u32[]{:S(2)}, u32[]{:S(2)}) %all-to-all-start) | async-done | bytes 3145760 | tf_op jit(solution)/shard_map/all_to_all | solution.py:885
  202.8 15.4 %collective-permute-done.15 = f32[16,5632]{1,0:T(8,128)} collective-permute-done((f32[16,5632]{1,0:T(8,128)}, f32[16,5632]{1,0:T(8,128)}, u32[]{:S(2)}, u32[]{:S(2)}) %collective-permute-start.15) | collective-permute-done | bytes 360480 | tf_op jit(solution)/shard_map/ppermute | solution.py:30
  220.5 35.3 %attend.3 = (bf16[4096,128]{1,0:T(8,128)(2,1)}, f32[4096,128]{1,0:T(8,128)}, f32[2,4096]{1,0:T(2,128)}) custom-call(bf16[4096,384]{1,0:T(8,128)(2,1)} %bitcast.36.qkv_ref), custom_call_target="tpu_custom_call" | custom-call | flops 17179869184 | bytes 6291456 | tf_op jit(solution)/shard_map/attend/pallas_call | solution.py:651
  255.8 11.2 %all-to-all-done.1 = bf16[8,512,384]{2,1,0:T(8,128)(2,1)} async-done(((bf16[8,512,384]{2,1,0:T(8,128)(2,1)}), bf16[8,512,384]{2,1,0:T(8,128)(2,1)}, u32[]{:S(2)}, u32[]{:S(2)}) %all-to-all-start.1) | async-done | bytes 3145760 | tf_op jit(solution)/shard_map/all_to_all | solution.py:885
  274.7 35.3 %attend.2 = (bf16[4096,128]{1,0:T(8,128)(2,1)}, f32[4096,128]{1,0:T(8,128)}, f32[2,4096]{1,0:T(2,128)}) custom-call(bf16[4096,384]{1,0:T(8,128)(2,1)} %bitcast.34.qkv_ref), custom_call_target="tpu_custom_call" | custom-call | flops 17179869184 | bytes 6291456 | tf_op jit(solution)/shard_map/attend/pallas_call | solution.py:651
  317.0 38.3 %middle.2 = (bf16[2,512,1024]{2,1,0:T(8,128)(2,1)}, f32[512,1024]{1,0:T(8,128)}, bf16[512,1024]{1,0:T(8,128)(2,1)}, bf16[512,1024]{1,0:T(8,128)(2,1)}, bf16[512,...) custom-call(s32[1]{0:T(128)} %bitcast.clip_ref.index_ref, ...), custom_call_target="tpu_custom_call" | custom-call | flops 2147483648 | bytes 4718592 | tf_op jit(solution)/shard_map/middle/pallas_call | solution.py:436
  365.2 38.2 %middle.3 = (bf16[2,512,1024]{2,1,0:T(8,128)(2,1)}, f32[512,1024]{1,0:T(8,128)}, bf16[512,1024]{1,0:T(8,128)(2,1)}, bf16[512,1024]{1,0:T(8,128)(2,1)}, bf16[512,...) custom-call(s32[1]{0:T(128)} %bitcast.clip_ref.index_ref, ...), custom_call_target="tpu_custom_call", output_to_operand_aliasing={{0}: (20, {})} | custom-call | flops 2147483648 | bytes 4718592 | tf_op jit(solution)/shard_map/middle/pallas_call | solution.py:436
  409.8 59.1 %attend_back.2 = bf16[4096,384]{1,0:T(8,128)(2,1)} custom-call(bf16[4096,384]{1,0:T(8,128)(2,1)} %bitcast.36.qkv_ref, bf16[4096,128]{1,0:T(8,128)(2,1)} %bitcast.198, f32[4096,128]{1,0:T(8,128)} %get-tuple-element.118.full_ref, f32[2,4096]{1,0:T(2,128)} %get-tuple-element.119.log_ref, f32[4096,128]{1,0:T(8,128)} %bitcast.194, f32[4096,128]{1,0:T(8,128)} %bitcast.192), custom_call_target="tpu_custom_call" | custom-call | flops 42949672960 | bytes 13631488 | tf_op jit(solution)/shard_map/attend_back/pallas_call | solution.py:746
  477.3 59.1 %attend_back.3 = bf16[4096,384]{1,0:T(8,128)(2,1)} custom-call(bf16[4096,384]{1,0:T(8,128)(2,1)} %bitcast.34.qkv_ref, bf16[4096,128]{1,0:T(8,128)(2,1)} %bitcast.199, f32[4096,128]{1,0:T(8,128)} %get-tuple-element.121.full_ref, f32[2,4096]{1,0:T(2,128)} %get-tuple-element.122.log_ref, f32[4096,128]{1,0:T(8,128)} %bitcast.195, f32[4096,128]{1,0:T(8,128)} %bitcast.193), custom_call_target="tpu_custom_call" | custom-call | flops 42949672960 | bytes 13631488 | tf_op jit(solution)/shard_map/attend_back/pallas_call | solution.py:746
  545.7 14.1 %weight_part.15 = bf16[4,512,1024]{2,1,0:T(8,128)(2,1)} custom-call(s32[4]{0:T(128)} %pad_add_fusion.7.index_ref, bf16[512,4096]{1,0:T(8,128)(2,1)} %get-tuple-element.126.refs_0_, bf16[512,4096]{1,0:T(8,128)(2,1)} %get-tuple-element.127.refs_1_, bf16[512,1024]{1,0:T(8,128)(2,1)} %get-tuple-element.174.refs_2_, bf16[512,1024]{1,0:T(8,128)(2,1)} %get-tuple-element.175.refs_3_), custom_call_target="tpu_custom_call" | custom-call | flops 4294967296 | bytes 14680064 | tf_op jit(solution)/shard_map/weight_part/pallas_call | solution.py:525
  559.8 17.0 %weight_part.16 = bf16[2,256,4096]{2,1,0:T(8,128)(2,1)} custom-call(s32[2]{0:T(128)} %pad_add_fusion.6.index_ref, bf16[512,1024]{1,0:T(8,128)(2,1)} %get-tuple-element.132.refs_0_, bf16[512,1024]{1,0:T(8,128)(2,1)} %get-tuple-element.133.refs_1_, bf16[512,4096]{1,0:T(8,128)(2,1)} %get-tuple-element.170.refs_2_, bf16[512,4096]{1,0:T(8,128)(2,1)} %get-tuple-element.171.refs_3_), custom_call_target="tpu_custom_call" | custom-call | flops 4294967296 | bytes 17825792 | tf_op jit(solution)/shard_map/weight_part/pallas_call | solution.py:525
  610.7 12.1 %project_back.2 = (f32[2,512,1024]{2,1,0:T(8,128)}, bf16[512,3072]{1,0:T(8,128)(2,1)}, f32[2,2,1024]{2,1,0:T(2,128)}, f32[1,3072]{1,0:T(1,128)}) custom-call(bf16[8,512,384]{2,1,0:T(8,128)(2,1)} %copy-done.3, bf16[1024,3072]{1,0:T(8,128)(2,1)} %all-gather.4.cloned.1.call-done.wq_ref.wk_ref.wv_ref, ...), custom_call_target="tpu_custom_call" | custom-call | flops 3221225472 | bytes 17825792 | tf_op jit(solution)/shard_map/project_back/pallas_call | solution.py:253
  622.8 35.2 %all-to-all-done.6.back_ref = bf16[8,512,384]{2,1,0:T(8,128)(2,1)S(1)} async-done(((bf16[8,512,384]{2,1,0:T(8,128)(2,1)}), bf16[8,512,384]{2,1,0:T(8,128)(2,1)S(1)}, u32[]{:S(2)}, u32[]{:S(2)}) %all-to-all-start.6) | async-done | bytes 3145760 | tf_op jit(solution)/shard_map/all_to_all | solution.py:885
  658.0 10.3 %collective-permute-done.26.refs_5_ = bf16[2,512,1024]{2,1,0:T(8,128)(2,1)} collective-permute-done((bf16[2,512,1024]{2,1,0:T(8,128)(2,1)}, bf16[2,512,1024]{2,1,0:T(8,128)(2,1)}, u32[]{:S(2)}, u32[]{:S(2)}) %collective-permute-start.26) | collective-permute-done | bytes 2097184 | tf_op jit(solution)/shard_map/ppermute | solution.py:30
  668.3 12.1 %project_back.3 = (f32[2,512,1024]{2,1,0:T(8,128)}, bf16[512,3072]{1,0:T(8,128)(2,1)}, f32[2,2,1024]{2,1,0:T(2,128)}, f32[1,3072]{1,0:T(1,128)}) custom-call(bf16[8,512,384]{2,1,0:T(8,128)(2,1)} %copy-done.4, bf16[1024,3072]{1,0:T(8,128)(2,1)} %all-gather.4.cloned.1.call-done.wq_ref.wk_ref.wv_ref, ...), custom_call_target="tpu_custom_call", output_to_operand_aliasing={{0}: (7, {})} | custom-call | flops 3221225472 | bytes 17825792 | tf_op jit(solution)/shard_map/project_back/pallas_call | solution.py:253
  680.4 13.6 %weight_part.20 = bf16[2,256,3072]{2,1,0:T(8,128)(2,1)} custom-call(s32[2]{0:T(128)} %pad_add_fusion.6.index_ref, bf16[512,1024]{1,0:T(8,128)(2,1)} %get-tuple-element.166.refs_0_, bf16[512,1024]{1,0:T(8,128)(2,1)} %get-tuple-element.167.refs_1_, bf16[512,3072]{1,0:T(8,128)(2,1)} %get-tuple-element.157.refs_2_, bf16[512,3072]{1,0:T(8,128)(2,1)} %get-tuple-element.158.refs_3_), custom_call_target="tpu_custom_call" | custom-call | flops 3221225472 | bytes 13631488 | tf_op jit(solution)/shard_map/weight_part/pallas_call | solution.py:525
  725.9 9.7 %collective-permute-done.51.refs_6_ = bf16[1,512,1024]{2,1,0:T(8,128)(2,1)} collective-permute-done((bf16[1,512,1024]{2,1,0:T(8,128)(2,1)}, bf16[1,512,1024]{2,1,0:T(8,128)(2,1)}, u32[]{:S(2)}, u32[]{:S(2)}) %collective-permute-start.51) | collective-permute-done | bytes 1048608 | tf_op jit(solution)/shard_map/ppermute | solution.py:30
  748.4 10.4 %weight_part.27 = f32[1,256,4096]{2,1,0:T(8,128)} custom-call(s32[1]{0:T(128)} %bitcast.clip_ref.index_ref, bf16[512,1024]{1,0:T(8,128)(2,1)} %get-tuple-element.132.refs_0_, bf16[512,1024]{1,0:T(8,128)(2,1)} %get-tuple-element.133.refs_1_, bf16[512,4096]{1,0:T(8,128)(2,1)} %get-tuple-element.170.refs_2_, bf16[512,4096]{1,0:T(8,128)(2,1)} %get-tuple-element.171.refs_3_, ...), custom_call_target="tpu_custom_call" | custom-call | flops 2147483648 | bytes 13107200 | tf_op jit(solution)/shard_map/weight_part/pallas_call | solution.py:525
  842.7 15.1 %collective-permute-done.37 = bf16[2,1,1,32,1536]{4,3,2,1,0:T(8,128)(2,1)S(1)} collective-permute-done((bf16[2,1,1,32,1536]{4,3,2,1,0:T(8,128)(2,1)S(1)}, bf16[2,1,1,32,1536]{4,3,2,1,0:T(8,128)(2,1)S(1)}, u32[]{:S(2)}, u32[]{:S(2)}) %collective-permute-start.37) | collective-permute-done | bytes 196640 | tf_op jit(solution)/shard_map/ppermute | solution.py:30
  876.4 11.5 %collective-permute-done.50 = bf16[1,1,1,32,4096]{4,3,2,1,0:T(8,128)(2,1)S(1)} collective-permute-done((bf16[1,1,1,32,4096]{4,3,2,1,0:T(8,128)(2,1)S(1)}, bf16[1,1,1,32,4096]{4,3,2,1,0:T(8,128)(2,1)S(1)}, u32[]{:S(2)}, u32[]{:S(2)}) %collective-permute-start.50) | collective-permute-done | bytes 262176 | tf_op jit(solution)/shard_map/ppermute | solution.py:30
  (423 shorter events, 340.3 us)
Async XLA Ops:
  7.3 99.4 %all-gather.4.cloned.1.call-start = ((), (), s32[]{:S(2)}) async-start(), calls=%async_computation.8 | async-start | bytes 6488064 | tf_op jit(solution)/shard_map/all_gather | solution.py:846
  31.6 89.0 %collective-permute-start.13 = (f32[64,5632]{1,0:T(8,128)}, f32[64,5632]{1,0:T(8,128)}, u32[]{:S(2)}, u32[]{:S(2)}) collective-permute-start(f32[64,5632]{1,0:T(8,128)} %constant_dynamic-slice_fusion.4), channel_id=1, source_target_pairs={{0,8},{8,0},{16,24},{24,16},{1,9},{9,1},{17,25},{25,17},{2,10},{10... | collective-permute-start | bytes 4325384 | tf_op jit(solution)/shard_map/ppermute | solution.py:30
  68.3 55.6 %collective-permute-start.11 = (bf16[4,4,32,1024]{3,2,1,0:T(8,128)(2,1)}, bf16[4,4,32,1024]{3,2,1,0:T(8,128)(2,1)}, u32[]{:S(2)}, u32[]{:S(2)}) collective-permute-start(bf16[4,4,32,1024]{3,2,1,0:T(8,128)(2,1)} %bitcast.18), channel_id=1, source_target_pairs={{0,1},{1,0},{2,3},{3,2},{4,5},{5,4},{6,7},{7,6},{8,9},{9,8},{10,11... | collective-permute-start | bytes 3145736 | tf_op jit(solution)/shard_map/ppermute | solution.py:30
  97.3 55.4 %collective-permute-start.12 = (bf16[4,5,32,1024]{3,2,1,0:T(8,128)(2,1)}, bf16[4,5,32,1024]{3,2,1,0:T(8,128)(2,1)}, u32[]{:S(2)}, u32[]{:S(2)}) collective-permute-start(bf16[4,5,32,1024]{3,2,1,0:T(8,128)(2,1)} %bitcast.28), channel_id=1, source_target_pairs={{0,16},{8,24},{16,0},{24,8},{1,17},{9,25},{17,1},{25,9},{2,18},{10... | collective-permute-start | bytes 3932168 | tf_op jit(solution)/shard_map/ppermute | solution.py:30
  98.7 50.4 %collective-permute-start.18 = (bf16[4,5,32,1024]{3,2,1,0:T(8,128)(2,1)}, bf16[4,5,32,1024]{3,2,1,0:T(8,128)(2,1)}, u32[]{:S(2)}, u32[]{:S(2)}) collective-permute-start(bf16[4,5,32,1024]{3,2,1,0:T(8,128)(2,1)} %bitcast.28), channel_id=1, source_target_pairs={{0,1},{1,0},{2,3},{3,2},{4,5},{5,4},{6,7},{7,6},{8,9},{9,8},{10,11... | collective-permute-start | bytes 3932168 | tf_op jit(solution)/shard_map/ppermute | solution.py:30
  115.9 76.1 %all-to-all-start = ((bf16[8,512,384]{2,1,0:T(8,128)(2,1)}), bf16[8,512,384]{2,1,0:T(8,128)(2,1)}, u32[]{:S(2)}, u32[]{:S(2)}) async-start(bf16[8,512,384]{2,1,0:T(8,128)(2,1)} %get-tuple-element.97), calls=%async_computation | async-start | bytes 6291456 | tf_op jit(solution)/shard_map/all_to_all | solution.py:885
  127.0 189.9 %collective-permute-start.23 = (bf16[4,2,4,32,1024]{4,3,2,1,0:T(8,128)(2,1)}, bf16[4,2,4,32,1024]{4,3,2,1,0:T(8,128)(2,1)}, u32[]{:S(2)}, u32[]{:S(2)}) collective-permute-start(bf16[4,2,4,32,1024]{4,3,2,1,0:T(8,128)(2,1)} %pad_maximum_fusion.3.refs_8_), channel_id=1, source_target_pairs={{0,8},{8,0},{16,24},{24,16},{1,9},{9,1},{17,25},{25,17},{2,10},{10... | collective-permute-start | bytes 6291464 | tf_op jit(solution)/shard_map/ppermute | solution.py:30
  127.1 182.9 %collective-permute-start.22 = (bf16[8,4,32,1024]{3,2,1,0:T(8,128)(2,1)}, bf16[8,4,32,1024]{3,2,1,0:T(8,128)(2,1)}, u32[]{:S(2)}, u32[]{:S(2)}) collective-permute-start(bf16[8,4,32,1024]{3,2,1,0:T(8,128)(2,1)} %bitcast.32), channel_id=1, source_target_pairs={{0,16},{8,24},{16,0},{24,8},{1,17},{9,25},{17,1},{25,9},{2,18},{10... | collective-permute-start | bytes 6291464 | tf_op jit(solution)/shard_map/ppermute | solution.py:30
  152.7 45.6 %collective-permute-start.20 = (bf16[4,2,5,32,1024]{4,3,2,0,1:T(8,128)(2,1)}, bf16[4,2,5,32,1024]{4,3,2,0,1:T(8,128)(2,1)}, u32[]{:S(2)}, u32[]{:S(2)}) collective-permute-start(bf16[4,2,5,32,1024]{4,3,2,0,1:T(8,128)(2,1)} %pad_maximum_fusion.1), channel_id=1, source_target_pairs={{0,8},{8,0},{16,24},{24,16},{1,9},{9,1},{17,25},{25,17},{2,10},{10... | collective-permute-start | bytes 7864328 | tf_op jit(solution)/shard_map/ppermute | solution.py:30
  156.4 61.9 %collective-permute-start.15 = (f32[16,5632]{1,0:T(8,128)}, f32[16,5632]{1,0:T(8,128)}, u32[]{:S(2)}, u32[]{:S(2)}) collective-permute-start(f32[16,5632]{1,0:T(8,128)} %constant_dynamic-slice_fusion.2), channel_id=1, source_target_pairs={{0,1},{1,0},{2,3},{3,2},{4,5},{5,4},{6,7},{7,6},{8,9},{9,8},{10,11... | collective-permute-start | bytes 1081352 | tf_op jit(solution)/shard_map/ppermute | solution.py:30
  192.0 75.0 %all-to-all-start.1 = ((bf16[8,512,384]{2,1,0:T(8,128)(2,1)}), bf16[8,512,384]{2,1,0:T(8,128)(2,1)}, u32[]{:S(2)}, u32[]{:S(2)}) async-start(bf16[8,512,384]{2,1,0:T(8,128)(2,1)} %get-tuple-element.98), calls=%async_computation.1 | async-start | bytes 6291456 | tf_op jit(solution)/shard_map/all_to_all | solution.py:885
  310.5 44.8 %all-to-all-start.3 = ((bf16[8,512,128]{2,1,0:T(8,128)(2,1)}), bf16[8,512,128]{2,1,0:T(8,128)(2,1)}, u32[]{:S(2)}, u32[]{:S(2)}) async-start(bf16[8,512,128]{2,1,0:T(8,128)(2,1)} %bitcast.197), calls=%async_computation.3 | async-start | bytes 2097152 | tf_op jit(solution)/shard_map/all_to_all | solution.py:885
  355.3 48.1 %all-to-all-start.4 = ((bf16[8,512,128]{2,1,0:T(8,128)(2,1)}), bf16[8,512,128]{2,1,0:T(8,128)(2,1)S(1)}, u32[]{:S(2)}, u32[]{:S(2)}) async-start(bf16[8,512,128]{2,1,0:T(8,128)(2,1)} %get-tuple-element.115), calls=%async_computation.4 | async-start | bytes 2097152 | tf_op jit(solution)/shard_map/all_to_all | solution.py:885
  403.4 65.5 %all-to-all-start.5 = ((bf16[8,512,128]{2,1,0:T(8,128)(2,1)}), bf16[8,512,128]{2,1,0:T(8,128)(2,1)S(1)}, u32[]{:S(2)}, u32[]{:S(2)}) async-start(bf16[8,512,128]{2,1,0:T(8,128)(2,1)} %get-tuple-element.116), calls=%async_computation.5 | async-start | bytes 2097152 | tf_op jit(solution)/shard_map/all_to_all | solution.py:885
  469.9 75.7 %all-to-all-start.7 = ((bf16[8,512,384]{2,1,0:T(8,128)(2,1)}), bf16[8,512,384]{2,1,0:T(8,128)(2,1)S(1)}, u32[]{:S(2)}, u32[]{:S(2)}) async-start(bf16[8,512,384]{2,1,0:T(8,128)(2,1)} %bitcast.189), calls=%async_computation.7 | async-start | bytes 6291456 | tf_op jit(solution)/shard_map/all_to_all | solution.py:885
  577.3 80.7 %all-to-all-start.6 = ((bf16[8,512,384]{2,1,0:T(8,128)(2,1)}), bf16[8,512,384]{2,1,0:T(8,128)(2,1)S(1)}, u32[]{:S(2)}, u32[]{:S(2)}) async-start(bf16[8,512,384]{2,1,0:T(8,128)(2,1)} %bitcast.188), calls=%async_computation.6 | async-start | bytes 6291456 | tf_op jit(solution)/shard_map/all_to_all | solution.py:885
  581.1 113.3 %all-gather.6.cloned.1.call-start = ((), (), s32[]{:S(2)}) async-start(), calls=%async_computation.9 | async-start | bytes 2973696 | tf_op jit(solution)/shard_map/all_gather | solution.py:977
  600.5 57.6 %collective-permute-start.28 = (bf16[1,256,4096]{2,1,0:T(8,128)(2,1)}, bf16[1,256,4096]{2,1,0:T(8,128)(2,1)}, u32[]{:S(2)}, u32[]{:S(2)}) collective-permute-start(bf16[1,256,4096]{2,1,0:T(8,128)(2,1)} %weight_part.18), channel_id=1, source_target_pairs={{0,16},{8,24},{16,0},{24,8},{1,17},{9,25},{17,1},{25,9},{2,18},{10... | collective-permute-start | bytes 6291464 | tf_op jit(solution)/shard_map/ppermute | solution.py:30
  602.0 66.2 %collective-permute-start.26 = (bf16[2,512,1024]{2,1,0:T(8,128)(2,1)}, bf16[2,512,1024]{2,1,0:T(8,128)(2,1)}, u32[]{:S(2)}, u32[]{:S(2)}) collective-permute-start(bf16[2,512,1024]{2,1,0:T(8,128)(2,1)} %weight_part.17), channel_id=1, source_target_pairs={{0,1},{1,0},{2,3},{3,2},{4,5},{5,4},{6,7},{7,6},{8,9},{9,8},{10,11... | collective-permute-start | bytes 6291464 | tf_op jit(solution)/shard_map/ppermute | solution.py:30
  717.1 44.5 %collective-permute-start.43 = (bf16[2,256,1024]{2,1,0:T(8,128)(2,1)}, bf16[2,256,1024]{2,1,0:T(8,128)(2,1)}, u32[]{:S(2)}, u32[]{:S(2)}) collective-permute-start(bf16[2,256,1024]{2,1,0:T(8,128)(2,1)} %weight_part.19), channel_id=1, source_target_pairs={{0,8},{8,0},{16,24},{24,16},{1,9},{9,1},{17,25},{25,17},{2,10},{10... | collective-permute-start | bytes 3145736 | tf_op jit(solution)/shard_map/ppermute | solution.py:30
  724.2 94.4 %collective-permute-start.35 = (bf16[1,256,1536]{2,1,0:T(8,128)(2,1)}, bf16[1,256,1536]{2,1,0:T(8,128)(2,1)}, u32[]{:S(2)}, u32[]{:S(2)}) collective-permute-start(bf16[1,256,1536]{2,1,0:T(8,128)(2,1)} %weight_part.21), channel_id=1, source_target_pairs={{0,16},{8,24},{16,0},{24,8},{1,17},{9,25},{17,1},{25,9},{2,18},{10... | collective-permute-start | bytes 2359304 | tf_op jit(solution)/shard_map/ppermute | solution.py:30
  743.3 55.5 %collective-permute-start.52 = (bf16[2,1,128,1024]{3,2,1,0:T(8,128)(2,1)}, bf16[2,1,128,1024]{3,2,1,0:T(8,128)(2,1)}, u32[]{:S(2)}, u32[]{:S(2)}) collective-permute-start(bf16[2,1,128,1024]{3,2,1,0:T(8,128)(2,1)} %dynamic-slice_convert_fusion.2), channel_id=1, source_target_pairs={{0,2},{1,3},{2,0},{3,1},{4,6},{5,7},{6,4},{7,5},{8,10},{9,11},{10,... | collective-permute-start | bytes 1572872 | tf_op jit(solution)/shard_map/ppermute | solution.py:30
  761.5 75.8 %collective-permute-start.48 = (bf16[2,2,1,32,4096]{4,3,2,1,0:T(8,128)(2,1)}, bf16[2,2,1,32,4096]{4,3,2,1,0:T(8,128)(2,1)}, u32[]{:S(2)}, u32[]{:S(2)}) collective-permute-start(bf16[2,2,1,32,4096]{4,3,2,1,0:T(8,128)(2,1)} %dynamic-slice_convert_fusion), channel_id=1, source_target_pairs={{0,1},{1,0},{2,3},{3,2},{4,5},{5,4},{6,7},{7,6},{8,9},{9,8},{10,11... | collective-permute-start | bytes 3145736 | tf_op jit(solution)/shard_map/ppermute | solution.py:30
  817.7 48.0 %collective-permute-start.34 = (f32[64,2816]{1,0:T(8,128)}, f32[64,2816]{1,0:T(8,128)}, u32[]{:S(2)}, u32[]{:S(2)}) collective-permute-start(f32[64,2816]{1,0:T(8,128)} %pad_maximum_fusion.7), channel_id=1, source_target_pairs={{0,8},{8,0},{16,24},{24,16},{1,9},{9,1},{17,25},{25,17},{2,10},{10... | collective-permute-start | bytes 2162696 | tf_op jit(solution)/shard_map/ppermute | solution.py:30
  (94 other events, 1224.8 us)
Sparse Core Ops, SparseCore 0:
  14.7 91.8 all-gather.3
  585.4 97.6 all-gather.5

commit v5 on v4

--- a/solution.py
+++ b/solution.py
@@ -52,14 +52,15 @@
 
 
 def halve_sum(parts, bits, wire=f32):
-    parts = parts.reshape((2,) * len(bits) + parts.shape[1:])
+    addends = [parts.reshape((2,) * len(bits) + parts.shape[1:])]
     for place in exchange_order(bits):
         axis, bit = bits[place]
         mine = own_bit(axis, bit)
-        keep = lax.dynamic_index_in_dim(parts, mine, place)
-        send = lax.dynamic_index_in_dim(parts, 1 - mine, place)
-        parts = keep + swap_bit(send.astype(wire), axis, bit).astype(f32)
-    return parts.reshape(parts.shape[len(bits) :])
+        send = sum(lax.dynamic_index_in_dim(a, 1 - mine, place).astype(f32) for a in addends)
+        addends = [lax.dynamic_index_in_dim(a, mine, place) for a in addends]
+        addends.append(swap_bit(send.astype(wire), axis, bit))
+    total = sum(a.astype(f32) for a in addends)
+    return total.reshape(total.shape[len(bits) :])
 
 
 def near_order():
@@ -79,12 +80,18 @@
     return parts
 
 
-def spread_rows(rows, bits):
+def collect_rows(rows, bits):
     for axis, bit in reversed(bits):
-        other = swap_bit(rows, axis, bit)
-        low = own_bit(axis, bit) == 0
-        rows = jnp.concatenate([jnp.where(low, rows, other), jnp.where(low, other, rows)], axis=0)
+        rows = jnp.concatenate([rows, swap_bit(rows, axis, bit)], axis=0)
     return rows
+
+
+def relative_rows(rows, bits):
+    shape = rows.shape
+    rows = rows.reshape((2,) * len(bits) + (-1,) + shape[1:])
+    for place, (axis, bit) in enumerate(bits):
+        rows = jnp.where(own_bit(axis, bit) == 0, rows, jnp.flip(rows, place))
+    return rows.reshape(shape)
 
 
 def after(value, *others):
@@ -201,7 +208,7 @@
             jax.ShapeDtypeStruct((groups, rows, 3 * span), bf16),
             jax.ShapeDtypeStruct((rows, width), bf16),
         ),
-        compiler_params=pltpu.CompilerParams(vmem_limit_bytes=60 << 20),
+        compiler_params=pltpu.CompilerParams(vmem_limit_bytes=32 << 20),
         cost_estimate=pl.CostEstimate(
             flops=6 * rows * width * width, bytes_accessed=6 * width * width + 10 * rows * width, transcendentals=0
         ),
@@ -271,7 +278,7 @@
         ),
         input_output_aliases={7: 0} if earlier else {},
         scratch_shapes=[pltpu.VMEM((rows, width), f32)],
-        compiler_params=pltpu.CompilerParams(vmem_limit_bytes=60 << 20),
+        compiler_params=pltpu.CompilerParams(vmem_limit_bytes=40 << 20),
         cost_estimate=pl.CostEstimate(
             flops=6 * rows * width * width, bytes_accessed=6 * width * width + 22 * rows * width, transcendentals=0
         ),
@@ -491,55 +498,77 @@
     )(mine, back, tokens, cot, mods, bias_out, bias_up, bias_down, *up_shares, *up_shares, *down_shares, *earlier)
 
 
-def weight_part_kernel(index_ref, *refs, clips, addends):
-    left, right = refs[:clips], refs[clips : 2 * clips]
-    extra = refs[2 * clips : 2 * clips + addends]
-    out_ref, flat_ref = refs[2 * clips + addends :]
-    rows = left[0].shape[0]
-
-    @pl.when(pl.program_id(1) == 0)
-    def _():
-        for c in range(clips):
-            flat_ref[:, c * rows : (c + 1) * rows] = jnp.transpose(left[c][...])
-
-    total = dot(flat_ref[:, 0:rows], right[0][...])
-    for c in range(1, clips):
-        total += dot(flat_ref[:, c * rows : (c + 1) * rows], right[c][...])
-    for ref in extra:
-        total += ref[0].astype(f32)
-    out_ref[0] = total.astype(out_ref.dtype)
-
-
-def weight_part(left, right, indices, addends, kind, height, first_column=0, columns=None):
-    rows = left[0].shape[0]
-    columns = right[0].shape[1] if columns is None else columns
+def weight_part_kernel(index_ref, *refs, clips, count, widths, addends):
+    sets = len(widths)
+    per_set = clips * (count + 1)
+    extra = refs[sets * per_set : sets * per_set + addends]
+    out_ref, flat_ref = refs[sets * per_set + addends :]
+    step = pl.program_id(0)
+    first = 0
+    for place, steps in enumerate(widths):
+        given = refs[place * per_set : (place + 1) * per_set]
+        left, right = given[: clips * count], given[clips * count :]
+        rows = right[0].shape[0]
+
+        @pl.when(step == first)
+        def _(left=left, rows=rows):
+            for c in range(clips):
+                for i in range(count):
+                    flat_ref[i, :, c * rows : (c + 1) * rows] = jnp.transpose(left[c * count + i][...])
+
+        @pl.when((step >= first) & (step < first + steps))
+        def _(right=right, rows=rows):
+            for i in range(count):
+                total = dot(flat_ref[i, :, 0:rows], right[0][...])
+                for c in range(1, clips):
+                    total += dot(flat_ref[i, :, c * rows : (c + 1) * rows], right[c][...])
+                for ref in extra:
+                    total += ref[i].astype(f32)
+                out_ref[i] = total.astype(out_ref.dtype)
+
+        first += steps
+
+
+def weight_part(pairs, indices, addends, kind, height):
     block = 512
-    start = first_column // block
     count = indices.shape[0]
-    in_specs = [pl.BlockSpec((rows, height), lambda i, j, q: (0, q[i]))] * len(left)
-    in_specs += [pl.BlockSpec((rows, block), lambda i, j, q: (0, start + j))] * len(right)
-    for array, first in addends:
-        shift = start if array.shape[2] > columns else 0
-        where = functools.partial(lambda first, shift, i, j, q: (first + i, 0, shift + j), first, shift)
-        in_specs.append(pl.BlockSpec((1, height, block), where))
+    clips = len(pairs[0][0])
+    rows = pairs[0][0][0].shape[0]
+    widths = [right[0].shape[1] // block for _, right in pairs]
+    columns = sum(widths) * block
+    in_specs, operands = [], []
+    first = 0
+    for (left, right), steps in zip(pairs, widths):
+        for array in left:
+            for i in range(count):
+                in_specs.append(pl.BlockSpec((rows, height), functools.partial(lambda i, j, q: (0, q[i]), i)))
+                operands.append(array)
+        where = functools.partial(lambda first, steps, j, q: (0, jnp.clip(j - first, 0, steps - 1)), first, steps)
+        in_specs += [pl.BlockSpec((rows, block), where)] * clips
+        operands += right
+        first += steps
+    for array, start in addends:
+        where = functools.partial(lambda start, j, q: (start, 0, j), start // count)
+        in_specs.append(pl.BlockSpec((count, height, block), where))
+        operands.append(array)
     return pl.pallas_call(
-        functools.partial(weight_part_kernel, clips=len(left), addends=len(addends)),
+        functools.partial(weight_part_kernel, clips=clips, count=count, widths=widths, addends=len(addends)),
         grid_spec=pltpu.PrefetchScalarGridSpec(
             num_scalar_prefetch=1,
-            grid=(count, columns // block),
+            grid=(columns // block,),
             in_specs=in_specs,
-            out_specs=pl.BlockSpec((1, height, block), lambda i, j, q: (i, 0, j)),
-            scratch_shapes=[pltpu.VMEM((height, len(left) * rows), bf16)],
+            out_specs=pl.BlockSpec((count, height, block), lambda j, q: (0, 0, j)),
+            scratch_shapes=[pltpu.VMEM((count, height, clips * rows), bf16)],
         ),
         out_shape=jax.ShapeDtypeStruct((count, height, columns), kind),
-        compiler_params=pltpu.CompilerParams(vmem_limit_bytes=60 << 20),
+        compiler_params=pltpu.CompilerParams(vmem_limit_bytes=32 << 20),
         cost_estimate=pl.CostEstimate(
-            flops=2 * count * len(left) * rows * height * columns,
-            bytes_accessed=len(left) * rows * (count * height + columns) * 2 + 4 * count * height * columns,
+            flops=2 * count * clips * rows * height * columns,
+            bytes_accessed=clips * rows * (count * height + columns) * 2 + 4 * count * height * columns,
             transcendentals=0,
         ),
         name="weight_part",
-    )(indices, *left, *right, *[array for array, _ in addends])
+    )(indices, *operands)
 
 
 def mine_on(axis):
@@ -550,44 +579,51 @@
     return list(lax.optimization_barrier((tuple(arrays), others))[0])
 
 
-def across_first(left, right):
+def height_of(pairs, parts):
+    return pairs[0][0][0].shape[1] // parts
+
+
+def across_first(pairs):
     mine = mine_on("clip")
-    return weight_part(left, right, jnp.stack([mine ^ 3, mine ^ 1]), (), bf16, left[0].shape[1] // 4)
-
-
-def across_second(left, right, core):
-    return weight_part(left, right, (mine_on("clip") ^ 2)[None], ((core, 0),), bf16, left[0].shape[1] // 4)
-
-
-def across_total(left, right, core, across):
-    height = left[0].shape[1] // 4
-    total = weight_part(left, right, mine_on("clip")[None], ((core, 1), (across, 0)), f32, height)
-    return halve_sum(total.reshape((lax.axis_size("seq"), -1, right[0].shape[1])), axis_bits("seq"), bf16)
+    return weight_part(pairs, jnp.stack([mine ^ 3, mine ^ 1]), (), bf16, height_of(pairs, 4))
+
+
+def across_second(pairs, core):
+    return weight_part(pairs, (mine_on("clip") ^ 2)[None], ((core, 0),), bf16, height_of(pairs, 4))
+
+
+def across_own(pairs, core, across):
+    addends = ((core, 1), (across, 0))
+    return weight_part(pairs, mine_on("clip")[None], addends, f32, height_of(pairs, 4))
+
+
+def along_seq(total):
+    return halve_sum(total.reshape((lax.axis_size("seq"), -1, total.shape[2])), axis_bits("seq"), bf16)
 
 
 def along_block(clip_flip, low_flip):
     return (mine_on("clip") ^ clip_flip) * 2 + ((mine_on("seq") & 1) ^ low_flip)
 
 
-def along_first(left, right):
+def along_first(pairs):
     blocks = jnp.stack([along_block(1, 1), along_block(3, 1), along_block(1, 0), along_block(3, 0)])
-    return weight_part(left, right, blocks, (), bf16, left[0].shape[1] // 8)
-
-
-def along_second(left, right, core):
+    return weight_part(pairs, blocks, (), bf16, height_of(pairs, 8))
+
+
+def along_second(pairs, core):
     blocks = jnp.stack([along_block(0, 1), along_block(2, 1)])
-    return weight_part(left, right, blocks, ((core, 0),), bf16, left[0].shape[1] // 8)
-
-
-def along_third(left, right, core, along):
-    return weight_part(left, right, along_block(2, 0)[None], ((core, 3), (along, 1)), bf16, left[0].shape[1] // 8)
-
-
-def along_total(left, right, core, along, across):
+    return weight_part(pairs, blocks, ((core, 0),), bf16, height_of(pairs, 8))
+
+
+def along_third(pairs, core, along):
+    return weight_part(pairs, along_block(2, 0)[None], ((core, 3), (along, 1)), bf16, height_of(pairs, 8))
+
+
+def along_total(pairs, core, along, across):
     addends = ((core, 2), (along, 0), (across, 0))
-    total = weight_part(left, right, along_block(0, 0)[None], addends, f32, left[0].shape[1] // 8)
+    total = weight_part(pairs, along_block(0, 0)[None], addends, f32, height_of(pairs, 8))
     bits = axis_bits("seq")[:-1]
-    return halve_sum(total.reshape((2 ** len(bits), -1, right[0].shape[1])), bits, bf16)
+    return halve_sum(total.reshape((2 ** len(bits), -1, total.shape[2])), bits, bf16)
 
 
 def attend_kernel(qkv_ref, mix_ref, full_ref, log_ref, vt_ref, *, total, span, block):
@@ -858,6 +894,7 @@
     near_levels = levels.reshape(flat_bits + (lines,)).transpose(turn)
     cond_near = condition(near_levels, here, mod_weight.shape[0], width)
     cond = condition(levels, here, mod_weight.shape[0], width)
+    cond_late = relative_rows(cond_near, order)
     mod_place = own_place(mod_bias, here)
 
     def modulate(columns, biases, gates=()):
@@ -937,80 +974,65 @@
         results.append(middle(back, tokens, cotangent, c, mods_two[c], up_shares, down_shares, (bias_out, bias_up, bias_down), outputs))
         d_mixed.append(exchange(after(results[c][8], backs[-1] if c == 0 else d_mixed[-1])))
 
+    def late(place):
+        return [r[place] for r in results]
+
+    mixed_all, normed_two, active, d_hidden, d_mlp, d_attn = [late(place) for place in (2, 3, 4, 5, 6, 7)]
+    def line_sums(sums):
+        return sums.transpose(1, 0, 2).reshape(frames, -1)
+
+    def with_bias(lines_now, vectors):
+        return jnp.concatenate([jnp.concatenate(lines_now, axis=0), jnp.concatenate(vectors).reshape(lines, -1)], axis=1)
+
+    bias_up_sum = sum(r[10][0] for r in results).reshape(near_owners).transpose(0, 2, 1, 3).reshape(-1)
+    bias_pair = sum(r[11] for r in results)
+    early = with_bias([line_sums(r[9]) for r in results], [bias_pair[0], bias_up_sum, bias_pair[1]])
+    early_rows = lax.all_gather(early, BOTH, axis=0, tiled=True)
+
     d_qkv, exchanged = [], []
     for c in range(clips):
-        grad = after(d_mixed[c], results[-1][8] if c == 0 else d_qkv[-1])
+        if c == clips - 1:
+            active = gate(active, *d_qkv)
+            down_first = along_first([(active, d_mlp)])
+            down_core = swap_bit(down_first, "clip", 1)
+            normed_two = gate(normed_two, down_first)
+            up_first = across_first([(normed_two, d_hidden), (mixed_all, d_attn)])
+            up_core = swap_bit(up_first, "clip", 1)
+        grad = after(d_mixed[c], results[-1][8] if c == 0 else up_first)
         grad = grad.reshape(total, span)
         d_qkv.append(attend_back(qkv[c].reshape(total, 3 * span), grad, fulls[c], logs[c], cos_all, sin_all, span))
         sent = d_qkv[c].reshape(seq_devices, rows, 3 * span)
         exchanged.append(exchange(after(sent, d_mixed[-1]) if c == 0 else sent))
 
-    def late(place):
-        return [r[place] for r in results]
-
-    mixed_all, normed_two, active, d_hidden, d_mlp, d_attn = [late(place) for place in (2, 3, 4, 5, 6, 7)]
-    active = gate(active, d_qkv[-1], exchanged[0])
-    down_first = along_first(active, d_mlp)
-    normed_two = gate(normed_two, down_first)
-    up_first = across_first(normed_two, d_hidden)
-    down_core, up_core = swap_bit(down_first, "clip", 1), swap_bit(up_first, "clip", 1)
-    d_mlp = gate(d_mlp, up_first)
-    down_second = along_second(active, d_mlp, down_core)
+    d_mlp = gate(d_mlp, exchanged[0])
+    down_second = along_second([(active, d_mlp)], down_core)
     d_hidden = gate(d_hidden, down_second)
-    up_second = across_second(normed_two, d_hidden, up_core)
-    mixed_all = gate(mixed_all, up_second)
-    out_first = across_first(mixed_all, d_attn)
-    out_core = swap_bit(out_first, "clip", 1)
+    up_second = across_second([(normed_two, d_hidden), (mixed_all, d_attn)], up_core)
     down_along, up_across = swap_bit(down_second, "seq", 1), swap_bit(up_second, "clip", 2)
-    exchanged[0] = after(exchanged[0], out_first)
+    exchanged[0] = after(exchanged[0], up_second)
     exchanged[-1] = after(exchanged[-1], down_along, up_across)
-
-    def line_sums(sums):
-        return sums.transpose(1, 0, 2).reshape(frames, -1)
-
-    def with_bias(lines_now, vectors):
-        return jnp.concatenate([jnp.concatenate(lines_now, axis=0), jnp.concatenate(vectors).reshape(lines, -1)], axis=1)
-
-    bias_up_sum = sum(r[10][0] for r in results).reshape(near_owners).transpose(0, 2, 1, 3).reshape(-1)
-    bias_pair = sum(r[11] for r in results)
-    early = with_bias([line_sums(r[9]) for r in results], [bias_pair[0], bias_up_sum, bias_pair[1]])
-    early_rows = lax.all_gather(early, BOTH, axis=0, tiled=True)
 
     last = []
     for c in range(clips):
         grads = last[-1][0] if last else None
         last.append(project_back(exchanged[c], full_qkv, tokens, c, mods_one[c][1], results[c][1], grads))
     d_projected = [r[1] for r in last]
-    mine = mine_on("clip")
-    height, half = width // 4, 3 * width // 2
-    qkv_first = across_first(normed, d_projected)
-    qkv_core = swap_bit(qkv_first, "clip", 1)
-    down_across = swap_bit(along_third(active, gate(d_mlp, qkv_first), down_core, down_along), "clip", 2)
-    qkv_second = weight_part(normed, d_projected, (mine ^ 2)[None], ((qkv_core, 0),), bf16, height, 0, half)
+    qkv_pairs = [(normed, d_projected)]
+    qkv_core = swap_bit(across_first(qkv_pairs), "clip", 1)
+    qkv_second = across_second(qkv_pairs, qkv_core)
     qkv_across = swap_bit(qkv_second, "clip", 2)
-    far_part = weight_part(
-        gate(normed, qkv_second), d_projected, (mine ^ 2)[None], ((qkv_core, 0),), f32, height, half, half
-    )
-    near_part = weight_part(
-        gate(normed, qkv_second), d_projected, mine[None], ((qkv_core, 1),), f32, height, half, half
-    )
-    pair = jnp.stack([near_part[0], far_part[0]]).reshape(2, seq_devices // 2, 2, -1, half)
-    low = own_bit("seq", 1)
-    along = swap_bit(lax.dynamic_index_in_dim(pair, 1 - low, 2, keepdims=False).astype(bf16), "seq", 1)
-    d_attn = gate(d_attn, qkv_second)
-    out_across = swap_bit(across_second(mixed_all, d_attn, out_core), "clip", 2)
-    pair = lax.dynamic_index_in_dim(pair, low, 2, keepdims=False) + along.astype(f32)
-    grad_second = pair[0] + swap_bit(pair[1].astype(bf16), "clip", 2).astype(f32)
-    grad_second = halve_sum(grad_second, axis_bits("seq")[:-1], bf16)
-    total_first = weight_part(normed, d_projected, mine[None], ((qkv_core, 1), (qkv_across, 0)), f32, height, 0, half)
-    grad_first = halve_sum(total_first.reshape(seq_devices, -1, half), axis_bits("seq"), bf16)
-    grad_qkv = jnp.concatenate([grad_first, grad_second], axis=1)
-    grad_up = across_total(normed_two, gate(d_hidden, qkv_second), up_core, up_across)
-    grad_down = along_total(active, gate(d_mlp, qkv_second), down_core, down_along, down_across)
-    grad_up = grad_up.reshape((-1,) + near_owners).transpose(0, 1, 3, 2, 4).reshape(-1, 4 * width)
-    grad_out = across_total(mixed_all, d_attn, out_core, out_across)
+    d_hidden = gate(d_hidden, qkv_second)
+    up_total = across_own([(normed_two, d_hidden), (mixed_all, d_attn)], up_core, up_across)
+    qkv_total = across_own(qkv_pairs, qkv_core, qkv_across)
+    d_mlp = gate(d_mlp, qkv_total)
+    down_across = swap_bit(along_third([(active, d_mlp)], down_core, down_along), "clip", 2)
+    grad_up, grad_qkv = along_seq(up_total), along_seq(qkv_total)
+    grad_down = along_total([(active, d_mlp)], down_core, down_along, down_across)
+    grad_out = grad_up[:, 4 * width :]
+    grad_up = grad_up[:, : 4 * width].reshape((-1,) + near_owners).transpose(0, 1, 3, 2, 4).reshape(-1, 4 * width)
     late_rows = with_bias([line_sums(r[2]) for r in last], [sum(r[3][0] for r in last)])
-    late_rows = spread_rows(after(late_rows, qkv_second), order)
+    late_rows = collect_rows(after(late_rows, qkv_total), order)
+    early_rows = after(early_rows, qkv_total)
 
     def own_columns(sums, shard):
         return lax.dynamic_slice_in_dim(sums, here * shard.shape[0], shard.shape[0], 0)
@@ -1024,7 +1046,7 @@
     grad_mod = jnp.concatenate(
         [
             lax.dot_general(rows_cond.astype(f32), r, TN, precision=highest, preferred_element_type=f32)
-            for rows_cond, r in ((cond_near, late_mod), (cond, early_mod))
+            for rows_cond, r in ((cond_late, late_mod), (cond, early_mod))
         ],
         axis=1,
     )

time: 908 us -> 896 us (0.987)
  Pallas kernels: 425 us -> 371 us
  local copies, waits for them, and re-layouts: 51 us -> 99.8 us
  starting transfers between devices: 114 us -> 96.5 us
  waiting for transfers between devices: 234 us -> 246 us
    pallas_call x15 -> x10, Pallas kernels: 117 us -> 73.3 us  [weight_part(): pl.pallas_call(functools.partial(weight_part_kernel, clips=clips, count=c...]
    unnamed x113 -> x220, local copies, waits for them, and re-layouts: 11.2 us -> 52 us
    ppermute x54 -> x45, starting transfers between devices: 72.6 us -> 53.1 us  [swap_bit(): return lax.ppermute(value, axis, [(i, i ^ bit) for i in range(count)])]
    convert_element_type x0 -> x6, other arithmetic: none -> 9.36 us  [the longest x5 8.79 us: halve_sum(): addends.append(swap_bit(send.astype(wire), axis, bit))]
    ppermute x54 -> x45, waiting for transfers between devices: 152 us -> 150 us  [swap_bit(): return lax.ppermute(value, axis, [(i, i ^ bit) for i in range(count)])]
  transfers between devices with their start and end apart: 64 -> 55, of which waited for: 22 -> 20; matrix products, arithmetic and copies ran while one was open for 11% -> 11% of each run, Pallas kernels for 46% -> 42%
where the time goes in v5:
time: 896 us; the launch traced here: 885 us
  Pallas kernels  371 us (41%)
  waiting for transfers between devices  246 us (27%)
  local copies, waits for them, and re-layouts  99.8 us (11%)
  starting transfers between devices  96.5 us (11%)
  other arithmetic  50.9 us (6%)
  between operations  15.9 us (2%)
    ppermute x45, waiting for transfers between devices, swap_bit(): return lax.ppermute(value, axis, [(i, i ^ bit) for i in range(count)])  150 us
    pallas_call x2, Pallas kernels, attend_back(): pl.pallas_call(functools.partial(attend_back_kernel, total=total, span=sp...  118 us
    all_to_all x8, waiting for transfers between devices, exchange(): return lax.all_to_all(value, 'seq', 0, 0, tiled=True)  82.7 us
    pallas_call x2, Pallas kernels, middle(): pl.pallas_call(middle_kernel, grid_spec=pltpu.PrefetchScalarGridSpec(num_...  76.4 us
    pallas_call x10, Pallas kernels, weight_part(): pl.pallas_call(functools.partial(weight_part_kernel, clips=clips, count=c...  73.3 us
    pallas_call x2, Pallas kernels, attend(): pl.pallas_call(functools.partial(attend_kernel, total=total, span=span, b...  70.6 us
    ppermute x45, starting transfers between devices, swap_bit(): return lax.ppermute(value, axis, [(i, i ^ bit) for i in range(count)])  53.1 us
    unnamed x220, local copies, waits for them, and re-layouts  52 us
  transfers between devices with their start and end apart: 55, of which 20 were waited for; matrix products, arithmetic and copies ran while one was open for 11% of the time, Pallas kernels for 42%

profile of v5, /device:TPU:0, one launch (start us, length us, event | category | flops | bytes accessed | tf_op | source)
XLA Modules:
  0.0 885.3 jit_solution(16363996730348683064)
XLA Ops:
  50.5 10.5 %collective-permute-done.8 = bf16[2,4,32,1024]{3,2,1,0:T(8,128)(2,1)S(1)} collective-permute-done((bf16[2,4,32,1024]{3,2,1,0:T(8,128)(2,1)S(1)}, bf16[2,4,32,1024]{3,2,1,0:T(8,128)(2,1)S(1)}, u32[]{:S(2)}, u32[]{:S(2)}) %collective-permute-start.8) | collective-permute-done | bytes 524320 | tf_op jit(solution)/shard_map/ppermute | solution.py:30
  64.1 19.5 %collective-permute-done.10 = bf16[2,5,32,1024]{3,2,1,0:T(8,128)(2,1)S(1)} collective-permute-done((bf16[2,5,32,1024]{3,2,1,0:T(8,128)(2,1)S(1)}, bf16[2,5,32,1024]{3,2,1,0:T(8,128)(2,1)S(1)}, u32[]{:S(2)}, u32[]{:S(2)}) %collective-permute-start.10) | collective-permute-done | bytes 655392 | tf_op jit(solution)/shard_map/ppermute | solution.py:30
  95.8 13.1 %all-gather.4.cloned.1.call-done.wq_ref.wk_ref.wv_ref = bf16[1024,3072]{1,0:T(8,128)(2,1)} async-done(((bf16[32,3072]{1,0:T(8,128)(2,1)}), bf16[1024,3072]{1,0:T(8,128)(2,1)}) %all-gather.4.cloned.1.call-update) | async-done | bytes 6291472 | tf_op jit(solution)/shard_map/all_gather | solution.py:882
  139.9 7.9 collective-permute-done.14
  162.9 35.3 %all-to-all-done = bf16[8,512,384]{2,1,0:T(8,128)(2,1)} async-done(((bf16[8,512,384]{2,1,0:T(8,128)(2,1)}), bf16[8,512,384]{2,1,0:T(8,128)(2,1)}, u32[]{:S(2)}, u32[]{:S(2)}) %all-to-all-start) | async-done | bytes 3145760 | tf_op jit(solution)/shard_map/all_to_all | solution.py:922
  213.0 35.3 %attend.3 = (bf16[4096,128]{1,0:T(8,128)(2,1)}, f32[4096,128]{1,0:T(8,128)}, f32[2,4096]{1,0:T(2,128)}) custom-call(bf16[4096,384]{1,0:T(8,128)(2,1)} %bitcast.36.qkv_ref), custom_call_target="tpu_custom_call" | custom-call | flops 17179869184 | bytes 6291456 | tf_op jit(solution)/shard_map/attend/pallas_call | solution.py:687
  248.3 9.7 %collective-permute-done.16 = f32[8,5632]{1,0:T(8,128)S(1)} collective-permute-done((f32[8,5632]{1,0:T(8,128)S(1)}, f32[8,5632]{1,0:T(8,128)S(1)}, u32[]{:S(2)}, u32[]{:S(2)}) %collective-permute-start.16) | collective-permute-done | bytes 180256 | tf_op jit(solution)/shard_map/ppermute | solution.py:30
  258.1 15.2 %all-to-all-done.1 = bf16[8,512,384]{2,1,0:T(8,128)(2,1)} async-done(((bf16[8,512,384]{2,1,0:T(8,128)(2,1)}), bf16[8,512,384]{2,1,0:T(8,128)(2,1)}, u32[]{:S(2)}, u32[]{:S(2)}) %all-to-all-start.1) | async-done | bytes 3145760 | tf_op jit(solution)/shard_map/all_to_all | solution.py:922
  280.6 35.3 %attend.2 = (bf16[4096,128]{1,0:T(8,128)(2,1)}, f32[4096,128]{1,0:T(8,128)}, f32[2,4096]{1,0:T(2,128)}) custom-call(bf16[4096,384]{1,0:T(8,128)(2,1)} %bitcast.34.qkv_ref), custom_call_target="tpu_custom_call" | custom-call | flops 17179869184 | bytes 6291456 | tf_op jit(solution)/shard_map/attend/pallas_call | solution.py:687
  324.4 38.2 %middle.2 = (bf16[2,512,1024]{2,1,0:T(8,128)(2,1)}, f32[512,1024]{1,0:T(8,128)}, bf16[512,1024]{1,0:T(8,128)(2,1)}, bf16[512,1024]{1,0:T(8,128)(2,1)}, bf16[512,...) custom-call(s32[1]{0:T(128)} %bitcast.clip_ref.index_ref, ...), custom_call_target="tpu_custom_call" | custom-call | flops 2147483648 | bytes 4718592 | tf_op jit(solution)/shard_map/middle/pallas_call | solution.py:443
  372.5 38.2 %middle.3 = (bf16[2,512,1024]{2,1,0:T(8,128)(2,1)}, f32[512,1024]{1,0:T(8,128)}, bf16[512,1024]{1,0:T(8,128)(2,1)}, bf16[512,1024]{1,0:T(8,128)(2,1)}, bf16[512,...) custom-call(s32[1]{0:T(128)} %bitcast.clip_ref.index_ref, ...), custom_call_target="tpu_custom_call", output_to_operand_aliasing={{0}: (20, {})} | custom-call | flops 2147483648 | bytes 4718592 | tf_op jit(solution)/shard_map/middle/pallas_call | solution.py:443
  417.3 59.0 %attend_back.2 = bf16[4096,384]{1,0:T(8,128)(2,1)} custom-call(bf16[4096,384]{1,0:T(8,128)(2,1)} %bitcast.36.qkv_ref, bf16[4096,128]{1,0:T(8,128)(2,1)} %bitcast.192, f32[4096,128]{1,0:T(8,128)} %get-tuple-element.115.full_ref, f32[2,4096]{1,0:T(2,128)} %get-tuple-element.116.log_ref, f32[4096,128]{1,0:T(8,128)} %bitcast.188, f32[4096,128]{1,0:T(8,128)} %bitcast.186), custom_call_target="tpu_custom_call" | custom-call | flops 42949672960 | bytes 13631488 | tf_op jit(solution)/shard_map/attend_back/pallas_call | solution.py:782
  488.3 8.4 weight_part.10
  498.0 11.3 %weight_part.11 = bf16[2,256,5120]{2,1,0:T(8,128)(2,1)} custom-call(s32[2]{0:T(128)S(1)} %pad_add_fusion.5.index_ref, bf16[512,1024]{1,0:T(8,128)(2,1)S(1)} %copy-done.37, bf16[512,1024]{1,0:T(8,128)(2,1)S(1)} %copy-done.37, bf16[512,1024]{1,0:T(8,128)(2,1)S(1)} %copy-done.43, bf16[512,1024]{1,0:T(8,128)(2,1)S(1)} %copy-done.43, ...), custom_call_target="tpu_custom_call" | custom-call | flops 5368709120 | bytes 22020096 | tf_op jit(solution)/shard_map/weight_part/pallas_call | solution.py:554
  509.8 59.0 %attend_back.3 = bf16[4096,384]{1,0:T(8,128)(2,1)} custom-call(bf16[4096,384]{1,0:T(8,128)(2,1)} %bitcast.34.qkv_ref, bf16[4096,128]{1,0:T(8,128)(2,1)} %bitcast.193, f32[4096,128]{1,0:T(8,128)} %get-tuple-element.130.full_ref, f32[2,4096]{1,0:T(2,128)} %get-tuple-element.131.log_ref, f32[4096,128]{1,0:T(8,128)} %bitcast.189, f32[4096,128]{1,0:T(8,128)} %bitcast.187), custom_call_target="tpu_custom_call" | custom-call | flops 42949672960 | bytes 13631488 | tf_op jit(solution)/shard_map/attend_back/pallas_call | solution.py:782
  588.7 9.6 %weight_part.13 = bf16[1,256,5120]{2,1,0:T(8,128)(2,1)} custom-call(s32[1]{0:T(128)} %bitcast.64.index_ref, bf16[512,1024]{1,0:T(8,128)(2,1)S(1)} %copy-done.38, bf16[512,1024]{1,0:T(8,128)(2,1)S(1)} %copy-done.44, bf16[512,4096]{1,0:T(8,128)(2,1)S(1)} %copy-done.12, bf16[512,4096]{1,0:T(8,128)(2,1)S(1)} %copy-done.15, bf16[512,1024]{1,0:T(8,128)(2,1)S(1)} %copy-done.35, ...), custom_call_target="tpu_custom_call" | custom-call | flops 2684354560 | bytes 16252928 | tf_op jit(solution)/shard_map/weight_part/pallas_call | solution.py:554
  604.3 9.8 %project_back.2 = (f32[2,512,1024]{2,1,0:T(8,128)}, bf16[512,3072]{1,0:T(8,128)(2,1)S(1)}, f32[2,2,1024]{2,1,0:T(2,128)S(1)}, f32[1,3072]{1,0:T(1,128)S(1)}) custom-call(bf16[8,512,384]{2,1,0:T(8,128)(2,1)} %all-to-all-done.7.back_ref, bf16[1024,3072]{1,0:T(8,128)(2,1)} %all-gather.4.cloned.1.call-done.wq_ref.wk_ref.wv_ref, ...), custom_call_target="tpu_custom_call" | custom-call | flops 3221225472 | bytes 17825792 | tf_op jit(solution)/shard_map/project_back/pallas_call | solution.py:260
  615.7 32.2 %all-to-all-done.6.back_ref = bf16[8,512,384]{2,1,0:T(8,128)(2,1)} async-done(((bf16[8,512,384]{2,1,0:T(8,128)(2,1)}), bf16[8,512,384]{2,1,0:T(8,128)(2,1)}, u32[]{:S(2)}, u32[]{:S(2)}) %all-to-all-start.6) | async-done | bytes 3145760 | tf_op jit(solution)/shard_map/all_to_all | solution.py:922
  647.8 16.1 %collective-permute-done.26.refs_5_ = bf16[2,512,1024]{2,1,0:T(8,128)(2,1)} collective-permute-done((bf16[2,512,1024]{2,1,0:T(8,128)(2,1)}, bf16[2,512,1024]{2,1,0:T(8,128)(2,1)}, u32[]{:S(2)}, u32[]{:S(2)}) %collective-permute-start.26) | collective-permute-done | bytes 2097184 | tf_op jit(solution)/shard_map/ppermute | solution.py:30
  665.6 9.9 %project_back.3 = (f32[2,512,1024]{2,1,0:T(8,128)}, bf16[512,3072]{1,0:T(8,128)(2,1)S(1)}, f32[2,2,1024]{2,1,0:T(2,128)S(1)}, f32[1,3072]{1,0:T(1,128)S(1)}) custom-call(bf16[8,512,384]{2,1,0:T(8,128)(2,1)} %all-to-all-done.6.back_ref, bf16[1024,3072]{1,0:T(8,128)(2,1)} %all-gather.4.cloned.1.call-done.wq_ref.wk_ref.wv_ref, ...), custom_call_target="tpu_custom_call", output_to_operand_aliasing={{0}: (7, {})} | custom-call | flops 3221225472 | bytes 17825792 | tf_op jit(solution)/shard_map/project_back/pallas_call | solution.py:260
  704.0 9.5 %weight_part.17 = f32[1,256,5120]{2,1,0:T(8,128)S(1)} custom-call(s32[1]{0:T(128)} %bitcast.clip_ref.index_ref, bf16[512,1024]{1,0:T(8,128)(2,1)S(1)} %copy-done.39, bf16[512,1024]{1,0:T(8,128)(2,1)S(1)} %copy-done.45, bf16[512,4096]{1,0:T(8,128)(2,1)S(1)} %copy-done.13, bf16[512,4096]{1,0:T(8,128)(2,1)S(1)} %copy-done.16, bf16[512,1024]{1,0:T(8,128)(2,1)S(1)} %copy-done.36, ...), custom_call_target="tpu_custom_call" | custom-call | flops 2684354560 | bytes 16252928 | tf_op jit(solution)/shard_map/weight_part/pallas_call | solution.py:554
  723.5 24.7 %collective-permute-done.39 = bf16[2,2,1,32,5120]{4,3,2,1,0:T(8,128)(2,1)} collective-permute-done((bf16[2,2,1,32,5120]{4,3,2,1,0:T(8,128)(2,1)}, bf16[2,2,1,32,5120]{4,3,2,1,0:T(8,128)(2,1)}, u32[]{:S(2)}, u32[]{:S(2)}) %collective-permute-start.39) | collective-permute-done | bytes 1310752 | tf_op jit(solution)/shard_map/ppermute | solution.py:30
  797.6 17.7 %collective-permute-done.34 = f32[32,2816]{1,0:T(8,128)} collective-permute-done((f32[32,2816]{1,0:T(8,128)S(1)}, f32[32,2816]{1,0:T(8,128)}, u32[]{:S(2)}, u32[]{:S(2)}) %collective-permute-start.34) | collective-permute-done | bytes 360480 | tf_op jit(solution)/shard_map/ppermute | solution.py:30
  864.4 12.1 %collective-permute-done.44 = bf16[1,1,128,1024]{3,2,1,0:T(8,128)(2,1)S(1)} collective-permute-done((bf16[1,1,128,1024]{3,2,1,0:T(8,128)(2,1)S(1)}, bf16[1,1,128,1024]{3,2,1,0:T(8,128)(2,1)S(1)}, u32[]{:S(2)}, u32[]{:S(2)}) %collective-permute-start.44) | collective-permute-done | bytes 262176 | tf_op jit(solution)/shard_map/ppermute | solution.py:30
  (493 shorter events, 331.9 us)
Async XLA Ops:
  7.2 101.6 %all-gather.4.cloned.1.call-start = ((), (), s32[]{:S(2)}) async-start(), calls=%async_computation.8 | async-start | bytes 6488064 | tf_op jit(solution)/shard_map/all_gather | solution.py:882
  32.9 93.9 %collective-permute-start.13 = (f32[64,5632]{1,0:T(8,128)}, f32[64,5632]{1,0:T(8,128)}, u32[]{:S(2)}, u32[]{:S(2)}) collective-permute-start(f32[64,5632]{1,0:T(8,128)} %constant_dynamic-slice_fusion.4), channel_id=1, source_target_pairs={{0,8},{8,0},{16,24},{24,16},{1,9},{9,1},{17,25},{25,17},{2,10},{10... | collective-permute-start | bytes 4325384 | tf_op jit(solution)/shard_map/ppermute | solution.py:30
  62.2 68.2 %collective-permute-start.11 = (bf16[4,4,32,1024]{3,2,1,0:T(8,128)(2,1)}, bf16[4,4,32,1024]{3,2,1,0:T(8,128)(2,1)}, u32[]{:S(2)}, u32[]{:S(2)}) collective-permute-start(bf16[4,4,32,1024]{3,2,1,0:T(8,128)(2,1)} %bitcast.18), channel_id=1, source_target_pairs={{0,1},{1,0},{2,3},{3,2},{4,5},{5,4},{6,7},{7,6},{8,9},{9,8},{10,11... | collective-permute-start | bytes 3145736 | tf_op jit(solution)/shard_map/ppermute | solution.py:30
  91.0 46.9 %collective-permute-start.12 = (bf16[4,5,32,1024]{3,2,1,0:T(8,128)(2,1)}, bf16[4,5,32,1024]{3,2,1,0:T(8,128)(2,1)}, u32[]{:S(2)}, u32[]{:S(2)}) collective-permute-start(bf16[4,5,32,1024]{3,2,1,0:T(8,128)(2,1)} %bitcast.28), channel_id=1, source_target_pairs={{0,16},{8,24},{16,0},{24,8},{1,17},{9,25},{17,1},{25,9},{2,18},{10... | collective-permute-start | bytes 3932168 | tf_op jit(solution)/shard_map/ppermute | solution.py:30
  121.9 76.4 %all-to-all-start = ((bf16[8,512,384]{2,1,0:T(8,128)(2,1)}), bf16[8,512,384]{2,1,0:T(8,128)(2,1)}, u32[]{:S(2)}, u32[]{:S(2)}) async-start(bf16[8,512,384]{2,1,0:T(8,128)(2,1)} %copy-done.60), calls=%async_computation | async-start | bytes 6291456 | tf_op jit(solution)/shard_map/all_to_all | solution.py:922
  133.6 189.5 %collective-permute-start.23 = (bf16[4,2,4,32,1024]{4,3,2,1,0:T(8,128)(2,1)}, bf16[4,2,4,32,1024]{4,3,2,1,0:T(8,128)(2,1)}, u32[]{:S(2)}, u32[]{:S(2)}) collective-permute-start(bf16[4,2,4,32,1024]{4,3,2,1,0:T(8,128)(2,1)} %pad_maximum_fusion.2.refs_8_), channel_id=1, source_target_pairs={{0,8},{8,0},{16,24},{24,16},{1,9},{9,1},{17,25},{25,17},{2,10},{10... | collective-permute-start | bytes 6291464 | tf_op jit(solution)/shard_map/ppermute | solution.py:30
  133.6 182.4 %collective-permute-start.22 = (bf16[8,4,32,1024]{3,2,1,0:T(8,128)(2,1)}, bf16[8,4,32,1024]{3,2,1,0:T(8,128)(2,1)}, u32[]{:S(2)}, u32[]{:S(2)}) collective-permute-start(bf16[8,4,32,1024]{3,2,1,0:T(8,128)(2,1)} %bitcast.32), channel_id=1, source_target_pairs={{0,16},{8,24},{16,0},{24,8},{1,17},{9,25},{17,1},{25,9},{2,18},{10... | collective-permute-start | bytes 6291464 | tf_op jit(solution)/shard_map/ppermute | solution.py:30
  137.7 68.6 %collective-permute-start.20 = (bf16[4,2,5,32,1024]{4,3,2,0,1:T(8,128)(2,1)}, bf16[4,2,5,32,1024]{4,3,2,0,1:T(8,128)(2,1)}, u32[]{:S(2)}, u32[]{:S(2)}) collective-permute-start(bf16[4,2,5,32,1024]{4,3,2,0,1:T(8,128)(2,1)} %pad_maximum_fusion), channel_id=1, source_target_pairs={{0,8},{8,0},{16,24},{24,16},{1,9},{9,1},{17,25},{25,17},{2,10},{10... | collective-permute-start | bytes 7864328 | tf_op jit(solution)/shard_map/ppermute | solution.py:30
  138.0 64.7 %collective-permute-start.19 = (bf16[4,5,32,1024]{3,2,1,0:T(8,128)(2,1)}, bf16[4,5,32,1024]{3,2,1,0:T(8,128)(2,1)}, u32[]{:S(2)}, u32[]{:S(2)}) collective-permute-start(bf16[4,5,32,1024]{3,2,1,0:T(8,128)(2,1)} %collective-permute-done.12), channel_id=1, source_target_pairs={{0,1},{1,0},{2,3},{3,2},{4,5},{5,4},{6,7},{7,6},{8,9},{9,8},{10,11... | collective-permute-start | bytes 3932168 | tf_op jit(solution)/shard_map/ppermute | solution.py:30
  148.0 62.0 %collective-permute-start.15 = (f32[16,5632]{1,0:T(8,128)S(1)}, f32[16,5632]{1,0:T(8,128)}, u32[]{:S(2)}, u32[]{:S(2)}) collective-permute-start(f32[16,5632]{1,0:T(8,128)S(1)} %constant_dynamic-slice_fusion.2), channel_id=1, source_target_pairs={{0,1},{1,0},{2,3},{3,2},{4,5},{5,4},{6,7},{7,6},{8,9},{9,8},{10,11... | collective-permute-start | bytes 1081352 | tf_op jit(solution)/shard_map/ppermute | solution.py:30
  198.2 75.0 %all-to-all-start.1 = ((bf16[8,512,384]{2,1,0:T(8,128)(2,1)}), bf16[8,512,384]{2,1,0:T(8,128)(2,1)}, u32[]{:S(2)}, u32[]{:S(2)}) async-start(bf16[8,512,384]{2,1,0:T(8,128)(2,1)} %copy-done.61), calls=%async_computation.1 | async-start | bytes 6291456 | tf_op jit(solution)/shard_map/all_to_all | solution.py:922
  211.1 47.0 %collective-permute-start.16 = (f32[8,5632]{1,0:T(8,128)S(1)}, f32[8,5632]{1,0:T(8,128)S(1)}, u32[]{:S(2)}, u32[]{:S(2)}) collective-permute-start(f32[8,5632]{1,0:T(8,128)S(1)} %constant_dynamic-slice_fusion.1), channel_id=1, source_target_pairs={{0,2},{1,3},{2,0},{3,1},{4,6},{5,7},{6,4},{7,5},{8,10},{9,11},{10,... | collective-permute-start | bytes 540680 | tf_op jit(solution)/shard_map/ppermute | solution.py:30
  316.5 46.0 %all-to-all-start.3 = ((bf16[8,512,128]{2,1,0:T(8,128)(2,1)}), bf16[8,512,128]{2,1,0:T(8,128)(2,1)}, u32[]{:S(2)}, u32[]{:S(2)}) async-start(bf16[8,512,128]{2,1,0:T(8,128)(2,1)} %bitcast.191), calls=%async_computation.3 | async-start | bytes 2097152 | tf_op jit(solution)/shard_map/all_to_all | solution.py:922
  362.6 48.2 %all-to-all-start.4 = ((bf16[8,512,128]{2,1,0:T(8,128)(2,1)}), bf16[8,512,128]{2,1,0:T(8,128)(2,1)S(1)}, u32[]{:S(2)}, u32[]{:S(2)}) async-start(bf16[8,512,128]{2,1,0:T(8,128)(2,1)} %get-tuple-element.108), calls=%async_computation.4 | async-start | bytes 2097152 | tf_op jit(solution)/shard_map/all_to_all | solution.py:922
  410.8 65.6 %all-to-all-start.5 = ((bf16[8,512,128]{2,1,0:T(8,128)(2,1)}), bf16[8,512,128]{2,1,0:T(8,128)(2,1)S(1)}, u32[]{:S(2)}, u32[]{:S(2)}) async-start(bf16[8,512,128]{2,1,0:T(8,128)(2,1)} %get-tuple-element.109), calls=%async_computation.5 | async-start | bytes 2097152 | tf_op jit(solution)/shard_map/all_to_all | solution.py:922
  477.3 91.5 %all-to-all-start.7 = ((bf16[8,512,384]{2,1,0:T(8,128)(2,1)}), bf16[8,512,384]{2,1,0:T(8,128)(2,1)}, u32[]{:S(2)}, u32[]{:S(2)}) async-start(bf16[8,512,384]{2,1,0:T(8,128)(2,1)} %bitcast.185), calls=%async_computation.7 | async-start | bytes 6291456 | tf_op jit(solution)/shard_map/all_to_all | solution.py:922
  496.7 78.3 %collective-permute-start.25 = (bf16[4,512,1024]{2,1,0:T(8,128)(2,1)}, bf16[4,512,1024]{2,1,0:T(8,128)(2,1)}, u32[]{:S(2)}, u32[]{:S(2)}) collective-permute-start(bf16[4,512,1024]{2,1,0:T(8,128)(2,1)} %weight_part.10), channel_id=1, source_target_pairs={{0,8},{8,0},{16,24},{24,16},{1,9},{9,1},{17,25},{25,17},{2,10},{10... | collective-permute-start | bytes 12582920 | tf_op jit(solution)/shard_map/ppermute | solution.py:30
  509.3 77.1 %collective-permute-start.27 = (bf16[2,256,5120]{2,1,0:T(8,128)(2,1)}, bf16[2,256,5120]{2,1,0:T(8,128)(2,1)}, u32[]{:S(2)}, u32[]{:S(2)}) collective-permute-start(bf16[2,256,5120]{2,1,0:T(8,128)(2,1)} %weight_part.11), channel_id=1, source_target_pairs={{0,8},{8,0},{16,24},{24,16},{1,9},{9,1},{17,25},{25,17},{2,10},{10... | collective-permute-start | bytes 15728648 | tf_op jit(solution)/shard_map/ppermute | solution.py:30
  568.8 79.0 %all-to-all-start.6 = ((bf16[8,512,384]{2,1,0:T(8,128)(2,1)}), bf16[8,512,384]{2,1,0:T(8,128)(2,1)}, u32[]{:S(2)}, u32[]{:S(2)}) async-start(bf16[8,512,384]{2,1,0:T(8,128)(2,1)} %bitcast.184), calls=%async_computation.6 | async-start | bytes 6291456 | tf_op jit(solution)/shard_map/all_to_all | solution.py:922
  574.8 144.0 %all-gather.6.cloned.1.call-start = ((), (), s32[]{:S(2)}) async-start(), calls=%async_computation.9 | async-start | bytes 2973696 | tf_op jit(solution)/shard_map/all_gather | solution.py:990
  598.3 65.6 %collective-permute-start.28 = (bf16[1,256,5120]{2,1,0:T(8,128)(2,1)}, bf16[1,256,5120]{2,1,0:T(8,128)(2,1)}, u32[]{:S(2)}, u32[]{:S(2)}) collective-permute-start(bf16[1,256,5120]{2,1,0:T(8,128)(2,1)} %weight_part.13), channel_id=1, source_target_pairs={{0,16},{8,24},{16,0},{24,8},{1,17},{9,25},{17,1},{25,9},{2,18},{10... | collective-permute-start | bytes 7864328 | tf_op jit(solution)/shard_map/ppermute | solution.py:30
  599.8 64.2 %collective-permute-start.26 = (bf16[2,512,1024]{2,1,0:T(8,128)(2,1)}, bf16[2,512,1024]{2,1,0:T(8,128)(2,1)}, u32[]{:S(2)}, u32[]{:S(2)}) collective-permute-start(bf16[2,512,1024]{2,1,0:T(8,128)(2,1)} %weight_part.12), channel_id=1, source_target_pairs={{0,1},{1,0},{2,3},{3,2},{4,5},{5,4},{6,7},{7,6},{8,9},{9,8},{10,11... | collective-permute-start | bytes 6291464 | tf_op jit(solution)/shard_map/ppermute | solution.py:30
  771.0 48.0 %collective-permute-start.36 = (bf16[2,2,1,32,3072]{4,3,2,1,0:T(8,128)(2,1)}, bf16[2,2,1,32,3072]{4,3,2,1,0:T(8,128)(2,1)}, u32[]{:S(2)}, u32[]{:S(2)}) collective-permute-start(bf16[2,2,1,32,3072]{4,3,2,1,0:T(8,128)(2,1)} %dynamic-slice_convert_fusion.1), channel_id=1, source_target_pairs={{0,1},{1,0},{2,3},{3,2},{4,5},{5,4},{6,7},{7,6},{8,9},{9,8},{10,11... | collective-permute-start | bytes 2359304 | tf_op jit(solution)/shard_map/ppermute | solution.py:30
  784.0 51.5 %collective-permute-start.42 = (bf16[1,512,1024]{2,1,0:T(8,128)(2,1)}, bf16[1,512,1024]{2,1,0:T(8,128)(2,1)S(1)}, u32[]{:S(2)}, u32[]{:S(2)}) collective-permute-start(bf16[1,512,1024]{2,1,0:T(8,128)(2,1)} %weight_part.18), channel_id=1, source_target_pairs={{0,16},{8,24},{16,0},{24,8},{1,17},{9,25},{17,1},{25,9},{2,18},{10... | collective-permute-start | bytes 3145736 | tf_op jit(solution)/shard_map/ppermute | solution.py:30
  (140 other events, 2161.1 us)
Sparse Core Ops, SparseCore 0:
  11.0 97.8 all-gather.3
  602.8 86.0 all-gather.5

commit v6 on v5

--- a/solution.py
+++ b/solution.py
@@ -51,14 +51,17 @@
     return axis_bits("clip") + axis_bits("seq")
 
 
-def halve_sum(parts, bits, wire=f32):
+def halve_sum(parts, bits, wire=f32, hold=None):
     addends = [parts.reshape((2,) * len(bits) + parts.shape[1:])]
     for place in exchange_order(bits):
         axis, bit = bits[place]
         mine = own_bit(axis, bit)
         send = sum(lax.dynamic_index_in_dim(a, 1 - mine, place).astype(f32) for a in addends)
         addends = [lax.dynamic_index_in_dim(a, mine, place) for a in addends]
-        addends.append(swap_bit(send.astype(wire), axis, bit))
+        received = swap_bit(send.astype(wire), axis, bit)
+        if hold is not None and len(addends) == 1:
+            received = after(received, hold)
+        addends.append(received)
     total = sum(a.astype(f32) for a in addends)
     return total.reshape(total.shape[len(bits) :])
 
@@ -561,7 +564,7 @@
             scratch_shapes=[pltpu.VMEM((count, height, clips * rows), bf16)],
         ),
         out_shape=jax.ShapeDtypeStruct((count, height, columns), kind),
-        compiler_params=pltpu.CompilerParams(vmem_limit_bytes=32 << 20),
+        compiler_params=pltpu.CompilerParams(vmem_limit_bytes=60 << 20),
         cost_estimate=pl.CostEstimate(
             flops=2 * count * clips * rows * height * columns,
             bytes_accessed=clips * rows * (count * height + columns) * 2 + 4 * count * height * columns,
@@ -597,8 +600,8 @@
     return weight_part(pairs, mine_on("clip")[None], addends, f32, height_of(pairs, 4))
 
 
-def along_seq(total):
-    return halve_sum(total.reshape((lax.axis_size("seq"), -1, total.shape[2])), axis_bits("seq"), bf16)
+def along_seq(total, hold=None):
+    return halve_sum(total.reshape((lax.axis_size("seq"), -1, total.shape[2])), axis_bits("seq"), bf16, hold)
 
 
 def along_block(clip_flip, low_flip):
@@ -619,11 +622,14 @@
     return weight_part(pairs, along_block(2, 0)[None], ((core, 3), (along, 1)), bf16, height_of(pairs, 8))
 
 
-def along_total(pairs, core, along, across):
+def along_own(pairs, core, along, across):
     addends = ((core, 2), (along, 0), (across, 0))
-    total = weight_part(pairs, along_block(0, 0)[None], addends, f32, height_of(pairs, 8))
+    return weight_part(pairs, along_block(0, 0)[None], addends, f32, height_of(pairs, 8))
+
+
+def along_high(total, hold=None):
     bits = axis_bits("seq")[:-1]
-    return halve_sum(total.reshape((2 ** len(bits), -1, total.shape[2])), bits, bf16)
+    return halve_sum(total.reshape((2 ** len(bits), -1, total.shape[2])), bits, bf16, hold)
 
 
 def attend_kernel(qkv_ref, mix_ref, full_ref, log_ref, vt_ref, *, total, span, block):
@@ -992,42 +998,48 @@
     d_qkv, exchanged = [], []
     for c in range(clips):
         if c == clips - 1:
-            active = gate(active, *d_qkv)
-            down_first = along_first([(active, d_mlp)])
+            active = gate(active, *d_qkv, d_mixed[-1])
+            down_pairs, up_pairs = [(active, d_mlp)], [(normed_two, d_hidden), (mixed_all, d_attn)]
+            down_first = along_first(down_pairs)
             down_core = swap_bit(down_first, "clip", 1)
-            normed_two = gate(normed_two, down_first)
-            up_first = across_first([(normed_two, d_hidden), (mixed_all, d_attn)])
+            up_pairs[0] = (gate(normed_two, down_first), d_hidden)
+            up_first = across_first(up_pairs)
             up_core = swap_bit(up_first, "clip", 1)
-        grad = after(d_mixed[c], results[-1][8] if c == 0 else up_first)
+            down_pairs = [(active, gate(d_mlp, up_first))]
+            down_second = along_second(down_pairs, down_core)
+            down_along = swap_bit(down_second, "seq", 1)
+            up_pairs[0] = (normed_two, gate(d_hidden, down_second))
+            up_second = across_second(up_pairs, up_core)
+            up_across = swap_bit(up_second, "clip", 2)
+        grad = after(d_mixed[c], results[-1][8] if c == 0 else up_second)
         grad = grad.reshape(total, span)
         d_qkv.append(attend_back(qkv[c].reshape(total, 3 * span), grad, fulls[c], logs[c], cos_all, sin_all, span))
         sent = d_qkv[c].reshape(seq_devices, rows, 3 * span)
-        exchanged.append(exchange(after(sent, d_mixed[-1]) if c == 0 else sent))
-
-    d_mlp = gate(d_mlp, exchanged[0])
-    down_second = along_second([(active, d_mlp)], down_core)
-    d_hidden = gate(d_hidden, down_second)
-    up_second = across_second([(normed_two, d_hidden), (mixed_all, d_attn)], up_core)
-    down_along, up_across = swap_bit(down_second, "seq", 1), swap_bit(up_second, "clip", 2)
-    exchanged[0] = after(exchanged[0], up_second)
-    exchanged[-1] = after(exchanged[-1], down_along, up_across)
+        exchanged.append(exchange(after(sent, d_mixed[-1]) if c == 0 else after(sent, down_along, up_across)))
+
+    down_pairs = [(active, gate(d_mlp, exchanged[0]))]
+    down_third = along_third(down_pairs, down_core, down_along)
+    down_across = swap_bit(down_third, "clip", 2)
+    exchanged[0] = after(exchanged[0], down_third)
 
     last = []
     for c in range(clips):
         grads = last[-1][0] if last else None
+        if c == clips - 1:
+            up_pairs[0] = (normed_two, gate(d_hidden, last[0][1]))
+            up_total = across_own(up_pairs, up_core, up_across)
+            down_pairs = [(active, gate(d_mlp, up_total))]
+            down_total = along_own(down_pairs, down_core, down_along, down_across)
+            exchanged[-1] = after(exchanged[-1], down_total)
         last.append(project_back(exchanged[c], full_qkv, tokens, c, mods_one[c][1], results[c][1], grads))
     d_projected = [r[1] for r in last]
     qkv_pairs = [(normed, d_projected)]
     qkv_core = swap_bit(across_first(qkv_pairs), "clip", 1)
     qkv_second = across_second(qkv_pairs, qkv_core)
     qkv_across = swap_bit(qkv_second, "clip", 2)
-    d_hidden = gate(d_hidden, qkv_second)
-    up_total = across_own([(normed_two, d_hidden), (mixed_all, d_attn)], up_core, up_across)
     qkv_total = across_own(qkv_pairs, qkv_core, qkv_across)
-    d_mlp = gate(d_mlp, qkv_total)
-    down_across = swap_bit(along_third([(active, d_mlp)], down_core, down_along), "clip", 2)
-    grad_up, grad_qkv = along_seq(up_total), along_seq(qkv_total)
-    grad_down = along_total([(active, d_mlp)], down_core, down_along, down_across)
+    grad_up, grad_down = along_seq(up_total, qkv_second), along_high(down_total, qkv_second)
+    grad_qkv = along_seq(qkv_total)
     grad_out = grad_up[:, 4 * width :]
     grad_up = grad_up[:, : 4 * width].reshape((-1,) + near_owners).transpose(0, 1, 3, 2, 4).reshape(-1, 4 * width)
     late_rows = with_bias([line_sums(r[2]) for r in last], [sum(r[3][0] for r in last)])

time: 896 us -> 855 us (0.954)
  waiting for transfers between devices: 246 us -> 216 us
  local copies, waits for them, and re-layouts: 99.8 us -> 76.2 us
  Pallas kernels: 371 us -> 390 us
    ppermute x45, waiting for transfers between devices: 150 us -> 114 us  [swap_bit(): return lax.ppermute(value, axis, [(i, i ^ bit) for i in range(count)])]
    unnamed x220 -> x114, local copies, waits for them, and re-layouts: 52 us -> 23.8 us
    pallas_call x10, Pallas kernels: 73.3 us -> 92.5 us  [weight_part(): pl.pallas_call(functools.partial(weight_part_kernel, clips=clips, count=c...]
  transfers between devices with their start and end apart: 55 -> 55, of which waited for: 20 -> 21; matrix products, arithmetic and copies ran while one was open for 11% -> 11% of each run, Pallas kernels for 42% -> 43%
where the time goes in v6:
time: 855 us; the launch traced here: 843 us
  Pallas kernels  390 us (46%)
  waiting for transfers between devices  216 us (25%)
  starting transfers between devices  92 us (11%)
  local copies, waits for them, and re-layouts  76.2 us (9%)
  other arithmetic  50.1 us (6%)
  between operations  15.9 us (2%)
    pallas_call x2, Pallas kernels, attend_back(): pl.pallas_call(functools.partial(attend_back_kernel, total=total, span=sp...  118 us
    ppermute x45, waiting for transfers between devices, swap_bit(): return lax.ppermute(value, axis, [(i, i ^ bit) for i in range(count)])  114 us
    pallas_call x10, Pallas kernels, weight_part(): pl.pallas_call(functools.partial(weight_part_kernel, clips=clips, count=c...  92.5 us
    all_to_all x8, waiting for transfers between devices, exchange(): return lax.all_to_all(value, 'seq', 0, 0, tiled=True)  86.8 us
    pallas_call x2, Pallas kernels, middle(): pl.pallas_call(middle_kernel, grid_spec=pltpu.PrefetchScalarGridSpec(num_...  76.5 us
    pallas_call x2, Pallas kernels, attend(): pl.pallas_call(functools.partial(attend_kernel, total=total, span=span, b...  70.5 us
    ppermute x45, starting transfers between devices, swap_bit(): return lax.ppermute(value, axis, [(i, i ^ bit) for i in range(count)])  50.3 us
    all_to_all x8, starting transfers between devices, exchange(): return lax.all_to_all(value, 'seq', 0, 0, tiled=True)  41.6 us
  transfers between devices with their start and end apart: 55, of which 21 were waited for; matrix products, arithmetic and copies ran while one was open for 11% of the time, Pallas kernels for 43%

profile of v6, /device:TPU:0, one launch (start us, length us, event | category | flops | bytes accessed | tf_op | source)
XLA Modules:
  0.0 843.3 jit_solution(3580695067674652954)
XLA Ops:
  50.5 9.5 %collective-permute-done.8 = bf16[2,4,32,1024]{3,2,1,0:T(8,128)(2,1)S(1)} collective-permute-done((bf16[2,4,32,1024]{3,2,1,0:T(8,128)(2,1)S(1)}, bf16[2,4,32,1024]{3,2,1,0:T(8,128)(2,1)S(1)}, u32[]{:S(2)}, u32[]{:S(2)}) %collective-permute-start.8) | collective-permute-done | bytes 524320 | tf_op jit(solution)/shard_map/ppermute | solution.py:30
  63.0 18.2 %collective-permute-done.10 = bf16[2,5,32,1024]{3,2,1,0:T(8,128)(2,1)S(1)} collective-permute-done((bf16[2,5,32,1024]{3,2,1,0:T(8,128)(2,1)S(1)}, bf16[2,5,32,1024]{3,2,1,0:T(8,128)(2,1)S(1)}, u32[]{:S(2)}, u32[]{:S(2)}) %collective-permute-start.10) | collective-permute-done | bytes 655392 | tf_op jit(solution)/shard_map/ppermute | solution.py:30
  95.0 14.9 %all-gather.4.cloned.1.call-done.wq_ref.wk_ref.wv_ref = bf16[1024,3072]{1,0:T(8,128)(2,1)} async-done(((bf16[32,3072]{1,0:T(8,128)(2,1)}), bf16[1024,3072]{1,0:T(8,128)(2,1)}) %all-gather.4.cloned.1.call-update) | async-done | bytes 6291472 | tf_op jit(solution)/shard_map/all_gather | solution.py:888
  139.7 7.9 collective-permute-done.14
  162.6 35.3 %all-to-all-done = bf16[8,512,384]{2,1,0:T(8,128)(2,1)} async-done(((bf16[8,512,384]{2,1,0:T(8,128)(2,1)}), bf16[8,512,384]{2,1,0:T(8,128)(2,1)}, u32[]{:S(2)}, u32[]{:S(2)}) %all-to-all-start) | async-done | bytes 3145760 | tf_op jit(solution)/shard_map/all_to_all | solution.py:928
  212.3 35.3 %attend.3 = (bf16[4096,128]{1,0:T(8,128)(2,1)}, f32[4096,128]{1,0:T(8,128)}, f32[2,4096]{1,0:T(2,128)}) custom-call(bf16[4096,384]{1,0:T(8,128)(2,1)} %bitcast.36.qkv_ref), custom_call_target="tpu_custom_call" | custom-call | flops 17179869184 | bytes 6291456 | tf_op jit(solution)/shard_map/attend/pallas_call | solution.py:693
  247.6 10.2 %collective-permute-done.16 = f32[8,5632]{1,0:T(8,128)S(1)} collective-permute-done((f32[8,5632]{1,0:T(8,128)S(1)}, f32[8,5632]{1,0:T(8,128)S(1)}, u32[]{:S(2)}, u32[]{:S(2)}) %collective-permute-start.16) | collective-permute-done | bytes 180256 | tf_op jit(solution)/shard_map/ppermute | solution.py:30
  257.8 15.2 %all-to-all-done.1 = bf16[8,512,384]{2,1,0:T(8,128)(2,1)} async-done(((bf16[8,512,384]{2,1,0:T(8,128)(2,1)}), bf16[8,512,384]{2,1,0:T(8,128)(2,1)}, u32[]{:S(2)}, u32[]{:S(2)}) %all-to-all-start.1) | async-done | bytes 3145760 | tf_op jit(solution)/shard_map/all_to_all | solution.py:928
  280.6 35.3 %attend.2 = (bf16[4096,128]{1,0:T(8,128)(2,1)}, f32[4096,128]{1,0:T(8,128)}, f32[2,4096]{1,0:T(2,128)}) custom-call(bf16[4096,384]{1,0:T(8,128)(2,1)} %bitcast.34.qkv_ref), custom_call_target="tpu_custom_call" | custom-call | flops 17179869184 | bytes 6291456 | tf_op jit(solution)/shard_map/attend/pallas_call | solution.py:693
  323.0 38.3 %middle.2 = (bf16[2,512,1024]{2,1,0:T(8,128)(2,1)}, f32[512,1024]{1,0:T(8,128)}, bf16[512,1024]{1,0:T(8,128)(2,1)}, bf16[512,1024]{1,0:T(8,128)(2,1)}, bf16[512,...) custom-call(s32[1]{0:T(128)} %bitcast.clip_ref.index_ref, ...), custom_call_target="tpu_custom_call" | custom-call | flops 2147483648 | bytes 4718592 | tf_op jit(solution)/shard_map/middle/pallas_call | solution.py:446
  372.4 38.2 %middle.3 = (bf16[2,512,1024]{2,1,0:T(8,128)(2,1)}, f32[512,1024]{1,0:T(8,128)}, bf16[512,1024]{1,0:T(8,128)(2,1)}, bf16[512,1024]{1,0:T(8,128)(2,1)}, bf16[512,...) custom-call(s32[1]{0:T(128)} %bitcast.clip_ref.index_ref, ...), custom_call_target="tpu_custom_call", output_to_operand_aliasing={{0}: (20, {})} | custom-call | flops 2147483648 | bytes 4718592 | tf_op jit(solution)/shard_map/middle/pallas_call | solution.py:446
  417.1 59.1 %attend_back.2 = bf16[4096,384]{1,0:T(8,128)(2,1)} custom-call(bf16[4096,384]{1,0:T(8,128)(2,1)} %bitcast.36.qkv_ref, bf16[4096,128]{1,0:T(8,128)(2,1)} %bitcast.191, f32[4096,128]{1,0:T(8,128)} %get-tuple-element.122.full_ref, f32[2,4096]{1,0:T(2,128)} %get-tuple-element.123.log_ref, f32[4096,128]{1,0:T(8,128)} %bitcast.188, f32[4096,128]{1,0:T(8,128)} %bitcast.186), custom_call_target="tpu_custom_call" | custom-call | flops 42949672960 | bytes 13631488 | tf_op jit(solution)/shard_map/attend_back/pallas_call | solution.py:788
  476.2 10.5 %weight_part.10 = bf16[4,512,1024]{2,1,0:T(8,128)(2,1)} custom-call(s32[4]{0:T(128)} %pad_add_fusion.7.index_ref, bf16[512,4096]{1,0:T(8,128)(2,1)} %get-tuple-element.124.refs_0_.refs_1_.refs_2_.refs_3_, bf16[512,4096]{1,0:T(8,128)(2,1)} %get-tuple-element.124.refs_0_.refs_1_.refs_2_.refs_3_, ...), custom_call_target="tpu_custom_call" | custom-call | flops 4294967296 | bytes 14680064 | tf_op jit(solution)/shard_map/weight_part/pallas_call | solution.py:557
  486.8 14.5 %weight_part.11 = bf16[2,256,5120]{2,1,0:T(8,128)(2,1)} custom-call(s32[2]{0:T(128)} %pad_add_fusion.6.index_ref, bf16[512,1024]{1,0:T(8,128)(2,1)} %get-tuple-element.128.refs_0_.refs_1_, bf16[512,1024]{1,0:T(8,128)(2,1)} %get-tuple-element.128.refs_0_.refs_1_, bf16[512,1024]{1,0:T(8,128)(2,1)} %get-tuple-element.129.refs_2_.refs_3_.refs_1_, ...), custom_call_target="tpu_custom_call" | custom-call | flops 5368709120 | bytes 22020096 | tf_op jit(solution)/shard_map/weight_part/pallas_call | solution.py:557
  525.6 11.7 %weight_part.13 = bf16[1,256,5120]{2,1,0:T(8,128)(2,1)} custom-call(s32[1]{0:T(128)} %bitcast.50.index_ref, bf16[512,1024]{1,0:T(8,128)(2,1)} %get-tuple-element.128.refs_0_.refs_1_, bf16[512,1024]{1,0:T(8,128)(2,1)} %get-tuple-element.129.refs_2_.refs_3_.refs_1_, bf16[512,4096]{1,0:T(8,128)(2,1)} %get-tuple-element.148.refs_4_.refs_2_, ...), custom_call_target="tpu_custom_call" | custom-call | flops 2684354560 | bytes 16252928 | tf_op jit(solution)/shard_map/weight_part/pallas_call | solution.py:557
  538.8 59.3 %attend_back.3 = bf16[4096,384]{1,0:T(8,128)(2,1)} custom-call(bf16[4096,384]{1,0:T(8,128)(2,1)} %bitcast.34.qkv_ref, bf16[4096,128]{1,0:T(8,128)(2,1)} %bitcast.193, f32[4096,128]{1,0:T(8,128)} %get-tuple-element.139.full_ref, f32[2,4096]{1,0:T(2,128)} %get-tuple-element.140.log_ref, f32[4096,128]{1,0:T(8,128)} %bitcast.189, f32[4096,128]{1,0:T(8,128)} %bitcast.187), custom_call_target="tpu_custom_call" | custom-call | flops 42949672960 | bytes 13631488 | tf_op jit(solution)/shard_map/attend_back/pallas_call | solution.py:788
  614.2 9.2 %project_back.2 = (f32[2,512,1024]{2,1,0:T(8,128)}, bf16[512,3072]{1,0:T(8,128)(2,1)S(1)}, f32[2,2,1024]{2,1,0:T(2,128)S(1)}, f32[1,3072]{1,0:T(1,128)S(1)}) custom-call(bf16[8,512,384]{2,1,0:T(8,128)(2,1)S(1)} %copy-done.8, bf16[1024,3072]{1,0:T(8,128)(2,1)} %all-gather.4.cloned.1.call-done.wq_ref.wk_ref.wv_ref, ...), custom_call_target="tpu_custom_call" | custom-call | flops 3221225472 | bytes 17825792 | tf_op jit(solution)/shard_map/project_back/pallas_call | solution.py:263
  625.2 13.0 %weight_part.15 = f32[1,256,5120]{2,1,0:T(8,128)} custom-call(s32[1]{0:T(128)} %bitcast.clip_ref.index_ref, bf16[512,1024]{1,0:T(8,128)(2,1)} %get-tuple-element.128.refs_0_.refs_1_, bf16[512,1024]{1,0:T(8,128)(2,1)} %get-tuple-element.129.refs_2_.refs_3_.refs_1_, bf16[512,4096]{1,0:T(8,128)(2,1)} %get-tuple-element.148.refs_4_.refs_2_, ...), custom_call_target="tpu_custom_call" | custom-call | flops 2684354560 | bytes 16252928 | tf_op jit(solution)/shard_map/weight_part/pallas_call | solution.py:557
  644.5 36.3 %all-to-all-done.6.back_ref = bf16[8,512,384]{2,1,0:T(8,128)(2,1)} async-done(((bf16[8,512,384]{2,1,0:T(8,128)(2,1)}), bf16[8,512,384]{2,1,0:T(8,128)(2,1)}, u32[]{:S(2)}, u32[]{:S(2)}) %all-to-all-start.6) | async-done | bytes 3145760 | tf_op jit(solution)/shard_map/all_to_all | solution.py:928
  682.4 9.8 %project_back.3 = (f32[2,512,1024]{2,1,0:T(8,128)}, bf16[512,3072]{1,0:T(8,128)(2,1)S(1)}, f32[2,2,1024]{2,1,0:T(2,128)S(1)}, f32[1,3072]{1,0:T(1,128)S(1)}) custom-call(bf16[8,512,384]{2,1,0:T(8,128)(2,1)} %all-to-all-done.6.back_ref, bf16[1024,3072]{1,0:T(8,128)(2,1)} %all-gather.4.cloned.1.call-done.wq_ref.wk_ref.wv_ref, ...), custom_call_target="tpu_custom_call", output_to_operand_aliasing={{0}: (7, {})} | custom-call | flops 3221225472 | bytes 17825792 | tf_op jit(solution)/shard_map/project_back/pallas_call | solution.py:263
  693.9 9.4 %weight_part.17 = bf16[2,256,3072]{2,1,0:T(8,128)(2,1)} custom-call(s32[2]{0:T(128)} %pad_add_fusion.6.index_ref, bf16[512,1024]{1,0:T(8,128)(2,1)} %copy-done.5, bf16[512,1024]{1,0:T(8,128)(2,1)} %copy-done.5, bf16[512,1024]{1,0:T(8,128)(2,1)} %copy-done.6, bf16[512,1024]{1,0:T(8,128)(2,1)} %copy-done.6, bf16[512,3072]{1,0:T(8,128)(2,1)} %copy-done.3, ...), custom_call_target="tpu_custom_call" | custom-call | flops 3221225472 | bytes 13631488 | tf_op jit(solution)/shard_map/weight_part/pallas_call | solution.py:557
  726.3 12.1 %collective-permute-done.40 = bf16[2,2,1,32,5120]{4,3,2,1,0:T(8,128)(2,1)} collective-permute-done((bf16[2,2,1,32,5120]{4,3,2,1,0:T(8,128)(2,1)}, bf16[2,2,1,32,5120]{4,3,2,1,0:T(8,128)(2,1)}, u32[]{:S(2)}, u32[]{:S(2)}) %collective-permute-start.40) | collective-permute-done | bytes 1310752 | tf_op jit(solution)/shard_map/ppermute | solution.py:30
  744.2 15.5 %collective-permute-done.44 = bf16[1,1,128,1024]{3,2,1,0:T(8,128)(2,1)S(1)} collective-permute-done((bf16[1,1,128,1024]{3,2,1,0:T(8,128)(2,1)S(1)}, bf16[1,1,128,1024]{3,2,1,0:T(8,128)(2,1)S(1)}, u32[]{:S(2)}, u32[]{:S(2)}) %collective-permute-start.44) | collective-permute-done | bytes 262176 | tf_op jit(solution)/shard_map/ppermute | solution.py:30
  767.6 8.1 weight_part.19
  (387 shorter events, 300.6 us)
Async XLA Ops:
  7.2 102.7 %all-gather.4.cloned.1.call-start = ((), (), s32[]{:S(2)}) async-start(), calls=%async_computation.8 | async-start | bytes 6488064 | tf_op jit(solution)/shard_map/all_gather | solution.py:888
  31.7 94.8 %collective-permute-start.13 = (f32[64,5632]{1,0:T(8,128)}, f32[64,5632]{1,0:T(8,128)}, u32[]{:S(2)}, u32[]{:S(2)}) collective-permute-start(f32[64,5632]{1,0:T(8,128)} %constant_dynamic-slice_fusion.4), channel_id=1, source_target_pairs={{0,8},{8,0},{16,24},{24,16},{1,9},{9,1},{17,25},{25,17},{2,10},{10... | collective-permute-start | bytes 4325384 | tf_op jit(solution)/shard_map/ppermute | solution.py:30
  61.1 69.0 %collective-permute-start.11 = (bf16[4,4,32,1024]{3,2,1,0:T(8,128)(2,1)}, bf16[4,4,32,1024]{3,2,1,0:T(8,128)(2,1)}, u32[]{:S(2)}, u32[]{:S(2)}) collective-permute-start(bf16[4,4,32,1024]{3,2,1,0:T(8,128)(2,1)} %bitcast.18), channel_id=1, source_target_pairs={{0,1},{1,0},{2,3},{3,2},{4,5},{5,4},{6,7},{7,6},{8,9},{9,8},{10,11... | collective-permute-start | bytes 3145736 | tf_op jit(solution)/shard_map/ppermute | solution.py:30
  91.1 46.7 %collective-permute-start.12 = (bf16[4,5,32,1024]{3,2,1,0:T(8,128)(2,1)}, bf16[4,5,32,1024]{3,2,1,0:T(8,128)(2,1)}, u32[]{:S(2)}, u32[]{:S(2)}) collective-permute-start(bf16[4,5,32,1024]{3,2,1,0:T(8,128)(2,1)} %bitcast.28), channel_id=1, source_target_pairs={{0,16},{8,24},{16,0},{24,8},{1,17},{9,25},{17,1},{25,9},{2,18},{10... | collective-permute-start | bytes 3932168 | tf_op jit(solution)/shard_map/ppermute | solution.py:30
  92.5 41.4 %collective-permute-start.18 = (bf16[4,5,32,1024]{3,2,1,0:T(8,128)(2,1)}, bf16[4,5,32,1024]{3,2,1,0:T(8,128)(2,1)}, u32[]{:S(2)}, u32[]{:S(2)}) collective-permute-start(bf16[4,5,32,1024]{3,2,1,0:T(8,128)(2,1)} %bitcast.28), channel_id=1, source_target_pairs={{0,1},{1,0},{2,3},{3,2},{4,5},{5,4},{6,7},{7,6},{8,9},{9,8},{10,11... | collective-permute-start | bytes 3932168 | tf_op jit(solution)/shard_map/ppermute | solution.py:30
  121.9 76.1 %all-to-all-start = ((bf16[8,512,384]{2,1,0:T(8,128)(2,1)}), bf16[8,512,384]{2,1,0:T(8,128)(2,1)}, u32[]{:S(2)}, u32[]{:S(2)}) async-start(bf16[8,512,384]{2,1,0:T(8,128)(2,1)} %copy-done.9), calls=%async_computation | async-start | bytes 6291456 | tf_op jit(solution)/shard_map/all_to_all | solution.py:928
  133.3 189.7 %collective-permute-start.23 = (bf16[4,2,4,32,1024]{4,3,2,1,0:T(8,128)(2,1)}, bf16[4,2,4,32,1024]{4,3,2,1,0:T(8,128)(2,1)}, u32[]{:S(2)}, u32[]{:S(2)}) collective-permute-start(bf16[4,2,4,32,1024]{4,3,2,1,0:T(8,128)(2,1)} %pad_maximum_fusion.2.refs_8_), channel_id=1, source_target_pairs={{0,8},{8,0},{16,24},{24,16},{1,9},{9,1},{17,25},{25,17},{2,10},{10... | collective-permute-start | bytes 6291464 | tf_op jit(solution)/shard_map/ppermute | solution.py:30
  133.4 182.6 %collective-permute-start.22 = (bf16[8,4,32,1024]{3,2,1,0:T(8,128)(2,1)}, bf16[8,4,32,1024]{3,2,1,0:T(8,128)(2,1)}, u32[]{:S(2)}, u32[]{:S(2)}) collective-permute-start(bf16[8,4,32,1024]{3,2,1,0:T(8,128)(2,1)} %bitcast.32), channel_id=1, source_target_pairs={{0,16},{8,24},{16,0},{24,8},{1,17},{9,25},{17,1},{25,9},{2,18},{10... | collective-permute-start | bytes 6291464 | tf_op jit(solution)/shard_map/ppermute | solution.py:30
  137.5 67.1 %collective-permute-start.20 = (bf16[4,2,5,32,1024]{4,3,2,0,1:T(8,128)(2,1)}, bf16[4,2,5,32,1024]{4,3,2,0,1:T(8,128)(2,1)}, u32[]{:S(2)}, u32[]{:S(2)}) collective-permute-start(bf16[4,2,5,32,1024]{4,3,2,0,1:T(8,128)(2,1)} %pad_maximum_fusion), channel_id=1, source_target_pairs={{0,8},{8,0},{16,24},{24,16},{1,9},{9,1},{17,25},{25,17},{2,10},{10... | collective-permute-start | bytes 7864328 | tf_op jit(solution)/shard_map/ppermute | solution.py:30
  137.7 64.7 %collective-permute-start.19 = (bf16[4,5,32,1024]{3,2,1,0:T(8,128)(2,1)}, bf16[4,5,32,1024]{3,2,1,0:T(8,128)(2,1)}, u32[]{:S(2)}, u32[]{:S(2)}) collective-permute-start(bf16[4,5,32,1024]{3,2,1,0:T(8,128)(2,1)} %collective-permute-done.12), channel_id=1, source_target_pairs={{0,1},{1,0},{2,3},{3,2},{4,5},{5,4},{6,7},{7,6},{8,9},{9,8},{10,11... | collective-permute-start | bytes 3932168 | tf_op jit(solution)/shard_map/ppermute | solution.py:30
  147.7 61.6 %collective-permute-start.15 = (f32[16,5632]{1,0:T(8,128)S(1)}, f32[16,5632]{1,0:T(8,128)}, u32[]{:S(2)}, u32[]{:S(2)}) collective-permute-start(f32[16,5632]{1,0:T(8,128)S(1)} %constant_dynamic-slice_fusion.2), channel_id=1, source_target_pairs={{0,1},{1,0},{2,3},{3,2},{4,5},{5,4},{6,7},{7,6},{8,9},{9,8},{10,11... | collective-permute-start | bytes 1081352 | tf_op jit(solution)/shard_map/ppermute | solution.py:30
  198.0 75.0 %all-to-all-start.1 = ((bf16[8,512,384]{2,1,0:T(8,128)(2,1)}), bf16[8,512,384]{2,1,0:T(8,128)(2,1)}, u32[]{:S(2)}, u32[]{:S(2)}) async-start(bf16[8,512,384]{2,1,0:T(8,128)(2,1)} %copy-done.10), calls=%async_computation.1 | async-start | bytes 6291456 | tf_op jit(solution)/shard_map/all_to_all | solution.py:928
  210.4 47.4 %collective-permute-start.16 = (f32[8,5632]{1,0:T(8,128)S(1)}, f32[8,5632]{1,0:T(8,128)S(1)}, u32[]{:S(2)}, u32[]{:S(2)}) collective-permute-start(f32[8,5632]{1,0:T(8,128)S(1)} %constant_dynamic-slice_fusion.1), channel_id=1, source_target_pairs={{0,2},{1,3},{2,0},{3,1},{4,6},{5,7},{6,4},{7,5},{8,10},{9,11},{10,... | collective-permute-start | bytes 540680 | tf_op jit(solution)/shard_map/ppermute | solution.py:30
  273.0 43.5 %all-to-all-start.2 = ((bf16[8,512,128]{2,1,0:T(8,128)(2,1)}), bf16[8,512,128]{2,1,0:T(8,128)(2,1)}, u32[]{:S(2)}, u32[]{:S(2)}) async-start(bf16[8,512,128]{2,1,0:T(8,128)(2,1)} %bitcast.194), calls=%async_computation.2 | async-start | bytes 2097152 | tf_op jit(solution)/shard_map/all_to_all | solution.py:928
  280.6 42.4 %collective-permute-start.21 = (bf16[4,2,5,32,1024]{4,3,2,1,0:T(8,128)(2,1)S(1)}, bf16[4,2,5,32,1024]{4,3,2,1,0:T(8,128)(2,1)}, u32[]{:S(2)}, u32[]{:S(2)}) collective-permute-start(bf16[4,2,5,32,1024]{4,3,2,1,0:T(8,128)(2,1)S(1)} %pad_maximum_fusion.1.refs_1_.refs_5_), channel_id=1, source_target_pairs={{0,8},{8,0},{16,24},{24,16},{1,9},{9,1},{17,25},{25,17},{2,10},{10... | collective-permute-start | bytes 7864328 | tf_op jit(solution)/shard_map/ppermute | solution.py:30
  316.5 44.8 %all-to-all-start.3 = ((bf16[8,512,128]{2,1,0:T(8,128)(2,1)}), bf16[8,512,128]{2,1,0:T(8,128)(2,1)}, u32[]{:S(2)}, u32[]{:S(2)}) async-start(bf16[8,512,128]{2,1,0:T(8,128)(2,1)} %bitcast.192), calls=%async_computation.3 | async-start | bytes 2097152 | tf_op jit(solution)/shard_map/all_to_all | solution.py:928
  361.3 49.3 %all-to-all-start.4 = ((bf16[8,512,128]{2,1,0:T(8,128)(2,1)}), bf16[8,512,128]{2,1,0:T(8,128)(2,1)S(1)}, u32[]{:S(2)}, u32[]{:S(2)}) async-start(bf16[8,512,128]{2,1,0:T(8,128)(2,1)} %get-tuple-element.113), calls=%async_computation.4 | async-start | bytes 2097152 | tf_op jit(solution)/shard_map/all_to_all | solution.py:928
  410.6 65.6 %all-to-all-start.5 = ((bf16[8,512,128]{2,1,0:T(8,128)(2,1)}), bf16[8,512,128]{2,1,0:T(8,128)(2,1)S(1)}, u32[]{:S(2)}, u32[]{:S(2)}) async-start(bf16[8,512,128]{2,1,0:T(8,128)(2,1)} %get-tuple-element.114), calls=%async_computation.5 | async-start | bytes 2097152 | tf_op jit(solution)/shard_map/all_to_all | solution.py:928
  501.8 96.3 %all-to-all-start.7 = ((bf16[8,512,384]{2,1,0:T(8,128)(2,1)}), bf16[8,512,384]{2,1,0:T(8,128)(2,1)S(1)}, u32[]{:S(2)}, u32[]{:S(2)}) async-start(bf16[8,512,384]{2,1,0:T(8,128)(2,1)} %bitcast.185), calls=%async_computation.7 | async-start | bytes 6291456 | tf_op jit(solution)/shard_map/all_to_all | solution.py:928
  523.6 74.4 %collective-permute-start.27 = (bf16[2,512,1024]{2,1,0:T(8,128)(2,1)}, bf16[2,512,1024]{2,1,0:T(8,128)(2,1)}, u32[]{:S(2)}, u32[]{:S(2)}) collective-permute-start(bf16[2,512,1024]{2,1,0:T(8,128)(2,1)} %weight_part.12), channel_id=1, source_target_pairs={{0,1},{1,0},{2,3},{3,2},{4,5},{5,4},{6,7},{7,6},{8,9},{9,8},{10,11... | collective-permute-start | bytes 6291464 | tf_op jit(solution)/shard_map/ppermute | solution.py:30
  537.3 60.7 %collective-permute-start.28 = (bf16[1,256,5120]{2,1,0:T(8,128)(2,1)}, bf16[1,256,5120]{2,1,0:T(8,128)(2,1)}, u32[]{:S(2)}, u32[]{:S(2)}) collective-permute-start(bf16[1,256,5120]{2,1,0:T(8,128)(2,1)} %weight_part.13), channel_id=1, source_target_pairs={{0,16},{8,24},{16,0},{24,8},{1,17},{9,25},{17,1},{25,9},{2,18},{10... | collective-permute-start | bytes 7864328 | tf_op jit(solution)/shard_map/ppermute | solution.py:30
  599.8 81.0 %all-to-all-start.6 = ((bf16[8,512,384]{2,1,0:T(8,128)(2,1)}), bf16[8,512,384]{2,1,0:T(8,128)(2,1)}, u32[]{:S(2)}, u32[]{:S(2)}) async-start(bf16[8,512,384]{2,1,0:T(8,128)(2,1)} %bitcast.184), calls=%async_computation.6 | async-start | bytes 6291456 | tf_op jit(solution)/shard_map/all_to_all | solution.py:928
  604.3 105.1 %all-gather.6.cloned.1.call-start = ((), (), s32[]{:S(2)}) async-start(), calls=%async_computation.9 | async-start | bytes 2973696 | tf_op jit(solution)/shard_map/all_gather | solution.py:996
  725.4 40.9 %collective-permute-start.31 = (bf16[1,256,3072]{2,1,0:T(8,128)(2,1)}, bf16[1,256,3072]{2,1,0:T(8,128)(2,1)S(1)}, u32[]{:S(2)}, u32[]{:S(2)}) collective-permute-start(bf16[1,256,3072]{2,1,0:T(8,128)(2,1)} %weight_part.18), channel_id=1, source_target_pairs={{0,16},{8,24},{16,0},{24,8},{1,17},{9,25},{17,1},{25,9},{2,18},{10... | collective-permute-start | bytes 4718600 | tf_op jit(solution)/shard_map/ppermute | solution.py:30
  (87 other events, 961.1 us)
Sparse Core Ops, SparseCore 0:
  11.0 98.9 all-gather.3
  608.6 92.6 all-gather.5

commit v7 on v5

--- a/solution.py
+++ b/solution.py
@@ -51,14 +51,17 @@
     return axis_bits("clip") + axis_bits("seq")
 
 
-def halve_sum(parts, bits, wire=f32):
+def halve_sum(parts, bits, wire=f32, hold=None):
     addends = [parts.reshape((2,) * len(bits) + parts.shape[1:])]
     for place in exchange_order(bits):
         axis, bit = bits[place]
         mine = own_bit(axis, bit)
         send = sum(lax.dynamic_index_in_dim(a, 1 - mine, place).astype(f32) for a in addends)
         addends = [lax.dynamic_index_in_dim(a, mine, place) for a in addends]
-        addends.append(swap_bit(send.astype(wire), axis, bit))
+        received = swap_bit(send.astype(wire), axis, bit)
+        if hold is not None and len(addends) == 1:
+            received = after(received, hold)
+        addends.append(received)
     total = sum(a.astype(f32) for a in addends)
     return total.reshape(total.shape[len(bits) :])
 
@@ -498,132 +501,173 @@
     )(mine, back, tokens, cot, mods, bias_out, bias_up, bias_down, *up_shares, *up_shares, *down_shares, *earlier)
 
 
-def weight_part_kernel(index_ref, *refs, clips, count, widths, addends):
-    sets = len(widths)
-    per_set = clips * (count + 1)
-    extra = refs[sets * per_set : sets * per_set + addends]
-    out_ref, flat_ref = refs[sets * per_set + addends :]
+def near_place(place, count):
+    bits = count.bit_length() - 1
+    return sum(((place >> b) & 1) << (bits - 1 - b) for b in range(bits))
+
+
+def weight_grad_kernel(index_ref, *refs, clips, counts, widths, owners, swapped):
+    send_ref, keep_ref, flat_ref = refs[-3:]
     step = pl.program_id(0)
-    first = 0
-    for place, steps in enumerate(widths):
-        given = refs[place * per_set : (place + 1) * per_set]
-        left, right = given[: clips * count], given[clips * count :]
-        rows = right[0].shape[0]
+    first, taken = 0, 0
+    for count, steps in zip(counts, widths):
+        left, right = refs[taken : taken + clips * count], refs[taken + clips * count : taken + clips * (count + 1)]
+        taken += clips * (count + 1)
+        rows, height = left[0].shape
+        piece = height // owners
 
         @pl.when(step == first)
-        def _(left=left, rows=rows):
+        def _(left=left, count=count, rows=rows, height=height, piece=piece):
             for c in range(clips):
                 for i in range(count):
-                    flat_ref[i, :, c * rows : (c + 1) * rows] = jnp.transpose(left[c * count + i][...])
+                    flat = jnp.transpose(left[c * count + i][...])
+                    for owner in range(owners):
+                        place = i * height + near_place(owner, owners) * piece
+                        flat_ref[place : place + piece, c * rows : (c + 1) * rows] = flat[owner * piece : (owner + 1) * piece]
 
         @pl.when((step >= first) & (step < first + steps))
         def _(right=right, rows=rows):
-            for i in range(count):
-                total = dot(flat_ref[i, :, 0:rows], right[0][...])
-                for c in range(1, clips):
-                    total += dot(flat_ref[i, :, c * rows : (c + 1) * rows], right[c][...])
-                for ref in extra:
-                    total += ref[i].astype(f32)
-                out_ref[i] = total.astype(out_ref.dtype)
+            total = dot(flat_ref[:, 0:rows], right[0][...])
+            for c in range(1, clips):
+                total += dot(flat_ref[:, c * rows : (c + 1) * rows], right[c][...])
+            total = total.astype(bf16)
+            if swapped:
+
+                @pl.when(step < pl.num_programs(0) // 2)
+                def _():
+                    send_ref[0] = total
+
+                @pl.when(step >= pl.num_programs(0) // 2)
+                def _():
+                    keep_ref[0] = total
+
+            else:
+                half = total.shape[0] // 2
+                for ref, part in ((send_ref, total[:half]), (keep_ref, total[half:])):
+                    for i in range(ref.shape[0]):
+                        ref[i] = part[i * ref.shape[1] : (i + 1) * ref.shape[1]]
 
         first += steps
 
 
-def weight_part(pairs, indices, addends, kind, height):
-    block = 512
-    count = indices.shape[0]
+def weight_grad_call(in_specs, operands, indices, steps, shapes, specs, width, depth, **options):
+    return pl.pallas_call(
+        functools.partial(weight_grad_kernel, **options),
+        grid_spec=pltpu.PrefetchScalarGridSpec(
+            num_scalar_prefetch=1,
+            grid=(steps,),
+            in_specs=in_specs,
+            out_specs=specs,
+            scratch_shapes=[pltpu.VMEM((width, depth), bf16)],
+        ),
+        out_shape=tuple(jax.ShapeDtypeStruct(shape, bf16) for shape in shapes),
+        compiler_params=pltpu.CompilerParams(vmem_limit_bytes=60 << 20),
+        cost_estimate=pl.CostEstimate(
+            flops=1024 * steps * width * depth, bytes_accessed=steps * 1024 * (width + depth) + 4 * width * depth, transcendentals=0
+        ),
+        name="weight_grad",
+    )(indices, *operands)
+
+
+BLOCK = 512
+
+
+def rows_grad(pairs):
     clips = len(pairs[0][0])
-    rows = pairs[0][0][0].shape[0]
-    widths = [right[0].shape[1] // block for _, right in pairs]
-    columns = sum(widths) * block
+    rows, width = pairs[0][0][0].shape
+    height = width // 4
+    mine = mine_on("clip")
+    widths = [right[0].shape[1] // BLOCK for _, right in pairs]
     in_specs, operands = [], []
     first = 0
     for (left, right), steps in zip(pairs, widths):
         for array in left:
-            for i in range(count):
+            for i in range(4):
                 in_specs.append(pl.BlockSpec((rows, height), functools.partial(lambda i, j, q: (0, q[i]), i)))
                 operands.append(array)
         where = functools.partial(lambda first, steps, j, q: (0, jnp.clip(j - first, 0, steps - 1)), first, steps)
-        in_specs += [pl.BlockSpec((rows, block), where)] * clips
+        in_specs += [pl.BlockSpec((rows, BLOCK), where)] * clips
         operands += right
         first += steps
-    for array, start in addends:
-        where = functools.partial(lambda start, j, q: (start, 0, j), start // count)
-        in_specs.append(pl.BlockSpec((count, height, block), where))
-        operands.append(array)
-    return pl.pallas_call(
-        functools.partial(weight_part_kernel, clips=clips, count=count, widths=widths, addends=len(addends)),
-        grid_spec=pltpu.PrefetchScalarGridSpec(
-            num_scalar_prefetch=1,
-            grid=(columns // block,),
-            in_specs=in_specs,
-            out_specs=pl.BlockSpec((count, height, block), lambda j, q: (0, 0, j)),
-            scratch_shapes=[pltpu.VMEM((count, height, clips * rows), bf16)],
+    shape = (2, height, first * BLOCK)
+    spec = pl.BlockSpec((2, height, BLOCK), lambda j, q: (0, 0, j))
+    return weight_grad_call(
+        in_specs,
+        operands,
+        jnp.stack([mine ^ 3, mine ^ 1, mine ^ 2, mine]),
+        first,
+        (shape, shape),
+        (spec, spec),
+        width,
+        clips * rows,
+        clips=clips,
+        counts=[4] * len(pairs),
+        widths=widths,
+        owners=lax.axis_size("seq"),
+        swapped=False,
+    )
+
+
+def columns_grad(left, right):
+    clips = len(left)
+    rows, width = right[0].shape
+    mine, low = mine_on("clip"), mine_on("seq") & 1
+
+    def block(clip_flip, low_flip):
+        return (mine ^ clip_flip) * 2 + (low ^ low_flip)
+
+    flips = ((0, 1), (2, 1), (0, 0), (2, 0))
+    indices = jnp.stack([block(c ^ 1, s) for c, s in flips] + [block(c, s) for c, s in flips])
+    in_specs = [pl.BlockSpec((rows, width), lambda j, q: (0, 0))] * clips
+    in_specs += [pl.BlockSpec((rows, BLOCK), lambda j, q: (0, q[j]))] * clips
+    shape = (4, width, BLOCK)
+    return weight_grad_call(
+        in_specs,
+        right + left,
+        indices,
+        8,
+        (shape, shape),
+        (
+            pl.BlockSpec((1, width, BLOCK), lambda j, q: (jnp.minimum(j, 3), 0, 0)),
+            pl.BlockSpec((1, width, BLOCK), lambda j, q: (jnp.maximum(j - 4, 0), 0, 0)),
         ),
-        out_shape=jax.ShapeDtypeStruct((count, height, columns), kind),
-        compiler_params=pltpu.CompilerParams(vmem_limit_bytes=32 << 20),
-        cost_estimate=pl.CostEstimate(
-            flops=2 * count * clips * rows * height * columns,
-            bytes_accessed=clips * rows * (count * height + columns) * 2 + 4 * count * height * columns,
-            transcendentals=0,
-        ),
-        name="weight_part",
-    )(indices, *operands)
+        width,
+        clips * rows,
+        clips=clips,
+        counts=[1],
+        widths=[8],
+        owners=1,
+        swapped=True,
+    )
 
 
 def mine_on(axis):
     return lax.axis_index(axis).astype(jnp.int32)
 
 
+def rounded_sum(addends):
+    return sum(a.astype(f32) for a in addends).astype(bf16)
+
+
+def halve(addends, bits, dim, hold=None):
+    for place, (axis, bit) in enumerate(bits):
+        half = addends[0].shape[dim] // 2
+        mine = own_bit(axis, bit)
+        send = rounded_sum([lax.dynamic_slice_in_dim(a, (1 - mine) * half, half, dim) for a in addends])
+        addends = [lax.dynamic_slice_in_dim(a, mine * half, half, dim) for a in addends]
+        received = swap_bit(send, axis, bit)
+        if hold is not None and place == 0:
+            received = after(received, hold)
+        addends.append(received)
+    return sum(a.astype(f32) for a in addends)
+
+
 def gate(arrays, *others):
     return list(lax.optimization_barrier((tuple(arrays), others))[0])
 
 
 def height_of(pairs, parts):
     return pairs[0][0][0].shape[1] // parts
-
-
-def across_first(pairs):
-    mine = mine_on("clip")
-    return weight_part(pairs, jnp.stack([mine ^ 3, mine ^ 1]), (), bf16, height_of(pairs, 4))
-
-
-def across_second(pairs, core):
-    return weight_part(pairs, (mine_on("clip") ^ 2)[None], ((core, 0),), bf16, height_of(pairs, 4))
-
-
-def across_own(pairs, core, across):
-    addends = ((core, 1), (across, 0))
-    return weight_part(pairs, mine_on("clip")[None], addends, f32, height_of(pairs, 4))
-
-
-def along_seq(total):
-    return halve_sum(total.reshape((lax.axis_size("seq"), -1, total.shape[2])), axis_bits("seq"), bf16)
-
-
-def along_block(clip_flip, low_flip):
-    return (mine_on("clip") ^ clip_flip) * 2 + ((mine_on("seq") & 1) ^ low_flip)
-
-
-def along_first(pairs):
-    blocks = jnp.stack([along_block(1, 1), along_block(3, 1), along_block(1, 0), along_block(3, 0)])
-    return weight_part(pairs, blocks, (), bf16, height_of(pairs, 8))
-
-
-def along_second(pairs, core):
-    blocks = jnp.stack([along_block(0, 1), along_block(2, 1)])
-    return weight_part(pairs, blocks, ((core, 0),), bf16, height_of(pairs, 8))
-
-
-def along_third(pairs, core, along):
-    return weight_part(pairs, along_block(2, 0)[None], ((core, 3), (along, 1)), bf16, height_of(pairs, 8))
-
-
-def along_total(pairs, core, along, across):
-    addends = ((core, 2), (along, 0), (across, 0))
-    total = weight_part(pairs, along_block(0, 0)[None], addends, f32, height_of(pairs, 8))
-    bits = axis_bits("seq")[:-1]
-    return halve_sum(total.reshape((2 ** len(bits), -1, total.shape[2])), bits, bf16)
 
 
 def attend_kernel(qkv_ref, mix_ref, full_ref, log_ref, vt_ref, *, total, span, block):
@@ -881,10 +925,17 @@
 
     full_qkv = lax.all_gather(qkv_weight, BOTH, axis=0, tiled=True)
     unit = down_weight.shape[0]
-    owners = (4, seq_devices // 2, 2, unit)
-    near_owners = (4, 2, seq_devices // 2, unit)
+    seq_bits = len(axis_bits("seq"))
+    owners = (4,) + (2,) * seq_bits + (unit,)
+    by_nearness = (0,) + tuple(range(1, seq_bits + 1))[::-1] + (seq_bits + 1,)
+
+    def reorder(vectors):
+        lead = vectors.shape[:-1]
+        turn = tuple(range(len(lead))) + tuple(len(lead) + d for d in by_nearness)
+        return vectors.reshape(lead + owners).transpose(turn).reshape(vectors.shape)
+
     down_shard = down_weight.reshape(4, piece, width)
-    up_shard = up_weight.reshape((piece,) + owners).transpose(1, 0, 3, 2, 4).reshape(4, piece, width)
+    up_shard = reorder(up_weight).reshape(piece, 4, width).transpose(1, 0, 2)
     up_shard = jnp.concatenate([up_shard, out_weight[None]], axis=0)
 
     levels = level_rows(ctx_count, noise_level, rows)
@@ -921,16 +972,16 @@
     def exchange(value):
         return lax.all_to_all(value, "seq", 0, 0, tiled=True)
 
-    def doubled(share, axis, bit):
+    def doubled(share, axis, bit, dim=1):
         other = swap_bit(share, axis, bit)
         mine = own_bit(axis, bit) == 0
-        pair = jnp.stack([jnp.where(mine, share, other), jnp.where(mine, other, share)], axis=1)
+        pair = jnp.stack([jnp.where(mine, share, other), jnp.where(mine, other, share)], axis=dim)
         return pair.reshape((-1,) + share.shape[1:])
 
     high_bits, low_bit = axis_bits("seq")[:-1], axis_bits("seq")[-1]
     down_share, up_share = down_shard[None], up_shard[None]
     for axis, bit in high_bits:
-        down_share, up_share = doubled(down_share, axis, bit), doubled(up_share, axis, bit)
+        down_share, up_share = doubled(down_share, axis, bit, 0), doubled(up_share, axis, bit)
     full_qkv = after(full_qkv, down_share, up_share)
     up_pair = (up_share, swap_bit(up_share, "clip", 2))
     down_share = doubled(down_share, *low_bit)
@@ -956,7 +1007,7 @@
     )
     mods_two = blocks(mod_rest)
     bias_out = bias_rest[:, :width]
-    bias_up = bias_rest[:, width : 5 * width].reshape(owners).transpose(0, 2, 1, 3).reshape(1, -1)
+    bias_up = reorder(bias_rest[:, width : 5 * width])
     bias_down = bias_rest[:, 5 * width :]
     def from_clips(pair):
         near, across = [p.reshape((seq_devices // 2, 2) + p.shape[1:]) for p in pair]
@@ -984,7 +1035,7 @@
     def with_bias(lines_now, vectors):
         return jnp.concatenate([jnp.concatenate(lines_now, axis=0), jnp.concatenate(vectors).reshape(lines, -1)], axis=1)
 
-    bias_up_sum = sum(r[10][0] for r in results).reshape(near_owners).transpose(0, 2, 1, 3).reshape(-1)
+    bias_up_sum = reorder(sum(r[10][0] for r in results))
     bias_pair = sum(r[11] for r in results)
     early = with_bias([line_sums(r[9]) for r in results], [bias_pair[0], bias_up_sum, bias_pair[1]])
     early_rows = lax.all_gather(early, BOTH, axis=0, tiled=True)
@@ -992,24 +1043,24 @@
     d_qkv, exchanged = [], []
     for c in range(clips):
         if c == clips - 1:
-            active = gate(active, *d_qkv)
-            down_first = along_first([(active, d_mlp)])
-            down_core = swap_bit(down_first, "clip", 1)
-            normed_two = gate(normed_two, down_first)
-            up_first = across_first([(normed_two, d_hidden), (mixed_all, d_attn)])
-            up_core = swap_bit(up_first, "clip", 1)
-        grad = after(d_mixed[c], results[-1][8] if c == 0 else up_first)
+            active = gate(active, *d_qkv, d_mixed[-1])
+            down_send, down_keep = columns_grad(active, d_mlp)
+            down_core = swap_bit(down_send, "clip", 1)
+            normed_two = gate(normed_two, down_send)
+            up_send, up_keep = rows_grad([(normed_two, d_hidden), (mixed_all, d_attn)])
+            up_core = swap_bit(up_send, "clip", 1)
+        grad = after(d_mixed[c], results[-1][8] if c == 0 else up_send)
         grad = grad.reshape(total, span)
         d_qkv.append(attend_back(qkv[c].reshape(total, 3 * span), grad, fulls[c], logs[c], cos_all, sin_all, span))
         sent = d_qkv[c].reshape(seq_devices, rows, 3 * span)
         exchanged.append(exchange(after(sent, d_mixed[-1]) if c == 0 else sent))
 
-    d_mlp = gate(d_mlp, exchanged[0])
-    down_second = along_second([(active, d_mlp)], down_core)
-    d_hidden = gate(d_hidden, down_second)
-    up_second = across_second([(normed_two, d_hidden), (mixed_all, d_attn)], up_core)
-    down_along, up_across = swap_bit(down_second, "seq", 1), swap_bit(up_second, "clip", 2)
-    exchanged[0] = after(exchanged[0], up_second)
+    down_core, up_core = gate((down_core, up_core), exchanged[0])
+    down_sent = rounded_sum([down_keep[:2], down_core[:2]])
+    down_along = swap_bit(down_sent, "seq", 1)
+    up_sent = rounded_sum([up_keep[0], up_core[0]])
+    up_across = swap_bit(up_sent, "clip", 2)
+    exchanged[0] = after(exchanged[0], down_sent, up_sent)
     exchanged[-1] = after(exchanged[-1], down_along, up_across)
 
     last = []
@@ -1017,22 +1068,23 @@
         grads = last[-1][0] if last else None
         last.append(project_back(exchanged[c], full_qkv, tokens, c, mods_one[c][1], results[c][1], grads))
     d_projected = [r[1] for r in last]
-    qkv_pairs = [(normed, d_projected)]
-    qkv_core = swap_bit(across_first(qkv_pairs), "clip", 1)
-    qkv_second = across_second(qkv_pairs, qkv_core)
-    qkv_across = swap_bit(qkv_second, "clip", 2)
-    d_hidden = gate(d_hidden, qkv_second)
-    up_total = across_own([(normed_two, d_hidden), (mixed_all, d_attn)], up_core, up_across)
-    qkv_total = across_own(qkv_pairs, qkv_core, qkv_across)
-    d_mlp = gate(d_mlp, qkv_total)
-    down_across = swap_bit(along_third([(active, d_mlp)], down_core, down_along), "clip", 2)
-    grad_up, grad_qkv = along_seq(up_total), along_seq(qkv_total)
-    grad_down = along_total([(active, d_mlp)], down_core, down_along, down_across)
+    qkv_send, qkv_keep = rows_grad([(normed, d_projected)])
+    qkv_core = swap_bit(qkv_send, "clip", 1)
+    qkv_sent = rounded_sum([qkv_keep[0], qkv_core[0]])
+    qkv_across = swap_bit(qkv_sent, "clip", 2)
+    down_far = rounded_sum([down_keep[3], down_core[3], after(down_along[1], qkv_send)])
+    down_across = swap_bit(down_far, "clip", 2)
+    near_seq = axis_bits("seq")[::-1]
+    grad_up = halve([up_keep[1], up_core[1], up_across], near_seq, 0, qkv_sent)
+    down_addends = [down_keep[2], down_core[2], down_along[0], after(down_across, qkv_sent)]
+    grad_down = jnp.transpose(halve(down_addends, near_seq[1:], 1))
+    qkv_last = after(qkv_across, up_across)
+    grad_qkv = halve([qkv_keep[1], qkv_core[1], qkv_last], near_seq, 0)
     grad_out = grad_up[:, 4 * width :]
-    grad_up = grad_up[:, : 4 * width].reshape((-1,) + near_owners).transpose(0, 1, 3, 2, 4).reshape(-1, 4 * width)
+    grad_up = reorder(grad_up[:, : 4 * width])
     late_rows = with_bias([line_sums(r[2]) for r in last], [sum(r[3][0] for r in last)])
-    late_rows = collect_rows(after(late_rows, qkv_total), order)
-    early_rows = after(early_rows, qkv_total)
+    late_rows = collect_rows(after(late_rows, qkv_sent), order)
+    early_rows = after(early_rows, qkv_sent)
 
     def own_columns(sums, shard):
         return lax.dynamic_slice_in_dim(sums, here * shard.shape[0], shard.shape[0], 0)

time: 896 us -> 876 us (0.978)
  Pallas kernels: 371 us -> 347 us
  other arithmetic: 50.9 us -> 71.7 us
  local copies, waits for them, and re-layouts: 99.8 us -> 80.7 us
  starting transfers between devices: 96.5 us -> 107 us
    unnamed x220 -> x131, local copies, waits for them, and re-layouts: 52 us -> 18.3 us
    pallas_call x10 -> x3, Pallas kernels: 73.3 us -> 49.5 us  [weight_grad_call(): pl.pallas_call(functools.partial(weight_grad_kernel, **options), grid_spe...]
    convert_element_type x5 -> x12, other arithmetic: 8.79 us -> 32.6 us  [rounded_sum(): return sum((a.astype(f32) for a in addends)).astype(bf16)]
    slice x2 -> x9, local copies, waits for them, and re-layouts: 0.83 us -> 17.5 us  [the longest x2 5.27 us: body_by_heads(): grad_up = halve([up_keep[1], up_core[1], up_across], near_seq, 0, qkv_sent)]
    ppermute x45, starting transfers between devices: 53.1 us -> 64 us  [swap_bit(): return lax.ppermute(value, axis, [(i, i ^ bit) for i in range(count)])]
    all_to_all x8, waiting for transfers between devices: 82.7 us -> 92.7 us  [exchange(): return lax.all_to_all(value, 'seq', 0, 0, tiled=True)]
    ppermute x45, waiting for transfers between devices: 150 us -> 140 us  [swap_bit(): return lax.ppermute(value, axis, [(i, i ^ bit) for i in range(count)])]
  transfers between devices with their start and end apart: 55 -> 55, of which waited for: 20 -> 21; matrix products, arithmetic and copies ran while one was open for 11% -> 15% of each run, Pallas kernels for 42% -> 40%
where the time goes in v7:
time: 876 us; the launch traced here: 865 us
  Pallas kernels  347 us (40%)
  waiting for transfers between devices  238 us (27%)
  starting transfers between devices  107 us (12%)
  local copies, waits for them, and re-layouts  80.7 us (9%)
  other arithmetic  71.7 us (8%)
  between operations  16.1 us (2%)
    ppermute x45, waiting for transfers between devices, swap_bit(): return lax.ppermute(value, axis, [(i, i ^ bit) for i in range(count)])  140 us
    pallas_call x2, Pallas kernels, attend_back(): pl.pallas_call(functools.partial(attend_back_kernel, total=total, span=sp...  118 us
    all_to_all x8, waiting for transfers between devices, exchange(): return lax.all_to_all(value, 'seq', 0, 0, tiled=True)  92.7 us
    pallas_call x2, Pallas kernels, middle(): pl.pallas_call(middle_kernel, grid_spec=pltpu.PrefetchScalarGridSpec(num_...  76.6 us
    pallas_call x2, Pallas kernels, attend(): pl.pallas_call(functools.partial(attend_kernel, total=total, span=span, b...  70.6 us
    ppermute x45, starting transfers between devices, swap_bit(): return lax.ppermute(value, axis, [(i, i ^ bit) for i in range(count)])  64 us
    pallas_call x3, Pallas kernels, weight_grad_call(): pl.pallas_call(functools.partial(weight_grad_kernel, **options), grid_spe...  49.5 us
    all_to_all x8, starting transfers between devices, exchange(): return lax.all_to_all(value, 'seq', 0, 0, tiled=True)  42.9 us
  transfers between devices with their start and end apart: 55, of which 21 were waited for; matrix products, arithmetic and copies ran while one was open for 15% of the time, Pallas kernels for 40%

profile of v7, /device:TPU:0, one launch (start us, length us, event | category | flops | bytes accessed | tf_op | source)
XLA Modules:
  0.0 864.5 jit_solution(13869498178841971541)
XLA Ops:
  30.6 14.3 %collective-permute-done.7 = bf16[1,4,32,1024]{3,2,1,0:T(8,128)(2,1)} collective-permute-done((bf16[1,4,32,1024]{3,2,1,0:T(8,128)(2,1)}, bf16[1,4,32,1024]{3,2,1,0:T(8,128)(2,1)}, u32[]{:S(2)}, u32[]{:S(2)}) %collective-permute-start.7) | collective-permute-done | bytes 262176 | tf_op jit(solution)/shard_map/ppermute | solution.py:30
  51.2 9.6 %collective-permute-done.3 = f32[32,2816]{1,0:T(8,128)S(1)} collective-permute-done((f32[32,2816]{1,0:T(8,128)S(1)}, f32[32,2816]{1,0:T(8,128)S(1)}, u32[]{:S(2)}, u32[]{:S(2)}) %collective-permute-start.3) | collective-permute-done | bytes 360480 | tf_op jit(solution)/shard_map/ppermute | solution.py:30
  70.8 20.5 %collective-permute-done.10 = bf16[2,5,32,1024]{3,2,1,0:T(8,128)(2,1)S(1)} collective-permute-done((bf16[2,5,32,1024]{3,2,1,0:T(8,128)(2,1)S(1)}, bf16[2,5,32,1024]{3,2,1,0:T(8,128)(2,1)S(1)}, u32[]{:S(2)}, u32[]{:S(2)}) %collective-permute-start.10) | collective-permute-done | bytes 655392 | tf_op jit(solution)/shard_map/ppermute | solution.py:30
  130.9 18.4 %collective-permute-done.18 = bf16[4,5,32,1024]{3,2,1,0:T(8,128)(2,1)} collective-permute-done((bf16[4,5,32,1024]{3,2,1,0:T(8,128)(2,1)}, bf16[4,5,32,1024]{3,2,1,0:T(8,128)(2,1)}, u32[]{:S(2)}, u32[]{:S(2)}) %collective-permute-start.18) | collective-permute-done | bytes 1310752 | tf_op jit(solution)/shard_map/ppermute | solution.py:30
  168.6 26.4 %all-to-all-done = bf16[8,512,384]{2,1,0:T(8,128)(2,1)} async-done(((bf16[8,512,384]{2,1,0:T(8,128)(2,1)}), bf16[8,512,384]{2,1,0:T(8,128)(2,1)}, u32[]{:S(2)}, u32[]{:S(2)}) %all-to-all-start) | async-done | bytes 3145760 | tf_op jit(solution)/shard_map/all_to_all | solution.py:973
  210.4 10.6 %collective-permute-start.16 = (f32[8,5632]{1,0:T(8,128)S(1)}, f32[8,5632]{1,0:T(8,128)S(1)}, u32[]{:S(2)}, u32[]{:S(2)}) collective-permute-start(f32[8,5632]{1,0:T(8,128)S(1)} %constant_dynamic-slice_fusion.1), channel_id=1, source_target_pairs={{0,2},{1,3},{2,0},{3,1},{4,6},{5,7},{6,4},{7,5},{8,10},{9,11},{10,... | collective-permute-start | bytes 540680 | tf_op jit(solution)/shard_map/ppermute | solution.py:30
  221.1 35.3 %attend.3 = (bf16[4096,128]{1,0:T(8,128)(2,1)}, f32[4096,128]{1,0:T(8,128)}, f32[2,4096]{1,0:T(2,128)}) custom-call(bf16[4096,384]{1,0:T(8,128)(2,1)} %bitcast.37.qkv_ref), custom_call_target="tpu_custom_call" | custom-call | flops 17179869184 | bytes 6291456 | tf_op jit(solution)/shard_map/attend/pallas_call | solution.py:731
  256.3 13.7 %all-to-all-done.1 = bf16[8,512,384]{2,1,0:T(8,128)(2,1)} async-done(((bf16[8,512,384]{2,1,0:T(8,128)(2,1)}), bf16[8,512,384]{2,1,0:T(8,128)(2,1)}, u32[]{:S(2)}, u32[]{:S(2)}) %all-to-all-start.1) | async-done | bytes 3145760 | tf_op jit(solution)/shard_map/all_to_all | solution.py:973
  277.7 35.3 %attend.2 = (bf16[4096,128]{1,0:T(8,128)(2,1)}, f32[4096,128]{1,0:T(8,128)}, f32[2,4096]{1,0:T(2,128)}) custom-call(bf16[4096,384]{1,0:T(8,128)(2,1)} %bitcast.35.qkv_ref), custom_call_target="tpu_custom_call" | custom-call | flops 17179869184 | bytes 6291456 | tf_op jit(solution)/shard_map/attend/pallas_call | solution.py:731
  320.0 38.3 %middle.2 = (bf16[2,512,1024]{2,1,0:T(8,128)(2,1)}, f32[512,1024]{1,0:T(8,128)}, bf16[512,1024]{1,0:T(8,128)(2,1)}, bf16[512,1024]{1,0:T(8,128)(2,1)}, bf16[512,...) custom-call(s32[1]{0:T(128)} %bitcast.clip_ref, ...), custom_call_target="tpu_custom_call" | custom-call | flops 2147483648 | bytes 4718592 | tf_op jit(solution)/shard_map/middle/pallas_call | solution.py:446
  369.5 38.3 %middle.3 = (bf16[2,512,1024]{2,1,0:T(8,128)(2,1)}, f32[512,1024]{1,0:T(8,128)}, bf16[512,1024]{1,0:T(8,128)(2,1)}, bf16[512,1024]{1,0:T(8,128)(2,1)}, bf16[512,...) custom-call(s32[1]{0:T(128)} %bitcast.clip_ref, ...), custom_call_target="tpu_custom_call", output_to_operand_aliasing={{0}: (20, {})} | custom-call | flops 2147483648 | bytes 4718592 | tf_op jit(solution)/shard_map/middle/pallas_call | solution.py:446
  414.3 59.2 %attend_back.2 = bf16[4096,384]{1,0:T(8,128)(2,1)} custom-call(bf16[4096,384]{1,0:T(8,128)(2,1)} %bitcast.37.qkv_ref, bf16[4096,128]{1,0:T(8,128)(2,1)} %bitcast.256, f32[4096,128]{1,0:T(8,128)} %get-tuple-element.121.full_ref, f32[2,4096]{1,0:T(2,128)} %get-tuple-element.122.log_ref, f32[4096,128]{1,0:T(8,128)} %bitcast.253, f32[4096,128]{1,0:T(8,128)} %bitcast.251), custom_call_target="tpu_custom_call" | custom-call | flops 42949672960 | bytes 13631488 | tf_op jit(solution)/shard_map/attend_back/pallas_call | solution.py:826
  480.5 16.2 %weight_grad.3 = (bf16[4,1024,512]{2,1,0:T(8,128)(2,1)}, bf16[4,1024,512]{2,1,0:T(8,128)(2,1)}) custom-call(s32[8]{0:T(128)} %stack.141.index_ref, bf16[512,1024]{1,0:T(8,128)(2,1)} %get-tuple-element.116.refs_0_, bf16[512,1024]{1,0:T(8,128)(2,1)} %get-tuple-element.117.refs_1_, bf16[512,4096]{1,0:T(8,128)(2,1)} %get-tuple-element.123.refs_2_, ...), custom_call_target="tpu_custom_call" | custom-call | flops 8589934592 | bytes 20971520 | tf_op jit(solution)/shard_map/weight_grad/pallas_call | solution.py:554
  496.6 20.4 %weight_grad.4 = (bf16[2,256,5120]{2,1,0:T(8,128)(2,1)}, bf16[2,256,5120]{2,1,0:T(8,128)(2,1)}) custom-call(s32[4]{0:T(128)} %pad_add_fusion.5.index_ref, bf16[512,1024]{1,0:T(8,128)(2,1)} %get-tuple-element.126.refs_0_.refs_1_.refs_2_.refs_3_, bf16[512,1024]{1,0:T(8,128)(2,1)} %get-tuple-element.126.refs_0_.refs_1_.refs_2_.refs_3_, ...), custom_call_target="tpu_custom_call" | custom-call | flops 10737418240 | bytes 25165824 | tf_op jit(solution)/shard_map/weight_grad/pallas_call | solution.py:554
  517.6 59.2 %attend_back.3 = bf16[4096,384]{1,0:T(8,128)(2,1)} custom-call(bf16[4096,384]{1,0:T(8,128)(2,1)} %bitcast.35.qkv_ref, bf16[4096,128]{1,0:T(8,128)(2,1)} %bitcast.258, f32[4096,128]{1,0:T(8,128)} %get-tuple-element.136.full_ref, f32[2,4096]{1,0:T(2,128)} %get-tuple-element.137.log_ref, f32[4096,128]{1,0:T(8,128)} %bitcast.254, f32[4096,128]{1,0:T(8,128)} %bitcast.252), custom_call_target="tpu_custom_call" | custom-call | flops 42949672960 | bytes 13631488 | tf_op jit(solution)/shard_map/attend_back/pallas_call | solution.py:826
  597.5 9.5 %project_back.2 = (f32[2,512,1024]{2,1,0:T(8,128)}, bf16[512,3072]{1,0:T(8,128)(2,1)S(1)}, f32[2,2,1024]{2,1,0:T(2,128)S(1)}, f32[1,3072]{1,0:T(1,128)S(1)}) custom-call(bf16[8,512,384]{2,1,0:T(8,128)(2,1)S(1)} %copy-done.4, bf16[1024,3072]{1,0:T(8,128)(2,1)} %all-gather.4.cloned.1.call-done.wq_ref.wk_ref.wv_ref, ...), custom_call_target="tpu_custom_call" | custom-call | flops 3221225472 | bytes 17825792 | tf_op jit(solution)/shard_map/project_back/pallas_call | solution.py:263
  608.7 52.6 %all-to-all-done.6.back_ref = bf16[8,512,384]{2,1,0:T(8,128)(2,1)} async-done(((bf16[8,512,384]{2,1,0:T(8,128)(2,1)}), bf16[8,512,384]{2,1,0:T(8,128)(2,1)}, u32[]{:S(2)}, u32[]{:S(2)}) %all-to-all-start.6) | async-done | bytes 3145760 | tf_op jit(solution)/shard_map/all_to_all | solution.py:973
  669.8 9.8 %project_back.3 = (f32[2,512,1024]{2,1,0:T(8,128)}, bf16[512,3072]{1,0:T(8,128)(2,1)S(1)}, f32[2,2,1024]{2,1,0:T(2,128)S(1)}, f32[1,3072]{1,0:T(1,128)S(1)}) custom-call(bf16[8,512,384]{2,1,0:T(8,128)(2,1)} %all-to-all-done.6.back_ref, bf16[1024,3072]{1,0:T(8,128)(2,1)} %all-gather.4.cloned.1.call-done.wq_ref.wk_ref.wv_ref, ...), custom_call_target="tpu_custom_call", output_to_operand_aliasing={{0}: (7, {})} | custom-call | flops 3221225472 | bytes 17825792 | tf_op jit(solution)/shard_map/project_back/pallas_call | solution.py:263
  681.2 12.9 %weight_grad.5 = (bf16[2,256,3072]{2,1,0:T(8,128)(2,1)}, bf16[2,256,3072]{2,1,0:T(8,128)(2,1)}) custom-call(s32[4]{0:T(128)} %pad_add_fusion.5.index_ref, bf16[512,1024]{1,0:T(8,128)(2,1)} %copy-done.11, bf16[512,1024]{1,0:T(8,128)(2,1)} %copy-done.11, bf16[512,1024]{1,0:T(8,128)(2,1)} %copy-done.11, bf16[512,1024]{1,0:T(8,128)(2,1)} %copy-done.11, ...), custom_call_target="tpu_custom_call" | custom-call | flops 6442450944 | bytes 16777216 | tf_op jit(solution)/shard_map/weight_grad/pallas_call | solution.py:554
  725.9 21.3 %collective-permute-done.39 = bf16[128,5120]{1,0:T(8,128)(2,1)} collective-permute-done((bf16[128,5120]{1,0:T(8,128)(2,1)}, bf16[128,5120]{1,0:T(8,128)(2,1)}, u32[]{:S(2)}, u32[]{:S(2)}) %collective-permute-start.39) | collective-permute-done | bytes 1310752 | tf_op jit(solution)/shard_map/ppermute | solution.py:30
  766.4 7.5 collective-permute-start.31
  799.1 10.9 %collective-permute-done.44 = bf16[1024,128]{1,0:T(8,128)(2,1)} collective-permute-done((bf16[1024,128]{1,0:T(8,128)(2,1)S(1)}, bf16[1024,128]{1,0:T(8,128)(2,1)}, u32[]{:S(2)}, u32[]{:S(2)}) %collective-permute-start.44) | collective-permute-done | bytes 262176 | tf_op jit(solution)/shard_map/ppermute | solution.py:30
  836.8 7.9 collective-permute-done.37
  848.0 7.1 collective-permute-done.38
  (406 shorter events, 293.3 us)
Async XLA Ops:
  7.3 99.7 %all-gather.4.cloned.1.call-start = ((), (), s32[]{:S(2)}) async-start(), calls=%async_computation.8 | async-start | bytes 6488064 | tf_op jit(solution)/shard_map/all_gather | solution.py:926
  30.6 93.0 %collective-permute-start.13 = (f32[64,5632]{1,0:T(8,128)}, f32[64,5632]{1,0:T(8,128)}, u32[]{:S(2)}, u32[]{:S(2)}) collective-permute-start(f32[64,5632]{1,0:T(8,128)} %constant_dynamic-slice_fusion.4), channel_id=1, source_target_pairs={{0,8},{8,0},{16,24},{24,16},{1,9},{9,1},{17,25},{25,17},{2,10},{10... | collective-permute-start | bytes 4325384 | tf_op jit(solution)/shard_map/ppermute | solution.py:30
  68.6 58.6 %collective-permute-start.11 = (bf16[4,4,32,1024]{3,2,1,0:T(8,128)(2,1)}, bf16[4,4,32,1024]{3,2,1,0:T(8,128)(2,1)}, u32[]{:S(2)}, u32[]{:S(2)}) collective-permute-start(bf16[4,4,32,1024]{3,2,1,0:T(8,128)(2,1)} %bitcast.18), channel_id=1, source_target_pairs={{0,1},{1,0},{2,3},{3,2},{4,5},{5,4},{6,7},{7,6},{8,9},{9,8},{10,11... | collective-permute-start | bytes 3145736 | tf_op jit(solution)/shard_map/ppermute | solution.py:30
  97.5 55.4 %collective-permute-start.12 = (bf16[4,5,32,1024]{3,2,1,0:T(8,128)(2,1)}, bf16[4,5,32,1024]{3,2,1,0:T(8,128)(2,1)}, u32[]{:S(2)}, u32[]{:S(2)}) collective-permute-start(bf16[4,5,32,1024]{3,2,1,0:T(8,128)(2,1)} %bitcast.29), channel_id=1, source_target_pairs={{0,16},{8,24},{16,0},{24,8},{1,17},{9,25},{17,1},{25,9},{2,18},{10... | collective-permute-start | bytes 3932168 | tf_op jit(solution)/shard_map/ppermute | solution.py:30
  99.0 50.3 %collective-permute-start.18 = (bf16[4,5,32,1024]{3,2,1,0:T(8,128)(2,1)}, bf16[4,5,32,1024]{3,2,1,0:T(8,128)(2,1)}, u32[]{:S(2)}, u32[]{:S(2)}) collective-permute-start(bf16[4,5,32,1024]{3,2,1,0:T(8,128)(2,1)} %bitcast.29), channel_id=1, source_target_pairs={{0,1},{1,0},{2,3},{3,2},{4,5},{5,4},{6,7},{7,6},{8,9},{9,8},{10,11... | collective-permute-start | bytes 3932168 | tf_op jit(solution)/shard_map/ppermute | solution.py:30
  118.9 76.2 %all-to-all-start = ((bf16[8,512,384]{2,1,0:T(8,128)(2,1)}), bf16[8,512,384]{2,1,0:T(8,128)(2,1)}, u32[]{:S(2)}, u32[]{:S(2)}) async-start(bf16[8,512,384]{2,1,0:T(8,128)(2,1)} %copy-done.5), calls=%async_computation | async-start | bytes 6291456 | tf_op jit(solution)/shard_map/all_to_all | solution.py:973
  130.4 189.6 %collective-permute-start.23 = (bf16[4,2,4,32,1024]{4,3,2,1,0:T(8,128)(2,1)}, bf16[4,2,4,32,1024]{4,3,2,1,0:T(8,128)(2,1)}, u32[]{:S(2)}, u32[]{:S(2)}) collective-permute-start(bf16[4,2,4,32,1024]{4,3,2,1,0:T(8,128)(2,1)} %pad_maximum_fusion.2.refs_8_), channel_id=1, source_target_pairs={{0,8},{8,0},{16,24},{24,16},{1,9},{9,1},{17,25},{25,17},{2,10},{10... | collective-permute-start | bytes 6291464 | tf_op jit(solution)/shard_map/ppermute | solution.py:30
  130.4 182.6 %collective-permute-start.22 = (bf16[8,4,32,1024]{3,2,1,0:T(8,128)(2,1)}, bf16[8,4,32,1024]{3,2,1,0:T(8,128)(2,1)}, u32[]{:S(2)}, u32[]{:S(2)}) collective-permute-start(bf16[8,4,32,1024]{3,2,1,0:T(8,128)(2,1)} %bitcast.33), channel_id=1, source_target_pairs={{0,16},{8,24},{16,0},{24,8},{1,17},{9,25},{17,1},{25,9},{2,18},{10... | collective-permute-start | bytes 6291464 | tf_op jit(solution)/shard_map/ppermute | solution.py:30
  152.9 48.8 %collective-permute-start.20 = (bf16[4,2,5,32,1024]{4,3,2,0,1:T(8,128)(2,1)}, bf16[4,2,5,32,1024]{4,3,2,0,1:T(8,128)(2,1)}, u32[]{:S(2)}, u32[]{:S(2)}) collective-permute-start(bf16[4,2,5,32,1024]{4,3,2,0,1:T(8,128)(2,1)} %pad_maximum_fusion), channel_id=1, source_target_pairs={{0,8},{8,0},{16,24},{24,16},{1,9},{9,1},{17,25},{25,17},{2,10},{10... | collective-permute-start | bytes 7864328 | tf_op jit(solution)/shard_map/ppermute | solution.py:30
  152.9 46.6 %collective-permute-start.19 = (bf16[4,5,32,1024]{3,2,1,0:T(8,128)(2,1)}, bf16[4,5,32,1024]{3,2,1,0:T(8,128)(2,1)}, u32[]{:S(2)}, u32[]{:S(2)}) collective-permute-start(bf16[4,5,32,1024]{3,2,1,0:T(8,128)(2,1)} %collective-permute-done.12), channel_id=1, source_target_pairs={{0,1},{1,0},{2,3},{3,2},{4,5},{5,4},{6,7},{7,6},{8,9},{9,8},{10,11... | collective-permute-start | bytes 3932168 | tf_op jit(solution)/shard_map/ppermute | solution.py:30
  155.6 53.8 %collective-permute-start.15 = (f32[16,5632]{1,0:T(8,128)S(1)}, f32[16,5632]{1,0:T(8,128)}, u32[]{:S(2)}, u32[]{:S(2)}) collective-permute-start(f32[16,5632]{1,0:T(8,128)S(1)} %constant_dynamic-slice_fusion.2), channel_id=1, source_target_pairs={{0,1},{1,0},{2,3},{3,2},{4,5},{5,4},{6,7},{7,6},{8,9},{9,8},{10,11... | collective-permute-start | bytes 1081352 | tf_op jit(solution)/shard_map/ppermute | solution.py:30
  195.1 75.0 %all-to-all-start.1 = ((bf16[8,512,384]{2,1,0:T(8,128)(2,1)}), bf16[8,512,384]{2,1,0:T(8,128)(2,1)}, u32[]{:S(2)}, u32[]{:S(2)}) async-start(bf16[8,512,384]{2,1,0:T(8,128)(2,1)} %copy-done.6), calls=%async_computation.1 | async-start | bytes 6291456 | tf_op jit(solution)/shard_map/all_to_all | solution.py:973
  210.4 45.9 %collective-permute-start.16 = (f32[8,5632]{1,0:T(8,128)S(1)}, f32[8,5632]{1,0:T(8,128)S(1)}, u32[]{:S(2)}, u32[]{:S(2)}) collective-permute-start(f32[8,5632]{1,0:T(8,128)S(1)} %constant_dynamic-slice_fusion.1), channel_id=1, source_target_pairs={{0,2},{1,3},{2,0},{3,1},{4,6},{5,7},{6,4},{7,5},{8,10},{9,11},{10,... | collective-permute-start | bytes 540680 | tf_op jit(solution)/shard_map/ppermute | solution.py:30
  313.5 44.9 %all-to-all-start.3 = ((bf16[8,512,128]{2,1,0:T(8,128)(2,1)}), bf16[8,512,128]{2,1,0:T(8,128)(2,1)}, u32[]{:S(2)}, u32[]{:S(2)}) async-start(bf16[8,512,128]{2,1,0:T(8,128)(2,1)} %bitcast.257), calls=%async_computation.3 | async-start | bytes 2097152 | tf_op jit(solution)/shard_map/all_to_all | solution.py:973
  358.4 49.4 %all-to-all-start.4 = ((bf16[8,512,128]{2,1,0:T(8,128)(2,1)}), bf16[8,512,128]{2,1,0:T(8,128)(2,1)S(1)}, u32[]{:S(2)}, u32[]{:S(2)}) async-start(bf16[8,512,128]{2,1,0:T(8,128)(2,1)} %get-tuple-element.112), calls=%async_computation.4 | async-start | bytes 2097152 | tf_op jit(solution)/shard_map/all_to_all | solution.py:973
  407.8 65.7 %all-to-all-start.5 = ((bf16[8,512,128]{2,1,0:T(8,128)(2,1)}), bf16[8,512,128]{2,1,0:T(8,128)(2,1)S(1)}, u32[]{:S(2)}, u32[]{:S(2)}) async-start(bf16[8,512,128]{2,1,0:T(8,128)(2,1)} %get-tuple-element.113), calls=%async_computation.5 | async-start | bytes 2097152 | tf_op jit(solution)/shard_map/all_to_all | solution.py:973
  474.5 102.3 %all-to-all-start.7 = ((bf16[8,512,384]{2,1,0:T(8,128)(2,1)}), bf16[8,512,384]{2,1,0:T(8,128)(2,1)S(1)}, u32[]{:S(2)}, u32[]{:S(2)}) async-start(bf16[8,512,384]{2,1,0:T(8,128)(2,1)} %bitcast.248), calls=%async_computation.7 | async-start | bytes 6291456 | tf_op jit(solution)/shard_map/all_to_all | solution.py:973
  496.6 88.8 %collective-permute-start.25 = (bf16[4,1024,512]{2,1,0:T(8,128)(2,1)}, bf16[4,1024,512]{2,1,0:T(8,128)(2,1)}, u32[]{:S(2)}, u32[]{:S(2)}) collective-permute-start(bf16[4,1024,512]{2,1,0:T(8,128)(2,1)} %get-tuple-element.125), channel_id=1, source_target_pairs={{0,8},{8,0},{16,24},{24,16},{1,9},{9,1},{17,25},{25,17},{2,10},{10... | collective-permute-start | bytes 12582920 | tf_op jit(solution)/shard_map/ppermute | solution.py:30
  517.1 68.4 %collective-permute-start.26 = (bf16[2,256,5120]{2,1,0:T(8,128)(2,1)}, bf16[2,256,5120]{2,1,0:T(8,128)(2,1)}, u32[]{:S(2)}, u32[]{:S(2)}) collective-permute-start(bf16[2,256,5120]{2,1,0:T(8,128)(2,1)} %get-tuple-element.134), channel_id=1, source_target_pairs={{0,8},{8,0},{16,24},{24,16},{1,9},{9,1},{17,25},{25,17},{2,10},{10... | collective-permute-start | bytes 15728648 | tf_op jit(solution)/shard_map/ppermute | solution.py:30
  578.5 82.8 %all-to-all-start.6 = ((bf16[8,512,384]{2,1,0:T(8,128)(2,1)}), bf16[8,512,384]{2,1,0:T(8,128)(2,1)}, u32[]{:S(2)}, u32[]{:S(2)}) async-start(bf16[8,512,384]{2,1,0:T(8,128)(2,1)} %bitcast.247), calls=%async_computation.6 | async-start | bytes 6291456 | tf_op jit(solution)/shard_map/all_to_all | solution.py:973
  584.5 117.1 %all-gather.6.cloned.1.call-start = ((), (), s32[]{:S(2)}) async-start(), calls=%async_computation.9 | async-start | bytes 2973696 | tf_op jit(solution)/shard_map/all_gather | solution.py:1041
  590.5 77.6 %collective-permute-start.28 = (bf16[256,5120]{1,0:T(8,128)(2,1)}, bf16[256,5120]{1,0:T(8,128)(2,1)}, u32[]{:S(2)}, u32[]{:S(2)}) collective-permute-start(bf16[256,5120]{1,0:T(8,128)(2,1)} %fusion), channel_id=1, source_target_pairs={{0,16},{8,24},{16,0},{24,8},{1,17},{9,25},{17,1},{25,9},{2,18},{10... | collective-permute-start | bytes 7864328 | tf_op jit(solution)/shard_map/ppermute | solution.py:30
  595.5 72.6 %collective-permute-start.27 = (bf16[2,1024,512]{2,1,0:T(8,128)(2,1)}, bf16[2,1024,512]{2,1,0:T(8,128)(2,1)}, u32[]{:S(2)}, u32[]{:S(2)}) collective-permute-start(bf16[2,1024,512]{2,1,0:T(8,128)(2,1)} %add_convert_fusion.1), channel_id=1, source_target_pairs={{0,1},{1,0},{2,3},{3,2},{4,5},{5,4},{6,7},{7,6},{8,9},{9,8},{10,11... | collective-permute-start | bytes 6291464 | tf_op jit(solution)/shard_map/ppermute | solution.py:30
  725.0 88.1 %collective-permute-start.35 = (bf16[256,3072]{1,0:T(8,128)(2,1)}, bf16[256,3072]{1,0:T(8,128)(2,1)}, u32[]{:S(2)}, u32[]{:S(2)}) collective-permute-start(bf16[256,3072]{1,0:T(8,128)(2,1)} %fusion.5), channel_id=1, source_target_pairs={{0,16},{8,24},{16,0},{24,8},{1,17},{9,25},{17,1},{25,9},{2,18},{10... | collective-permute-start | bytes 4718600 | tf_op jit(solution)/shard_map/ppermute | solution.py:30
  (94 other events, 1254.5 us)
Sparse Core Ops, SparseCore 0:
  14.9 92.0 all-gather.3
  588.7 94.5 all-gather.5

commit v8 on v7

--- a/solution.py
+++ b/solution.py
@@ -507,7 +507,8 @@
 
 
 def weight_grad_kernel(index_ref, *refs, clips, counts, widths, owners, swapped):
-    send_ref, keep_ref, flat_ref = refs[-3:]
+    outs = refs[-1 - len(COLUMN_PLACES if swapped else ROW_FLIPS) : -1]
+    flat_ref = refs[-1]
     step = pl.program_id(0)
     first, taken = 0, 0
     for count, steps in zip(counts, widths):
@@ -532,20 +533,16 @@
                 total += dot(flat_ref[:, c * rows : (c + 1) * rows], right[c][...])
             total = total.astype(bf16)
             if swapped:
-
-                @pl.when(step < pl.num_programs(0) // 2)
-                def _():
-                    send_ref[0] = total
-
-                @pl.when(step >= pl.num_programs(0) // 2)
-                def _():
-                    keep_ref[0] = total
+                for ref, (start, blocks) in zip(outs, COLUMN_PLACES):
+
+                    @pl.when((step >= start) & (step < start + blocks))
+                    def _(ref=ref):
+                        ref[0] = total
 
             else:
-                half = total.shape[0] // 2
-                for ref, part in ((send_ref, total[:half]), (keep_ref, total[half:])):
-                    for i in range(ref.shape[0]):
-                        ref[i] = part[i * ref.shape[1] : (i + 1) * ref.shape[1]]
+                height = total.shape[0] // len(outs)
+                for place, ref in enumerate(outs):
+                    ref[...] = total[place * height : (place + 1) * height]
 
         first += steps
 
@@ -570,6 +567,8 @@
 
 
 BLOCK = 512
+ROW_FLIPS = (3, 1, 2, 0)
+COLUMN_PLACES = ((0, 2), (2, 1), (3, 1), (4, 2), (6, 1), (7, 1))
 
 
 def rows_grad(pairs):
@@ -589,15 +588,15 @@
         in_specs += [pl.BlockSpec((rows, BLOCK), where)] * clips
         operands += right
         first += steps
-    shape = (2, height, first * BLOCK)
-    spec = pl.BlockSpec((2, height, BLOCK), lambda j, q: (0, 0, j))
+    shape = (height, first * BLOCK)
+    spec = pl.BlockSpec((height, BLOCK), lambda j, q: (0, j))
     return weight_grad_call(
         in_specs,
         operands,
-        jnp.stack([mine ^ 3, mine ^ 1, mine ^ 2, mine]),
+        jnp.stack([mine ^ flip for flip in ROW_FLIPS]),
         first,
-        (shape, shape),
-        (spec, spec),
+        [shape] * 4,
+        [spec] * 4,
         width,
         clips * rows,
         clips=clips,
@@ -620,17 +619,16 @@
     indices = jnp.stack([block(c ^ 1, s) for c, s in flips] + [block(c, s) for c, s in flips])
     in_specs = [pl.BlockSpec((rows, width), lambda j, q: (0, 0))] * clips
     in_specs += [pl.BlockSpec((rows, BLOCK), lambda j, q: (0, q[j]))] * clips
-    shape = (4, width, BLOCK)
+    def place_index(start, blocks, j, q):
+        return (jnp.clip(j - start, 0, blocks - 1), 0, 0)
+
     return weight_grad_call(
         in_specs,
         right + left,
         indices,
         8,
-        (shape, shape),
-        (
-            pl.BlockSpec((1, width, BLOCK), lambda j, q: (jnp.minimum(j, 3), 0, 0)),
-            pl.BlockSpec((1, width, BLOCK), lambda j, q: (jnp.maximum(j - 4, 0), 0, 0)),
-        ),
+        [(blocks, width, BLOCK) for _, blocks in COLUMN_PLACES],
+        [pl.BlockSpec((1, width, BLOCK), functools.partial(place_index, *place)) for place in COLUMN_PLACES],
         width,
         clips * rows,
         clips=clips,
@@ -1044,21 +1042,21 @@
     for c in range(clips):
         if c == clips - 1:
             active = gate(active, *d_qkv, d_mixed[-1])
-            down_send, down_keep = columns_grad(active, d_mlp)
-            down_core = swap_bit(down_send, "clip", 1)
-            normed_two = gate(normed_two, down_send)
-            up_send, up_keep = rows_grad([(normed_two, d_hidden), (mixed_all, d_attn)])
-            up_core = swap_bit(up_send, "clip", 1)
-        grad = after(d_mixed[c], results[-1][8] if c == 0 else up_send)
+            down_parts = columns_grad(active, d_mlp)
+            down_core = [swap_bit(p, "clip", 1) for p in down_parts[:3]]
+            normed_two = gate(normed_two, down_parts[0])
+            up_parts = rows_grad([(normed_two, d_hidden), (mixed_all, d_attn)])
+            up_core = [swap_bit(p, "clip", 1) for p in up_parts[:2]]
+        grad = after(d_mixed[c], results[-1][8] if c == 0 else up_parts[0])
         grad = grad.reshape(total, span)
         d_qkv.append(attend_back(qkv[c].reshape(total, 3 * span), grad, fulls[c], logs[c], cos_all, sin_all, span))
         sent = d_qkv[c].reshape(seq_devices, rows, 3 * span)
         exchanged.append(exchange(after(sent, d_mixed[-1]) if c == 0 else sent))
 
-    down_core, up_core = gate((down_core, up_core), exchanged[0])
-    down_sent = rounded_sum([down_keep[:2], down_core[:2]])
+    down_core = gate(down_core, exchanged[0])
+    down_sent = rounded_sum([down_parts[3], down_core[0]])
     down_along = swap_bit(down_sent, "seq", 1)
-    up_sent = rounded_sum([up_keep[0], up_core[0]])
+    up_sent = rounded_sum([up_parts[2], after(up_core[0], exchanged[0])])
     up_across = swap_bit(up_sent, "clip", 2)
     exchanged[0] = after(exchanged[0], down_sent, up_sent)
     exchanged[-1] = after(exchanged[-1], down_along, up_across)
@@ -1068,18 +1066,17 @@
         grads = last[-1][0] if last else None
         last.append(project_back(exchanged[c], full_qkv, tokens, c, mods_one[c][1], results[c][1], grads))
     d_projected = [r[1] for r in last]
-    qkv_send, qkv_keep = rows_grad([(normed, d_projected)])
-    qkv_core = swap_bit(qkv_send, "clip", 1)
-    qkv_sent = rounded_sum([qkv_keep[0], qkv_core[0]])
+    qkv_parts = rows_grad([(normed, d_projected)])
+    qkv_core = [swap_bit(p, "clip", 1) for p in qkv_parts[:2]]
+    qkv_sent = rounded_sum([qkv_parts[2], qkv_core[0]])
     qkv_across = swap_bit(qkv_sent, "clip", 2)
-    down_far = rounded_sum([down_keep[3], down_core[3], after(down_along[1], qkv_send)])
-    down_across = swap_bit(down_far, "clip", 2)
     near_seq = axis_bits("seq")[::-1]
-    grad_up = halve([up_keep[1], up_core[1], up_across], near_seq, 0, qkv_sent)
-    down_addends = [down_keep[2], down_core[2], down_along[0], after(down_across, qkv_sent)]
-    grad_down = jnp.transpose(halve(down_addends, near_seq[1:], 1))
-    qkv_last = after(qkv_across, up_across)
-    grad_qkv = halve([qkv_keep[1], qkv_core[1], qkv_last], near_seq, 0)
+    down_along, up_across = after(down_along, qkv_sent), after(up_across, qkv_sent)
+    down_across = swap_bit(rounded_sum([down_parts[5][0], down_core[2][0], down_along[1]]), "clip", 2)
+    grad_up = halve([up_parts[3], up_core[1], up_across], near_seq, 0)
+    down_own = sum(a.astype(f32) for a in (down_parts[4][0], down_core[1][0], down_along[0]))
+    grad_down = jnp.transpose(halve([down_own, down_across], near_seq[1:], 1))
+    grad_qkv = halve([qkv_parts[3], qkv_core[1], qkv_across], near_seq, 0)
     grad_out = grad_up[:, 4 * width :]
     grad_up = reorder(grad_up[:, : 4 * width])
     late_rows = with_bias([line_sums(r[2]) for r in last], [sum(r[3][0] for r in last)])

time: 876 us -> 881 us (level)
  waiting for transfers between devices: 238 us -> 265 us
  local copies, waits for them, and re-layouts: 80.7 us -> 63.7 us
    slice x7 -> x0, local copies, waits for them, and re-layouts: 17.4 us -> none  [the longest x2 5.27 us: body_by_heads(): grad_up = halve([up_keep[1], up_core[1], up_across], near_seq, 0, qkv_sent)]
    ppermute x45 -> x49, waiting for transfers between devices: 140 us -> 155 us  [swap_bit(): return lax.ppermute(value, axis, [(i, i ^ bit) for i in range(count)])]
    ppermute x45 -> x49, starting transfers between devices: 64 us -> 56.9 us  [swap_bit(): return lax.ppermute(value, axis, [(i, i ^ bit) for i in range(count)])]
    unnamed x131 -> x109, local copies, waits for them, and re-layouts: 18.3 us -> 21.9 us
  transfers between devices with their start and end apart: 55 -> 59, of which waited for: 21 -> 19; matrix products, arithmetic and copies ran while one was open for 15% -> 13% of each run, Pallas kernels for 40% -> 40%
where the time goes in v8:
time: 881 us; the launch traced here: 871 us
  Pallas kernels  348 us (40%)
  waiting for transfers between devices  265 us (30%)
  starting transfers between devices  99.8 us (11%)
  other arithmetic  73.8 us (8%)
  local copies, waits for them, and re-layouts  63.7 us (7%)
  between operations  16 us (2%)
    ppermute x49, waiting for transfers between devices, swap_bit(): return lax.ppermute(value, axis, [(i, i ^ bit) for i in range(count)])  155 us
    pallas_call x2, Pallas kernels, attend_back(): pl.pallas_call(functools.partial(attend_back_kernel, total=total, span=sp...  118 us
    all_to_all x8, waiting for transfers between devices, exchange(): return lax.all_to_all(value, 'seq', 0, 0, tiled=True)  99.3 us
    pallas_call x2, Pallas kernels, middle(): pl.pallas_call(middle_kernel, grid_spec=pltpu.PrefetchScalarGridSpec(num_...  76.4 us
    pallas_call x2, Pallas kernels, attend(): pl.pallas_call(functools.partial(attend_kernel, total=total, span=span, b...  70.6 us
    ppermute x49, starting transfers between devices, swap_bit(): return lax.ppermute(value, axis, [(i, i ^ bit) for i in range(count)])  56.9 us
    pallas_call x3, Pallas kernels, weight_grad_call(): pl.pallas_call(functools.partial(weight_grad_kernel, **options), grid_spe...  50.7 us
    all_to_all x8, starting transfers between devices, exchange(): return lax.all_to_all(value, 'seq', 0, 0, tiled=True)  42.9 us
  transfers between devices with their start and end apart: 59, of which 19 were waited for; matrix products, arithmetic and copies ran while one was open for 13% of the time, Pallas kernels for 40%

profile of v8, /device:TPU:0, one launch (start us, length us, event | category | flops | bytes accessed | tf_op | source)
XLA Modules:
  0.0 870.6 jit_solution(4773643300685054042)
XLA Ops:
  31.9 15.2 %collective-permute-done.7 = bf16[1,4,32,1024]{3,2,1,0:T(8,128)(2,1)} collective-permute-done((bf16[1,4,32,1024]{3,2,1,0:T(8,128)(2,1)}, bf16[1,4,32,1024]{3,2,1,0:T(8,128)(2,1)}, u32[]{:S(2)}, u32[]{:S(2)}) %collective-permute-start.7) | collective-permute-done | bytes 262176 | tf_op jit(solution)/shard_map/ppermute | solution.py:30
  53.2 11.8 %collective-permute-done.3 = f32[32,2816]{1,0:T(8,128)S(1)} collective-permute-done((f32[32,2816]{1,0:T(8,128)S(1)}, f32[32,2816]{1,0:T(8,128)S(1)}, u32[]{:S(2)}, u32[]{:S(2)}) %collective-permute-start.3) | collective-permute-done | bytes 360480 | tf_op jit(solution)/shard_map/ppermute | solution.py:30
  74.4 19.5 %collective-permute-done.10 = bf16[2,5,32,1024]{3,2,1,0:T(8,128)(2,1)S(1)} collective-permute-done((bf16[2,5,32,1024]{3,2,1,0:T(8,128)(2,1)S(1)}, bf16[2,5,32,1024]{3,2,1,0:T(8,128)(2,1)S(1)}, u32[]{:S(2)}, u32[]{:S(2)}) %collective-permute-start.10) | collective-permute-done | bytes 655392 | tf_op jit(solution)/shard_map/ppermute | solution.py:30
  103.1 10.6 %all-gather.4.cloned.1.call-done.wq_ref.wk_ref.wv_ref = bf16[1024,3072]{1,0:T(8,128)(2,1)} async-done(((bf16[32,3072]{1,0:T(8,128)(2,1)}), bf16[1024,3072]{1,0:T(8,128)(2,1)}) %all-gather.4.cloned.1.call-update) | async-done | bytes 6291472 | tf_op jit(solution)/shard_map/all_gather | solution.py:924
  143.4 8.0 collective-permute-done.14
  166.4 35.4 %all-to-all-done = bf16[8,512,384]{2,1,0:T(8,128)(2,1)} async-done(((bf16[8,512,384]{2,1,0:T(8,128)(2,1)}), bf16[8,512,384]{2,1,0:T(8,128)(2,1)}, u32[]{:S(2)}, u32[]{:S(2)}) %all-to-all-start) | async-done | bytes 3145760 | tf_op jit(solution)/shard_map/all_to_all | solution.py:971
  216.1 35.3 %attend.3 = (bf16[4096,128]{1,0:T(8,128)(2,1)}, f32[4096,128]{1,0:T(8,128)}, f32[2,4096]{1,0:T(2,128)}) custom-call(bf16[4096,384]{1,0:T(8,128)(2,1)} %bitcast.37.qkv_ref), custom_call_target="tpu_custom_call" | custom-call | flops 17179869184 | bytes 6291456 | tf_op jit(solution)/shard_map/attend/pallas_call | solution.py:729
  251.4 10.3 %collective-permute-done.16 = f32[8,5632]{1,0:T(8,128)S(1)} collective-permute-done((f32[8,5632]{1,0:T(8,128)S(1)}, f32[8,5632]{1,0:T(8,128)S(1)}, u32[]{:S(2)}, u32[]{:S(2)}) %collective-permute-start.16) | collective-permute-done | bytes 180256 | tf_op jit(solution)/shard_map/ppermute | solution.py:30
  261.7 15.2 %all-to-all-done.1 = bf16[8,512,384]{2,1,0:T(8,128)(2,1)} async-done(((bf16[8,512,384]{2,1,0:T(8,128)(2,1)}), bf16[8,512,384]{2,1,0:T(8,128)(2,1)}, u32[]{:S(2)}, u32[]{:S(2)}) %all-to-all-start.1) | async-done | bytes 3145760 | tf_op jit(solution)/shard_map/all_to_all | solution.py:971
  284.5 35.3 %attend.2 = (bf16[4096,128]{1,0:T(8,128)(2,1)}, f32[4096,128]{1,0:T(8,128)}, f32[2,4096]{1,0:T(2,128)}) custom-call(bf16[4096,384]{1,0:T(8,128)(2,1)} %bitcast.35.qkv_ref), custom_call_target="tpu_custom_call" | custom-call | flops 17179869184 | bytes 6291456 | tf_op jit(solution)/shard_map/attend/pallas_call | solution.py:729
  326.9 38.2 %middle.2 = (bf16[2,512,1024]{2,1,0:T(8,128)(2,1)}, f32[512,1024]{1,0:T(8,128)}, bf16[512,1024]{1,0:T(8,128)(2,1)}, bf16[512,1024]{1,0:T(8,128)(2,1)}, bf16[512,...) custom-call(s32[1]{0:T(128)} %bitcast.clip_ref, ...), custom_call_target="tpu_custom_call" | custom-call | flops 2147483648 | bytes 4718592 | tf_op jit(solution)/shard_map/middle/pallas_call | solution.py:446
  376.2 38.2 %middle.3 = (bf16[2,512,1024]{2,1,0:T(8,128)(2,1)}, f32[512,1024]{1,0:T(8,128)}, bf16[512,1024]{1,0:T(8,128)(2,1)}, bf16[512,1024]{1,0:T(8,128)(2,1)}, bf16[512,...) custom-call(s32[1]{0:T(128)} %bitcast.clip_ref, ...), custom_call_target="tpu_custom_call", output_to_operand_aliasing={{0}: (20, {})} | custom-call | flops 2147483648 | bytes 4718592 | tf_op jit(solution)/shard_map/middle/pallas_call | solution.py:446
  420.9 59.2 %attend_back.2 = bf16[4096,384]{1,0:T(8,128)(2,1)} custom-call(bf16[4096,384]{1,0:T(8,128)(2,1)} %bitcast.37.qkv_ref, bf16[4096,128]{1,0:T(8,128)(2,1)} %bitcast.196, f32[4096,128]{1,0:T(8,128)} %get-tuple-element.129.full_ref, f32[2,4096]{1,0:T(2,128)} %get-tuple-element.130.log_ref, f32[4096,128]{1,0:T(8,128)} %bitcast.193, f32[4096,128]{1,0:T(8,128)} %bitcast.191), custom_call_target="tpu_custom_call" | custom-call | flops 42949672960 | bytes 13631488 | tf_op jit(solution)/shard_map/attend_back/pallas_call | solution.py:824
  487.1 17.5 %weight_grad.3 = (bf16[2,1024,512]{2,1,0:T(8,128)(2,1)}, bf16[1,1024,512]{2,1,0:T(8,128)(2,1)}, bf16[1,1024,512]{2,1,0:T(8,128)(2,1)}, bf16[2,1024,512]{2,1,0:T(...) custom-call(s32[8]{0:T(128)} %stack.141.index_ref, ...), custom_call_target="tpu_custom_call" | custom-call | flops 8589934592 | bytes 20971520 | tf_op jit(solution)/shard_map/weight_grad/pallas_call | solution.py:551
  504.6 20.5 %weight_grad.4 = (bf16[256,5120]{1,0:T(8,128)(2,1)}, bf16[256,5120]{1,0:T(8,128)(2,1)}, bf16[256,5120]{1,0:T(8,128)(2,1)}, bf16[256,5120]{1,0:T(8,128)(2,1)}) custom-call(s32[4]{0:T(128)} %pad_add_fusion.5.index_ref, bf16[512,1024]{1,0:T(8,128)(2,1)} %get-tuple-element.134.refs_0_.refs_1_.refs_2_.refs_3_, ...), custom_call_target="tpu_custom_call" | custom-call | flops 10737418240 | bytes 25165824 | tf_op jit(solution)/shard_map/weight_grad/pallas_call | solution.py:551
  526.2 59.3 %attend_back.3 = bf16[4096,384]{1,0:T(8,128)(2,1)} custom-call(bf16[4096,384]{1,0:T(8,128)(2,1)} %bitcast.35.qkv_ref, bf16[4096,128]{1,0:T(8,128)(2,1)} %bitcast.198, f32[4096,128]{1,0:T(8,128)} %get-tuple-element.144.full_ref, f32[2,4096]{1,0:T(2,128)} %get-tuple-element.145.log_ref, f32[4096,128]{1,0:T(8,128)} %bitcast.194, f32[4096,128]{1,0:T(8,128)} %bitcast.192), custom_call_target="tpu_custom_call" | custom-call | flops 42949672960 | bytes 13631488 | tf_op jit(solution)/shard_map/attend_back/pallas_call | solution.py:824
  610.0 9.4 %project_back.2 = (f32[2,512,1024]{2,1,0:T(8,128)}, bf16[512,3072]{1,0:T(8,128)(2,1)S(1)}, f32[2,2,1024]{2,1,0:T(2,128)S(1)}, f32[1,3072]{1,0:T(1,128)S(1)}) custom-call(bf16[8,512,384]{2,1,0:T(8,128)(2,1)S(1)} %copy-done.4, bf16[1024,3072]{1,0:T(8,128)(2,1)} %all-gather.4.cloned.1.call-done.wq_ref.wk_ref.wv_ref, ...), custom_call_target="tpu_custom_call" | custom-call | flops 3221225472 | bytes 17825792 | tf_op jit(solution)/shard_map/project_back/pallas_call | solution.py:263
  621.2 48.7 %all-to-all-done.6.back_ref = bf16[8,512,384]{2,1,0:T(8,128)(2,1)} async-done(((bf16[8,512,384]{2,1,0:T(8,128)(2,1)}), bf16[8,512,384]{2,1,0:T(8,128)(2,1)}, u32[]{:S(2)}, u32[]{:S(2)}) %all-to-all-start.6) | async-done | bytes 3145760 | tf_op jit(solution)/shard_map/all_to_all | solution.py:971
  679.3 9.8 %project_back.3 = (f32[2,512,1024]{2,1,0:T(8,128)}, bf16[512,3072]{1,0:T(8,128)(2,1)S(1)}, f32[2,2,1024]{2,1,0:T(2,128)S(1)}, f32[1,3072]{1,0:T(1,128)S(1)}) custom-call(bf16[8,512,384]{2,1,0:T(8,128)(2,1)} %all-to-all-done.6.back_ref, bf16[1024,3072]{1,0:T(8,128)(2,1)} %all-gather.4.cloned.1.call-done.wq_ref.wk_ref.wv_ref, ...), custom_call_target="tpu_custom_call", output_to_operand_aliasing={{0}: (7, {})} | custom-call | flops 3221225472 | bytes 17825792 | tf_op jit(solution)/shard_map/project_back/pallas_call | solution.py:263
  690.7 12.7 %weight_grad.5 = (bf16[256,3072]{1,0:T(8,128)(2,1)}, bf16[256,3072]{1,0:T(8,128)(2,1)}, bf16[256,3072]{1,0:T(8,128)(2,1)}, bf16[256,3072]{1,0:T(8,128)(2,1)}) custom-call(s32[4]{0:T(128)} %pad_add_fusion.5.index_ref, bf16[512,1024]{1,0:T(8,128)(2,1)} %copy-done.11, bf16[512,1024]{1,0:T(8,128)(2,1)} %copy-done.11, bf16[512,1024]{1,0:T(8,128)(2,1)} %copy-done.11, ...), custom_call_target="tpu_custom_call" | custom-call | flops 6442450944 | bytes 16777216 | tf_op jit(solution)/shard_map/weight_grad/pallas_call | solution.py:551
  738.6 21.5 %collective-permute-done.34 = f32[16,2816]{1,0:T(8,128)S(1)} collective-permute-done((f32[16,2816]{1,0:T(8,128)S(1)}, f32[16,2816]{1,0:T(8,128)S(1)}, u32[]{:S(2)}, u32[]{:S(2)}) %collective-permute-start.34) | collective-permute-done | bytes 180256 | tf_op jit(solution)/shard_map/ppermute | solution.py:30
  764.0 18.7 %collective-permute-done.35 = f32[32,2816]{1,0:T(8,128)} collective-permute-done((f32[32,2816]{1,0:T(8,128)S(1)}, f32[32,2816]{1,0:T(8,128)}, u32[]{:S(2)}, u32[]{:S(2)}) %collective-permute-start.35) | collective-permute-done | bytes 360480 | tf_op jit(solution)/shard_map/ppermute | solution.py:30
  814.5 14.3 %collective-permute-done.48 = bf16[1024,128]{1,0:T(8,128)(2,1)S(1)} collective-permute-done((bf16[1024,128]{1,0:T(8,128)(2,1)S(1)}, bf16[1024,128]{1,0:T(8,128)(2,1)S(1)}, u32[]{:S(2)}, u32[]{:S(2)}) %collective-permute-start.48) | collective-permute-done | bytes 262176 | tf_op jit(solution)/shard_map/ppermute | solution.py:30
  837.4 12.4 %collective-permute-done.40 = bf16[64,3072]{1,0:T(8,128)(2,1)S(1)} collective-permute-done((bf16[64,3072]{1,0:T(8,128)(2,1)S(1)}, bf16[64,3072]{1,0:T(8,128)(2,1)S(1)}, u32[]{:S(2)}, u32[]{:S(2)}) %collective-permute-start.40) | collective-permute-done | bytes 393248 | tf_op jit(solution)/shard_map/ppermute | solution.py:30
  (385 shorter events, 277.7 us)
Async XLA Ops:
  7.2 106.5 %all-gather.4.cloned.1.call-start = ((), (), s32[]{:S(2)}) async-start(), calls=%async_computation.8 | async-start | bytes 6488064 | tf_op jit(solution)/shard_map/all_gather | solution.py:924
  31.9 98.5 %collective-permute-start.13 = (f32[64,5632]{1,0:T(8,128)}, f32[64,5632]{1,0:T(8,128)}, u32[]{:S(2)}, u32[]{:S(2)}) collective-permute-start(f32[64,5632]{1,0:T(8,128)} %constant_dynamic-slice_fusion.4), channel_id=1, source_target_pairs={{0,8},{8,0},{16,24},{24,16},{1,9},{9,1},{17,25},{25,17},{2,10},{10... | collective-permute-start | bytes 4325384 | tf_op jit(solution)/shard_map/ppermute | solution.py:30
  72.7 61.3 %collective-permute-start.11 = (bf16[4,4,32,1024]{3,2,1,0:T(8,128)(2,1)}, bf16[4,4,32,1024]{3,2,1,0:T(8,128)(2,1)}, u32[]{:S(2)}, u32[]{:S(2)}) collective-permute-start(bf16[4,4,32,1024]{3,2,1,0:T(8,128)(2,1)} %bitcast.18), channel_id=1, source_target_pairs={{0,1},{1,0},{2,3},{3,2},{4,5},{5,4},{6,7},{7,6},{8,9},{9,8},{10,11... | collective-permute-start | bytes 3145736 | tf_op jit(solution)/shard_map/ppermute | solution.py:30
  125.7 76.1 %all-to-all-start = ((bf16[8,512,384]{2,1,0:T(8,128)(2,1)}), bf16[8,512,384]{2,1,0:T(8,128)(2,1)}, u32[]{:S(2)}, u32[]{:S(2)}) async-start(bf16[8,512,384]{2,1,0:T(8,128)(2,1)} %copy-done.5), calls=%async_computation | async-start | bytes 6291456 | tf_op jit(solution)/shard_map/all_to_all | solution.py:971
  137.1 189.7 %collective-permute-start.23 = (bf16[4,2,4,32,1024]{4,3,2,1,0:T(8,128)(2,1)}, bf16[4,2,4,32,1024]{4,3,2,1,0:T(8,128)(2,1)}, u32[]{:S(2)}, u32[]{:S(2)}) collective-permute-start(bf16[4,2,4,32,1024]{4,3,2,1,0:T(8,128)(2,1)} %pad_maximum_fusion.2.refs_8_), channel_id=1, source_target_pairs={{0,8},{8,0},{16,24},{24,16},{1,9},{9,1},{17,25},{25,17},{2,10},{10... | collective-permute-start | bytes 6291464 | tf_op jit(solution)/shard_map/ppermute | solution.py:30
  137.1 182.7 %collective-permute-start.22 = (bf16[8,4,32,1024]{3,2,1,0:T(8,128)(2,1)}, bf16[8,4,32,1024]{3,2,1,0:T(8,128)(2,1)}, u32[]{:S(2)}, u32[]{:S(2)}) collective-permute-start(bf16[8,4,32,1024]{3,2,1,0:T(8,128)(2,1)} %bitcast.33), channel_id=1, source_target_pairs={{0,16},{8,24},{16,0},{24,8},{1,17},{9,25},{17,1},{25,9},{2,18},{10... | collective-permute-start | bytes 6291464 | tf_op jit(solution)/shard_map/ppermute | solution.py:30
  141.3 67.2 %collective-permute-start.20 = (bf16[4,2,5,32,1024]{4,3,2,0,1:T(8,128)(2,1)}, bf16[4,2,5,32,1024]{4,3,2,0,1:T(8,128)(2,1)}, u32[]{:S(2)}, u32[]{:S(2)}) collective-permute-start(bf16[4,2,5,32,1024]{4,3,2,0,1:T(8,128)(2,1)} %pad_maximum_fusion), channel_id=1, source_target_pairs={{0,8},{8,0},{16,24},{24,16},{1,9},{9,1},{17,25},{25,17},{2,10},{10... | collective-permute-start | bytes 7864328 | tf_op jit(solution)/shard_map/ppermute | solution.py:30
  141.5 64.8 %collective-permute-start.19 = (bf16[4,5,32,1024]{3,2,1,0:T(8,128)(2,1)}, bf16[4,5,32,1024]{3,2,1,0:T(8,128)(2,1)}, u32[]{:S(2)}, u32[]{:S(2)}) collective-permute-start(bf16[4,5,32,1024]{3,2,1,0:T(8,128)(2,1)} %collective-permute-done.12), channel_id=1, source_target_pairs={{0,1},{1,0},{2,3},{3,2},{4,5},{5,4},{6,7},{7,6},{8,9},{9,8},{10,11... | collective-permute-start | bytes 3932168 | tf_op jit(solution)/shard_map/ppermute | solution.py:30
  151.5 61.5 %collective-permute-start.15 = (f32[16,5632]{1,0:T(8,128)S(1)}, f32[16,5632]{1,0:T(8,128)}, u32[]{:S(2)}, u32[]{:S(2)}) collective-permute-start(f32[16,5632]{1,0:T(8,128)S(1)} %constant_dynamic-slice_fusion.2), channel_id=1, source_target_pairs={{0,1},{1,0},{2,3},{3,2},{4,5},{5,4},{6,7},{7,6},{8,9},{9,8},{10,11... | collective-permute-start | bytes 1081352 | tf_op jit(solution)/shard_map/ppermute | solution.py:30
  201.8 75.0 %all-to-all-start.1 = ((bf16[8,512,384]{2,1,0:T(8,128)(2,1)}), bf16[8,512,384]{2,1,0:T(8,128)(2,1)}, u32[]{:S(2)}, u32[]{:S(2)}) async-start(bf16[8,512,384]{2,1,0:T(8,128)(2,1)} %copy-done.6), calls=%async_computation.1 | async-start | bytes 6291456 | tf_op jit(solution)/shard_map/all_to_all | solution.py:971
  414.4 65.7 %all-to-all-start.5 = ((bf16[8,512,128]{2,1,0:T(8,128)(2,1)}), bf16[8,512,128]{2,1,0:T(8,128)(2,1)S(1)}, u32[]{:S(2)}, u32[]{:S(2)}) async-start(bf16[8,512,128]{2,1,0:T(8,128)(2,1)} %get-tuple-element.121), calls=%async_computation.5 | async-start | bytes 2097152 | tf_op jit(solution)/shard_map/all_to_all | solution.py:971
  481.1 104.4 %all-to-all-start.7 = ((bf16[8,512,384]{2,1,0:T(8,128)(2,1)}), bf16[8,512,384]{2,1,0:T(8,128)(2,1)S(1)}, u32[]{:S(2)}, u32[]{:S(2)}) async-start(bf16[8,512,384]{2,1,0:T(8,128)(2,1)} %bitcast.188), calls=%async_computation.7 | async-start | bytes 6291456 | tf_op jit(solution)/shard_map/all_to_all | solution.py:971
  504.6 88.8 %collective-permute-start.25 = (bf16[2,1024,512]{2,1,0:T(8,128)(2,1)}, bf16[2,1024,512]{2,1,0:T(8,128)(2,1)}, u32[]{:S(2)}, u32[]{:S(2)}) collective-permute-start(bf16[2,1024,512]{2,1,0:T(8,128)(2,1)} %get-tuple-element.133), channel_id=1, source_target_pairs={{0,8},{8,0},{16,24},{24,16},{1,9},{9,1},{17,25},{25,17},{2,10},{10... | collective-permute-start | bytes 6291464 | tf_op jit(solution)/shard_map/ppermute | solution.py:30
  525.1 68.2 %collective-permute-start.29 = (bf16[256,5120]{1,0:T(8,128)(2,1)}, bf16[256,5120]{1,0:T(8,128)(2,1)}, u32[]{:S(2)}, u32[]{:S(2)}) collective-permute-start(bf16[256,5120]{1,0:T(8,128)(2,1)} %get-tuple-element.142), channel_id=1, source_target_pairs={{0,8},{8,0},{16,24},{24,16},{1,9},{9,1},{17,25},{25,17},{2,10},{10... | collective-permute-start | bytes 7864328 | tf_op jit(solution)/shard_map/ppermute | solution.py:30
  525.7 67.7 %collective-permute-start.26 = (bf16[1,1024,512]{2,1,0:T(8,128)(2,1)}, bf16[1,1024,512]{2,1,0:T(8,128)(2,1)}, u32[]{:S(2)}, u32[]{:S(2)}) collective-permute-start(bf16[1,1024,512]{2,1,0:T(8,128)(2,1)} %get-tuple-element.147), channel_id=1, source_target_pairs={{0,8},{8,0},{16,24},{24,16},{1,9},{9,1},{17,25},{25,17},{2,10},{10... | collective-permute-start | bytes 3145736 | tf_op jit(solution)/shard_map/ppermute | solution.py:30
  525.8 67.6 %collective-permute-start.27 = (bf16[1,1024,512]{2,1,0:T(8,128)(2,1)}, bf16[1,1024,512]{2,1,0:T(8,128)(2,1)}, u32[]{:S(2)}, u32[]{:S(2)}) collective-permute-start(bf16[1,1024,512]{2,1,0:T(8,128)(2,1)} %get-tuple-element.148), channel_id=1, source_target_pairs={{0,8},{8,0},{16,24},{24,16},{1,9},{9,1},{17,25},{25,17},{2,10},{10... | collective-permute-start | bytes 3145736 | tf_op jit(solution)/shard_map/ppermute | solution.py:30
  587.1 82.7 %all-to-all-start.6 = ((bf16[8,512,384]{2,1,0:T(8,128)(2,1)}), bf16[8,512,384]{2,1,0:T(8,128)(2,1)}, u32[]{:S(2)}, u32[]{:S(2)}) async-start(bf16[8,512,384]{2,1,0:T(8,128)(2,1)} %bitcast.187), calls=%async_computation.6 | async-start | bytes 6291456 | tf_op jit(solution)/shard_map/all_to_all | solution.py:971
  593.1 118.8 %all-gather.6.cloned.1.call-start = ((), (), s32[]{:S(2)}) async-start(), calls=%async_computation.9 | async-start | bytes 2973696 | tf_op jit(solution)/shard_map/all_gather | solution.py:1039
  598.6 79.1 %collective-permute-start.30 = (bf16[256,5120]{1,0:T(8,128)(2,1)}, bf16[256,5120]{1,0:T(8,128)(2,1)}, u32[]{:S(2)}, u32[]{:S(2)}) collective-permute-start(bf16[256,5120]{1,0:T(8,128)(2,1)} %add_convert_fusion), channel_id=1, source_target_pairs={{0,16},{8,24},{16,0},{24,8},{1,17},{9,25},{17,1},{25,9},{2,18},{10... | collective-permute-start | bytes 7864328 | tf_op jit(solution)/shard_map/ppermute | solution.py:30
  603.7 73.9 %collective-permute-start.28 = (bf16[2,1024,512]{2,1,0:T(8,128)(2,1)}, bf16[2,1024,512]{2,1,0:T(8,128)(2,1)}, u32[]{:S(2)}, u32[]{:S(2)}) collective-permute-start(bf16[2,1024,512]{2,1,0:T(8,128)(2,1)} %add_convert_fusion.1), channel_id=1, source_target_pairs={{0,1},{1,0},{2,3},{3,2},{4,5},{5,4},{6,7},{7,6},{8,9},{9,8},{10,11... | collective-permute-start | bytes 6291464 | tf_op jit(solution)/shard_map/ppermute | solution.py:30
  715.2 87.7 %collective-permute-start.37 = (bf16[256,3072]{1,0:T(8,128)(2,1)}, bf16[256,3072]{1,0:T(8,128)(2,1)}, u32[]{:S(2)}, u32[]{:S(2)}) collective-permute-start(bf16[256,3072]{1,0:T(8,128)(2,1)} %get-tuple-element.177), channel_id=1, source_target_pairs={{0,8},{8,0},{16,24},{24,16},{1,9},{9,1},{17,25},{25,17},{2,10},{10... | collective-permute-start | bytes 4718600 | tf_op jit(solution)/shard_map/ppermute | solution.py:30
  715.3 87.6 %collective-permute-start.38 = (bf16[256,3072]{1,0:T(8,128)(2,1)}, bf16[256,3072]{1,0:T(8,128)(2,1)}, u32[]{:S(2)}, u32[]{:S(2)}) collective-permute-start(bf16[256,3072]{1,0:T(8,128)(2,1)} %add_convert_fusion.2), channel_id=1, source_target_pairs={{0,16},{8,24},{16,0},{24,8},{1,17},{9,25},{17,1},{25,9},{2,18},{10... | collective-permute-start | bytes 4718600 | tf_op jit(solution)/shard_map/ppermute | solution.py:30
  725.2 70.8 %collective-permute-start.43 = (bf16[128,5120]{1,0:T(8,128)(2,1)}, bf16[128,5120]{1,0:T(8,128)(2,1)}, u32[]{:S(2)}, u32[]{:S(2)}) collective-permute-start(bf16[128,5120]{1,0:T(8,128)(2,1)} %add_convert_fusion.3), channel_id=1, source_target_pairs={{0,1},{1,0},{2,3},{3,2},{4,5},{5,4},{6,7},{7,6},{8,9},{9,8},{10,11... | collective-permute-start | bytes 3932168 | tf_op jit(solution)/shard_map/ppermute | solution.py:30
  732.1 56.1 %collective-permute-start.46 = (bf16[1024,512]{1,0:T(8,128)(2,1)}, bf16[1024,512]{1,0:T(8,128)(2,1)}, u32[]{:S(2)}, u32[]{:S(2)}) collective-permute-start(bf16[1024,512]{1,0:T(8,128)(2,1)} %get-tuple-element.262), channel_id=1, source_target_pairs={{0,16},{8,24},{16,0},{24,8},{1,17},{9,25},{17,1},{25,9},{2,18},{10... | collective-permute-start | bytes 3145736 | tf_op jit(solution)/shard_map/ppermute | solution.py:30
  (87 other events, 1238.4 us)
Sparse Core Ops, SparseCore 0:
  16.1 97.5 all-gather.3
  606.5 84.8 all-gather.5

commit v9 on v8

--- a/solution.py
+++ b/solution.py
@@ -647,15 +647,15 @@
     return sum(a.astype(f32) for a in addends).astype(bf16)
 
 
-def halve(addends, bits, dim, hold=None):
-    for place, (axis, bit) in enumerate(bits):
+def halve(addends, bits, dim, trace=None):
+    for axis, bit in bits:
         half = addends[0].shape[dim] // 2
         mine = own_bit(axis, bit)
         send = rounded_sum([lax.dynamic_slice_in_dim(a, (1 - mine) * half, half, dim) for a in addends])
         addends = [lax.dynamic_slice_in_dim(a, mine * half, half, dim) for a in addends]
         received = swap_bit(send, axis, bit)
-        if hold is not None and place == 0:
-            received = after(received, hold)
+        if trace is not None:
+            trace.append((send, received))
         addends.append(received)
     return sum(a.astype(f32) for a in addends)
 
@@ -1047,40 +1047,49 @@
             normed_two = gate(normed_two, down_parts[0])
             up_parts = rows_grad([(normed_two, d_hidden), (mixed_all, d_attn)])
             up_core = [swap_bit(p, "clip", 1) for p in up_parts[:2]]
-        grad = after(d_mixed[c], results[-1][8] if c == 0 else up_parts[0])
+            down_sent = rounded_sum([down_parts[3], after(down_core[0], up_parts[0])])
+            down_along = swap_bit(down_sent, "seq", 1)
+            up_sent = rounded_sum([up_parts[2], after(up_core[0], down_sent)])
+            up_across = swap_bit(up_sent, "clip", 2)
+        grad = after(d_mixed[c], results[-1][8] if c == 0 else up_sent)
         grad = grad.reshape(total, span)
         d_qkv.append(attend_back(qkv[c].reshape(total, 3 * span), grad, fulls[c], logs[c], cos_all, sin_all, span))
         sent = d_qkv[c].reshape(seq_devices, rows, 3 * span)
-        exchanged.append(exchange(after(sent, d_mixed[-1]) if c == 0 else sent))
-
-    down_core = gate(down_core, exchanged[0])
-    down_sent = rounded_sum([down_parts[3], down_core[0]])
-    down_along = swap_bit(down_sent, "seq", 1)
-    up_sent = rounded_sum([up_parts[2], after(up_core[0], exchanged[0])])
-    up_across = swap_bit(up_sent, "clip", 2)
-    exchanged[0] = after(exchanged[0], down_sent, up_sent)
-    exchanged[-1] = after(exchanged[-1], down_along, up_across)
+        exchanged.append(exchange(after(sent, d_mixed[-1]) if c == 0 else after(sent, down_along, up_across)))
+
+    near_seq = axis_bits("seq")[::-1]
+    down_along, up_across = after(down_along, exchanged[0]), after(up_across, exchanged[0])
+    down_across = swap_bit(rounded_sum([down_parts[5][0], down_core[2][0], down_along[1]]), "clip", 2)
 
     last = []
     for c in range(clips):
         grads = last[-1][0] if last else None
+        if c == clips - 1:
+            half = up_parts[3].shape[0] // 2
+            theirs = (1 - own_bit(*near_seq[0])) * half
+            up_near = rounded_sum(
+                [lax.dynamic_slice_in_dim(a, theirs, half, 0) for a in (up_parts[3], up_core[1], up_across)]
+            )
+            up_near = swap_bit(up_near, *near_seq[0])
+            exchanged[-1] = after(exchanged[-1], up_near, down_across)
         last.append(project_back(exchanged[c], full_qkv, tokens, c, mods_one[c][1], results[c][1], grads))
     d_projected = [r[1] for r in last]
     qkv_parts = rows_grad([(normed, d_projected)])
     qkv_core = [swap_bit(p, "clip", 1) for p in qkv_parts[:2]]
     qkv_sent = rounded_sum([qkv_parts[2], qkv_core[0]])
     qkv_across = swap_bit(qkv_sent, "clip", 2)
-    near_seq = axis_bits("seq")[::-1]
-    down_along, up_across = after(down_along, qkv_sent), after(up_across, qkv_sent)
-    down_across = swap_bit(rounded_sum([down_parts[5][0], down_core[2][0], down_along[1]]), "clip", 2)
-    grad_up = halve([up_parts[3], up_core[1], up_across], near_seq, 0)
+    qkv_trace = []
+    grad_qkv = halve([qkv_parts[3], qkv_core[1], qkv_across], near_seq, 0, qkv_trace)
+    near_send = qkv_trace[0][0]
+    mine = own_bit(*near_seq[0]) * half
+    up_addends = [lax.dynamic_slice_in_dim(a, mine, half, 0) for a in (up_parts[3], up_core[1], up_across)]
+    grad_up = halve(up_addends + [after(up_near, near_send)], near_seq[1:], 0)
     down_own = sum(a.astype(f32) for a in (down_parts[4][0], down_core[1][0], down_along[0]))
-    grad_down = jnp.transpose(halve([down_own, down_across], near_seq[1:], 1))
-    grad_qkv = halve([qkv_parts[3], qkv_core[1], qkv_across], near_seq, 0)
+    grad_down = jnp.transpose(halve([down_own, after(down_across, near_send)], near_seq[1:], 1))
     grad_out = grad_up[:, 4 * width :]
     grad_up = reorder(grad_up[:, : 4 * width])
     late_rows = with_bias([line_sums(r[2]) for r in last], [sum(r[3][0] for r in last)])
-    late_rows = collect_rows(after(late_rows, qkv_sent), order)
+    late_rows = collect_rows(after(late_rows, near_send), order)
     early_rows = after(early_rows, qkv_sent)
 
     def own_columns(sums, shard):

time: 881 us -> 855 us (0.970)
    all_to_all x8, waiting for transfers between devices: 99.3 us -> 60.5 us  [exchange(): return lax.all_to_all(value, 'seq', 0, 0, tiled=True)]
    ppermute x49, waiting for transfers between devices: 155 us -> 187 us  [swap_bit(): return lax.ppermute(value, axis, [(i, i ^ bit) for i in range(count)])]
    convert_element_type x12 -> x11, other arithmetic: 35.4 us -> 26.6 us  [rounded_sum(): return sum((a.astype(f32) for a in addends)).astype(bf16)]
    unnamed x109 -> x119, local copies, waits for them, and re-layouts: 21.9 us -> 18.5 us
  transfers between devices with their start and end apart: 59 -> 59, of which waited for: 19 -> 25; matrix products, arithmetic and copies ran while one was open for 13% -> 12% of each run, Pallas kernels for 40% -> 37%
where the time goes in v9:
time: 855 us; the launch traced here: 844 us
  Pallas kernels  348 us (41%)
  waiting for transfers between devices  258 us (30%)
  starting transfers between devices  94.1 us (11%)
  other arithmetic  69.6 us (8%)
  local copies, waits for them, and re-layouts  55.4 us (6%)
  between operations  16 us (2%)
    ppermute x49, waiting for transfers between devices, swap_bit(): return lax.ppermute(value, axis, [(i, i ^ bit) for i in range(count)])  187 us
    pallas_call x2, Pallas kernels, attend_back(): pl.pallas_call(functools.partial(attend_back_kernel, total=total, span=sp...  118 us
    pallas_call x2, Pallas kernels, middle(): pl.pallas_call(middle_kernel, grid_spec=pltpu.PrefetchScalarGridSpec(num_...  76.4 us
    pallas_call x2, Pallas kernels, attend(): pl.pallas_call(functools.partial(attend_kernel, total=total, span=span, b...  70.6 us
    all_to_all x8, waiting for transfers between devices, exchange(): return lax.all_to_all(value, 'seq', 0, 0, tiled=True)  60.5 us
    ppermute x49, starting transfers between devices, swap_bit(): return lax.ppermute(value, axis, [(i, i ^ bit) for i in range(count)])  52.2 us
    pallas_call x3, Pallas kernels, weight_grad_call(): pl.pallas_call(functools.partial(weight_grad_kernel, **options), grid_spe...  50.8 us
    all_to_all x8, starting transfers between devices, exchange(): return lax.all_to_all(value, 'seq', 0, 0, tiled=True)  41.6 us
  transfers between devices with their start and end apart: 59, of which 25 were waited for; matrix products, arithmetic and copies ran while one was open for 12% of the time, Pallas kernels for 37%

profile of v9, /device:TPU:0, one launch (start us, length us, event | category | flops | bytes accessed | tf_op | source)
XLA Modules:
  0.0 844.3 jit_solution(11166030776704828062)
XLA Ops:
  31.9 15.2 %collective-permute-done.7 = bf16[1,4,32,1024]{3,2,1,0:T(8,128)(2,1)} collective-permute-done((bf16[1,4,32,1024]{3,2,1,0:T(8,128)(2,1)}, bf16[1,4,32,1024]{3,2,1,0:T(8,128)(2,1)}, u32[]{:S(2)}, u32[]{:S(2)}) %collective-permute-start.7) | collective-permute-done | bytes 262176 | tf_op jit(solution)/shard_map/ppermute | solution.py:30
  53.2 11.8 %collective-permute-done.3 = f32[32,2816]{1,0:T(8,128)S(1)} collective-permute-done((f32[32,2816]{1,0:T(8,128)S(1)}, f32[32,2816]{1,0:T(8,128)S(1)}, u32[]{:S(2)}, u32[]{:S(2)}) %collective-permute-start.3) | collective-permute-done | bytes 360480 | tf_op jit(solution)/shard_map/ppermute | solution.py:30
  74.4 19.5 %collective-permute-done.10 = bf16[2,5,32,1024]{3,2,1,0:T(8,128)(2,1)S(1)} collective-permute-done((bf16[2,5,32,1024]{3,2,1,0:T(8,128)(2,1)S(1)}, bf16[2,5,32,1024]{3,2,1,0:T(8,128)(2,1)S(1)}, u32[]{:S(2)}, u32[]{:S(2)}) %collective-permute-start.10) | collective-permute-done | bytes 655392 | tf_op jit(solution)/shard_map/ppermute | solution.py:30
  103.1 10.6 %all-gather.4.cloned.1.call-done.wq_ref.wk_ref.wv_ref = bf16[1024,3072]{1,0:T(8,128)(2,1)} async-done(((bf16[32,3072]{1,0:T(8,128)(2,1)}), bf16[1024,3072]{1,0:T(8,128)(2,1)}) %all-gather.4.cloned.1.call-update) | async-done | bytes 6291472 | tf_op jit(solution)/shard_map/all_gather | solution.py:924
  166.5 35.3 %all-to-all-done = bf16[8,512,384]{2,1,0:T(8,128)(2,1)} async-done(((bf16[8,512,384]{2,1,0:T(8,128)(2,1)}), bf16[8,512,384]{2,1,0:T(8,128)(2,1)}, u32[]{:S(2)}, u32[]{:S(2)}) %all-to-all-start) | async-done | bytes 3145760 | tf_op jit(solution)/shard_map/all_to_all | solution.py:971
  216.1 35.3 %attend.3 = (bf16[4096,128]{1,0:T(8,128)(2,1)}, f32[4096,128]{1,0:T(8,128)}, f32[2,4096]{1,0:T(2,128)}) custom-call(bf16[4096,384]{1,0:T(8,128)(2,1)} %bitcast.37.qkv_ref), custom_call_target="tpu_custom_call" | custom-call | flops 17179869184 | bytes 6291456 | tf_op jit(solution)/shard_map/attend/pallas_call | solution.py:729
  251.3 10.3 %collective-permute-done.16 = f32[8,5632]{1,0:T(8,128)S(1)} collective-permute-done((f32[8,5632]{1,0:T(8,128)S(1)}, f32[8,5632]{1,0:T(8,128)S(1)}, u32[]{:S(2)}, u32[]{:S(2)}) %collective-permute-start.16) | collective-permute-done | bytes 180256 | tf_op jit(solution)/shard_map/ppermute | solution.py:30
  261.6 15.2 %all-to-all-done.1 = bf16[8,512,384]{2,1,0:T(8,128)(2,1)} async-done(((bf16[8,512,384]{2,1,0:T(8,128)(2,1)}), bf16[8,512,384]{2,1,0:T(8,128)(2,1)}, u32[]{:S(2)}, u32[]{:S(2)}) %all-to-all-start.1) | async-done | bytes 3145760 | tf_op jit(solution)/shard_map/all_to_all | solution.py:971
  284.4 35.3 %attend.2 = (bf16[4096,128]{1,0:T(8,128)(2,1)}, f32[4096,128]{1,0:T(8,128)}, f32[2,4096]{1,0:T(2,128)}) custom-call(bf16[4096,384]{1,0:T(8,128)(2,1)} %bitcast.35.qkv_ref), custom_call_target="tpu_custom_call" | custom-call | flops 17179869184 | bytes 6291456 | tf_op jit(solution)/shard_map/attend/pallas_call | solution.py:729
  326.8 38.2 %middle.2 = (bf16[2,512,1024]{2,1,0:T(8,128)(2,1)}, f32[512,1024]{1,0:T(8,128)}, bf16[512,1024]{1,0:T(8,128)(2,1)}, bf16[512,1024]{1,0:T(8,128)(2,1)}, bf16[512,...) custom-call(s32[1]{0:T(128)} %bitcast.clip_ref, ...), custom_call_target="tpu_custom_call" | custom-call | flops 2147483648 | bytes 4718592 | tf_op jit(solution)/shard_map/middle/pallas_call | solution.py:446
  376.2 38.2 %middle.3 = (bf16[2,512,1024]{2,1,0:T(8,128)(2,1)}, f32[512,1024]{1,0:T(8,128)}, bf16[512,1024]{1,0:T(8,128)(2,1)}, bf16[512,1024]{1,0:T(8,128)(2,1)}, bf16[512,...) custom-call(s32[1]{0:T(128)} %bitcast.clip_ref, ...), custom_call_target="tpu_custom_call", output_to_operand_aliasing={{0}: (20, {})} | custom-call | flops 2147483648 | bytes 4718592 | tf_op jit(solution)/shard_map/middle/pallas_call | solution.py:446
  420.9 59.2 %attend_back.2 = bf16[4096,384]{1,0:T(8,128)(2,1)} custom-call(bf16[4096,384]{1,0:T(8,128)(2,1)} %bitcast.37.qkv_ref, bf16[4096,128]{1,0:T(8,128)(2,1)} %bitcast.196, f32[4096,128]{1,0:T(8,128)} %get-tuple-element.129.full_ref, f32[2,4096]{1,0:T(2,128)} %get-tuple-element.130.log_ref, f32[4096,128]{1,0:T(8,128)} %bitcast.193, f32[4096,128]{1,0:T(8,128)} %bitcast.191), custom_call_target="tpu_custom_call" | custom-call | flops 42949672960 | bytes 13631488 | tf_op jit(solution)/shard_map/attend_back/pallas_call | solution.py:824
  480.1 17.5 %weight_grad.3 = (bf16[2,1024,512]{2,1,0:T(8,128)(2,1)}, bf16[1,1024,512]{2,1,0:T(8,128)(2,1)}, bf16[1,1024,512]{2,1,0:T(8,128)(2,1)}, bf16[2,1024,512]{2,1,0:T(...) custom-call(s32[8]{0:T(128)} %stack.141.index_ref, ...), custom_call_target="tpu_custom_call" | custom-call | flops 8589934592 | bytes 20971520 | tf_op jit(solution)/shard_map/weight_grad/pallas_call | solution.py:551
  497.6 20.5 %weight_grad.4 = (bf16[256,5120]{1,0:T(8,128)(2,1)}, bf16[256,5120]{1,0:T(8,128)(2,1)}, bf16[256,5120]{1,0:T(8,128)(2,1)}, bf16[256,5120]{1,0:T(8,128)(2,1)}) custom-call(s32[4]{0:T(128)} %pad_add_fusion.5.index_ref, bf16[512,1024]{1,0:T(8,128)(2,1)} %get-tuple-element.134.refs_0_.refs_1_.refs_2_.refs_3_, ...), custom_call_target="tpu_custom_call" | custom-call | flops 10737418240 | bytes 25165824 | tf_op jit(solution)/shard_map/weight_grad/pallas_call | solution.py:551
  538.4 59.1 %attend_back.3 = bf16[4096,384]{1,0:T(8,128)(2,1)} custom-call(bf16[4096,384]{1,0:T(8,128)(2,1)} %bitcast.35.qkv_ref, bf16[4096,128]{1,0:T(8,128)(2,1)} %bitcast.197, f32[4096,128]{1,0:T(8,128)} %get-tuple-element.148.full_ref, f32[2,4096]{1,0:T(2,128)} %get-tuple-element.149.log_ref, f32[4096,128]{1,0:T(8,128)} %bitcast.194, f32[4096,128]{1,0:T(8,128)} %bitcast.192), custom_call_target="tpu_custom_call" | custom-call | flops 42949672960 | bytes 13631488 | tf_op jit(solution)/shard_map/attend_back/pallas_call | solution.py:824
  630.9 9.3 %project_back.2 = (f32[2,512,1024]{2,1,0:T(8,128)}, bf16[512,3072]{1,0:T(8,128)(2,1)S(1)}, f32[2,2,1024]{2,1,0:T(2,128)S(1)}, f32[1,3072]{1,0:T(1,128)S(1)}) custom-call(bf16[8,512,384]{2,1,0:T(8,128)(2,1)S(1)} %copy-done.4, bf16[1024,3072]{1,0:T(8,128)(2,1)} %all-gather.4.cloned.1.call-done.wq_ref.wk_ref.wv_ref, ...), custom_call_target="tpu_custom_call" | custom-call | flops 3221225472 | bytes 17825792 | tf_op jit(solution)/shard_map/project_back/pallas_call | solution.py:263
  641.9 12.4 %collective-permute-done.32 = bf16[1024,512]{1,0:T(8,128)(2,1)S(1)} collective-permute-done((bf16[1024,512]{1,0:T(8,128)(2,1)S(1)}, bf16[1024,512]{1,0:T(8,128)(2,1)S(1)}, u32[]{:S(2)}, u32[]{:S(2)}) %collective-permute-start.32) | collective-permute-done | bytes 1048608 | tf_op jit(solution)/shard_map/ppermute | solution.py:30
  655.3 23.7 %collective-permute-done.30 = bf16[128,5120]{1,0:T(8,128)(2,1)} collective-permute-done((bf16[128,5120]{1,0:T(8,128)(2,1)S(1)}, bf16[128,5120]{1,0:T(8,128)(2,1)}, u32[]{:S(2)}, u32[]{:S(2)}) %collective-permute-start.30) | collective-permute-done | bytes 1310752 | tf_op jit(solution)/shard_map/ppermute | solution.py:30
  678.9 10.0 %all-to-all-done.6.back_ref = bf16[8,512,384]{2,1,0:T(8,128)(2,1)} async-done(((bf16[8,512,384]{2,1,0:T(8,128)(2,1)}), bf16[8,512,384]{2,1,0:T(8,128)(2,1)}, u32[]{:S(2)}, u32[]{:S(2)}) %all-to-all-start.6) | async-done | bytes 3145760 | tf_op jit(solution)/shard_map/all_to_all | solution.py:971
  690.5 9.9 %project_back.3 = (f32[2,512,1024]{2,1,0:T(8,128)}, bf16[512,3072]{1,0:T(8,128)(2,1)S(1)}, f32[2,2,1024]{2,1,0:T(2,128)S(1)}, f32[1,3072]{1,0:T(1,128)S(1)}) custom-call(bf16[8,512,384]{2,1,0:T(8,128)(2,1)} %all-to-all-done.6.back_ref, bf16[1024,3072]{1,0:T(8,128)(2,1)} %all-gather.4.cloned.1.call-done.wq_ref.wk_ref.wv_ref, ...), custom_call_target="tpu_custom_call", output_to_operand_aliasing={{0}: (7, {})} | custom-call | flops 3221225472 | bytes 17825792 | tf_op jit(solution)/shard_map/project_back/pallas_call | solution.py:263
  702.1 12.8 %weight_grad.5 = (bf16[256,3072]{1,0:T(8,128)(2,1)}, bf16[256,3072]{1,0:T(8,128)(2,1)}, bf16[256,3072]{1,0:T(8,128)(2,1)}, bf16[256,3072]{1,0:T(8,128)(2,1)}) custom-call(s32[4]{0:T(128)} %pad_add_fusion.5.index_ref, bf16[512,1024]{1,0:T(8,128)(2,1)} %copy-done.11, bf16[512,1024]{1,0:T(8,128)(2,1)} %copy-done.11, bf16[512,1024]{1,0:T(8,128)(2,1)} %copy-done.11, ...), custom_call_target="tpu_custom_call" | custom-call | flops 6442450944 | bytes 16777216 | tf_op jit(solution)/shard_map/weight_grad/pallas_call | solution.py:551
  733.2 25.3 %collective-permute-done.35 = bf16[256,3072]{1,0:T(8,128)(2,1)} collective-permute-done((bf16[256,3072]{1,0:T(8,128)(2,1)}, bf16[256,3072]{1,0:T(8,128)(2,1)}, u32[]{:S(2)}, u32[]{:S(2)}) %collective-permute-start.35) | collective-permute-done | bytes 1572896 | tf_op jit(solution)/shard_map/ppermute | solution.py:30
  776.2 9.3 %collective-permute-done.38 = f32[16,2816]{1,0:T(8,128)S(1)} collective-permute-done((f32[16,2816]{1,0:T(8,128)S(1)}, f32[16,2816]{1,0:T(8,128)S(1)}, u32[]{:S(2)}, u32[]{:S(2)}) %collective-permute-start.38) | collective-permute-done | bytes 180256 | tf_op jit(solution)/shard_map/ppermute | solution.py:30
  815.2 9.7 %collective-permute-done.45 = bf16[32,5120]{1,0:T(8,128)(2,1)} collective-permute-done((bf16[32,5120]{1,0:T(8,128)(2,1)}, bf16[32,5120]{1,0:T(8,128)(2,1)}, u32[]{:S(2)}, u32[]{:S(2)}) %collective-permute-start.45) | collective-permute-done | bytes 327712 | tf_op jit(solution)/shard_map/ppermute | solution.py:30
  (395 shorter events, 284.8 us)
Async XLA Ops:
  7.2 106.5 %all-gather.4.cloned.1.call-start = ((), (), s32[]{:S(2)}) async-start(), calls=%async_computation.8 | async-start | bytes 6488064 | tf_op jit(solution)/shard_map/all_gather | solution.py:924
  31.9 98.5 %collective-permute-start.13 = (f32[64,5632]{1,0:T(8,128)}, f32[64,5632]{1,0:T(8,128)}, u32[]{:S(2)}, u32[]{:S(2)}) collective-permute-start(f32[64,5632]{1,0:T(8,128)} %constant_dynamic-slice_fusion.4), channel_id=1, source_target_pairs={{0,8},{8,0},{16,24},{24,16},{1,9},{9,1},{17,25},{25,17},{2,10},{10... | collective-permute-start | bytes 4325384 | tf_op jit(solution)/shard_map/ppermute | solution.py:30
  51.9 42.0 %collective-permute-start.10 = (bf16[2,5,32,1024]{3,2,1,0:T(8,128)(2,1)S(1)}, bf16[2,5,32,1024]{3,2,1,0:T(8,128)(2,1)S(1)}, u32[]{:S(2)}, u32[]{:S(2)}) collective-permute-start(bf16[2,5,32,1024]{3,2,1,0:T(8,128)(2,1)S(1)} %maximum_bitcast_fusion), channel_id=1, source_target_pairs={{0,2},{1,3},{2,0},{3,1},{4,6},{5,7},{6,4},{7,5},{8,10},{9,11},{10,... | collective-permute-start | bytes 1966088 | tf_op jit(solution)/shard_map/ppermute | solution.py:30
  72.7 61.2 %collective-permute-start.11 = (bf16[4,4,32,1024]{3,2,1,0:T(8,128)(2,1)}, bf16[4,4,32,1024]{3,2,1,0:T(8,128)(2,1)}, u32[]{:S(2)}, u32[]{:S(2)}) collective-permute-start(bf16[4,4,32,1024]{3,2,1,0:T(8,128)(2,1)} %bitcast.18), channel_id=1, source_target_pairs={{0,1},{1,0},{2,3},{3,2},{4,5},{5,4},{6,7},{7,6},{8,9},{9,8},{10,11... | collective-permute-start | bytes 3145736 | tf_op jit(solution)/shard_map/ppermute | solution.py:30
  99.4 42.1 %collective-permute-start.12 = (bf16[4,5,32,1024]{3,2,1,0:T(8,128)(2,1)}, bf16[4,5,32,1024]{3,2,1,0:T(8,128)(2,1)}, u32[]{:S(2)}, u32[]{:S(2)}) collective-permute-start(bf16[4,5,32,1024]{3,2,1,0:T(8,128)(2,1)} %bitcast.29), channel_id=1, source_target_pairs={{0,16},{8,24},{16,0},{24,8},{1,17},{9,25},{17,1},{25,9},{2,18},{10... | collective-permute-start | bytes 3932168 | tf_op jit(solution)/shard_map/ppermute | solution.py:30
  125.7 76.1 %all-to-all-start = ((bf16[8,512,384]{2,1,0:T(8,128)(2,1)}), bf16[8,512,384]{2,1,0:T(8,128)(2,1)}, u32[]{:S(2)}, u32[]{:S(2)}) async-start(bf16[8,512,384]{2,1,0:T(8,128)(2,1)} %copy-done.5), calls=%async_computation | async-start | bytes 6291456 | tf_op jit(solution)/shard_map/all_to_all | solution.py:971
  137.1 189.7 %collective-permute-start.23 = (bf16[4,2,4,32,1024]{4,3,2,1,0:T(8,128)(2,1)}, bf16[4,2,4,32,1024]{4,3,2,1,0:T(8,128)(2,1)}, u32[]{:S(2)}, u32[]{:S(2)}) collective-permute-start(bf16[4,2,4,32,1024]{4,3,2,1,0:T(8,128)(2,1)} %pad_maximum_fusion.2.refs_8_), channel_id=1, source_target_pairs={{0,8},{8,0},{16,24},{24,16},{1,9},{9,1},{17,25},{25,17},{2,10},{10... | collective-permute-start | bytes 6291464 | tf_op jit(solution)/shard_map/ppermute | solution.py:30
  137.1 182.7 %collective-permute-start.22 = (bf16[8,4,32,1024]{3,2,1,0:T(8,128)(2,1)}, bf16[8,4,32,1024]{3,2,1,0:T(8,128)(2,1)}, u32[]{:S(2)}, u32[]{:S(2)}) collective-permute-start(bf16[8,4,32,1024]{3,2,1,0:T(8,128)(2,1)} %bitcast.33), channel_id=1, source_target_pairs={{0,16},{8,24},{16,0},{24,8},{1,17},{9,25},{17,1},{25,9},{2,18},{10... | collective-permute-start | bytes 6291464 | tf_op jit(solution)/shard_map/ppermute | solution.py:30
  141.2 67.2 %collective-permute-start.20 = (bf16[4,2,5,32,1024]{4,3,2,0,1:T(8,128)(2,1)}, bf16[4,2,5,32,1024]{4,3,2,0,1:T(8,128)(2,1)}, u32[]{:S(2)}, u32[]{:S(2)}) collective-permute-start(bf16[4,2,5,32,1024]{4,3,2,0,1:T(8,128)(2,1)} %pad_maximum_fusion), channel_id=1, source_target_pairs={{0,8},{8,0},{16,24},{24,16},{1,9},{9,1},{17,25},{25,17},{2,10},{10... | collective-permute-start | bytes 7864328 | tf_op jit(solution)/shard_map/ppermute | solution.py:30
  141.5 64.8 %collective-permute-start.19 = (bf16[4,5,32,1024]{3,2,1,0:T(8,128)(2,1)}, bf16[4,5,32,1024]{3,2,1,0:T(8,128)(2,1)}, u32[]{:S(2)}, u32[]{:S(2)}) collective-permute-start(bf16[4,5,32,1024]{3,2,1,0:T(8,128)(2,1)} %collective-permute-done.12), channel_id=1, source_target_pairs={{0,1},{1,0},{2,3},{3,2},{4,5},{5,4},{6,7},{7,6},{8,9},{9,8},{10,11... | collective-permute-start | bytes 3932168 | tf_op jit(solution)/shard_map/ppermute | solution.py:30
  151.5 61.5 %collective-permute-start.15 = (f32[16,5632]{1,0:T(8,128)S(1)}, f32[16,5632]{1,0:T(8,128)}, u32[]{:S(2)}, u32[]{:S(2)}) collective-permute-start(f32[16,5632]{1,0:T(8,128)S(1)} %constant_dynamic-slice_fusion.2), channel_id=1, source_target_pairs={{0,1},{1,0},{2,3},{3,2},{4,5},{5,4},{6,7},{7,6},{8,9},{9,8},{10,11... | collective-permute-start | bytes 1081352 | tf_op jit(solution)/shard_map/ppermute | solution.py:30
  201.8 75.0 %all-to-all-start.1 = ((bf16[8,512,384]{2,1,0:T(8,128)(2,1)}), bf16[8,512,384]{2,1,0:T(8,128)(2,1)}, u32[]{:S(2)}, u32[]{:S(2)}) async-start(bf16[8,512,384]{2,1,0:T(8,128)(2,1)} %copy-done.6), calls=%async_computation.1 | async-start | bytes 6291456 | tf_op jit(solution)/shard_map/all_to_all | solution.py:971
  214.1 47.5 %collective-permute-start.16 = (f32[8,5632]{1,0:T(8,128)S(1)}, f32[8,5632]{1,0:T(8,128)S(1)}, u32[]{:S(2)}, u32[]{:S(2)}) collective-permute-start(f32[8,5632]{1,0:T(8,128)S(1)} %constant_dynamic-slice_fusion.1), channel_id=1, source_target_pairs={{0,2},{1,3},{2,0},{3,1},{4,6},{5,7},{6,4},{7,5},{8,10},{9,11},{10,... | collective-permute-start | bytes 540680 | tf_op jit(solution)/shard_map/ppermute | solution.py:30
  276.8 43.5 %all-to-all-start.2 = ((bf16[8,512,128]{2,1,0:T(8,128)(2,1)}), bf16[8,512,128]{2,1,0:T(8,128)(2,1)}, u32[]{:S(2)}, u32[]{:S(2)}) async-start(bf16[8,512,128]{2,1,0:T(8,128)(2,1)} %bitcast.199), calls=%async_computation.2 | async-start | bytes 2097152 | tf_op jit(solution)/shard_map/all_to_all | solution.py:971
  284.4 42.4 %collective-permute-start.21 = (bf16[4,2,5,32,1024]{4,3,2,1,0:T(8,128)(2,1)S(1)}, bf16[4,2,5,32,1024]{4,3,2,1,0:T(8,128)(2,1)}, u32[]{:S(2)}, u32[]{:S(2)}) collective-permute-start(bf16[4,2,5,32,1024]{4,3,2,1,0:T(8,128)(2,1)S(1)} %pad_maximum_fusion.1.refs_1_.refs_5_), channel_id=1, source_target_pairs={{0,8},{8,0},{16,24},{24,16},{1,9},{9,1},{17,25},{25,17},{2,10},{10... | collective-permute-start | bytes 7864328 | tf_op jit(solution)/shard_map/ppermute | solution.py:30
  320.3 44.7 %all-to-all-start.3 = ((bf16[8,512,128]{2,1,0:T(8,128)(2,1)}), bf16[8,512,128]{2,1,0:T(8,128)(2,1)}, u32[]{:S(2)}, u32[]{:S(2)}) async-start(bf16[8,512,128]{2,1,0:T(8,128)(2,1)} %bitcast.198), calls=%async_computation.3 | async-start | bytes 2097152 | tf_op jit(solution)/shard_map/all_to_all | solution.py:971
  365.1 49.3 %all-to-all-start.4 = ((bf16[8,512,128]{2,1,0:T(8,128)(2,1)}), bf16[8,512,128]{2,1,0:T(8,128)(2,1)S(1)}, u32[]{:S(2)}, u32[]{:S(2)}) async-start(bf16[8,512,128]{2,1,0:T(8,128)(2,1)} %get-tuple-element.120), calls=%async_computation.4 | async-start | bytes 2097152 | tf_op jit(solution)/shard_map/all_to_all | solution.py:971
  414.4 65.7 %all-to-all-start.5 = ((bf16[8,512,128]{2,1,0:T(8,128)(2,1)}), bf16[8,512,128]{2,1,0:T(8,128)(2,1)S(1)}, u32[]{:S(2)}, u32[]{:S(2)}) async-start(bf16[8,512,128]{2,1,0:T(8,128)(2,1)} %get-tuple-element.121), calls=%async_computation.5 | async-start | bytes 2097152 | tf_op jit(solution)/shard_map/all_to_all | solution.py:971
  518.6 87.6 %all-to-all-start.7 = ((bf16[8,512,384]{2,1,0:T(8,128)(2,1)}), bf16[8,512,384]{2,1,0:T(8,128)(2,1)S(1)}, u32[]{:S(2)}, u32[]{:S(2)}) async-start(bf16[8,512,384]{2,1,0:T(8,128)(2,1)} %bitcast.188), calls=%async_computation.7 | async-start | bytes 6291456 | tf_op jit(solution)/shard_map/all_to_all | solution.py:971
  530.7 75.5 %collective-permute-start.27 = (bf16[2,1024,512]{2,1,0:T(8,128)(2,1)}, bf16[2,1024,512]{2,1,0:T(8,128)(2,1)}, u32[]{:S(2)}, u32[]{:S(2)}) collective-permute-start(bf16[2,1024,512]{2,1,0:T(8,128)(2,1)} %add_convert_fusion.1), channel_id=1, source_target_pairs={{0,1},{1,0},{2,3},{3,2},{4,5},{5,4},{6,7},{7,6},{8,9},{9,8},{10,11... | collective-permute-start | bytes 6291464 | tf_op jit(solution)/shard_map/ppermute | solution.py:30
  536.9 69.2 %collective-permute-start.28 = (bf16[256,5120]{1,0:T(8,128)(2,1)}, bf16[256,5120]{1,0:T(8,128)(2,1)}, u32[]{:S(2)}, u32[]{:S(2)}) collective-permute-start(bf16[256,5120]{1,0:T(8,128)(2,1)} %add_convert_fusion), channel_id=1, source_target_pairs={{0,16},{8,24},{16,0},{24,8},{1,17},{9,25},{17,1},{25,9},{2,18},{10... | collective-permute-start | bytes 7864328 | tf_op jit(solution)/shard_map/ppermute | solution.py:30
  607.9 81.1 %all-to-all-start.6 = ((bf16[8,512,384]{2,1,0:T(8,128)(2,1)}), bf16[8,512,384]{2,1,0:T(8,128)(2,1)}, u32[]{:S(2)}, u32[]{:S(2)}) async-start(bf16[8,512,384]{2,1,0:T(8,128)(2,1)} %bitcast.187), calls=%async_computation.6 | async-start | bytes 6291456 | tf_op jit(solution)/shard_map/all_to_all | solution.py:971
  612.4 111.6 %all-gather.6.cloned.1.call-start = ((), (), s32[]{:S(2)}) async-start(), calls=%async_computation.9 | async-start | bytes 2973696 | tf_op jit(solution)/shard_map/all_gather | solution.py:1039
  622.6 56.3 %collective-permute-start.30 = (bf16[128,5120]{1,0:T(8,128)(2,1)S(1)}, bf16[128,5120]{1,0:T(8,128)(2,1)}, u32[]{:S(2)}, u32[]{:S(2)}) collective-permute-start(bf16[128,5120]{1,0:T(8,128)(2,1)S(1)} %add_convert_fusion.3), channel_id=1, source_target_pairs={{0,1},{1,0},{2,3},{3,2},{4,5},{5,4},{6,7},{7,6},{8,9},{9,8},{10,11... | collective-permute-start | bytes 3932168 | tf_op jit(solution)/shard_map/ppermute | solution.py:30
  (92 other events, 1123.4 us)
Sparse Core Ops, SparseCore 0:
  16.1 97.5 all-gather.3
  616.7 93.6 all-gather.5

commit v10 on v9

--- a/solution.py
+++ b/solution.py
@@ -1041,51 +1041,50 @@
     d_qkv, exchanged = [], []
     for c in range(clips):
         if c == clips - 1:
-            active = gate(active, *d_qkv, d_mixed[-1])
-            down_parts = columns_grad(active, d_mlp)
-            down_core = [swap_bit(p, "clip", 1) for p in down_parts[:3]]
-            normed_two = gate(normed_two, down_parts[0])
+            normed_two = gate(normed_two, *d_qkv, d_mixed[-1])
             up_parts = rows_grad([(normed_two, d_hidden), (mixed_all, d_attn)])
             up_core = [swap_bit(p, "clip", 1) for p in up_parts[:2]]
-            down_sent = rounded_sum([down_parts[3], after(down_core[0], up_parts[0])])
-            down_along = swap_bit(down_sent, "seq", 1)
-            up_sent = rounded_sum([up_parts[2], after(up_core[0], down_sent)])
+            up_sent = rounded_sum([up_parts[2], up_core[0]])
             up_across = swap_bit(up_sent, "clip", 2)
         grad = after(d_mixed[c], results[-1][8] if c == 0 else up_sent)
         grad = grad.reshape(total, span)
         d_qkv.append(attend_back(qkv[c].reshape(total, 3 * span), grad, fulls[c], logs[c], cos_all, sin_all, span))
         sent = d_qkv[c].reshape(seq_devices, rows, 3 * span)
-        exchanged.append(exchange(after(sent, d_mixed[-1]) if c == 0 else after(sent, down_along, up_across)))
+        exchanged.append(exchange(after(sent, d_mixed[-1]) if c == 0 else after(sent, up_across)))
 
     near_seq = axis_bits("seq")[::-1]
-    down_along, up_across = after(down_along, exchanged[0]), after(up_across, exchanged[0])
-    down_across = swap_bit(rounded_sum([down_parts[5][0], down_core[2][0], down_along[1]]), "clip", 2)
+    half = up_parts[3].shape[0] // 2
+    mine = own_bit(*near_seq[0])
+    up_across = after(up_across, exchanged[0])
+    up_addends = [up_parts[3], up_core[1], up_across]
+    up_near_sent = rounded_sum([lax.dynamic_slice_in_dim(a, (1 - mine) * half, half, 0) for a in up_addends])
+    up_near = after(swap_bit(up_near_sent, *near_seq[0]), exchanged[-1])
+    active = gate(active, d_qkv[-1], up_near_sent)
+    down_parts = columns_grad(active, d_mlp)
+    exchanged[0] = after(exchanged[0], down_parts[0])
+    down_core = [after(swap_bit(p, "clip", 1), exchanged[-1]) for p in down_parts[:3]]
 
     last = []
     for c in range(clips):
         grads = last[-1][0] if last else None
-        if c == clips - 1:
-            half = up_parts[3].shape[0] // 2
-            theirs = (1 - own_bit(*near_seq[0])) * half
-            up_near = rounded_sum(
-                [lax.dynamic_slice_in_dim(a, theirs, half, 0) for a in (up_parts[3], up_core[1], up_across)]
-            )
-            up_near = swap_bit(up_near, *near_seq[0])
-            exchanged[-1] = after(exchanged[-1], up_near, down_across)
         last.append(project_back(exchanged[c], full_qkv, tokens, c, mods_one[c][1], results[c][1], grads))
     d_projected = [r[1] for r in last]
     qkv_parts = rows_grad([(normed, d_projected)])
     qkv_core = [swap_bit(p, "clip", 1) for p in qkv_parts[:2]]
+    down_sent = rounded_sum([down_parts[3], after(down_core[0], qkv_parts[0])])
+    down_along = swap_bit(down_sent, "seq", 1)
     qkv_sent = rounded_sum([qkv_parts[2], qkv_core[0]])
     qkv_across = swap_bit(qkv_sent, "clip", 2)
+    up_own = [lax.dynamic_slice_in_dim(a, mine * half, half, 0) for a in up_addends]
+    grad_up = halve(up_own + [after(up_near, qkv_sent)], near_seq[1:], 0)
     qkv_trace = []
     grad_qkv = halve([qkv_parts[3], qkv_core[1], qkv_across], near_seq, 0, qkv_trace)
     near_send = qkv_trace[0][0]
-    mine = own_bit(*near_seq[0]) * half
-    up_addends = [lax.dynamic_slice_in_dim(a, mine, half, 0) for a in (up_parts[3], up_core[1], up_across)]
-    grad_up = halve(up_addends + [after(up_near, near_send)], near_seq[1:], 0)
+    down_along = after(down_along, near_send)
+    down_far = rounded_sum([down_parts[5][0], down_core[2][0], down_along[1]])
+    down_across = swap_bit(down_far, "clip", 2)
     down_own = sum(a.astype(f32) for a in (down_parts[4][0], down_core[1][0], down_along[0]))
-    grad_down = jnp.transpose(halve([down_own, after(down_across, near_send)], near_seq[1:], 1))
+    grad_down = jnp.transpose(halve([down_own, down_across], near_seq[1:], 1))
     grad_out = grad_up[:, 4 * width :]
     grad_up = reorder(grad_up[:, : 4 * width])
     late_rows = with_bias([line_sums(r[2]) for r in last], [sum(r[3][0] for r in last)])

time: 855 us -> 879 us (1.028)
  waiting for transfers between devices: 258 us -> 270 us
    all_to_all x8, waiting for transfers between devices: 60.5 us -> 90.6 us  [exchange(): return lax.all_to_all(value, 'seq', 0, 0, tiled=True)]
    ppermute x49, waiting for transfers between devices: 187 us -> 169 us  [swap_bit(): return lax.ppermute(value, axis, [(i, i ^ bit) for i in range(count)])]
    convert_element_type x11 -> x12, other arithmetic: 26.6 us -> 35 us  [rounded_sum(): return sum((a.astype(f32) for a in addends)).astype(bf16)]
    unnamed x119 -> x125, local copies, waits for them, and re-layouts: 18.5 us -> 21 us
  transfers between devices with their start and end apart: 59 -> 59, of which waited for: 25 -> 22; matrix products, arithmetic and copies ran while one was open for 12% -> 14% of each run, Pallas kernels for 37% -> 38%
where the time goes in v10:
time: 879 us; the launch traced here: 868 us
  Pallas kernels  348 us (40%)
  waiting for transfers between devices  270 us (31%)
  starting transfers between devices  89 us (10%)
  other arithmetic  76.2 us (9%)
  local copies, waits for them, and re-layouts  62.9 us (7%)
  between operations  16 us (2%)
    ppermute x49, waiting for transfers between devices, swap_bit(): return lax.ppermute(value, axis, [(i, i ^ bit) for i in range(count)])  169 us
    pallas_call x2, Pallas kernels, attend_back(): pl.pallas_call(functools.partial(attend_back_kernel, total=total, span=sp...  118 us
    all_to_all x8, waiting for transfers between devices, exchange(): return lax.all_to_all(value, 'seq', 0, 0, tiled=True)  90.6 us
    pallas_call x2, Pallas kernels, middle(): pl.pallas_call(middle_kernel, grid_spec=pltpu.PrefetchScalarGridSpec(num_...  76.4 us
    pallas_call x2, Pallas kernels, attend(): pl.pallas_call(functools.partial(attend_kernel, total=total, span=span, b...  70.5 us
    pallas_call x3, Pallas kernels, weight_grad_call(): pl.pallas_call(functools.partial(weight_grad_kernel, **options), grid_spe...  50.9 us
    ppermute x49, starting transfers between devices, swap_bit(): return lax.ppermute(value, axis, [(i, i ^ bit) for i in range(count)])  47.2 us
    all_to_all x8, starting transfers between devices, exchange(): return lax.all_to_all(value, 'seq', 0, 0, tiled=True)  41.5 us
  transfers between devices with their start and end apart: 59, of which 22 were waited for; matrix products, arithmetic and copies ran while one was open for 14% of the time, Pallas kernels for 38%

profile of v10, /device:TPU:0, one launch (start us, length us, event | category | flops | bytes accessed | tf_op | source)
XLA Modules:
  0.0 867.8 jit_solution(2792075070877377685)
XLA Ops:
  31.9 15.2 %collective-permute-done.7 = bf16[1,4,32,1024]{3,2,1,0:T(8,128)(2,1)} collective-permute-done((bf16[1,4,32,1024]{3,2,1,0:T(8,128)(2,1)}, bf16[1,4,32,1024]{3,2,1,0:T(8,128)(2,1)}, u32[]{:S(2)}, u32[]{:S(2)}) %collective-permute-start.7) | collective-permute-done | bytes 262176 | tf_op jit(solution)/shard_map/ppermute | solution.py:30
  53.2 11.8 %collective-permute-done.3 = f32[32,2816]{1,0:T(8,128)S(1)} collective-permute-done((f32[32,2816]{1,0:T(8,128)S(1)}, f32[32,2816]{1,0:T(8,128)S(1)}, u32[]{:S(2)}, u32[]{:S(2)}) %collective-permute-start.3) | collective-permute-done | bytes 360480 | tf_op jit(solution)/shard_map/ppermute | solution.py:30
  74.4 19.5 %collective-permute-done.10 = bf16[2,5,32,1024]{3,2,1,0:T(8,128)(2,1)S(1)} collective-permute-done((bf16[2,5,32,1024]{3,2,1,0:T(8,128)(2,1)S(1)}, bf16[2,5,32,1024]{3,2,1,0:T(8,128)(2,1)S(1)}, u32[]{:S(2)}, u32[]{:S(2)}) %collective-permute-start.10) | collective-permute-done | bytes 655392 | tf_op jit(solution)/shard_map/ppermute | solution.py:30
  103.1 10.6 %all-gather.4.cloned.1.call-done.wq_ref.wk_ref.wv_ref = bf16[1024,3072]{1,0:T(8,128)(2,1)} async-done(((bf16[32,3072]{1,0:T(8,128)(2,1)}), bf16[1024,3072]{1,0:T(8,128)(2,1)}) %all-gather.4.cloned.1.call-update) | async-done | bytes 6291472 | tf_op jit(solution)/shard_map/all_gather | solution.py:924
  166.5 35.4 %all-to-all-done = bf16[8,512,384]{2,1,0:T(8,128)(2,1)} async-done(((bf16[8,512,384]{2,1,0:T(8,128)(2,1)}), bf16[8,512,384]{2,1,0:T(8,128)(2,1)}, u32[]{:S(2)}, u32[]{:S(2)}) %all-to-all-start) | async-done | bytes 3145760 | tf_op jit(solution)/shard_map/all_to_all | solution.py:971
  216.1 35.3 %attend.3 = (bf16[4096,128]{1,0:T(8,128)(2,1)}, f32[4096,128]{1,0:T(8,128)}, f32[2,4096]{1,0:T(2,128)}) custom-call(bf16[4096,384]{1,0:T(8,128)(2,1)} %bitcast.37.qkv_ref), custom_call_target="tpu_custom_call" | custom-call | flops 17179869184 | bytes 6291456 | tf_op jit(solution)/shard_map/attend/pallas_call | solution.py:729
  251.3 10.3 %collective-permute-done.16 = f32[8,5632]{1,0:T(8,128)S(1)} collective-permute-done((f32[8,5632]{1,0:T(8,128)S(1)}, f32[8,5632]{1,0:T(8,128)S(1)}, u32[]{:S(2)}, u32[]{:S(2)}) %collective-permute-start.16) | collective-permute-done | bytes 180256 | tf_op jit(solution)/shard_map/ppermute | solution.py:30
  261.7 15.2 %all-to-all-done.1 = bf16[8,512,384]{2,1,0:T(8,128)(2,1)} async-done(((bf16[8,512,384]{2,1,0:T(8,128)(2,1)}), bf16[8,512,384]{2,1,0:T(8,128)(2,1)}, u32[]{:S(2)}, u32[]{:S(2)}) %all-to-all-start.1) | async-done | bytes 3145760 | tf_op jit(solution)/shard_map/all_to_all | solution.py:971
  284.5 35.3 %attend.2 = (bf16[4096,128]{1,0:T(8,128)(2,1)}, f32[4096,128]{1,0:T(8,128)}, f32[2,4096]{1,0:T(2,128)}) custom-call(bf16[4096,384]{1,0:T(8,128)(2,1)} %bitcast.35.qkv_ref), custom_call_target="tpu_custom_call" | custom-call | flops 17179869184 | bytes 6291456 | tf_op jit(solution)/shard_map/attend/pallas_call | solution.py:729
  326.8 38.2 %middle.2 = (bf16[2,512,1024]{2,1,0:T(8,128)(2,1)}, f32[512,1024]{1,0:T(8,128)}, bf16[512,1024]{1,0:T(8,128)(2,1)}, bf16[512,1024]{1,0:T(8,128)(2,1)}, bf16[512,...) custom-call(s32[1]{0:T(128)} %bitcast.clip_ref, ...), custom_call_target="tpu_custom_call" | custom-call | flops 2147483648 | bytes 4718592 | tf_op jit(solution)/shard_map/middle/pallas_call | solution.py:446
  375.6 38.2 %middle.3 = (bf16[2,512,1024]{2,1,0:T(8,128)(2,1)}, f32[512,1024]{1,0:T(8,128)}, bf16[512,1024]{1,0:T(8,128)(2,1)}, bf16[512,1024]{1,0:T(8,128)(2,1)}, bf16[512,...) custom-call(s32[1]{0:T(128)} %bitcast.clip_ref, ...), custom_call_target="tpu_custom_call", output_to_operand_aliasing={{0}: (20, {})} | custom-call | flops 2147483648 | bytes 4718592 | tf_op jit(solution)/shard_map/middle/pallas_call | solution.py:446
  420.3 59.2 %attend_back.2 = bf16[4096,384]{1,0:T(8,128)(2,1)} custom-call(bf16[4096,384]{1,0:T(8,128)(2,1)} %bitcast.37.qkv_ref, bf16[4096,128]{1,0:T(8,128)(2,1)} %bitcast.196, f32[4096,128]{1,0:T(8,128)} %get-tuple-element.127.full_ref, f32[2,4096]{1,0:T(2,128)} %get-tuple-element.128.log_ref, f32[4096,128]{1,0:T(8,128)} %bitcast.193, f32[4096,128]{1,0:T(8,128)} %bitcast.191), custom_call_target="tpu_custom_call" | custom-call | flops 42949672960 | bytes 13631488 | tf_op jit(solution)/shard_map/attend_back/pallas_call | solution.py:824
  479.5 20.5 %weight_grad.3 = (bf16[256,5120]{1,0:T(8,128)(2,1)}, bf16[256,5120]{1,0:T(8,128)(2,1)}, bf16[256,5120]{1,0:T(8,128)(2,1)}, bf16[256,5120]{1,0:T(8,128)(2,1)}) custom-call(s32[4]{0:T(128)} %pad_add_fusion.5.index_ref, bf16[512,1024]{1,0:T(8,128)(2,1)} %get-tuple-element.129.refs_0_.refs_1_.refs_2_.refs_3_, ...), custom_call_target="tpu_custom_call" | custom-call | flops 10737418240 | bytes 25165824 | tf_op jit(solution)/shard_map/weight_grad/pallas_call | solution.py:551
  512.9 59.1 %attend_back.3 = bf16[4096,384]{1,0:T(8,128)(2,1)} custom-call(bf16[4096,384]{1,0:T(8,128)(2,1)} %bitcast.35.qkv_ref, bf16[4096,128]{1,0:T(8,128)(2,1)} %bitcast.198, f32[4096,128]{1,0:T(8,128)} %get-tuple-element.140.full_ref, f32[2,4096]{1,0:T(2,128)} %get-tuple-element.141.log_ref, f32[4096,128]{1,0:T(8,128)} %bitcast.194, f32[4096,128]{1,0:T(8,128)} %bitcast.192), custom_call_target="tpu_custom_call" | custom-call | flops 42949672960 | bytes 13631488 | tf_op jit(solution)/shard_map/attend_back/pallas_call | solution.py:824
  593.6 17.6 %weight_grad.4 = (bf16[2,1024,512]{2,1,0:T(8,128)(2,1)}, bf16[1,1024,512]{2,1,0:T(8,128)(2,1)}, bf16[1,1024,512]{2,1,0:T(8,128)(2,1)}, bf16[2,1024,512]{2,1,0:T(...) custom-call(s32[8]{0:T(128)} %stack.141.index_ref, ...), custom_call_target="tpu_custom_call" | custom-call | flops 8589934592 | bytes 20971520 | tf_op jit(solution)/shard_map/weight_grad/pallas_call | solution.py:551
  614.8 9.2 %project_back.2 = (f32[2,512,1024]{2,1,0:T(8,128)}, bf16[512,3072]{1,0:T(8,128)(2,1)S(1)}, f32[2,2,1024]{2,1,0:T(2,128)S(1)}, f32[1,3072]{1,0:T(1,128)S(1)}) custom-call(bf16[8,512,384]{2,1,0:T(8,128)(2,1)S(1)} %copy-done.4, bf16[1024,3072]{1,0:T(8,128)(2,1)} %all-gather.4.cloned.1.call-done.wq_ref.wk_ref.wv_ref, ...), custom_call_target="tpu_custom_call" | custom-call | flops 3221225472 | bytes 17825792 | tf_op jit(solution)/shard_map/project_back/pallas_call | solution.py:263
  625.8 34.4 %all-to-all-done.6.back_ref = bf16[8,512,384]{2,1,0:T(8,128)(2,1)} async-done(((bf16[8,512,384]{2,1,0:T(8,128)(2,1)}), bf16[8,512,384]{2,1,0:T(8,128)(2,1)}, u32[]{:S(2)}, u32[]{:S(2)}) %all-to-all-start.6) | async-done | bytes 3145760 | tf_op jit(solution)/shard_map/all_to_all | solution.py:971
  661.8 9.8 %project_back.3 = (f32[2,512,1024]{2,1,0:T(8,128)}, bf16[512,3072]{1,0:T(8,128)(2,1)S(1)}, f32[2,2,1024]{2,1,0:T(2,128)S(1)}, f32[1,3072]{1,0:T(1,128)S(1)}) custom-call(bf16[8,512,384]{2,1,0:T(8,128)(2,1)} %all-to-all-done.6.back_ref, bf16[1024,3072]{1,0:T(8,128)(2,1)} %all-gather.4.cloned.1.call-done.wq_ref.wk_ref.wv_ref, ...), custom_call_target="tpu_custom_call", output_to_operand_aliasing={{0}: (7, {})} | custom-call | flops 3221225472 | bytes 17825792 | tf_op jit(solution)/shard_map/project_back/pallas_call | solution.py:263
  673.3 12.8 %weight_grad.5 = (bf16[256,3072]{1,0:T(8,128)(2,1)}, bf16[256,3072]{1,0:T(8,128)(2,1)}, bf16[256,3072]{1,0:T(8,128)(2,1)}, bf16[256,3072]{1,0:T(8,128)(2,1)}) custom-call(s32[4]{0:T(128)} %pad_add_fusion.5.index_ref, bf16[512,1024]{1,0:T(8,128)(2,1)} %copy-done.11, bf16[512,1024]{1,0:T(8,128)(2,1)} %copy-done.11, bf16[512,1024]{1,0:T(8,128)(2,1)} %copy-done.11, ...), custom_call_target="tpu_custom_call" | custom-call | flops 6442450944 | bytes 16777216 | tf_op jit(solution)/shard_map/weight_grad/pallas_call | solution.py:551
  703.0 16.2 %collective-permute-done.39 = bf16[128,5120]{1,0:T(8,128)(2,1)} collective-permute-done((bf16[128,5120]{1,0:T(8,128)(2,1)}, bf16[128,5120]{1,0:T(8,128)(2,1)}, u32[]{:S(2)}, u32[]{:S(2)}) %collective-permute-start.39) | collective-permute-done | bytes 1310752 | tf_op jit(solution)/shard_map/ppermute | solution.py:30
  745.1 19.0 %collective-permute-done.44 = bf16[2,1024,512]{2,1,0:T(8,128)(2,1)} collective-permute-done((bf16[2,1024,512]{2,1,0:T(8,128)(2,1)}, bf16[2,1024,512]{2,1,0:T(8,128)(2,1)}, u32[]{:S(2)}, u32[]{:S(2)}) %collective-permute-start.44) | collective-permute-done | bytes 2097184 | tf_op jit(solution)/shard_map/ppermute | solution.py:30
  766.0 14.9 %collective-permute-done.36 = bf16[128,3072]{1,0:T(8,128)(2,1)S(1)} collective-permute-done((bf16[128,3072]{1,0:T(8,128)(2,1)S(1)}, bf16[128,3072]{1,0:T(8,128)(2,1)S(1)}, u32[]{:S(2)}, u32[]{:S(2)}) %collective-permute-start.36) | collective-permute-done | bytes 786464 | tf_op jit(solution)/shard_map/ppermute | solution.py:30
  801.1 18.0 %collective-permute-done.34 = f32[32,2816]{1,0:T(8,128)} collective-permute-done((f32[32,2816]{1,0:T(8,128)}, f32[32,2816]{1,0:T(8,128)}, u32[]{:S(2)}, u32[]{:S(2)}) %collective-permute-start.34) | collective-permute-done | bytes 360480 | tf_op jit(solution)/shard_map/ppermute | solution.py:30
  845.4 12.7 %collective-permute-done.48 = bf16[1024,128]{1,0:T(8,128)(2,1)S(1)} collective-permute-done((bf16[1024,128]{1,0:T(8,128)(2,1)S(1)}, bf16[1024,128]{1,0:T(8,128)(2,1)S(1)}, u32[]{:S(2)}, u32[]{:S(2)}) %collective-permute-start.48) | collective-permute-done | bytes 262176 | tf_op jit(solution)/shard_map/ppermute | solution.py:30
  (401 shorter events, 283.4 us)
Async XLA Ops:
  7.2 106.5 %all-gather.4.cloned.1.call-start = ((), (), s32[]{:S(2)}) async-start(), calls=%async_computation.8 | async-start | bytes 6488064 | tf_op jit(solution)/shard_map/all_gather | solution.py:924
  31.9 98.5 %collective-permute-start.13 = (f32[64,5632]{1,0:T(8,128)}, f32[64,5632]{1,0:T(8,128)}, u32[]{:S(2)}, u32[]{:S(2)}) collective-permute-start(f32[64,5632]{1,0:T(8,128)} %constant_dynamic-slice_fusion.4), channel_id=1, source_target_pairs={{0,8},{8,0},{16,24},{24,16},{1,9},{9,1},{17,25},{25,17},{2,10},{10... | collective-permute-start | bytes 4325384 | tf_op jit(solution)/shard_map/ppermute | solution.py:30
  72.7 61.2 %collective-permute-start.11 = (bf16[4,4,32,1024]{3,2,1,0:T(8,128)(2,1)}, bf16[4,4,32,1024]{3,2,1,0:T(8,128)(2,1)}, u32[]{:S(2)}, u32[]{:S(2)}) collective-permute-start(bf16[4,4,32,1024]{3,2,1,0:T(8,128)(2,1)} %bitcast.18), channel_id=1, source_target_pairs={{0,1},{1,0},{2,3},{3,2},{4,5},{5,4},{6,7},{7,6},{8,9},{9,8},{10,11... | collective-permute-start | bytes 3145736 | tf_op jit(solution)/shard_map/ppermute | solution.py:30
  125.7 76.1 %all-to-all-start = ((bf16[8,512,384]{2,1,0:T(8,128)(2,1)}), bf16[8,512,384]{2,1,0:T(8,128)(2,1)}, u32[]{:S(2)}, u32[]{:S(2)}) async-start(bf16[8,512,384]{2,1,0:T(8,128)(2,1)} %copy-done.5), calls=%async_computation | async-start | bytes 6291456 | tf_op jit(solution)/shard_map/all_to_all | solution.py:971
  137.1 189.6 %collective-permute-start.23 = (bf16[4,2,4,32,1024]{4,3,2,1,0:T(8,128)(2,1)}, bf16[4,2,4,32,1024]{4,3,2,1,0:T(8,128)(2,1)}, u32[]{:S(2)}, u32[]{:S(2)}) collective-permute-start(bf16[4,2,4,32,1024]{4,3,2,1,0:T(8,128)(2,1)} %pad_maximum_fusion.2.refs_8_), channel_id=1, source_target_pairs={{0,8},{8,0},{16,24},{24,16},{1,9},{9,1},{17,25},{25,17},{2,10},{10... | collective-permute-start | bytes 6291464 | tf_op jit(solution)/shard_map/ppermute | solution.py:30
  137.1 182.6 %collective-permute-start.22 = (bf16[8,4,32,1024]{3,2,1,0:T(8,128)(2,1)}, bf16[8,4,32,1024]{3,2,1,0:T(8,128)(2,1)}, u32[]{:S(2)}, u32[]{:S(2)}) collective-permute-start(bf16[8,4,32,1024]{3,2,1,0:T(8,128)(2,1)} %bitcast.33), channel_id=1, source_target_pairs={{0,16},{8,24},{16,0},{24,8},{1,17},{9,25},{17,1},{25,9},{2,18},{10... | collective-permute-start | bytes 6291464 | tf_op jit(solution)/shard_map/ppermute | solution.py:30
  141.3 67.2 %collective-permute-start.20 = (bf16[4,2,5,32,1024]{4,3,2,0,1:T(8,128)(2,1)}, bf16[4,2,5,32,1024]{4,3,2,0,1:T(8,128)(2,1)}, u32[]{:S(2)}, u32[]{:S(2)}) collective-permute-start(bf16[4,2,5,32,1024]{4,3,2,0,1:T(8,128)(2,1)} %pad_maximum_fusion), channel_id=1, source_target_pairs={{0,8},{8,0},{16,24},{24,16},{1,9},{9,1},{17,25},{25,17},{2,10},{10... | collective-permute-start | bytes 7864328 | tf_op jit(solution)/shard_map/ppermute | solution.py:30
  141.5 64.8 %collective-permute-start.19 = (bf16[4,5,32,1024]{3,2,1,0:T(8,128)(2,1)}, bf16[4,5,32,1024]{3,2,1,0:T(8,128)(2,1)}, u32[]{:S(2)}, u32[]{:S(2)}) collective-permute-start(bf16[4,5,32,1024]{3,2,1,0:T(8,128)(2,1)} %collective-permute-done.12), channel_id=1, source_target_pairs={{0,1},{1,0},{2,3},{3,2},{4,5},{5,4},{6,7},{7,6},{8,9},{9,8},{10,11... | collective-permute-start | bytes 3932168 | tf_op jit(solution)/shard_map/ppermute | solution.py:30
  151.6 61.5 %collective-permute-start.15 = (f32[16,5632]{1,0:T(8,128)S(1)}, f32[16,5632]{1,0:T(8,128)}, u32[]{:S(2)}, u32[]{:S(2)}) collective-permute-start(f32[16,5632]{1,0:T(8,128)S(1)} %constant_dynamic-slice_fusion.2), channel_id=1, source_target_pairs={{0,1},{1,0},{2,3},{3,2},{4,5},{5,4},{6,7},{7,6},{8,9},{9,8},{10,11... | collective-permute-start | bytes 1081352 | tf_op jit(solution)/shard_map/ppermute | solution.py:30
  201.8 75.0 %all-to-all-start.1 = ((bf16[8,512,384]{2,1,0:T(8,128)(2,1)}), bf16[8,512,384]{2,1,0:T(8,128)(2,1)}, u32[]{:S(2)}, u32[]{:S(2)}) async-start(bf16[8,512,384]{2,1,0:T(8,128)(2,1)} %copy-done.6), calls=%async_computation.1 | async-start | bytes 6291456 | tf_op jit(solution)/shard_map/all_to_all | solution.py:971
  214.1 47.5 %collective-permute-start.16 = (f32[8,5632]{1,0:T(8,128)S(1)}, f32[8,5632]{1,0:T(8,128)S(1)}, u32[]{:S(2)}, u32[]{:S(2)}) collective-permute-start(f32[8,5632]{1,0:T(8,128)S(1)} %constant_dynamic-slice_fusion.1), channel_id=1, source_target_pairs={{0,2},{1,3},{2,0},{3,1},{4,6},{5,7},{6,4},{7,5},{8,10},{9,11},{10,... | collective-permute-start | bytes 540680 | tf_op jit(solution)/shard_map/ppermute | solution.py:30
  276.8 43.4 %all-to-all-start.2 = ((bf16[8,512,128]{2,1,0:T(8,128)(2,1)}), bf16[8,512,128]{2,1,0:T(8,128)(2,1)}, u32[]{:S(2)}, u32[]{:S(2)}) async-start(bf16[8,512,128]{2,1,0:T(8,128)(2,1)} %bitcast.199), calls=%async_computation.2 | async-start | bytes 2097152 | tf_op jit(solution)/shard_map/all_to_all | solution.py:971
  284.5 42.3 %collective-permute-start.21 = (bf16[4,2,5,32,1024]{4,3,2,1,0:T(8,128)(2,1)S(1)}, bf16[4,2,5,32,1024]{4,3,2,1,0:T(8,128)(2,1)}, u32[]{:S(2)}, u32[]{:S(2)}) collective-permute-start(bf16[4,2,5,32,1024]{4,3,2,1,0:T(8,128)(2,1)S(1)} %pad_maximum_fusion.1.refs_1_.refs_5_), channel_id=1, source_target_pairs={{0,8},{8,0},{16,24},{24,16},{1,9},{9,1},{17,25},{25,17},{2,10},{10... | collective-permute-start | bytes 7864328 | tf_op jit(solution)/shard_map/ppermute | solution.py:30
  320.3 44.8 %all-to-all-start.3 = ((bf16[8,512,128]{2,1,0:T(8,128)(2,1)}), bf16[8,512,128]{2,1,0:T(8,128)(2,1)}, u32[]{:S(2)}, u32[]{:S(2)}) async-start(bf16[8,512,128]{2,1,0:T(8,128)(2,1)} %bitcast.197), calls=%async_computation.3 | async-start | bytes 2097152 | tf_op jit(solution)/shard_map/all_to_all | solution.py:971
  365.0 48.8 %all-to-all-start.4 = ((bf16[8,512,128]{2,1,0:T(8,128)(2,1)}), bf16[8,512,128]{2,1,0:T(8,128)(2,1)S(1)}, u32[]{:S(2)}, u32[]{:S(2)}) async-start(bf16[8,512,128]{2,1,0:T(8,128)(2,1)} %get-tuple-element.122), calls=%async_computation.4 | async-start | bytes 2097152 | tf_op jit(solution)/shard_map/all_to_all | solution.py:971
  413.9 65.6 %all-to-all-start.5 = ((bf16[8,512,128]{2,1,0:T(8,128)(2,1)}), bf16[8,512,128]{2,1,0:T(8,128)(2,1)S(1)}, u32[]{:S(2)}, u32[]{:S(2)}) async-start(bf16[8,512,128]{2,1,0:T(8,128)(2,1)} %get-tuple-element.123), calls=%async_computation.5 | async-start | bytes 2097152 | tf_op jit(solution)/shard_map/all_to_all | solution.py:971
  500.2 77.5 %all-to-all-start.7 = ((bf16[8,512,384]{2,1,0:T(8,128)(2,1)}), bf16[8,512,384]{2,1,0:T(8,128)(2,1)S(1)}, u32[]{:S(2)}, u32[]{:S(2)}) async-start(bf16[8,512,384]{2,1,0:T(8,128)(2,1)} %bitcast.188), calls=%async_computation.7 | async-start | bytes 6291456 | tf_op jit(solution)/shard_map/all_to_all | solution.py:971
  511.5 60.5 %collective-permute-start.26 = (bf16[256,5120]{1,0:T(8,128)(2,1)}, bf16[256,5120]{1,0:T(8,128)(2,1)}, u32[]{:S(2)}, u32[]{:S(2)}) collective-permute-start(bf16[256,5120]{1,0:T(8,128)(2,1)} %add_convert_fusion), channel_id=1, source_target_pairs={{0,16},{8,24},{16,0},{24,8},{1,17},{9,25},{17,1},{25,9},{2,18},{10... | collective-permute-start | bytes 7864328 | tf_op jit(solution)/shard_map/ppermute | solution.py:30
  579.4 80.8 %all-to-all-start.6 = ((bf16[8,512,384]{2,1,0:T(8,128)(2,1)}), bf16[8,512,384]{2,1,0:T(8,128)(2,1)}, u32[]{:S(2)}, u32[]{:S(2)}) async-start(bf16[8,512,384]{2,1,0:T(8,128)(2,1)} %bitcast.187), calls=%async_computation.6 | async-start | bytes 6291456 | tf_op jit(solution)/shard_map/all_to_all | solution.py:971
  583.9 105.8 %all-gather.6.cloned.1.call-start = ((), (), s32[]{:S(2)}) async-start(), calls=%async_computation.9 | async-start | bytes 2973696 | tf_op jit(solution)/shard_map/all_gather | solution.py:1039
  611.2 82.3 %collective-permute-start.43 = (bf16[2,1024,512]{2,1,0:T(8,128)(2,1)}, bf16[2,1024,512]{2,1,0:T(8,128)(2,1)}, u32[]{:S(2)}, u32[]{:S(2)}) collective-permute-start(bf16[2,1024,512]{2,1,0:T(8,128)(2,1)} %get-tuple-element.154), channel_id=1, source_target_pairs={{0,8},{8,0},{16,24},{24,16},{1,9},{9,1},{17,25},{25,17},{2,10},{10... | collective-permute-start | bytes 6291464 | tf_op jit(solution)/shard_map/ppermute | solution.py:30
  702.4 61.7 %collective-permute-start.44 = (bf16[2,1024,512]{2,1,0:T(8,128)(2,1)}, bf16[2,1024,512]{2,1,0:T(8,128)(2,1)}, u32[]{:S(2)}, u32[]{:S(2)}) collective-permute-start(bf16[2,1024,512]{2,1,0:T(8,128)(2,1)} %add_convert_fusion.1), channel_id=1, source_target_pairs={{0,1},{1,0},{2,3},{3,2},{4,5},{5,4},{6,7},{7,6},{8,9},{9,8},{10,11... | collective-permute-start | bytes 6291464 | tf_op jit(solution)/shard_map/ppermute | solution.py:30
  738.1 42.8 %collective-permute-start.36 = (bf16[128,3072]{1,0:T(8,128)(2,1)S(1)}, bf16[128,3072]{1,0:T(8,128)(2,1)S(1)}, u32[]{:S(2)}, u32[]{:S(2)}) collective-permute-start(bf16[128,3072]{1,0:T(8,128)(2,1)S(1)} %add_convert_fusion.5), channel_id=1, source_target_pairs={{0,1},{1,0},{2,3},{3,2},{4,5},{5,4},{6,7},{7,6},{8,9},{9,8},{10,11... | collective-permute-start | bytes 2359304 | tf_op jit(solution)/shard_map/ppermute | solution.py:30
  743.6 52.9 %collective-permute-start.41 = (bf16[32,5120]{1,0:T(8,128)(2,1)S(1)}, bf16[32,5120]{1,0:T(8,128)(2,1)S(1)}, u32[]{:S(2)}, u32[]{:S(2)}) collective-permute-start(bf16[32,5120]{1,0:T(8,128)(2,1)S(1)} %add_convert_fusion.8), channel_id=1, source_target_pairs={{0,4},{1,5},{2,6},{3,7},{4,0},{5,1},{6,2},{7,3},{8,12},{9,13},{10,... | collective-permute-start | bytes 983048 | tf_op jit(solution)/shard_map/ppermute | solution.py:30
  (95 other events, 1497.9 us)
Sparse Core Ops, SparseCore 0:
  16.1 97.5 all-gather.3
  588.1 93.2 all-gather.5
